TPU v7x, 32 devices: a whole 2x2x4 slice. The times are simulated.
32 devices in a mesh: tm: 8 (over z, x), chan: 4 (over y, core).
Axes of the slice: x: 2, y: 2, z: 4, core: 2. Of those that a mesh axis runs over, the one named last changes fastest.
Arguments:
- analysis_dep: bfloat16 [8, 1664, 2048], P('tm', 'chan')
- background_dep: bfloat16 [8, 1664, 2048], P('tm', 'chan')
- valid_counts: int32 [8], replicated, may hold values from 1 to 2048, as said below
Outputs:
- lag_covariance: float32 [1664, 5, 1664], P('tm', None, 'chan')
Inputs may be any that keep to these rules, and one draw needn't show every extreme that they name: valid_counts of the last cycle is 2048.
All inputs are finite; a program needn't handle non-finite values.
Results may differ from a plain program's by a relative error of at most 0.0003.
Values may be sent and summed in bfloat16 or wider, within the bound.
No kernel may reach another device: no remote copies, remote signals or barrier semaphores. Data moves between devices by JAX's collectives and lax.ppermute only.
A program may use at most 128 MiB of HBM per device.

v0:
```python
import jax
import jax.numpy as jnp
from jax import lax
from jax.sharding import PartitionSpec as P

MAXLAG = 2


def shifted(array, axis, by):
    peers = lax.axis_size(axis)
    pairs = [(i, i + by) for i in range(peers) if 0 <= i + by < peers]
    return lax.ppermute(array, axis, pairs)


def contract(left_rows, stacked):
    return lax.dot_general(
        left_rows, stacked, (((1,), (1,)), ((), ())), preferred_element_type=jnp.float32
    )


def body(analysis_dep, background_dep, valid_counts):
    cycle_total = valid_counts.shape[0]
    cycle_index = lax.axis_index("tm")
    own_count = jnp.sum(
        jnp.where(jnp.arange(cycle_total, dtype=jnp.int32) == cycle_index, valid_counts, 0)
    )
    loc_total = analysis_dep.shape[2]
    valid_cols = (jnp.arange(loc_total, dtype=jnp.int32) < own_count)[None, :]
    local_analysis = jnp.where(valid_cols, analysis_dep[0], jnp.zeros((), jnp.bfloat16))
    local_background = jnp.where(valid_cols, background_dep[0], jnp.zeros((), jnp.bfloat16))
    width_block = local_analysis.shape[0]
    lag_total = 2 * MAXLAG + 1
    pieces = [None] * lag_total
    pieces[MAXLAG] = local_analysis
    for offset in range(1, MAXLAG + 1):
        pieces[MAXLAG + offset] = shifted(local_analysis, "tm", offset)
        pieces[MAXLAG - offset] = shifted(local_analysis, "tm", -offset)
    stacked = jnp.concatenate(pieces, axis=0)
    denominators = []
    for offset in range(MAXLAG + 1):
        span = cycle_total - offset
        denominators.append(
            jnp.sum(jnp.minimum(valid_counts[:span], valid_counts[offset:])).astype(jnp.float32)
        )
    ordered = [denominators[abs(position - MAXLAG)] for position in range(lag_total)]
    divisor = jnp.stack(ordered)
    full_background = lax.all_gather(local_background, "chan", axis=0, tiled=True)
    partial_value = contract(full_background, stacked)
    summed = lax.psum_scatter(partial_value, "tm", scatter_dimension=0, tiled=True)
    shaped = summed.reshape(summed.shape[0], lag_total, width_block)
    return shaped / divisor[None, :, None]


def solution(mesh):
    in_specs = (P("tm", "chan", None), P("tm", "chan", None), P())
    out_specs = P("tm", None, "chan")
    return jax.shard_map(body, mesh=mesh, in_specs=in_specs, out_specs=out_specs, check_vma=False)
```

profile of v0, /device:TPU:0, one launch (start us, length us, event | category | flops | bytes accessed | tf_op | source)
XLA Modules:
  0.0 369.7 jit_solution(3590126342833992693)
XLA Ops:
  6.5 1.4 fusion.1
  7.9 0.7 iota_compare_fusion
  8.6 3.4 bitcast_select_fusion
  11.9 0.0 all-gather.2.cloned.1.call-update
  12.0 0.0 reduce-scatter.2.cloned.1.call-start
  12.0 1.3 collective-permute-start
  13.3 1.3 collective-permute-start.1
  14.6 5.6 %collective-permute-start.2 = (bf16[416,2048]{1,0:T(8,128)(2,1)S(1)}, bf16[416,2048]{1,0:T(8,128)(2,1)S(1)}, u32[]{:S(2)}, u32[]{:S(2)}) collective-permute-start(bf16[416,2048]{1,0:T(8,128)(2,1)S(1)} %get-tuple-element.7), channel_id=1, source_target_pairs={{0,4},{4,8},{8,12},{12,16},{16,20},{20,24},{24,28},{1,5},{5,9},{9,... | collective-permute-start | bytes 5111816 | tf_op jit(solution)/shard_map/ppermute | solution.py:12
  20.2 4.6 %collective-permute-start.3 = (bf16[416,2048]{1,0:T(8,128)(2,1)S(1)}, bf16[416,2048]{1,0:T(8,128)(2,1)S(1)}, u32[]{:S(2)}, u32[]{:S(2)}) collective-permute-start(bf16[416,2048]{1,0:T(8,128)(2,1)S(1)} %get-tuple-element.7), channel_id=1, source_target_pairs={{0,8},{4,12},{8,16},{12,20},{16,24},{20,28},{1,9},{5,13},{9,17},{1... | collective-permute-start | bytes 5111816 | tf_op jit(solution)/shard_map/ppermute | solution.py:12
  24.8 30.1 %collective-permute-done = bf16[416,2048]{1,0:T(8,128)(2,1)S(1)} collective-permute-done((bf16[416,2048]{1,0:T(8,128)(2,1)S(1)}, bf16[416,2048]{1,0:T(8,128)(2,1)S(1)}, u32[]{:S(2)}, u32[]{:S(2)}) %collective-permute-start) | collective-permute-done | bytes 1703968 | tf_op jit(solution)/shard_map/ppermute | solution.py:12
  55.0 1.3 constant_dynamic-update-slice_fusion.4
  56.3 1.3 constant_dynamic-update-slice_fusion.3
  57.6 1.3 constant_dynamic-update-slice_fusion.2
  58.9 34.1 %collective-permute-done.2 = bf16[416,2048]{1,0:T(8,128)(2,1)S(1)} collective-permute-done((bf16[416,2048]{1,0:T(8,128)(2,1)S(1)}, bf16[416,2048]{1,0:T(8,128)(2,1)S(1)}, u32[]{:S(2)}, u32[]{:S(2)}) %collective-permute-start.2) | collective-permute-done | bytes 1703968 | tf_op jit(solution)/shard_map/ppermute | solution.py:12
  93.1 1.3 constant_dynamic-update-slice_fusion.1
  94.4 1.3 constant_dynamic-update-slice_fusion
  95.7 22.7 %fusion.2 = f32[1664,2080]{1,0:T(8,128)} fusion(bf16[1664,2048]{1,0:T(8,128)(2,1)} %all-gather.2.cloned.1.call-done, bf16[2080,2048]{1,0:T(8,128)(2,1)} %constant_dynamic-update-slice_fusion), kind=kOutput, calls=%fused_computation.14 | convolution fusion | flops 14176747520 | bytes 29179904 | tf_op jit(solution)/shard_map/dot_general | solution.py:16
  119.1 0.7 minimum_reduce_fusion.1
  120.5 0.7 minimum_reduce_fusion
  121.8 0.1 stack.17
  121.9 234.2 %reduce-scatter.2.cloned.1.call-done = f32[208,2080]{1,0:T(8,128)} async-done(((f32[1664,2080]{1,0:T(8,128)}), f32[208,2080]{1,0:T(8,128)}) %reduce-scatter.2.cloned.1.call-update) | async-done | bytes 1730576 | tf_op jit(solution)/shard_map/reduce_scatter | solution.py:49
  356.1 2.9 copy.5
  359.0 1.8 broadcast_divide_fusion
  360.8 2.0 copy.6
  (7 shorter events, 0.0 us)
Async XLA Ops:
  6.5 89.2 %all-gather.2.cloned.1.call-start = ((), (), s32[]{:S(2)}) async-start(), calls=%async_computation.1 | async-start | bytes 8519680 | tf_op jit(solution)/shard_map/all_gather | solution.py:47
  12.0 344.1 %reduce-scatter.2.cloned.1.call-start = ((), (), s32[]{:S(2)}) async-start(), calls=%async_computation.2 | async-start | bytes 16293888 | tf_op jit(solution)/shard_map/reduce_scatter | solution.py:49
  12.0 43.0 %collective-permute-start = (bf16[416,2048]{1,0:T(8,128)(2,1)S(1)}, bf16[416,2048]{1,0:T(8,128)(2,1)S(1)}, u32[]{:S(2)}, u32[]{:S(2)}) collective-permute-start(bf16[416,2048]{1,0:T(8,128)(2,1)S(1)} %get-tuple-element.7), channel_id=1, source_target_pairs={{8,0},{12,4},{16,8},{20,12},{24,16},{28,20},{9,1},{13,5},{17,9},{2... | collective-permute-start | bytes 5111816 | tf_op jit(solution)/shard_map/ppermute | solution.py:12
  13.3 43.0 %collective-permute-start.1 = (bf16[416,2048]{1,0:T(8,128)(2,1)S(1)}, bf16[416,2048]{1,0:T(8,128)(2,1)S(1)}, u32[]{:S(2)}, u32[]{:S(2)}) collective-permute-start(bf16[416,2048]{1,0:T(8,128)(2,1)S(1)} %get-tuple-element.7), channel_id=1, source_target_pairs={{4,0},{8,4},{12,8},{16,12},{20,16},{24,20},{28,24},{5,1},{9,5},{13... | collective-permute-start | bytes 5111816 | tf_op jit(solution)/shard_map/ppermute | solution.py:12
  14.6 78.4 %collective-permute-start.2 = (bf16[416,2048]{1,0:T(8,128)(2,1)S(1)}, bf16[416,2048]{1,0:T(8,128)(2,1)S(1)}, u32[]{:S(2)}, u32[]{:S(2)}) collective-permute-start(bf16[416,2048]{1,0:T(8,128)(2,1)S(1)} %get-tuple-element.7), channel_id=1, source_target_pairs={{0,4},{4,8},{8,12},{12,16},{16,20},{20,24},{24,28},{1,5},{5,9},{9,... | collective-permute-start | bytes 5111816 | tf_op jit(solution)/shard_map/ppermute | solution.py:12
  20.2 74.2 %collective-permute-start.3 = (bf16[416,2048]{1,0:T(8,128)(2,1)S(1)}, bf16[416,2048]{1,0:T(8,128)(2,1)S(1)}, u32[]{:S(2)}, u32[]{:S(2)}) collective-permute-start(bf16[416,2048]{1,0:T(8,128)(2,1)S(1)} %get-tuple-element.7), channel_id=1, source_target_pairs={{0,8},{4,12},{8,16},{12,20},{16,24},{20,28},{1,9},{5,13},{9,17},{1... | collective-permute-start | bytes 5111816 | tf_op jit(solution)/shard_map/ppermute | solution.py:12
  118.4 0.7 copy-start
Sparse Core Ops, SparseCore 0:
  12.1 52.0 all-gather.1
  118.5 237.5 reduce-scatter.1
where the time goes:
time: 370 us
  waiting for transfers between devices  298 us (81%)
  matrix products  22.7 us (6%)
  between operations  15.5 us (4%)
  starting transfers between devices  12.8 us (3%)
  local copies, waits for them, and re-layouts  11.6 us (3%)
  other arithmetic  8.65 us (2%)
    reduce_scatter x1, waiting for transfers between devices, body(): lax.psum_scatter(partial_value, 'tm', scatter_dimension=0, tiled=True)  234 us
    ppermute x4, waiting for transfers between devices, shifted(): return lax.ppermute(array, axis, pairs)  64.3 us
    dot_general x1, matrix products, contract(): lax.dot_general(left_rows, stacked, (((1,), (1,)), ((), ())), preferred_e...  22.7 us
    ppermute x4, starting transfers between devices, shifted(): return lax.ppermute(array, axis, pairs)  12.8 us
  transfers between devices with their start and end apart: 6, of which 3 were waited for; matrix products, arithmetic and copies ran while one was open for 2% of the time, Pallas kernels for 0%

commit v1 on v0

v1 whole, which is shorter than its diff:
```python
import jax
import jax.numpy as jnp
from jax import lax
from jax.sharding import PartitionSpec as P


def contract(left, right):
    return lax.dot_general(
        left, right, (((0, 2), (0, 2)), ((), ())), preferred_element_type=jnp.float32
    )


def body(analysis_dep, background_dep, valid_counts):
    cycle_total = valid_counts.shape[0]
    tm_size = lax.axis_size("tm")
    chan_size = lax.axis_size("chan")
    lag_total = 5
    max_lag = (lag_total - 1) // 2
    cycle_index = lax.axis_index("tm")
    own_count = jnp.sum(
        jnp.where(jnp.arange(cycle_total, dtype=jnp.int32) == cycle_index, valid_counts, 0)
    )
    _, width_block, loc_total = analysis_dep.shape
    chan_total = width_block * chan_size
    row_block = chan_total // tm_size
    valid_cols = (jnp.arange(loc_total, dtype=jnp.int32) < own_count)[None, :]
    local_analysis = jnp.where(valid_cols, analysis_dep[0], jnp.zeros((), jnp.bfloat16))
    local_background = jnp.where(valid_cols, background_dep[0], jnp.zeros((), jnp.bfloat16))

    all_analysis = lax.all_gather(local_analysis, "tm", axis=0, tiled=False)

    by_loc = lax.all_to_all(local_background, "chan", 1, 0, tiled=True)
    by_loc = by_loc.reshape(tm_size, row_block, loc_total // chan_size)
    rows_here = lax.all_to_all(by_loc, "tm", 0, 0, tiled=True)
    all_background = lax.all_gather(rows_here, "chan", axis=2, tiled=True)

    pieces = [None] * lag_total
    for offset in range(max_lag + 1):
        span = cycle_total - offset
        pairs = jnp.sum(jnp.minimum(valid_counts[:span], valid_counts[offset:])).astype(jnp.float32)
        forward = contract(all_background[offset:], all_analysis[:span])
        pieces[max_lag + offset] = forward / pairs
        if offset > 0:
            backward = contract(all_background[:span], all_analysis[offset:])
            pieces[max_lag - offset] = backward / pairs
    return jnp.stack(pieces, axis=1)


def solution(mesh):
    in_specs = (P("tm", "chan", None), P("tm", "chan", None), P())
    out_specs = P("tm", None, "chan")
    return jax.shard_map(body, mesh=mesh, in_specs=in_specs, out_specs=out_specs, check_vma=False)
```

time: 370 us -> 378 us (1.022)
  blocking collectives: 0 us -> 71 us
  waiting for transfers between devices: 298 us -> 233 us
  matrix products: 22.7 us -> 46.1 us
  starting transfers between devices: 12.8 us -> 0.22 us
  local copies, waits for them, and re-layouts: 11.6 us -> 5.29 us
    reduce_scatter x1 -> x0, waiting for transfers between devices: 234 us -> none  [body(): lax.psum_scatter(partial_value, 'tm', scatter_dimension=0, tiled=True)]
    all_gather x1 -> x2, waiting for transfers between devices: 0.01 us -> 233 us  [the longest x1 191 us: body(): all_analysis = lax.all_gather(local_analysis, 'tm', axis=0, tiled=False)]
    all_to_all x0 -> x2, blocking collectives: none -> 71 us  [the longest x1 45.5 us: body(): rows_here = lax.all_to_all(by_loc, 'tm', 0, 0, tiled=True)]
    ppermute x4 -> x0, waiting for transfers between devices: 64.3 us -> none  [shifted(): return lax.ppermute(array, axis, pairs)]
    dot_general x1 -> x5, matrix products: 22.7 us -> 46.1 us  [contract(): lax.dot_general(left, right, (((0, 2), (0, 2)), ((), ())), preferred_elem...]
    ppermute x4 -> x0, starting transfers between devices: 12.8 us -> none  [shifted(): return lax.ppermute(array, axis, pairs)]
    squeeze x0 -> x1, local copies, waits for them, and re-layouts: none -> 3.94 us  [body(): background_dep[0]]
    unnamed x6 -> x12, local copies, waits for them, and re-layouts: 5.27 us -> 1.35 us
  transfers between devices with their start and end apart: 6 -> 2, of which waited for: 3 -> 2; matrix products, arithmetic and copies ran while one was open for 2% -> 1% of each run, Pallas kernels for 0% -> 0%
where the time goes in v1:
time: 378 us
  waiting for transfers between devices  233 us (62%)
  blocking collectives  71 us (19%)
  matrix products  46.1 us (12%)
  between operations  15.4 us (4%)
  other arithmetic  6.12 us (2%)
  local copies, waits for them, and re-layouts  5.29 us (1%)
    all_gather x1, waiting for transfers between devices, body(): all_analysis = lax.all_gather(local_analysis, 'tm', axis=0, tiled=False)  191 us
    dot_general x5, matrix products, contract(): lax.dot_general(left, right, (((0, 2), (0, 2)), ((), ())), preferred_elem...  46.1 us
    all_to_all x1, blocking collectives, body(): rows_here = lax.all_to_all(by_loc, 'tm', 0, 0, tiled=True)  45.5 us
    all_gather x1, waiting for transfers between devices, body(): all_background = lax.all_gather(rows_here, 'chan', axis=2, tiled=True)  41.8 us
    all_to_all x1, blocking collectives, body(): by_loc = lax.all_to_all(local_background, 'chan', 1, 0, tiled=True)  25.5 us
  transfers between devices with their start and end apart: 2, of which 2 were waited for; matrix products, arithmetic and copies ran while one was open for 1% of the time, Pallas kernels for 0%

profile of v1, /device:TPU:0, one launch (start us, length us, event | category | flops | bytes accessed | tf_op | source)
XLA Modules:
  0.0 377.5 jit_solution(10194569140651699854)
XLA Ops:
  6.5 1.3 fusion.60
  7.9 0.7 add_compare_fusion
  8.5 3.9 %squeeze.4 = bf16[416,4,512]{2,1,0:T(4,128)(2,1)S(1)} reshape(bf16[1,416,2048]{2,1,0:T(8,128)(2,1)} %param.4) | data formatting | bytes 3407872 | tf_op jit(solution)/shard_map/squeeze | solution.py:28
  12.5 0.0 copy-start
  12.5 0.7 copy_select_fusion
  13.1 0.0 copy-start.1
  13.2 25.5 %all_to_all.18 = bf16[416,4,512]{2,0,1:T(8,128)(2,1)S(1)} all-to-all(bf16[416,4,512]{2,0,1:T(8,128)(2,1)S(1)} %copy_select_fusion), channel_id=1, replica_groups=mesh['tm'=8,'chan'=4] {'chan'}, dimensions={1} | all-to-all | bytes 3407872 | tf_op jit(solution)/shard_map/all_to_all | solution.py:32
  38.7 45.5 %all_to_all.19 = bf16[8,208,512]{2,1,0:T(8,128)(2,1)} all-to-all(bf16[8,208,512]{2,1,0:T(8,128)(2,1)S(1)} %bitcast.69), channel_id=1, replica_groups=mesh['tm'=8,'chan'=4] {'tm'}, dimensions={0} | all-to-all | bytes 3407872 | tf_op jit(solution)/shard_map/all_to_all | solution.py:34
  84.2 0.0 all-gather.3.cloned.1.call-update
  84.2 0.2 all-gather.5.cloned.1.call-start
  84.5 0.7 iota_compare_fusion
  85.1 1.3 broadcast_select_fusion
  86.4 0.0 all-gather.5.cloned.1.call-update
  86.5 0.8 minimum_reduce_fusion.1
  87.9 0.8 minimum_reduce_fusion
  89.9 41.8 %all-gather.3.cloned.1.call-done = bf16[8,208,2048]{2,1,0:T(8,128)(2,1)} async-done(((bf16[8,208,512]{2,1,0:T(8,128)(2,1)}), bf16[8,208,2048]{2,1,0:T(8,128)(2,1)}) %all-gather.3.cloned.1.call-update) | async-done | bytes 6815760 | tf_op jit(solution)/shard_map/all_gather | solution.py:35
  131.7 191.4 %all-gather.5.cloned.1.call-done = bf16[8,416,2048]{2,1,0:T(8,128)(2,1)} async-done(((bf16[1,416,2048]{2,1,0:T(8,128)(2,1)}), bf16[8,416,2048]{2,1,0:T(8,128)(2,1)}) %all-gather.5.cloned.1.call-update) | async-done | bytes 13631504 | tf_op jit(solution)/shard_map/all_gather | solution.py:30
  323.1 8.8 %fusion.38 = f32[208,5,416]{2,0,1:T(8,128)S(1)} fusion(bf16[8,208,2048]{2,1,0:T(8,128)(2,1)} %all-gather.3.cloned.1.call-done, bf16[8,416,2048]{2,1,0:T(8,128)(2,1)} %all-gather.5.cloned.1.call-done, f32[]{:T(128)S(6)} %convert_element_type.9), kind=kOutput, calls=%fused_computation.23 | convolution fusion | flops 2126598656 | bytes 17465348 | tf_op jit(solution)/shard_map/dot_general | solution.py:8
  331.9 8.1 %fusion.56 = f32[208,5,416]{2,0,1:T(8,128)S(1)} fusion(f32[208,5,416]{2,0,1:T(8,128)S(1)} %fusion.38, bf16[8,208,2048]{2,1,0:T(8,128)(2,1)S(1)} %copy-done.2, bf16[8,416,2048]{2,1,0:T(8,128)(2,1)} %all-gather.5.cloned.1.call-done, f32[]{:T(128)S(6)} %convert_element_type.10), kind=kOutput, calls=%fused_computation.29 | convolution fusion | flops 2481017344 | bytes 19169284 | tf_op jit(solution)/shard_map/dot_general | solution.py:8
  340.1 11.1 %fusion.22 = f32[208,5,416]{2,0,1:T(8,128)S(1)} fusion(f32[208,5,416]{2,0,1:T(8,128)S(1)} %fusion.56, bf16[8,208,2048]{2,1,0:T(8,128)(2,1)} %all-gather.3.cloned.1.call-done, bf16[8,416,2048]{2,1,0:T(8,128)(2,1)} %all-gather.5.cloned.1.call-done, f32[]{:T(128)S(6)} %convert_element_type.11), kind=kOutput, calls=%fused_computation.17 | convolution fusion | flops 2835436032 | bytes 20873220 | tf_op jit(solution)/shard_map/dot_general | solution.py:8
  351.2 10.2 %fusion.47 = f32[208,5,416]{2,0,1:T(8,128)S(1)} fusion(f32[208,5,416]{2,0,1:T(8,128)S(1)} %fusion.22, bf16[8,208,2048]{2,1,0:T(8,128)(2,1)} %all-gather.3.cloned.1.call-done, bf16[8,416,2048]{2,1,0:T(8,128)(2,1)} %all-gather.5.cloned.1.call-done, f32[]{:T(128)S(6)} %convert_element_type.10), kind=kOutput, calls=%fused_computation.26 | convolution fusion | flops 2481017344 | bytes 19169284 | tf_op jit(solution)/shard_map/dot_general | solution.py:8
  361.4 0.0 copy-start.3
  361.5 1.3 copy-done.3
  362.8 7.9 %fusion.29 = f32[208,5,416]{2,0,1:T(8,128)} fusion(f32[208,5,416]{2,0,1:T(8,128)} %copy-done.3, bf16[8,208,2048]{2,1,0:T(8,128)(2,1)S(1)} %bitcast.71, bf16[8,416,2048]{2,1,0:T(8,128)(2,1)} %all-gather.5.cloned.1.call-done, f32[]{:T(128)S(6)} %convert_element_type.9), kind=kOutput, calls=%fused_computation.20 | convolution fusion | flops 2126598656 | bytes 17465348 | tf_op jit(solution)/shard_map/dot_general | solution.py:8
  (10 shorter events, 0.0 us)
Async XLA Ops:
  6.5 125.2 %all-gather.3.cloned.1.call-start = ((), (), s32[]{:S(2)}) async-start(), calls=%async_computation.2 | async-start | bytes 8519680 | tf_op jit(solution)/shard_map/all_gather | solution.py:35
  12.5 72.7 %copy-start = (bf16[1,416,2048]{2,1,0:T(8,128)(2,1)S(1)}, bf16[1,416,2048]{2,1,0:T(8,128)(2,1)}, u32[]{:S(2)}) copy-start(bf16[1,416,2048]{2,1,0:T(8,128)(2,1)} %param.3) | copy-start | bytes 5111812
  13.1 73.3 %copy-start.1 = (s32[8]{0:T(128)S(1)}, s32[8]{0:T(128)}, u32[]{:S(2)}) copy-start(s32[8]{0:T(128)} %param.5) | copy-start | bytes 100
  84.2 238.9 %all-gather.5.cloned.1.call-start = ((), (), s32[]{:S(2)}) async-start(), calls=%async_computation.3 | async-start | bytes 15335424 | tf_op jit(solution)/shard_map/all_gather | solution.py:30
  323.1 8.8 %copy-start.2 = (bf16[8,208,2048]{2,1,0:T(8,128)(2,1)S(1)}, bf16[8,208,2048]{2,1,0:T(8,128)(2,1)}, u32[]{:S(2)}) copy-start(bf16[8,208,2048]{2,1,0:T(8,128)(2,1)} %all-gather.3.cloned.1.call-done) | copy-start | bytes 20447236
  340.1 22.7 %slice-start = ((s8[6815744]{0:T(1024)(128)(4,1)}), s8[2621440]{0:T(1024)(128)(4,1)S(1)}, s32[]{:S(2)}) async-start(s8[6815744]{0:T(1024)(128)(4,1)} %bitcast.70), calls=%async_computation.4 | async-start | bytes 5242880
  351.2 11.5 %slice-start.1 = ((s8[6815744]{0:T(1024)(128)(4,1)}), s8[4194304]{0:T(1024)(128)(4,1)S(1)}, s32[]{:S(2)}) async-start(s8[6815744]{0:T(1024)(128)(4,1)} %bitcast.70), calls=%async_computation.5 | async-start | bytes 8388608
  361.4 1.3 copy-start.3
Sparse Core Ops, SparseCore 0:
  84.3 47.3 all-gather.2
  133.9 189.2 all-gather.4

commit v2 on v1

v2 whole, which is shorter than its diff:
```python
import jax
import jax.numpy as jnp
from jax import lax
from jax.sharding import Mesh, PartitionSpec as P

PAIR = 2


def contract(left, right):
    return lax.dot_general(
        left, right, (((0, 2), (0, 2)), ((), ())), preferred_element_type=jnp.float32
    )


def body(analysis_dep, background_dep, valid_counts):
    cycle_total = valid_counts.shape[0]
    quad_size = lax.axis_size("tq")
    chan_size = lax.axis_size("chan")
    lag_total = 5
    max_lag = (lag_total - 1) // 2
    cycle_index = lax.axis_index("tq") * PAIR + lax.axis_index("th")
    own_count = jnp.sum(
        jnp.where(jnp.arange(cycle_total, dtype=jnp.int32) == cycle_index, valid_counts, 0)
    )
    _, width_block, loc_total = analysis_dep.shape
    half = loc_total // PAIR
    piece = half // chan_size
    pair_rows = width_block * chan_size // quad_size
    valid_cols = (jnp.arange(loc_total, dtype=jnp.int32) < own_count)[None, :]
    local_analysis = jnp.where(valid_cols, analysis_dep[0], jnp.zeros((), jnp.bfloat16))
    local_background = jnp.where(valid_cols, background_dep[0], jnp.zeros((), jnp.bfloat16))

    halves = local_analysis.reshape(width_block, PAIR, half).transpose(1, 0, 2)
    pair_analysis = lax.all_to_all(halves, "th", 0, 0, tiled=True)
    all_analysis = lax.all_gather(pair_analysis, "tq", axis=0, tiled=True)

    split_b = local_background.reshape(width_block, PAIR, chan_size, piece)
    by_loc = lax.all_to_all(split_b, "chan", 2, 0, tiled=True)
    by_loc = by_loc.reshape(quad_size, pair_rows, PAIR, piece).transpose(0, 2, 1, 3)
    by_loc = by_loc.reshape(quad_size * PAIR, pair_rows, piece)
    rows_here = lax.all_to_all(by_loc, ("tq", "th"), 0, 0, tiled=True)
    all_background = lax.all_gather(rows_here, "chan", axis=2, tiled=True)

    pieces = [None] * lag_total
    for offset in range(max_lag + 1):
        span = cycle_total - offset
        pieces[max_lag + offset] = contract(all_background[offset:], all_analysis[:span])
        if offset > 0:
            pieces[max_lag - offset] = contract(all_background[:span], all_analysis[offset:])
    partial = jnp.stack(pieces, axis=1)
    summed = lax.psum_scatter(partial, "th", scatter_dimension=0, tiled=True)

    denominators = []
    for offset in range(max_lag + 1):
        span = cycle_total - offset
        denominators.append(
            jnp.sum(jnp.minimum(valid_counts[:span], valid_counts[offset:])).astype(jnp.float32)
        )
    divisor = jnp.stack([denominators[abs(k - max_lag)] for k in range(lag_total)])
    return summed / divisor[None, :, None]


def solution(mesh):
    tm_size, chan_size = mesh.devices.shape
    split = Mesh(mesh.devices.reshape(tm_size // PAIR, PAIR, chan_size), ("tq", "th", "chan"))
    in_specs = (P(("tq", "th"), "chan", None), P(("tq", "th"), "chan", None), P())
    out_specs = P(("tq", "th"), None, "chan")
    return jax.shard_map(body, mesh=split, in_specs=in_specs, out_specs=out_specs, check_vma=False)
```

time: 378 us -> 341 us (0.902)
  waiting for transfers between devices: 233 us -> 147 us
  blocking collectives: 71 us -> 138 us
  matrix products: 46.1 us -> 24.6 us
    all_gather x1, waiting for transfers between devices: 191 us -> 45.3 us  [body(): all_analysis = lax.all_gather(pair_analysis, 'tq', axis=0, tiled=True)]
    all_to_all x2 -> x3, blocking collectives: 71 us -> 138 us  [the longest x1 88.2 us: body(): rows_here = lax.all_to_all(by_loc, ('tq', 'th'), 0, 0, tiled=True)]
    reduce_scatter x0 -> x1, waiting for transfers between devices: none -> 51.2 us  [body(): summed = lax.psum_scatter(partial, 'th', scatter_dimension=0, tiled=True)]
    dot_general x5, matrix products: 46.1 us -> 24.6 us  [contract(): lax.dot_general(left, right, (((0, 2), (0, 2)), ((), ())), preferred_elem...]
    all_gather x1, waiting for transfers between devices: 41.8 us -> 50 us  [body(): all_background = lax.all_gather(rows_here, 'chan', axis=2, tiled=True)]
    squeeze x0 -> x1, local copies, waits for them, and re-layouts: none -> 4.35 us  [body(): analysis_dep[0]]
  transfers between devices with their start and end apart: 2 -> 3, of which waited for: 2 -> 3; matrix products, arithmetic and copies ran while one was open for 1% -> 1% of each run, Pallas kernels for 0% -> 0%
where the time goes in v2:
time: 341 us
  waiting for transfers between devices  147 us (43%)
  blocking collectives  138 us (40%)
  matrix products  24.6 us (7%)
  between operations  15 us (4%)
  other arithmetic  9.48 us (3%)
  local copies, waits for them, and re-layouts  6.89 us (2%)
    all_to_all x1, blocking collectives, body(): rows_here = lax.all_to_all(by_loc, ('tq', 'th'), 0, 0, tiled=True)  88.2 us
    reduce_scatter x1, waiting for transfers between devices, body(): summed = lax.psum_scatter(partial, 'th', scatter_dimension=0, tiled=True)  51.2 us
    all_gather x1, waiting for transfers between devices, body(): all_background = lax.all_gather(rows_here, 'chan', axis=2, tiled=True)  50 us
    all_gather x1, waiting for transfers between devices, body(): all_analysis = lax.all_gather(pair_analysis, 'tq', axis=0, tiled=True)  45.3 us
    all_to_all x1, blocking collectives, body(): pair_analysis = lax.all_to_all(halves, 'th', 0, 0, tiled=True)  25.6 us
    dot_general x5, matrix products, contract(): lax.dot_general(left, right, (((0, 2), (0, 2)), ((), ())), preferred_elem...  24.6 us
    all_to_all x1, blocking collectives, body(): by_loc = lax.all_to_all(split_b, 'chan', 2, 0, tiled=True)  24.3 us
  transfers between devices with their start and end apart: 3, of which 3 were waited for; matrix products, arithmetic and copies ran while one was open for 1% of the time, Pallas kernels for 0%

profile of v2, /device:TPU:0, one launch (start us, length us, event | category | flops | bytes accessed | tf_op | source)
XLA Modules:
  0.0 340.9 jit_solution(18133804362319293849)
XLA Ops:
  6.5 1.4 fusion.35
  7.9 0.7 add_compare_fusion
  8.6 4.3 %squeeze.7 = bf16[416,2,1024]{2,1,0:T(2,128)(2,1)S(1)} reshape(bf16[1,416,2048]{2,1,0:T(8,128)(2,1)} %param.3) | data formatting | bytes 3407872 | tf_op jit(solution)/shard_map/squeeze | solution.py:30
  13.0 1.3 fusion.8
  14.3 0.5 copy.10
  14.8 25.6 %all_to_all.25 = bf16[2,416,1024]{2,1,0:T(8,128)(2,1)} all-to-all(bf16[2,416,1024]{2,1,0:T(8,128)(2,1)S(1)} %copy.10), channel_id=1, replica_groups=mesh['tq'=4,'th'=2,'chan'=4] {'th'}, dimensions={0} | all-to-all | bytes 3407872 | tf_op jit(solution)/shard_map/all_to_all | solution.py:34
  40.5 1.3 squeeze.6
  41.8 0.7 add_compare_fusion.1
  42.5 0.7 copy_select_fusion
  43.2 24.3 %all_to_all.26 = bf16[416,2,4,256]{3,0,1,2:T(8,128)(2,1)S(1)} all-to-all(bf16[416,2,4,256]{3,0,1,2:T(8,128)(2,1)S(1)} %copy_select_fusion), channel_id=1, replica_groups=mesh['tq'=4,'th'=2,'chan'=4] {'chan'}, dimensions={2} | all-to-all | bytes 3407872 | tf_op jit(solution)/shard_map/all_to_all | solution.py:38
  67.5 88.2 %all_to_all.27 = bf16[8,416,256]{2,1,0:T(8,128)(2,1)} all-to-all(bf16[8,416,256]{2,1,0:T(8,128)(2,1)S(1)} %bitcast.45), channel_id=1, replica_groups=mesh['tq'=4,'th'=2,'chan'=4] {'tq','th'}, dimensions={0} | all-to-all | bytes 3407872 | tf_op jit(solution)/shard_map/all_to_all | solution.py:41
  155.7 0.2 reduce-scatter.2.cloned.1.call-start
  156.0 45.3 %all-gather.5.cloned.1.call-done = bf16[8,416,1024]{2,1,0:T(8,128)(2,1)} async-done(((bf16[2,416,1024]{2,1,0:T(8,128)(2,1)}), bf16[8,416,1024]{2,1,0:T(8,128)(2,1)}) %all-gather.5.cloned.1.call-update) | async-done | bytes 6815760 | tf_op jit(solution)/shard_map/all_gather | solution.py:35
  201.3 50.0 %all-gather.3.cloned.1.call-done = bf16[8,416,1024]{2,1,0:T(8,128)(2,1)} async-done(((bf16[8,416,256]{2,1,0:T(8,128)(2,1)}), bf16[8,416,1024]{2,1,0:T(8,128)(2,1)}) %all-gather.3.cloned.1.call-update) | async-done | bytes 6815760 | tf_op jit(solution)/shard_map/all_gather | solution.py:42
  251.3 7.9 %fusion.12 = f32[416,5,416]{2,0,1:T(8,128)} fusion(bf16[8,416,1024]{2,1,0:T(8,128)(2,1)} %all-gather.3.cloned.1.call-done, bf16[8,416,1024]{2,1,0:T(8,128)(2,1)} %all-gather.5.cloned.1.call-done), kind=kOutput, calls=%fused_computation.12 | convolution fusion | flops 2126512128 | bytes 12779520 | tf_op jit(solution)/shard_map/dot_general | solution.py:10
  259.1 4.2 %fusion.25 = f32[416,5,416]{2,0,1:T(8,128)} fusion(f32[416,5,416]{2,0,1:T(8,128)} %fusion.12, bf16[8,416,1024]{2,1,0:T(8,128)(2,1)S(1)} %copy-done.3, bf16[8,416,1024]{2,1,0:T(8,128)(2,1)S(1)} %copy-done.2), kind=kOutput, calls=%fused_computation.18 | convolution fusion | flops 2480930816 | bytes 13631488 | tf_op jit(solution)/shard_map/dot_general | solution.py:10
  263.3 4.6 %fusion.21 = f32[416,5,416]{2,0,1:T(8,128)} fusion(f32[416,5,416]{2,0,1:T(8,128)} %fusion.25, bf16[8,416,1024]{2,1,0:T(8,128)(2,1)S(1)} %copy-done.3, bf16[8,416,1024]{2,1,0:T(8,128)(2,1)S(1)} %copy-done.2), kind=kOutput, calls=%fused_computation.16 | convolution fusion | flops 2835349504 | bytes 14483456 | tf_op jit(solution)/shard_map/dot_general | solution.py:10
  267.9 4.2 %fusion.31 = f32[416,5,416]{2,0,1:T(8,128)} fusion(f32[416,5,416]{2,0,1:T(8,128)} %fusion.21, bf16[8,416,1024]{2,1,0:T(8,128)(2,1)S(1)} %copy-done.3, bf16[8,416,1024]{2,1,0:T(8,128)(2,1)S(1)} %copy-done.2), kind=kOutput, calls=%fused_computation.20 | convolution fusion | flops 2480930816 | bytes 13631488 | tf_op jit(solution)/shard_map/dot_general | solution.py:10
  272.1 3.7 %fusion.18 = f32[416,5,416]{2,0,1:T(8,128)} fusion(f32[416,5,416]{2,0,1:T(8,128)} %fusion.31, bf16[8,416,1024]{2,1,0:T(8,128)(2,1)S(1)} %copy-done.3, bf16[8,416,1024]{2,1,0:T(8,128)(2,1)S(1)} %copy-done.2), kind=kOutput, calls=%fused_computation.14 | convolution fusion | flops 2126512128 | bytes 12779520 | tf_op jit(solution)/shard_map/dot_general | solution.py:10
  275.9 0.6 copy-done.1
  276.5 0.7 minimum_reduce_fusion.1
  277.7 0.8 minimum_reduce_fusion
  279.8 51.2 %reduce-scatter.2.cloned.1.call-done = f32[208,5,416]{2,0,1:T(8,128)} async-done(((f32[416,5,416]{2,0,1:T(8,128)}), f32[208,5,416]{2,0,1:T(8,128)}) %reduce-scatter.2.cloned.1.call-update) | async-done | bytes 1730576 | tf_op jit(solution)/shard_map/reduce_scatter | solution.py:51
  331.0 3.3 broadcast_divide_fusion
  (13 shorter events, 0.2 us)
Async XLA Ops:
  6.5 194.7 %all-gather.5.cloned.1.call-start = ((), (), s32[]{:S(2)}) async-start(), calls=%async_computation.5 | async-start | bytes 8519680 | tf_op jit(solution)/shard_map/all_gather | solution.py:35
  14.3 26.2 %copy-start = (bf16[1,416,2048]{2,1,0:T(8,128)(2,1)S(1)}, bf16[1,416,2048]{2,1,0:T(8,128)(2,1)}, u32[]{:S(2)}) copy-start(bf16[1,416,2048]{2,1,0:T(8,128)(2,1)} %param.4) | copy-start | bytes 5111812
  40.4 210.9 %all-gather.3.cloned.1.call-start = ((), (), s32[]{:S(2)}) async-start(), calls=%async_computation.4 | async-start | bytes 8519680 | tf_op jit(solution)/shard_map/all_gather | solution.py:42
  155.7 175.3 %reduce-scatter.2.cloned.1.call-start = ((), (), s32[]{:S(2)}) async-start(), calls=%async_computation.6 | async-start | bytes 6389760 | tf_op jit(solution)/shard_map/reduce_scatter | solution.py:51
  251.3 7.9 %copy-start.2 = (bf16[8,416,1024]{2,1,0:T(8,128)(2,1)S(1)}, bf16[8,416,1024]{2,1,0:T(8,128)(2,1)}, u32[]{:S(2)}) copy-start(bf16[8,416,1024]{2,1,0:T(8,128)(2,1)} %all-gather.5.cloned.1.call-done) | copy-start | bytes 20447236
  251.3 7.9 %copy-start.3 = (bf16[8,416,1024]{2,1,0:T(8,128)(2,1)S(1)}, bf16[8,416,1024]{2,1,0:T(8,128)(2,1)}, u32[]{:S(2)}) copy-start(bf16[8,416,1024]{2,1,0:T(8,128)(2,1)} %all-gather.3.cloned.1.call-done) | copy-start | bytes 20447236
  275.8 0.7 copy-start.1
Sparse Core Ops, SparseCore 0:
  40.5 160.6 all-gather.4
  202.8 48.4 all-gather.2
  276.0 55.0 reduce-scatter.1

commit v3 on v2

--- a/solution.py
+++ b/solution.py
@@ -4,6 +4,26 @@
 from jax.sharding import Mesh, PartitionSpec as P
 
 PAIR = 2
+
+
+def swap_pair(x):
+    return lax.ppermute(x, "th", [(0, 1), (1, 0)])
+
+
+def gather_chan(x, axis):
+    size = lax.axis_size("chan")
+    me = lax.axis_index("chan")
+    bits = size.bit_length() - 1
+    held = x
+    for done, bit in enumerate(reversed(range(bits))):
+        got = lax.ppermute(held, "chan", [(c, c ^ (1 << bit)) for c in range(size)])
+        low = ((me >> bit) & 1) == 0
+        first = jnp.where(low, held, got)
+        second = jnp.where(low, got, held)
+        held = jnp.stack([first, second], axis=axis + done)
+    shape = list(x.shape)
+    shape[axis] *= size
+    return held.reshape(shape)
 
 
 def contract(left, right):
@@ -30,8 +50,12 @@
     local_analysis = jnp.where(valid_cols, analysis_dep[0], jnp.zeros((), jnp.bfloat16))
     local_background = jnp.where(valid_cols, background_dep[0], jnp.zeros((), jnp.bfloat16))
 
-    halves = local_analysis.reshape(width_block, PAIR, half).transpose(1, 0, 2)
-    pair_analysis = lax.all_to_all(halves, "th", 0, 0, tiled=True)
+    pair_index = lax.axis_index("th")
+    halves = local_analysis.reshape(width_block, PAIR, half)
+    keep = jnp.where(pair_index == 0, halves[:, 0], halves[:, 1])
+    give = jnp.where(pair_index == 0, halves[:, 1], halves[:, 0])
+    got = swap_pair(give)
+    pair_analysis = jnp.where(pair_index == 0, jnp.stack([keep, got]), jnp.stack([got, keep]))
     all_analysis = lax.all_gather(pair_analysis, "tq", axis=0, tiled=True)
 
     split_b = local_background.reshape(width_block, PAIR, chan_size, piece)
@@ -39,7 +63,7 @@
     by_loc = by_loc.reshape(quad_size, pair_rows, PAIR, piece).transpose(0, 2, 1, 3)
     by_loc = by_loc.reshape(quad_size * PAIR, pair_rows, piece)
     rows_here = lax.all_to_all(by_loc, ("tq", "th"), 0, 0, tiled=True)
-    all_background = lax.all_gather(rows_here, "chan", axis=2, tiled=True)
+    all_background = gather_chan(rows_here, 2)
 
     pieces = [None] * lag_total
     for offset in range(max_lag + 1):
@@ -48,7 +72,10 @@
         if offset > 0:
             pieces[max_lag - offset] = contract(all_background[:span], all_analysis[offset:])
     partial = jnp.stack(pieces, axis=1)
-    summed = lax.psum_scatter(partial, "th", scatter_dimension=0, tiled=True)
+    rows_out = partial.shape[0] // PAIR
+    upper = jnp.where(pair_index == 0, partial[rows_out:], partial[:rows_out])
+    lower = jnp.where(pair_index == 0, partial[:rows_out], partial[rows_out:])
+    summed = lower + swap_pair(upper)
 
     denominators = []
     for offset in range(max_lag + 1):

time: 341 us -> 412 us (1.21); the launches traced: 341 us -> 404 us
  blocking collectives: 138 us -> 0 us
  local copies, waits for them, and re-layouts: 6.89 us -> 144 us
  other arithmetic: 9.48 us -> 37.3 us
  starting transfers between devices: 0.27 us -> 21.2 us
  waiting for transfers between devices: 147 us -> 154 us
  matrix products: 24.6 us -> 31.4 us
    all_to_all x3 -> x0, blocking collectives: 138 us -> none  [the longest x1 88.2 us: body(): rows_here = lax.all_to_all(by_loc, ('tq', 'th'), 0, 0, tiled=True)]
    slice x0 -> x8, local copies, waits for them, and re-layouts: none -> 106 us  [the longest x4 57.1 us: body(): all_background[offset:]]
    ppermute x0 -> x4, waiting for transfers between devices: none -> 84.5 us  [the longest x2 48.8 us: swap_pair(): return lax.ppermute(x, 'th', [(0, 1), (1, 0)])]
    all_to_all x0 -> x2, waiting for transfers between devices: none -> 69.5 us  [the longest x1 58.9 us: body(): rows_here = lax.all_to_all(by_loc, ('tq', 'th'), 0, 0, tiled=True)]
    reduce_scatter x1 -> x0, waiting for transfers between devices: 51.2 us -> none  [body(): summed = lax.psum_scatter(partial, 'th', scatter_dimension=0, tiled=True)]
    all_gather x1 -> x0, waiting for transfers between devices: 50 us -> none  [body(): all_background = lax.all_gather(rows_here, 'chan', axis=2, tiled=True)]
    all_gather x1, waiting for transfers between devices: 45.3 us -> 0.01 us  [body(): all_analysis = lax.all_gather(pair_analysis, 'tq', axis=0, tiled=True)]
    another operation x0 -> x6, other arithmetic: none -> 16.8 us  [gather_chan(): held = jnp.stack([first, second], axis=axis + done)]
  transfers between devices with their start and end apart: 3 -> 7, of which waited for: 3 -> 6; matrix products, arithmetic and copies ran while one was open for 1% -> 41% of each run, Pallas kernels for 0% -> 0%
where the time goes in v3:
time: 412 us; the launch traced here: 404 us
  waiting for transfers between devices  154 us (37%)
  local copies, waits for them, and re-layouts  144 us (35%)
  other arithmetic  37.3 us (9%)
  matrix products  31.4 us (8%)
  starting transfers between devices  21.2 us (5%)
  between operations  16 us (4%)
    all_to_all x1, waiting for transfers between devices, body(): rows_here = lax.all_to_all(by_loc, ('tq', 'th'), 0, 0, tiled=True)  58.9 us
    slice x4, local copies, waits for them, and re-layouts, body(): all_background[offset:]  57.1 us
    slice x4, local copies, waits for them, and re-layouts, body(): all_background[:span]  49.3 us
    ppermute x2, waiting for transfers between devices, swap_pair(): return lax.ppermute(x, 'th', [(0, 1), (1, 0)])  48.8 us
    ppermute x2, waiting for transfers between devices, gather_chan(): got = lax.ppermute(held, 'chan', [(c, c ^ 1 << bit) for c in range(size)])  35.7 us
    dot_general x5, matrix products, contract(): lax.dot_general(left, right, (((0, 2), (0, 2)), ((), ())), preferred_elem...  31.4 us
    another operation x6, other arithmetic, gather_chan(): held = jnp.stack([first, second], axis=axis + done)  16.8 us
    another operation x1, local copies, waits for them, and re-layouts, gather_chan(): held = jnp.stack([first, second], axis=axis + done)  15.5 us
  transfers between devices with their start and end apart: 7, of which 6 were waited for; matrix products, arithmetic and copies ran while one was open for 41% of the time, Pallas kernels for 0%

profile of v3, /device:TPU:0, one launch (start us, length us, event | category | flops | bytes accessed | tf_op | source)
XLA Modules:
  0.0 404.2 jit_solution(12896254212793295044)
XLA Ops:
  30.3 10.6 %all-to-all-done = bf16[416,2,4,256]{3,0,1,2:T(8,128)(2,1)} async-done(((bf16[416,2,4,256]{3,0,1,2:T(8,128)(2,1)}), bf16[416,2,4,256]{3,0,1,2:T(8,128)(2,1)}, u32[]{:S(2)}, u32[]{:S(2)}) %all-to-all-start) | async-done | bytes 1703968 | tf_op jit(solution)/shard_map/all_to_all | solution.py:62
  40.9 6.7 %all-to-all-start.1 = ((bf16[8,416,256]{2,1,0:T(8,128)(2,1)}), bf16[8,416,256]{2,1,0:T(8,128)(2,1)S(1)}, u32[]{:S(2)}, u32[]{:S(2)}) async-start(bf16[8,416,256]{2,1,0:T(8,128)(2,1)} %bitcast.4), calls=%async_computation.1 | async-start | bytes 3407872 | tf_op jit(solution)/shard_map/all_to_all | solution.py:65
  47.9 5.4 %collective-permute-done.2 = bf16[416,1024]{1,0:T(8,128)(2,1)} collective-permute-done((bf16[416,1024]{1,0:T(8,128)(2,1)}, bf16[416,1024]{1,0:T(8,128)(2,1)}, u32[]{:S(2)}, u32[]{:S(2)}) %collective-permute-start.2) | collective-permute-done | bytes 852000 | tf_op jit(solution)/shard_map/ppermute | solution.py:10
  56.3 58.9 %all-to-all-done.1 = bf16[8,416,256]{2,1,0:T(8,128)(2,1)S(1)} async-done(((bf16[8,416,256]{2,1,0:T(8,128)(2,1)}), bf16[8,416,256]{2,1,0:T(8,128)(2,1)S(1)}, u32[]{:S(2)}, u32[]{:S(2)}) %all-to-all-start.1) | async-done | bytes 1703968 | tf_op jit(solution)/shard_map/all_to_all | solution.py:65
  115.4 29.6 %collective-permute-done = bf16[8,416,256]{2,1,0:T(8,128)(2,1)S(1)} collective-permute-done((bf16[8,416,256]{2,1,0:T(8,128)(2,1)S(1)}, bf16[8,416,256]{2,1,0:T(8,128)(2,1)S(1)}, u32[]{:S(2)}, u32[]{:S(2)}) %collective-permute-start) | collective-permute-done | bytes 1703968 | tf_op jit(solution)/shard_map/ppermute | solution.py:19
  146.9 6.2 %collective-permute-done.1 = bf16[8,416,2,256]{3,1,0,2:T(8,128)(2,1)} collective-permute-done((bf16[8,416,2,256]{3,1,0,2:T(8,128)(2,1)S(1)}, bf16[8,416,2,256]{3,1,0,2:T(8,128)(2,1)}, u32[]{:S(2)}, u32[]{:S(2)}) %collective-permute-start.1) | collective-permute-done | bytes 3407904 | tf_op jit(solution)/shard_map/ppermute | solution.py:19
  160.3 13.4 %copy.40 = bf16[7,416,2,2,256]{4,3,2,1,0:T(2,128)(2,1)} copy(bf16[7,416,2,2,256]{4,1,0,2,3:T(8,128)(2,1)S(1)} %get-tuple-element.10) | data formatting | bytes 11927552 | tf_op jit(solution)/shard_map/slice | solution.py:73
  173.7 13.8 %slice.70 = bf16[7,416,1024]{2,1,0:T(8,128)(2,1)} reshape(bf16[7,416,2,2,256]{4,3,2,1,0:T(2,128)(2,1)} %copy.40) | data formatting | bytes 11927552 | tf_op jit(solution)/shard_map/slice | solution.py:73
  187.5 6.5 %fusion.7 = (bf16[6,416,2,2,256]{4,1,0,2,3:T(8,128)(2,1)}, bf16[6,416,2,2,256]{4,1,0,2,3:T(8,128)(2,1)}) fusion(bf16[8,416,2,1,256]{4,1,0,2,3:T(8,128)(2,1)} %copy-done, bf16[8,416,2,1,256]{4,1,0,2,3:T(8,128)(2,1)S(1)} %get-tuple-element.11), kind=kLoop, calls=%fused_computation.16 | loop fusion | flops 5111808 | bytes 17039360 | tf_op jit(solution)/shard_map/stack | solution.py:23
  194.0 10.0 %copy.39 = bf16[6,416,2,2,256]{4,3,2,1,0:T(2,128)(2,1)} copy(bf16[6,416,2,2,256]{4,1,0,2,3:T(8,128)(2,1)} %get-tuple-element.8) | data formatting | bytes 10223616 | tf_op jit(solution)/shard_map/slice | solution.py:73
  204.0 12.1 %slice.65 = bf16[6,416,1024]{2,1,0:T(8,128)(2,1)} reshape(bf16[6,416,2,2,256]{4,3,2,1,0:T(2,128)(2,1)} %copy.39) | data formatting | bytes 10223616 | tf_op jit(solution)/shard_map/slice | solution.py:73
  218.7 15.5 %copy.41 = bf16[8,416,2,2,256]{4,3,2,1,0:T(2,128)(2,1)} copy(bf16[8,416,2,2,256]{4,1,0,2,3:T(8,128)(2,1)S(1)} %pad_maximum_fusion) | data formatting | bytes 13631488 | tf_op jit(solution)/shard_map/stack | solution.py:23
  234.2 12.0 %reshape.57 = bf16[8,416,1024]{2,1,0:T(8,128)(2,1)} reshape(bf16[8,416,2,2,256]{4,3,2,1,0:T(2,128)(2,1)} %copy.41) | data formatting | bytes 13631488 | tf_op jit(solution)/shard_map/reshape | solution.py:26
  246.2 21.2 %copy.42 = bf16[7,416,2,2,256]{4,3,2,1,0:T(2,128)(2,1)} copy(bf16[7,416,2,2,256]{4,1,0,2,3:T(8,128)(2,1)} %get-tuple-element.9) | data formatting | bytes 11927552 | tf_op jit(solution)/shard_map/slice | solution.py:71
  267.5 13.8 %slice.73 = bf16[7,416,1024]{2,1,0:T(8,128)(2,1)} reshape(bf16[7,416,2,2,256]{4,3,2,1,0:T(2,128)(2,1)} %copy.42) | data formatting | bytes 11927552 | tf_op jit(solution)/shard_map/slice | solution.py:71
  281.3 10.0 %copy.43 = bf16[6,416,2,2,256]{4,3,2,1,0:T(2,128)(2,1)} copy(bf16[6,416,2,2,256]{4,1,0,2,3:T(8,128)(2,1)} %get-tuple-element.7) | data formatting | bytes 10223616 | tf_op jit(solution)/shard_map/slice | solution.py:71
  291.2 12.1 %slice.76 = bf16[6,416,1024]{2,1,0:T(8,128)(2,1)} reshape(bf16[6,416,2,2,256]{4,3,2,1,0:T(2,128)(2,1)} %copy.43) | data formatting | bytes 10223616 | tf_op jit(solution)/shard_map/slice | solution.py:71
  303.3 7.0 %fusion.15 = f32[416,5,416]{2,0,1:T(8,128)S(1)} fusion(bf16[6,416,1024]{2,1,0:T(8,128)(2,1)} %slice.65, bf16[8,416,1024]{2,1,0:T(8,128)(2,1)} %all-gather.2.cloned.1.call-done), kind=kOutput, calls=%fused_computation.34 | convolution fusion | flops 2126512128 | bytes 11075584 | tf_op jit(solution)/shard_map/dot_general | solution.py:30
  310.4 7.7 %fusion.28 = f32[416,5,416]{2,0,1:T(8,128)S(1)} fusion(f32[416,5,416]{2,0,1:T(8,128)S(1)} %fusion.15, bf16[7,416,1024]{2,1,0:T(8,128)(2,1)} %slice.70, bf16[8,416,1024]{2,1,0:T(8,128)(2,1)} %all-gather.2.cloned.1.call-done), kind=kOutput, calls=%fused_computation.40 | convolution fusion | flops 2480930816 | bytes 12779520 | tf_op jit(solution)/shard_map/dot_general | solution.py:30
  318.1 6.1 %fusion.24 = f32[416,5,416]{2,0,1:T(8,128)S(1)} fusion(f32[416,5,416]{2,0,1:T(8,128)S(1)} %fusion.28, bf16[8,416,1024]{2,1,0:T(8,128)(2,1)S(1)} %bitcast.59, bf16[8,416,1024]{2,1,0:T(8,128)(2,1)} %all-gather.2.cloned.1.call-done), kind=kOutput, calls=%fused_computation.38 | convolution fusion | flops 2835349504 | bytes 14483456 | tf_op jit(solution)/shard_map/dot_general | solution.py:30
  324.2 5.4 %fusion.34 = f32[416,5,416]{2,0,1:T(8,128)S(1)} fusion(f32[416,5,416]{2,0,1:T(8,128)S(1)} %fusion.24, bf16[7,416,1024]{2,1,0:T(8,128)(2,1)S(1)} %bitcast.61, bf16[8,416,1024]{2,1,0:T(8,128)(2,1)} %all-gather.2.cloned.1.call-done), kind=kOutput, calls=%fused_computation.42 | convolution fusion | flops 2480930816 | bytes 12779520 | tf_op jit(solution)/shard_map/dot_general | solution.py:30
  329.6 5.3 %fusion.21 = f32[416,5,416]{2,0,1:T(8,128)S(1)} fusion(f32[416,5,416]{2,0,1:T(8,128)S(1)} %fusion.34, bf16[6,416,1024]{2,1,0:T(8,128)(2,1)S(1)} %bitcast.63, bf16[8,416,1024]{2,1,0:T(8,128)(2,1)} %all-gather.2.cloned.1.call-done), kind=kOutput, calls=%fused_computation.36 | convolution fusion | flops 2126512128 | bytes 11075584 | tf_op jit(solution)/shard_map/dot_general | solution.py:30
  338.7 7.0 %collective-permute-start.3 = (f32[208,5,416]{2,0,1:T(8,128)}, f32[208,5,416]{2,0,1:T(8,128)S(1)}, u32[]{:S(2)}, u32[]{:S(2)}) collective-permute-start(f32[208,5,416]{2,0,1:T(8,128)} %slice_select_fusion), channel_id=1, source_target_pairs={{0,4},{4,0},{1,5},{5,1},{2,6},{6,2},{3,7},{7,3},{8,12},{12,8},{9,1... | collective-permute-start | bytes 5191688 | tf_op jit(solution)/shard_map/ppermute | solution.py:10
  349.1 43.4 %collective-permute-done.3 = f32[208,5,416]{2,0,1:T(8,128)S(1)} collective-permute-done((f32[208,5,416]{2,0,1:T(8,128)}, f32[208,5,416]{2,0,1:T(8,128)S(1)}, u32[]{:S(2)}, u32[]{:S(2)}) %collective-permute-start.3) | collective-permute-done | bytes 1730592 | tf_op jit(solution)/shard_map/ppermute | solution.py:10
  (55 shorter events, 48.7 us)
Async XLA Ops:
  12.5 6.9 %copy-start.4 = (bf16[1,416,2048]{2,1,0:T(8,128)(2,1)S(1)}, bf16[1,416,2048]{2,1,0:T(8,128)(2,1)}, u32[]{:S(2)}) copy-start(bf16[1,416,2048]{2,1,0:T(8,128)(2,1)} %param.3) | copy-start | bytes 5111812
  14.3 26.6 %all-to-all-start = ((bf16[416,2,4,256]{3,0,1,2:T(8,128)(2,1)}), bf16[416,2,4,256]{3,0,1,2:T(8,128)(2,1)}, u32[]{:S(2)}, u32[]{:S(2)}) async-start(bf16[416,2,4,256]{3,0,1,2:T(8,128)(2,1)} %copy_select_fusion), calls=%async_computation | async-start | bytes 3407872 | tf_op jit(solution)/shard_map/all_to_all | solution.py:62
  27.3 25.9 %collective-permute-start.2 = (bf16[416,1024]{1,0:T(8,128)(2,1)}, bf16[416,1024]{1,0:T(8,128)(2,1)}, u32[]{:S(2)}, u32[]{:S(2)}) collective-permute-start(bf16[416,1024]{1,0:T(8,128)(2,1)} %bitcast.56), channel_id=1, source_target_pairs={{0,4},{4,0},{1,5},{5,1},{2,6},{6,2},{3,7},{7,3},{8,12},{12,8},{9,1... | collective-permute-start | bytes 2555912 | tf_op jit(solution)/shard_map/ppermute | solution.py:10
  40.9 74.3 %all-to-all-start.1 = ((bf16[8,416,256]{2,1,0:T(8,128)(2,1)}), bf16[8,416,256]{2,1,0:T(8,128)(2,1)S(1)}, u32[]{:S(2)}, u32[]{:S(2)}) async-start(bf16[8,416,256]{2,1,0:T(8,128)(2,1)} %bitcast.4), calls=%async_computation.1 | async-start | bytes 3407872 | tf_op jit(solution)/shard_map/all_to_all | solution.py:65
  47.6 255.7 %all-gather.2.cloned.1.call-start = ((), (), s32[]{:S(2)}) async-start(), calls=%async_computation.2 | async-start | bytes 8519680 | tf_op jit(solution)/shard_map/all_gather | solution.py:59
  115.2 29.8 %collective-permute-start = (bf16[8,416,256]{2,1,0:T(8,128)(2,1)S(1)}, bf16[8,416,256]{2,1,0:T(8,128)(2,1)S(1)}, u32[]{:S(2)}, u32[]{:S(2)}) collective-permute-start(bf16[8,416,256]{2,1,0:T(8,128)(2,1)S(1)} %all-to-all-done.1), channel_id=1, source_target_pairs={{0,2},{1,3},{2,0},{3,1},{4,6},{5,7},{6,4},{7,5},{8,10},{9,11},{10,... | collective-permute-start | bytes 5111816 | tf_op jit(solution)/shard_map/ppermute | solution.py:19
  145.2 1.3 copy-start.2
  145.2 1.7 copy-start.3
  146.9 6.2 %collective-permute-start.1 = (bf16[8,416,2,256]{3,1,0,2:T(8,128)(2,1)S(1)}, bf16[8,416,2,256]{3,1,0,2:T(8,128)(2,1)}, u32[]{:S(2)}, u32[]{:S(2)}) collective-permute-start(bf16[8,416,2,256]{3,1,0,2:T(8,128)(2,1)S(1)} %pad_maximum_fusion.1), channel_id=1, source_target_pairs={{0,1},{1,0},{2,3},{3,2},{4,5},{5,4},{6,7},{7,6},{8,9},{9,8},{10,11... | collective-permute-start | bytes 10223624 | tf_op jit(solution)/shard_map/ppermute | solution.py:19
  156.5 3.8 copy-start
  303.3 14.8 %slice-start = ((s8[6815744]{0:T(1024)(128)(4,1)}), s8[4194304]{0:T(1024)(128)(4,1)S(1)}, s32[]{:S(2)}) async-start(s8[6815744]{0:T(1024)(128)(4,1)} %bitcast.58), calls=%async_computation.3 | async-start | bytes 8388608
  310.4 7.7 %slice-start.1 = ((s8[6815744]{0:T(1024)(128)(4,1)}), s8[2621440]{0:T(1024)(128)(4,1)S(1)}, s32[]{:S(2)}) async-start(s8[6815744]{0:T(1024)(128)(4,1)} %bitcast.58), calls=%async_computation.4 | async-start | bytes 5242880
  310.4 13.8 %slice-start.2 = ((s8[5963776]{0:T(1024)(128)(4,1)}), s8[4194304]{0:T(1024)(128)(4,1)S(1)}, s32[]{:S(2)}) async-start(s8[5963776]{0:T(1024)(128)(4,1)} %bitcast.60), calls=%async_computation.5 | async-start | bytes 8388608
  310.4 19.2 %slice-start.4 = ((s8[5111808]{0:T(1024)(128)(4,1)}), s8[4194304]{0:T(1024)(128)(4,1)S(1)}, s32[]{:S(2)}) async-start(s8[5111808]{0:T(1024)(128)(4,1)} %bitcast.62), calls=%async_computation.7 | async-start | bytes 8388608
  318.1 6.1 %slice-start.3 = ((s8[5963776]{0:T(1024)(128)(4,1)}), s8[1769472]{0:T(1024)(128)(4,1)S(1)}, s32[]{:S(2)}) async-start(s8[5963776]{0:T(1024)(128)(4,1)} %bitcast.60), calls=%async_computation.6 | async-start | bytes 3538944
  318.1 11.5 %slice-start.5 = ((s8[5111808]{0:T(1024)(128)(4,1)}), s8[917504]{0:T(1024)(128)(4,1)S(1)}, s32[]{:S(2)}) async-start(s8[5111808]{0:T(1024)(128)(4,1)} %bitcast.62), calls=%async_computation.8 | async-start | bytes 1835008
  334.9 2.0 copy-start.1
  336.9 9.4 %copy-start.5 = (s32[8]{0:T(128)S(1)}, s32[8]{0:T(128)}, u32[]{:S(2)}) copy-start(s32[8]{0:T(128)} %param.5) | copy-start | bytes 100
  338.7 53.8 %collective-permute-start.3 = (f32[208,5,416]{2,0,1:T(8,128)}, f32[208,5,416]{2,0,1:T(8,128)S(1)}, u32[]{:S(2)}, u32[]{:S(2)}) collective-permute-start(f32[208,5,416]{2,0,1:T(8,128)} %slice_select_fusion), channel_id=1, source_target_pairs={{0,4},{4,0},{1,5},{5,1},{2,6},{6,2},{3,7},{7,3},{8,12},{12,8},{9,1... | collective-permute-start | bytes 5191688 | tf_op jit(solution)/shard_map/ppermute | solution.py:10
Sparse Core Ops, SparseCore 0:
  56.4 141.0 all-gather.1

commit v4 on v2

--- a/solution.py
+++ b/solution.py
@@ -4,6 +4,10 @@
 from jax.sharding import Mesh, PartitionSpec as P
 
 PAIR = 2
+
+
+def swap_pair(x):
+    return lax.ppermute(x, "th", [(0, 1), (1, 0)])
 
 
 def contract(left, right):
@@ -30,8 +34,12 @@
     local_analysis = jnp.where(valid_cols, analysis_dep[0], jnp.zeros((), jnp.bfloat16))
     local_background = jnp.where(valid_cols, background_dep[0], jnp.zeros((), jnp.bfloat16))
 
-    halves = local_analysis.reshape(width_block, PAIR, half).transpose(1, 0, 2)
-    pair_analysis = lax.all_to_all(halves, "th", 0, 0, tiled=True)
+    pair_index = lax.axis_index("th")
+    halves = local_analysis.reshape(width_block, PAIR, half)
+    keep = jnp.where(pair_index == 0, halves[:, 0], halves[:, 1])
+    give = jnp.where(pair_index == 0, halves[:, 1], halves[:, 0])
+    got = swap_pair(give)
+    pair_analysis = jnp.where(pair_index == 0, jnp.stack([keep, got]), jnp.stack([got, keep]))
     all_analysis = lax.all_gather(pair_analysis, "tq", axis=0, tiled=True)
 
     split_b = local_background.reshape(width_block, PAIR, chan_size, piece)
@@ -48,7 +56,10 @@
         if offset > 0:
             pieces[max_lag - offset] = contract(all_background[:span], all_analysis[offset:])
     partial = jnp.stack(pieces, axis=1)
-    summed = lax.psum_scatter(partial, "th", scatter_dimension=0, tiled=True)
+    rows_out = partial.shape[0] // PAIR
+    upper = jnp.where(pair_index == 0, partial[rows_out:], partial[:rows_out])
+    lower = jnp.where(pair_index == 0, partial[:rows_out], partial[rows_out:])
+    summed = lower + swap_pair(upper)
 
     denominators = []
     for offset in range(max_lag + 1):

time: 341 us -> 339 us (level)
  blocking collectives: 138 us -> 114 us
  waiting for transfers between devices: 147 us -> 158 us
  other arithmetic: 9.48 us -> 17.6 us
  matrix products: 24.6 us -> 20 us
  starting transfers between devices: 0.27 us -> 4.52 us
    ppermute x0 -> x2, waiting for transfers between devices: none -> 62.6 us  [swap_pair(): return lax.ppermute(x, 'th', [(0, 1), (1, 0)])]
    reduce_scatter x1 -> x0, waiting for transfers between devices: 51.2 us -> none  [body(): summed = lax.psum_scatter(partial, 'th', scatter_dimension=0, tiled=True)]
    all_to_all x1 -> x0, blocking collectives: 25.6 us -> none  [body(): pair_analysis = lax.all_to_all(halves, 'th', 0, 0, tiled=True)]
    select_n x0 -> x4, other arithmetic: none -> 8.62 us  [the longest x1 4.03 us: body(): keep = jnp.where(pair_index == 0, halves[:, 0], halves[:, 1])]
    dot_general x5, matrix products: 24.6 us -> 20 us  [contract(): lax.dot_general(left, right, (((0, 2), (0, 2)), ((), ())), preferred_elem...]
    ppermute x0 -> x2, starting transfers between devices: none -> 4.47 us  [swap_pair(): return lax.ppermute(x, 'th', [(0, 1), (1, 0)])]
  transfers between devices with their start and end apart: 3 -> 4, of which waited for: 3 -> 4; matrix products, arithmetic and copies ran while one was open for 1% -> 1% of each run, Pallas kernels for 0% -> 0%
where the time goes in v4:
time: 339 us; the launch traced here: 338 us
  waiting for transfers between devices  158 us (47%)
  blocking collectives  114 us (34%)
  matrix products  20 us (6%)
  other arithmetic  17.6 us (5%)
  between operations  15.3 us (5%)
  local copies, waits for them, and re-layouts  9.15 us (3%)
  starting transfers between devices  4.52 us (1%)
    all_to_all x1, blocking collectives, body(): rows_here = lax.all_to_all(by_loc, ('tq', 'th'), 0, 0, tiled=True)  89.3 us
    ppermute x2, waiting for transfers between devices, swap_pair(): return lax.ppermute(x, 'th', [(0, 1), (1, 0)])  62.6 us
    all_gather x1, waiting for transfers between devices, body(): all_background = lax.all_gather(rows_here, 'chan', axis=2, tiled=True)  50 us
    all_gather x1, waiting for transfers between devices, body(): all_analysis = lax.all_gather(pair_analysis, 'tq', axis=0, tiled=True)  45.5 us
    all_to_all x1, blocking collectives, body(): by_loc = lax.all_to_all(split_b, 'chan', 2, 0, tiled=True)  24.3 us
    dot_general x5, matrix products, contract(): lax.dot_general(left, right, (((0, 2), (0, 2)), ((), ())), preferred_elem...  20 us
  transfers between devices with their start and end apart: 4, of which 4 were waited for; matrix products, arithmetic and copies ran while one was open for 1% of the time, Pallas kernels for 0%

profile of v4, /device:TPU:0, one launch (start us, length us, event | category | flops | bytes accessed | tf_op | source)
XLA Modules:
  0.0 338.3 jit_solution(10938146271728744408)
XLA Ops:
  6.5 1.3 fusion.34
  8.4 4.3 %squeeze.5 = bf16[416,2,1024]{2,1,0:T(2,128)(2,1)S(1)} reshape(bf16[1,416,2048]{2,1,0:T(8,128)(2,1)} %param.3) | data formatting | bytes 3407872 | tf_op jit(solution)/shard_map/squeeze | solution.py:34
  12.8 1.3 broadcast_select_fusion
  14.1 4.0 %broadcast_select_fusion.2 = (bf16[416,1,1024]{2,1,0:T(2,128)(2,1)S(1)}, bf16[416,1,1024]{2,1,0:T(2,128)(2,1)S(1)}) fusion(pred[]{:T(512)S(6)} %eq.6, bf16[416,2,1024]{2,1,0:T(2,128)(2,1)S(1)} %broadcast_select_fusion), kind=kLoop, calls=%fused_computation.10 | loop fusion | flops 851968 | bytes 3407873 | tf_op jit(solution)/shard_map/jit(_where)/select_n | solution.py:39
  18.5 3.0 collective-permute-start
  21.8 18.6 %collective-permute-done = bf16[416,1024]{1,0:T(8,128)(2,1)S(1)} collective-permute-done((bf16[416,1024]{1,0:T(8,128)(2,1)S(1)}, bf16[416,1024]{1,0:T(8,128)(2,1)S(1)}, u32[]{:S(2)}, u32[]{:S(2)}) %collective-permute-start) | collective-permute-done | bytes 852000 | tf_op jit(solution)/shard_map/ppermute | solution.py:10
  40.4 1.4 maximum_select_fusion
  42.0 1.3 squeeze.4
  44.5 24.3 %all_to_all.20 = bf16[416,2,4,256]{3,0,1,2:T(8,128)(2,1)S(1)} all-to-all(bf16[416,2,4,256]{3,0,1,2:T(8,128)(2,1)S(1)} %copy_select_fusion), channel_id=1, replica_groups=mesh['tq'=4,'th'=2,'chan'=4] {'chan'}, dimensions={2} | all-to-all | bytes 3407872 | tf_op jit(solution)/shard_map/all_to_all | solution.py:46
  68.9 89.3 %all_to_all.21 = bf16[8,416,256]{2,1,0:T(8,128)(2,1)} all-to-all(bf16[8,416,256]{2,1,0:T(8,128)(2,1)S(1)} %bitcast.50), channel_id=1, replica_groups=mesh['tq'=4,'th'=2,'chan'=4] {'tq','th'}, dimensions={0} | all-to-all | bytes 3407872 | tf_op jit(solution)/shard_map/all_to_all | solution.py:49
  158.2 45.5 %all-gather.5.cloned.1.call-done = bf16[8,416,1024]{2,1,0:T(8,128)(2,1)} async-done(((bf16[2,416,1024]{2,1,0:T(8,128)(2,1)}), bf16[8,416,1024]{2,1,0:T(8,128)(2,1)}) %all-gather.5.cloned.1.call-update) | async-done | bytes 6815760 | tf_op jit(solution)/shard_map/all_gather | solution.py:43
  203.7 50.0 %all-gather.3.cloned.1.call-done = bf16[8,416,1024]{2,1,0:T(8,128)(2,1)} async-done(((bf16[8,416,256]{2,1,0:T(8,128)(2,1)}), bf16[8,416,1024]{2,1,0:T(8,128)(2,1)}) %all-gather.3.cloned.1.call-update) | async-done | bytes 6815760 | tf_op jit(solution)/shard_map/all_gather | solution.py:50
  253.7 7.0 %fusion.11 = f32[416,5,416]{2,0,1:T(8,128)S(1)} fusion(bf16[8,416,1024]{2,1,0:T(8,128)(2,1)} %all-gather.3.cloned.1.call-done, bf16[8,416,1024]{2,1,0:T(8,128)(2,1)} %all-gather.5.cloned.1.call-done), kind=kOutput, calls=%fused_computation.16 | convolution fusion | flops 2126512128 | bytes 12779520 | tf_op jit(solution)/shard_map/dot_general | solution.py:14
  260.7 0.8 copy-done.4
  261.5 3.3 fusion.24
  264.8 3.7 %fusion.20 = f32[416,5,416]{2,0,1:T(8,128)S(1)} fusion(f32[416,5,416]{2,0,1:T(8,128)S(1)} %fusion.24, bf16[8,416,1024]{2,1,0:T(8,128)(2,1)S(1)} %copy-done.4, bf16[8,416,1024]{2,1,0:T(8,128)(2,1)S(1)} %copy-done.3), kind=kOutput, calls=%fused_computation.20 | convolution fusion | flops 2835349504 | bytes 14483456 | tf_op jit(solution)/shard_map/dot_general | solution.py:14
  268.5 3.3 fusion.30
  271.7 2.8 fusion.17
  274.5 2.0 copy-done
  276.5 1.8 slice_select_fusion
  278.3 1.5 collective-permute-start.1
  279.8 0.7 minimum_reduce_fusion.1
  283.1 43.9 %collective-permute-done.1 = f32[208,5,416]{2,0,1:T(8,128)S(1)} collective-permute-done((f32[208,5,416]{2,0,1:T(8,128)}, f32[208,5,416]{2,0,1:T(8,128)S(1)}, u32[]{:S(2)}, u32[]{:S(2)}) %collective-permute-start.1) | collective-permute-done | bytes 1730592 | tf_op jit(solution)/shard_map/ppermute | solution.py:10
  327.0 4.4 %add_divide_fusion = f32[208,5,416]{2,0,1:T(8,128)} fusion(f32[208,5,416]{2,0,1:T(8,128)S(1)} %collective-permute-done.1, f32[416,5,416]{2,0,1:T(8,128)} %copy-done, f32[5]{0:T(128)S(1)} %stack.56, pred[]{:T(512)S(6)} %eq.6), kind=kLoop, calls=%fused_computation.11 | loop fusion | flops 1297920 | bytes 6922261 | tf_op jit(solution)/shard_map/div | solution.py:71
  (19 shorter events, 3.3 us)
Async XLA Ops:
  6.5 197.2 %all-gather.5.cloned.1.call-start = ((), (), s32[]{:S(2)}) async-start(), calls=%async_computation.3 | async-start | bytes 8519680 | tf_op jit(solution)/shard_map/all_gather | solution.py:43
  18.5 23.5 %copy-start.1 = (bf16[1,416,2048]{2,1,0:T(8,128)(2,1)S(1)}, bf16[1,416,2048]{2,1,0:T(8,128)(2,1)}, u32[]{:S(2)}) copy-start(bf16[1,416,2048]{2,1,0:T(8,128)(2,1)} %param.4) | copy-start | bytes 5111812
  18.5 21.9 %collective-permute-start = (bf16[416,1024]{1,0:T(8,128)(2,1)S(1)}, bf16[416,1024]{1,0:T(8,128)(2,1)S(1)}, u32[]{:S(2)}, u32[]{:S(2)}) collective-permute-start(bf16[416,1024]{1,0:T(8,128)(2,1)S(1)} %bitcast.52), channel_id=1, source_target_pairs={{0,4},{4,0},{1,5},{5,1},{2,6},{6,2},{3,7},{7,3},{8,12},{12,8},{9,1... | collective-permute-start | bytes 2555912 | tf_op jit(solution)/shard_map/ppermute | solution.py:10
  41.9 211.8 %all-gather.3.cloned.1.call-start = ((), (), s32[]{:S(2)}) async-start(), calls=%async_computation.2 | async-start | bytes 8519680 | tf_op jit(solution)/shard_map/all_gather | solution.py:50
  253.7 7.0 %copy-start.3 = (bf16[8,416,1024]{2,1,0:T(8,128)(2,1)S(1)}, bf16[8,416,1024]{2,1,0:T(8,128)(2,1)}, u32[]{:S(2)}) copy-start(bf16[8,416,1024]{2,1,0:T(8,128)(2,1)} %all-gather.5.cloned.1.call-done) | copy-start | bytes 20447236
  253.7 7.8 %copy-start.4 = (bf16[8,416,1024]{2,1,0:T(8,128)(2,1)S(1)}, bf16[8,416,1024]{2,1,0:T(8,128)(2,1)}, u32[]{:S(2)}) copy-start(bf16[8,416,1024]{2,1,0:T(8,128)(2,1)} %all-gather.3.cloned.1.call-done) | copy-start | bytes 20447236
  274.5 2.0 copy-start
  276.5 3.3 copy-start.2
  278.3 48.7 %collective-permute-start.1 = (f32[208,5,416]{2,0,1:T(8,128)}, f32[208,5,416]{2,0,1:T(8,128)S(1)}, u32[]{:S(2)}, u32[]{:S(2)}) collective-permute-start(f32[208,5,416]{2,0,1:T(8,128)} %slice_select_fusion), channel_id=1, source_target_pairs={{0,4},{4,0},{1,5},{5,1},{2,6},{6,2},{3,7},{7,3},{8,12},{12,8},{9,1... | collective-permute-start | bytes 5191688 | tf_op jit(solution)/shard_map/ppermute | solution.py:10
Sparse Core Ops, SparseCore 0:
  42.0 161.6 all-gather.4
  205.2 48.3 all-gather.2

commit v5 on v4

--- a/solution.py
+++ b/solution.py
@@ -10,10 +10,34 @@
     return lax.ppermute(x, "th", [(0, 1), (1, 0)])
 
 
+def gather_chan(x):
+    size = lax.axis_size("chan")
+    me = lax.axis_index("chan")
+    bits = size.bit_length() - 1
+    held = x[None]
+    for bit in reversed(range(bits)):
+        got = lax.ppermute(held, "chan", [(c, c ^ (1 << bit)) for c in range(size)])
+        low = ((me >> bit) & 1) == 0
+        first = jnp.where(low, held, got)
+        second = jnp.where(low, got, held)
+        held = jnp.concatenate([first, second], axis=0) if bit == bits - 1 else jnp.stack([first, second], axis=1).reshape((-1,) + x.shape)
+    return held
+
+
 def contract(left, right):
     return lax.dot_general(
-        left, right, (((0, 2), (0, 2)), ((), ())), preferred_element_type=jnp.float32
+        left, right, (((0, 1, 3), (0, 1, 3)), ((), ())), preferred_element_type=jnp.float32
     )
+
+
+def lag_block(background, analysis, cycle_total, max_lag, lag_total):
+    pieces = [None] * lag_total
+    for offset in range(max_lag + 1):
+        span = cycle_total - offset
+        pieces[max_lag + offset] = contract(background[:, offset:], analysis[:, :span])
+        if offset > 0:
+            pieces[max_lag - offset] = contract(background[:, :span], analysis[:, offset:])
+    return jnp.stack(pieces, axis=1)
 
 
 def body(analysis_dep, background_dep, valid_counts):
@@ -22,7 +46,8 @@
     chan_size = lax.axis_size("chan")
     lag_total = 5
     max_lag = (lag_total - 1) // 2
-    cycle_index = lax.axis_index("tq") * PAIR + lax.axis_index("th")
+    pair_index = lax.axis_index("th")
+    cycle_index = lax.axis_index("tq") * PAIR + pair_index
     own_count = jnp.sum(
         jnp.where(jnp.arange(cycle_total, dtype=jnp.int32) == cycle_index, valid_counts, 0)
     )
@@ -34,32 +59,26 @@
     local_analysis = jnp.where(valid_cols, analysis_dep[0], jnp.zeros((), jnp.bfloat16))
     local_background = jnp.where(valid_cols, background_dep[0], jnp.zeros((), jnp.bfloat16))
 
-    pair_index = lax.axis_index("th")
     halves = local_analysis.reshape(width_block, PAIR, half)
     keep = jnp.where(pair_index == 0, halves[:, 0], halves[:, 1])
     give = jnp.where(pair_index == 0, halves[:, 1], halves[:, 0])
     got = swap_pair(give)
     pair_analysis = jnp.where(pair_index == 0, jnp.stack([keep, got]), jnp.stack([got, keep]))
-    all_analysis = lax.all_gather(pair_analysis, "tq", axis=0, tiled=True)
+    pair_analysis = pair_analysis.reshape(PAIR, width_block, chan_size, piece).transpose(2, 0, 1, 3)
+    all_analysis = lax.all_gather(pair_analysis, "tq", axis=1, tiled=True)
 
     split_b = local_background.reshape(width_block, PAIR, chan_size, piece)
     by_loc = lax.all_to_all(split_b, "chan", 2, 0, tiled=True)
     by_loc = by_loc.reshape(quad_size, pair_rows, PAIR, piece).transpose(0, 2, 1, 3)
     by_loc = by_loc.reshape(quad_size * PAIR, pair_rows, piece)
     rows_here = lax.all_to_all(by_loc, ("tq", "th"), 0, 0, tiled=True)
-    all_background = lax.all_gather(rows_here, "chan", axis=2, tiled=True)
+    all_background = gather_chan(rows_here)
 
-    pieces = [None] * lag_total
-    for offset in range(max_lag + 1):
-        span = cycle_total - offset
-        pieces[max_lag + offset] = contract(all_background[offset:], all_analysis[:span])
-        if offset > 0:
-            pieces[max_lag - offset] = contract(all_background[:span], all_analysis[offset:])
-    partial = jnp.stack(pieces, axis=1)
-    rows_out = partial.shape[0] // PAIR
-    upper = jnp.where(pair_index == 0, partial[rows_out:], partial[:rows_out])
-    lower = jnp.where(pair_index == 0, partial[:rows_out], partial[rows_out:])
-    summed = lower + swap_pair(upper)
+    rows_out = pair_rows // PAIR
+    give_rows = lax.dynamic_slice_in_dim(all_background, (1 - pair_index) * rows_out, rows_out, axis=2)
+    keep_rows = lax.dynamic_slice_in_dim(all_background, pair_index * rows_out, rows_out, axis=2)
+    sent = swap_pair(lag_block(give_rows, all_analysis, cycle_total, max_lag, lag_total))
+    summed = lag_block(keep_rows, all_analysis, cycle_total, max_lag, lag_total) + sent
 
     denominators = []
     for offset in range(max_lag + 1):

time: 339 us -> 283 us (0.83)
  waiting for transfers between devices: 158 us -> 100 us
  blocking collectives: 114 us -> 87.6 us
  local copies, waits for them, and re-layouts: 9.15 us -> 18.6 us
  other arithmetic: 17.6 us -> 26.4 us
  matrix products: 20 us -> 25.1 us
  starting transfers between devices: 4.52 us -> 9.43 us
    all_gather x2 -> x1, waiting for transfers between devices: 95.5 us -> 4.73 us  [body(): all_analysis = lax.all_gather(pair_analysis, 'tq', axis=1, tiled=True)]
    ppermute x0 -> x2, waiting for transfers between devices: none -> 40.8 us  [gather_chan(): got = lax.ppermute(held, 'chan', [(c, c ^ 1 << bit) for c in range(size)])]
    all_to_all x1 -> x0, blocking collectives: 24.3 us -> none  [body(): by_loc = lax.all_to_all(split_b, 'chan', 2, 0, tiled=True)]
    ppermute x2, waiting for transfers between devices: 62.6 us -> 44.5 us  [swap_pair(): return lax.ppermute(x, 'th', [(0, 1), (1, 0)])]
    all_to_all x0 -> x1, waiting for transfers between devices: none -> 9.99 us  [body(): by_loc = lax.all_to_all(split_b, 'chan', 2, 0, tiled=True)]
    another operation x0 -> x2, other arithmetic: none -> 6.09 us  [gather_chan(): jnp.stack([first, second], axis=1).reshape((-1,) + x.shape)]
    another operation x0 -> x3, local copies, waits for them, and re-layouts: none -> 5.41 us  [the longest x1 3.28 us: gather_chan(): jnp.stack([first, second], axis=1).reshape((-1,) + x.shape)]
    dot_general x5 -> x10, matrix products: 20 us -> 25.1 us  [contract(): lax.dot_general(left, right, (((0, 1, 3), (0, 1, 3)), ((), ())), preferre...]
  transfers between devices with their start and end apart: 4 -> 6, of which waited for: 4 -> 6; matrix products, arithmetic and copies ran while one was open for 1% -> 13% of each run, Pallas kernels for 0% -> 0%
where the time goes in v5:
time: 283 us
  waiting for transfers between devices  100 us (35%)
  blocking collectives  87.6 us (31%)
  other arithmetic  26.4 us (9%)
  matrix products  25.1 us (9%)
  local copies, waits for them, and re-layouts  18.6 us (7%)
  between operations  15.5 us (5%)
  starting transfers between devices  9.43 us (3%)
    all_to_all x1, blocking collectives, body(): rows_here = lax.all_to_all(by_loc, ('tq', 'th'), 0, 0, tiled=True)  87.6 us
    ppermute x2, waiting for transfers between devices, swap_pair(): return lax.ppermute(x, 'th', [(0, 1), (1, 0)])  44.5 us
    ppermute x2, waiting for transfers between devices, gather_chan(): got = lax.ppermute(held, 'chan', [(c, c ^ 1 << bit) for c in range(size)])  40.8 us
    dot_general x10, matrix products, contract(): lax.dot_general(left, right, (((0, 1, 3), (0, 1, 3)), ((), ())), preferre...  25.1 us
    all_to_all x1, waiting for transfers between devices, body(): by_loc = lax.all_to_all(split_b, 'chan', 2, 0, tiled=True)  9.99 us
    select_n x1, other arithmetic, body(): keep = jnp.where(pair_index == 0, halves[:, 0], halves[:, 1])  6.66 us
    another operation x2, other arithmetic, gather_chan(): jnp.stack([first, second], axis=1).reshape((-1,) + x.shape)  6.09 us
  transfers between devices with their start and end apart: 6, of which 6 were waited for; matrix products, arithmetic and copies ran while one was open for 13% of the time, Pallas kernels for 0%

profile of v5, /device:TPU:0, one launch (start us, length us, event | category | flops | bytes accessed | tf_op | source)
XLA Modules:
  0.0 282.6 jit_solution(13103790644412454628)
XLA Ops:
  8.5 4.3 %squeeze.5 = bf16[416,2,1024]{2,1,0:T(2,128)(2,1)S(1)} reshape(bf16[1,416,2048]{2,1,0:T(8,128)(2,1)} %param.3) | data formatting | bytes 3407872 | tf_op jit(solution)/shard_map/squeeze | solution.py:59
  14.2 6.7 %fusion.28 = (bf16[416,1024]{1,0:T(8,128)(2,1)S(1)}, bf16[416,1,1024]{2,1,0:T(2,128)(2,1)S(1)}) fusion(pred[]{:T(512)S(6)} %eq.21, bf16[416,2,1024]{2,1,0:T(2,128)(2,1)S(1)} %broadcast_select_fusion), kind=kLoop, calls=%fused_computation.36 | loop fusion | flops 851968 | bytes 3407873 | tf_op jit(solution)/shard_map/jit(_where)/select_n | solution.py:63
  22.1 2.9 %collective-permute-start.2 = (bf16[416,1024]{1,0:T(8,128)(2,1)}, bf16[416,1024]{1,0:T(8,128)(2,1)}, u32[]{:S(2)}, u32[]{:S(2)}) collective-permute-start(bf16[416,1024]{1,0:T(8,128)(2,1)} %bitcast.106), channel_id=1, source_target_pairs={{0,4},{4,0},{1,5},{5,1},{2,6},{6,2},{3,7},{7,3},{8,12},{12,8},{9,1... | collective-permute-start | bytes 2555912 | tf_op jit(solution)/shard_map/ppermute | solution.py:10
  25.7 3.9 %squeeze.4 = bf16[416,2,4,256]{3,2,1,0:T(4,128)(2,1)S(1)} reshape(bf16[1,416,2048]{2,1,0:T(8,128)(2,1)} %param.4) | data formatting | bytes 3407872 | tf_op jit(solution)/shard_map/squeeze | solution.py:60
  30.3 2.5 copy.23
  32.8 3.6 %all-to-all-start = ((bf16[416,2,4,256]{3,1,0,2:T(2,128)(2,1)}), bf16[416,2,4,256]{3,1,0,2:T(2,128)(2,1)S(1)}, u32[]{:S(2)}, u32[]{:S(2)}) async-start(bf16[416,2,4,256]{3,1,0,2:T(2,128)(2,1)} %copy.23), calls=%async_computation | async-start | bytes 3407872 | tf_op jit(solution)/shard_map/all_to_all | solution.py:71
  37.2 7.1 %collective-permute-done.2 = bf16[416,1024]{1,0:T(8,128)(2,1)} collective-permute-done((bf16[416,1024]{1,0:T(8,128)(2,1)}, bf16[416,1024]{1,0:T(8,128)(2,1)}, u32[]{:S(2)}, u32[]{:S(2)}) %collective-permute-start.2) | collective-permute-done | bytes 852000 | tf_op jit(solution)/shard_map/ppermute | solution.py:10
  44.3 2.0 stack.74
  47.9 10.0 %all-to-all-done = bf16[416,2,4,256]{3,1,0,2:T(2,128)(2,1)S(1)} async-done(((bf16[416,2,4,256]{3,1,0,2:T(2,128)(2,1)}), bf16[416,2,4,256]{3,1,0,2:T(2,128)(2,1)S(1)}, u32[]{:S(2)}, u32[]{:S(2)}) %all-to-all-start) | async-done | bytes 1703968 | tf_op jit(solution)/shard_map/all_to_all | solution.py:71
  58.1 87.6 %all_to_all.20 = bf16[8,416,256]{2,1,0:T(8,128)(2,1)S(1)} all-to-all(bf16[8,416,256]{2,1,0:T(8,128)(2,1)S(1)} %bitcast.118), channel_id=1, replica_groups=mesh['tq'=4,'th'=2,'chan'=4] {'tq','th'}, dimensions={0} | all-to-all | bytes 3407872 | tf_op jit(solution)/shard_map/all_to_all | solution.py:74
  147.1 37.8 %collective-permute-done = bf16[1,8,416,256]{3,2,1,0:T(8,128)(2,1)} collective-permute-done((bf16[1,8,416,256]{3,2,1,0:T(8,128)(2,1)S(1)}, bf16[1,8,416,256]{3,2,1,0:T(8,128)(2,1)}, u32[]{:S(2)}, u32[]{:S(2)}) %collective-permute-start) | collective-permute-done | bytes 1703968 | tf_op jit(solution)/shard_map/ppermute | solution.py:19
  184.9 2.2 broadcast_select_fusion.5
  187.1 2.1 pad_maximum_fusion.1
  192.6 3.0 %collective-permute-done.1 = bf16[2,8,416,256]{3,2,1,0:T(8,128)(2,1)} collective-permute-done((bf16[2,8,416,256]{3,2,1,0:T(8,128)(2,1)}, bf16[2,8,416,256]{3,2,1,0:T(8,128)(2,1)}, u32[]{:S(2)}, u32[]{:S(2)}) %collective-permute-start.1) | collective-permute-done | bytes 3407904 | tf_op jit(solution)/shard_map/ppermute | solution.py:19
  195.6 3.5 %select_bitcast_fusion.1 = (bf16[2,1,8,416,256]{4,3,2,0,1:T(8,128)(2,1)S(1)}, bf16[2,1,8,416,256]{4,3,2,0,1:T(8,128)(2,1)}) fusion(bf16[2,8,416,256]{3,2,1,0:T(8,128)(2,1)} %collective-permute-done.1, pred[]{:T(512)S(6)} %eq.17, bf16[1,8,416,256]{3,2,1,0:T(8,128)(2,1)S(1)} %get-tuple-element.10, bf16[1,8,416,256]{3,2,1,0:T(8,128)(2,1)S(1)} %get-tuple-element.9), kind=kLoop, calls=%fused_computation.19 | loop fusion | flops 5111808 | bytes 13631489 | tf_op jit(solution)/shard_map/stack | solution.py:23
  199.1 2.6 pad_maximum_fusion
  201.6 3.3 %copy.25 = bf16[2,2,8,416,256]{4,3,2,1,0:T(8,128)(2,1)} copy(bf16[2,2,8,416,256]{4,3,2,0,1:T(8,128)(2,1)S(1)} %pad_maximum_fusion) | data formatting | bytes 13631488 | tf_op jit(solution)/shard_map/stack | solution.py:23
  204.9 4.7 %all-gather.2.cloned.1.call-done = bf16[4,8,416,256]{3,2,1,0:T(8,128)(2,1)} async-done(((bf16[4,2,416,256]{3,2,1,0:T(8,128)(2,1)}), bf16[4,8,416,256]{3,2,1,0:T(8,128)(2,1)}) %all-gather.2.cloned.1.call-update) | async-done | bytes 6815760 | tf_op jit(solution)/shard_map/all_gather | solution.py:68
  209.7 5.0 %fusion.97 = f32[208,5,416]{2,0,1:T(8,128)S(1)} fusion(bf16[4,8,416,256]{3,2,1,0:T(8,128)(2,1)} %all-gather.2.cloned.1.call-done, bf16[4,8,416,256]{3,2,1,0:T(8,128)(2,1)} %bitcast.107, s32[]{:T(128)S(6)} %select_n.95), kind=kOutput, calls=%fused_computation.57 | convolution fusion | flops 1063256064 | bytes 8945668 | tf_op jit(solution)/shard_map/dot_general | solution.py:28
  214.8 4.8 %fusion.45 = f32[208,5,416]{2,0,1:T(8,128)S(1)} fusion(f32[208,5,416]{2,0,1:T(8,128)S(1)} %fusion.97, bf16[4,8,416,256]{3,2,1,0:T(8,128)(2,1)} %all-gather.2.cloned.1.call-done, bf16[4,8,416,256]{3,2,1,0:T(8,128)(2,1)S(1)} %bitcast.108, s32[]{:T(128)S(6)} %select_n.95), kind=kOutput, calls=%fused_computation.45 | convolution fusion | flops 1240465408 | bytes 9797636 | tf_op jit(solution)/shard_map/dot_general | solution.py:28
  219.7 2.2 fusion.79
  221.9 1.9 fusion.65
  230.6 2.2 fusion.73
  236.4 37.4 %collective-permute-done.3 = f32[208,5,416]{2,0,1:T(8,128)S(1)} collective-permute-done((f32[208,5,416]{2,0,1:T(8,128)S(1)}, f32[208,5,416]{2,0,1:T(8,128)S(1)}, u32[]{:S(2)}, u32[]{:S(2)}) %collective-permute-start.3) | collective-permute-done | bytes 1730592 | tf_op jit(solution)/shard_map/ppermute | solution.py:10
  (36 shorter events, 23.7 us)
Async XLA Ops:
  22.1 22.2 %collective-permute-start.2 = (bf16[416,1024]{1,0:T(8,128)(2,1)}, bf16[416,1024]{1,0:T(8,128)(2,1)}, u32[]{:S(2)}, u32[]{:S(2)}) collective-permute-start(bf16[416,1024]{1,0:T(8,128)(2,1)} %bitcast.106), channel_id=1, source_target_pairs={{0,4},{4,0},{1,5},{5,1},{2,6},{6,2},{3,7},{7,3},{8,12},{12,8},{9,1... | collective-permute-start | bytes 2555912 | tf_op jit(solution)/shard_map/ppermute | solution.py:10
  32.8 25.0 %all-to-all-start = ((bf16[416,2,4,256]{3,1,0,2:T(2,128)(2,1)}), bf16[416,2,4,256]{3,1,0,2:T(2,128)(2,1)S(1)}, u32[]{:S(2)}, u32[]{:S(2)}) async-start(bf16[416,2,4,256]{3,1,0,2:T(2,128)(2,1)} %copy.23), calls=%async_computation | async-start | bytes 3407872 | tf_op jit(solution)/shard_map/all_to_all | solution.py:71
  36.4 173.2 %all-gather.2.cloned.1.call-start = ((), (), s32[]{:S(2)}) async-start(), calls=%async_computation.2 | async-start | bytes 8519680 | tf_op jit(solution)/shard_map/all_gather | solution.py:68
  145.7 1.4 copy-start.1
  145.7 39.1 %collective-permute-start = (bf16[1,8,416,256]{3,2,1,0:T(8,128)(2,1)S(1)}, bf16[1,8,416,256]{3,2,1,0:T(8,128)(2,1)}, u32[]{:S(2)}, u32[]{:S(2)}) collective-permute-start(bf16[1,8,416,256]{3,2,1,0:T(8,128)(2,1)S(1)} %bitcast.117), channel_id=1, source_target_pairs={{0,2},{1,3},{2,0},{3,1},{4,6},{5,7},{6,4},{7,5},{8,10},{9,11},{10,... | collective-permute-start | bytes 5111816 | tf_op jit(solution)/shard_map/ppermute | solution.py:19
  187.0 2.8 copy-start.2
  189.2 6.4 %collective-permute-start.1 = (bf16[2,8,416,256]{3,2,1,0:T(8,128)(2,1)}, bf16[2,8,416,256]{3,2,1,0:T(8,128)(2,1)}, u32[]{:S(2)}, u32[]{:S(2)}) collective-permute-start(bf16[2,8,416,256]{3,2,1,0:T(8,128)(2,1)} %pad_maximum_fusion.1), channel_id=1, source_target_pairs={{0,1},{1,0},{2,3},{3,2},{4,5},{5,4},{6,7},{7,6},{8,9},{9,8},{10,11... | collective-permute-start | bytes 10223624 | tf_op jit(solution)/shard_map/ppermute | solution.py:19
  209.7 5.2 %copy-start = (bf16[2,2,8,416,256]{4,3,2,1,0:T(8,128)(2,1)S(1)}, bf16[2,2,8,416,256]{4,3,2,1,0:T(8,128)(2,1)}, u32[]{:S(2)}) copy-start(bf16[2,2,8,416,256]{4,3,2,1,0:T(8,128)(2,1)} %copy.25) | copy-start | bytes 20447236
  209.7 10.0 %slice-start = ((s8[6815744]{0:T(1024)(128)(4,1)}), s8[4194304]{0:T(1024)(128)(4,1)S(1)}, s32[]{:S(2)}) async-start(s8[6815744]{0:T(1024)(128)(4,1)} %bitcast.119), calls=%async_computation.3 | async-start | bytes 8388608
  214.8 4.8 %slice-start.1 = ((s8[6815744]{0:T(1024)(128)(4,1)}), s8[2621440]{0:T(1024)(128)(4,1)S(1)}, s32[]{:S(2)}) async-start(s8[6815744]{0:T(1024)(128)(4,1)} %bitcast.119), calls=%async_computation.4 | async-start | bytes 5242880
  225.5 48.4 %collective-permute-start.3 = (f32[208,5,416]{2,0,1:T(8,128)S(1)}, f32[208,5,416]{2,0,1:T(8,128)S(1)}, u32[]{:S(2)}, u32[]{:S(2)}) collective-permute-start(f32[208,5,416]{2,0,1:T(8,128)S(1)} %fusion.117), channel_id=1, source_target_pairs={{0,4},{4,0},{1,5},{5,1},{2,6},{6,2},{3,7},{7,3},{8,12},{12,8},{9,1... | collective-permute-start | bytes 5191688 | tf_op jit(solution)/shard_map/ppermute | solution.py:10
Sparse Core Ops, SparseCore 0:
  48.0 161.6 all-gather.1

commit v6 on v5

--- a/solution.py
+++ b/solution.py
@@ -62,10 +62,15 @@
     halves = local_analysis.reshape(width_block, PAIR, half)
     keep = jnp.where(pair_index == 0, halves[:, 0], halves[:, 1])
     give = jnp.where(pair_index == 0, halves[:, 1], halves[:, 0])
+    def by_piece(x):
+        return x.reshape(width_block, chan_size, piece).transpose(1, 0, 2)[:, None]
+
+    same_parity = lax.all_gather(by_piece(keep), "tq", axis=1, tiled=True)
     got = swap_pair(give)
-    pair_analysis = jnp.where(pair_index == 0, jnp.stack([keep, got]), jnp.stack([got, keep]))
-    pair_analysis = pair_analysis.reshape(PAIR, width_block, chan_size, piece).transpose(2, 0, 1, 3)
-    all_analysis = lax.all_gather(pair_analysis, "tq", axis=1, tiled=True)
+    other_parity = lax.all_gather(by_piece(got), "tq", axis=1, tiled=True)
+    even = jnp.where(pair_index == 0, same_parity, other_parity)
+    odd = jnp.where(pair_index == 0, other_parity, same_parity)
+    all_analysis = jnp.stack([even, odd], axis=2).reshape(chan_size, cycle_total, width_block, piece)
 
     split_b = local_background.reshape(width_block, PAIR, chan_size, piece)
     by_loc = lax.all_to_all(split_b, "chan", 2, 0, tiled=True)

time: 283 us -> 284 us (level)
  blocking collectives: 87.6 us -> 25.5 us
  waiting for transfers between devices: 100 us -> 155 us
  other arithmetic: 26.4 us -> 31.9 us
    all_to_all x1, blocking collectives: 87.6 us -> 25.5 us  [body(): by_loc = lax.all_to_all(split_b, 'chan', 2, 0, tiled=True)]
    all_to_all x1, waiting for transfers between devices: 9.99 us -> 33.5 us  [body(): rows_here = lax.all_to_all(by_loc, ('tq', 'th'), 0, 0, tiled=True)]
    ppermute x2, waiting for transfers between devices: 44.5 us -> 66.9 us  [swap_pair(): return lax.ppermute(x, 'th', [(0, 1), (1, 0)])]
    all_gather x1 -> x2, waiting for transfers between devices: 4.73 us -> 17.2 us  [the longest x1 17.2 us: body(): other_parity = lax.all_gather(by_piece(got), 'tq', axis=1, tiled=True)]
    select_n x0 -> x1, other arithmetic: none -> 3.44 us  [body(): even = jnp.where(pair_index == 0, same_parity, other_parity)]
    another operation x0 -> x1, other arithmetic: none -> 3.38 us  [body(): jnp.stack([even, odd], axis=2)]
    ppermute x2, waiting for transfers between devices: 40.8 us -> 37.7 us  [gather_chan(): got = lax.ppermute(held, 'chan', [(c, c ^ 1 << bit) for c in range(size)])]
  transfers between devices with their start and end apart: 6 -> 7, of which waited for: 6 -> 5; matrix products, arithmetic and copies ran while one was open for 13% -> 12% of each run, Pallas kernels for 0% -> 0%
where the time goes in v6:
time: 284 us; the launch traced here: 283 us
  waiting for transfers between devices  155 us (55%)
  other arithmetic  31.9 us (11%)
  blocking collectives  25.5 us (9%)
  matrix products  25.1 us (9%)
  local copies, waits for them, and re-layouts  19 us (7%)
  between operations  15.6 us (5%)
  starting transfers between devices  10.8 us (4%)
    ppermute x2, waiting for transfers between devices, swap_pair(): return lax.ppermute(x, 'th', [(0, 1), (1, 0)])  66.9 us
    ppermute x2, waiting for transfers between devices, gather_chan(): got = lax.ppermute(held, 'chan', [(c, c ^ 1 << bit) for c in range(size)])  37.7 us
    all_to_all x1, waiting for transfers between devices, body(): rows_here = lax.all_to_all(by_loc, ('tq', 'th'), 0, 0, tiled=True)  33.5 us
    all_to_all x1, blocking collectives, body(): by_loc = lax.all_to_all(split_b, 'chan', 2, 0, tiled=True)  25.5 us
    dot_general x10, matrix products, contract(): lax.dot_general(left, right, (((0, 1, 3), (0, 1, 3)), ((), ())), preferre...  25.1 us
    all_gather x1, waiting for transfers between devices, body(): other_parity = lax.all_gather(by_piece(got), 'tq', axis=1, tiled=True)  17.2 us
    select_n x1, other arithmetic, body(): keep = jnp.where(pair_index == 0, halves[:, 0], halves[:, 1])  6.66 us
    another operation x2, other arithmetic, gather_chan(): jnp.stack([first, second], axis=1).reshape((-1,) + x.shape)  6.09 us
  transfers between devices with their start and end apart: 7, of which 5 were waited for; matrix products, arithmetic and copies ran while one was open for 12% of the time, Pallas kernels for 0%

profile of v6, /device:TPU:0, one launch (start us, length us, event | category | flops | bytes accessed | tf_op | source)
XLA Modules:
  0.0 283.2 jit_solution(16194565753097837672)
XLA Ops:
  8.6 4.3 %squeeze.5 = bf16[416,2,1024]{2,1,0:T(2,128)(2,1)S(1)} reshape(bf16[1,416,2048]{2,1,0:T(8,128)(2,1)} %param.3) | data formatting | bytes 3407872 | tf_op jit(solution)/shard_map/squeeze | solution.py:59
  14.3 6.7 %fusion.28 = (bf16[416,1024]{1,0:T(8,128)(2,1)S(1)}, bf16[416,1,1024]{2,1,0:T(2,128)(2,1)S(1)}) fusion(pred[]{:T(512)S(6)} %eq.22, bf16[416,2,1024]{2,1,0:T(2,128)(2,1)S(1)} %broadcast_select_fusion.2), kind=kLoop, calls=%fused_computation.39 | loop fusion | flops 851968 | bytes 3407873 | tf_op jit(solution)/shard_map/jit(_where)/select_n | solution.py:63
  22.5 3.9 %squeeze.4 = bf16[416,2,4,256]{3,2,1,0:T(4,128)(2,1)S(1)} reshape(bf16[1,416,2048]{2,1,0:T(8,128)(2,1)} %param.4) | data formatting | bytes 3407872 | tf_op jit(solution)/shard_map/squeeze | solution.py:60
  29.1 25.5 %all_to_all.20 = bf16[416,2,4,256]{3,1,0,2:T(2,128)(2,1)S(1)} all-to-all(bf16[416,2,4,256]{3,1,0,2:T(2,128)(2,1)S(1)} %copy.19), channel_id=1, replica_groups=mesh['tq'=4,'th'=2,'chan'=4] {'chan'}, dimensions={2} | all-to-all | bytes 3407872 | tf_op jit(solution)/shard_map/all_to_all | solution.py:76
  56.1 5.8 %all-to-all-start.1 = ((bf16[8,416,256]{2,1,0:T(8,128)(2,1)}), bf16[8,416,256]{2,1,0:T(8,128)(2,1)S(1)}, u32[]{:S(2)}, u32[]{:S(2)}) async-start(bf16[8,416,256]{2,1,0:T(8,128)(2,1)} %bitcast.139), calls=%async_computation.1 | async-start | bytes 3407872 | tf_op jit(solution)/shard_map/all_to_all | solution.py:79
  64.3 29.8 %collective-permute-done.2 = bf16[416,1024]{1,0:T(8,128)(2,1)S(1)} collective-permute-done((bf16[416,1024]{1,0:T(8,128)(2,1)S(1)}, bf16[416,1024]{1,0:T(8,128)(2,1)S(1)}, u32[]{:S(2)}, u32[]{:S(2)}) %collective-permute-start.2) | collective-permute-done | bytes 852000 | tf_op jit(solution)/shard_map/ppermute | solution.py:10
  95.6 33.5 %all-to-all-done.1 = bf16[8,416,256]{2,1,0:T(8,128)(2,1)S(1)} async-done(((bf16[8,416,256]{2,1,0:T(8,128)(2,1)}), bf16[8,416,256]{2,1,0:T(8,128)(2,1)S(1)}, u32[]{:S(2)}, u32[]{:S(2)}) %all-to-all-start.1) | async-done | bytes 1703968 | tf_op jit(solution)/shard_map/all_to_all | solution.py:79
  130.5 37.7 %collective-permute-done = bf16[1,8,416,256]{3,2,1,0:T(8,128)(2,1)} collective-permute-done((bf16[1,8,416,256]{3,2,1,0:T(8,128)(2,1)S(1)}, bf16[1,8,416,256]{3,2,1,0:T(8,128)(2,1)}, u32[]{:S(2)}, u32[]{:S(2)}) %collective-permute-start) | collective-permute-done | bytes 1703968 | tf_op jit(solution)/shard_map/ppermute | solution.py:19
  168.2 2.2 broadcast_select_fusion.7
  170.4 2.1 pad_maximum_fusion.2
  176.0 17.2 %all-gather.7.cloned.1.call-done = bf16[4,1664,256]{2,0,1:T(4,128)(2,1)} async-done(((bf16[4,416,256]{2,0,1:T(4,128)(2,1)}), bf16[4,1664,256]{2,0,1:T(4,128)(2,1)}) %all-gather.7.cloned.1.call-update) | async-done | bytes 3407888 | tf_op jit(solution)/shard_map/all_gather | solution.py:70
  193.2 3.4 %broadcast_select_fusion.1 = (bf16[8,832,256]{2,0,1:T(8,128)(2,1)S(1)}, bf16[8,832,256]{2,0,1:T(8,128)(2,1)S(1)}) fusion(bf16[8,832,256]{2,0,1:T(8,128)(2,1)} %bitcast.142, bf16[8,832,256]{2,0,1:T(8,128)(2,1)} %bitcast.143, pred[]{:T(512)S(6)} %eq.22), kind=kLoop, calls=%fused_computation.22 | loop fusion | flops 3407872 | bytes 13631489 | tf_op jit(solution)/shard_map/jit(_where)/select_n | solution.py:71
  197.8 3.4 %pad_maximum_fusion.1 = bf16[4,4,2,416,256]{4,3,2,1,0:T(8,128)(2,1)} fusion(bf16[4,4,1,416,256]{4,3,2,1,0:T(8,128)(2,1)S(1)} %copy.23, bf16[4,4,1,416,256]{4,3,2,1,0:T(8,128)(2,1)S(1)} %copy.22), kind=kLoop, calls=%fused_computation.1 | loop fusion | flops 3407872 | bytes 13631488 | tf_op jit(solution)/shard_map/stack | solution.py:73
  201.1 3.5 %select_bitcast_fusion.1 = (bf16[2,1,8,416,256]{4,3,2,0,1:T(8,128)(2,1)S(1)}, bf16[2,1,8,416,256]{4,3,2,0,1:T(8,128)(2,1)}) fusion(bf16[2,8,416,256]{3,2,1,0:T(8,128)(2,1)} %collective-permute-done.1, pred[]{:T(512)S(6)} %eq.18, bf16[1,8,416,256]{3,2,1,0:T(8,128)(2,1)S(1)} %get-tuple-element.12, bf16[1,8,416,256]{3,2,1,0:T(8,128)(2,1)S(1)} %get-tuple-element.11), kind=kLoop, calls=%fused_computation.20 | loop fusion | flops 5111808 | bytes 13631489 | tf_op jit(solution)/shard_map/stack | solution.py:23
  204.7 2.6 pad_maximum_fusion
  207.2 3.3 %copy.21 = bf16[2,2,8,416,256]{4,3,2,1,0:T(8,128)(2,1)} copy(bf16[2,2,8,416,256]{4,3,2,0,1:T(8,128)(2,1)S(1)} %pad_maximum_fusion) | data formatting | bytes 13631488 | tf_op jit(solution)/shard_map/stack | solution.py:23
  210.5 5.0 %fusion.96 = f32[208,5,416]{2,0,1:T(8,128)S(1)} fusion(bf16[4,8,416,256]{3,2,1,0:T(8,128)(2,1)} %bitcast.116, bf16[4,8,416,256]{3,2,1,0:T(8,128)(2,1)} %bitcast.128, s32[]{:T(128)S(6)} %select_n.92), kind=kOutput, calls=%fused_computation.58 | convolution fusion | flops 1063256064 | bytes 8945668 | tf_op jit(solution)/shard_map/dot_general | solution.py:28
  215.7 4.8 %fusion.44 = f32[208,5,416]{2,0,1:T(8,128)S(1)} fusion(f32[208,5,416]{2,0,1:T(8,128)S(1)} %fusion.96, bf16[4,8,416,256]{3,2,1,0:T(8,128)(2,1)} %bitcast.117, bf16[4,8,416,256]{3,2,1,0:T(8,128)(2,1)S(1)} %bitcast.129, s32[]{:T(128)S(6)} %select_n.92), kind=kOutput, calls=%fused_computation.46 | convolution fusion | flops 1240465408 | bytes 9797636 | tf_op jit(solution)/shard_map/dot_general | solution.py:28
  220.6 2.2 fusion.78
  222.7 1.9 fusion.64
  229.6 1.9 fusion.34
  231.5 2.2 fusion.72
  233.7 1.9 fusion.54
  237.3 37.2 %collective-permute-done.3 = f32[208,5,416]{2,0,1:T(8,128)S(1)} collective-permute-done((f32[208,5,416]{2,0,1:T(8,128)S(1)}, f32[208,5,416]{2,0,1:T(8,128)S(1)}, u32[]{:S(2)}, u32[]{:S(2)}) %collective-permute-start.3) | collective-permute-done | bytes 1730592 | tf_op jit(solution)/shard_map/ppermute | solution.py:10
  (40 shorter events, 25.5 us)
Async XLA Ops:
  6.5 169.5 %all-gather.5.cloned.1.call-start = ((), (), s32[]{:S(2)}) async-start(), calls=%async_computation.2 | async-start | bytes 4259840 | tf_op jit(solution)/shard_map/all_gather | solution.py:68
  56.1 73.0 %all-to-all-start.1 = ((bf16[8,416,256]{2,1,0:T(8,128)(2,1)}), bf16[8,416,256]{2,1,0:T(8,128)(2,1)S(1)}, u32[]{:S(2)}, u32[]{:S(2)}) async-start(bf16[8,416,256]{2,1,0:T(8,128)(2,1)} %bitcast.139), calls=%async_computation.1 | async-start | bytes 3407872 | tf_op jit(solution)/shard_map/all_to_all | solution.py:79
  61.9 131.3 %all-gather.7.cloned.1.call-start = ((), (), s32[]{:S(2)}) async-start(), calls=%async_computation.3 | async-start | bytes 4259840 | tf_op jit(solution)/shard_map/all_gather | solution.py:70
  62.4 31.6 %collective-permute-start.2 = (bf16[416,1024]{1,0:T(8,128)(2,1)S(1)}, bf16[416,1024]{1,0:T(8,128)(2,1)S(1)}, u32[]{:S(2)}, u32[]{:S(2)}) collective-permute-start(bf16[416,1024]{1,0:T(8,128)(2,1)S(1)} %bitcast.144), channel_id=1, source_target_pairs={{0,4},{4,0},{1,5},{5,1},{2,6},{6,2},{3,7},{7,3},{8,12},{12,8},{9,1... | collective-permute-start | bytes 2555912 | tf_op jit(solution)/shard_map/ppermute | solution.py:10
  129.1 1.4 copy-start.1
  129.1 39.1 %collective-permute-start = (bf16[1,8,416,256]{3,2,1,0:T(8,128)(2,1)S(1)}, bf16[1,8,416,256]{3,2,1,0:T(8,128)(2,1)}, u32[]{:S(2)}, u32[]{:S(2)}) collective-permute-start(bf16[1,8,416,256]{3,2,1,0:T(8,128)(2,1)S(1)} %bitcast.138), channel_id=1, source_target_pairs={{0,2},{1,3},{2,0},{3,1},{4,6},{5,7},{6,4},{7,5},{8,10},{9,11},{10,... | collective-permute-start | bytes 5111816 | tf_op jit(solution)/shard_map/ppermute | solution.py:19
  170.4 2.8 copy-start.2
  172.5 28.6 %collective-permute-start.1 = (bf16[2,8,416,256]{3,2,1,0:T(8,128)(2,1)}, bf16[2,8,416,256]{3,2,1,0:T(8,128)(2,1)}, u32[]{:S(2)}, u32[]{:S(2)}) collective-permute-start(bf16[2,8,416,256]{3,2,1,0:T(8,128)(2,1)} %pad_maximum_fusion.2), channel_id=1, source_target_pairs={{0,1},{1,0},{2,3},{3,2},{4,5},{5,4},{6,7},{7,6},{8,9},{9,8},{10,11... | collective-permute-start | bytes 10223624 | tf_op jit(solution)/shard_map/ppermute | solution.py:19
  210.5 5.2 %copy-start = (bf16[2,2,8,416,256]{4,3,2,1,0:T(8,128)(2,1)S(1)}, bf16[2,2,8,416,256]{4,3,2,1,0:T(8,128)(2,1)}, u32[]{:S(2)}) copy-start(bf16[2,2,8,416,256]{4,3,2,1,0:T(8,128)(2,1)} %copy.21) | copy-start | bytes 20447236
  210.5 10.0 %slice-start = ((s8[6815744]{0:T(1024)(128)(4,1)}), s8[4194304]{0:T(1024)(128)(4,1)S(1)}, s32[]{:S(2)}) async-start(s8[6815744]{0:T(1024)(128)(4,1)} %bitcast.118), calls=%async_computation.4 | async-start | bytes 8388608
  215.7 4.8 %slice-start.1 = ((s8[6815744]{0:T(1024)(128)(4,1)}), s8[2621440]{0:T(1024)(128)(4,1)S(1)}, s32[]{:S(2)}) async-start(s8[6815744]{0:T(1024)(128)(4,1)} %bitcast.118), calls=%async_computation.5 | async-start | bytes 5242880
  226.4 48.1 %collective-permute-start.3 = (f32[208,5,416]{2,0,1:T(8,128)S(1)}, f32[208,5,416]{2,0,1:T(8,128)S(1)}, u32[]{:S(2)}, u32[]{:S(2)}) collective-permute-start(f32[208,5,416]{2,0,1:T(8,128)S(1)} %fusion.116), channel_id=1, source_target_pairs={{0,4},{4,0},{1,5},{5,1},{2,6},{6,2},{3,7},{7,3},{8,12},{12,8},{9,1... | collective-permute-start | bytes 5191688 | tf_op jit(solution)/shard_map/ppermute | solution.py:10
Sparse Core Ops, SparseCore 0:
  22.6 102.2 all-gather.4
  126.5 66.7 all-gather.6

commit v7 on v6

--- a/solution.py
+++ b/solution.py
@@ -30,13 +30,11 @@
     )
 
 
-def lag_block(background, analysis, cycle_total, max_lag, lag_total):
-    pieces = [None] * lag_total
-    for offset in range(max_lag + 1):
-        span = cycle_total - offset
-        pieces[max_lag + offset] = contract(background[:, offset:], analysis[:, :span])
-        if offset > 0:
-            pieces[max_lag - offset] = contract(background[:, :span], analysis[:, offset:])
+def lag_block(shifted, even, odd, max_lag, lag_total):
+    pieces = []
+    for k in range(lag_total):
+        lag = k - max_lag
+        pieces.append(contract(shifted(lag), even) + contract(shifted(lag + 1), odd))
     return jnp.stack(pieces, axis=1)
 
 
@@ -70,20 +68,29 @@
     other_parity = lax.all_gather(by_piece(got), "tq", axis=1, tiled=True)
     even = jnp.where(pair_index == 0, same_parity, other_parity)
     odd = jnp.where(pair_index == 0, other_parity, same_parity)
-    all_analysis = jnp.stack([even, odd], axis=2).reshape(chan_size, cycle_total, width_block, piece)
 
     split_b = local_background.reshape(width_block, PAIR, chan_size, piece)
     by_loc = lax.all_to_all(split_b, "chan", 2, 0, tiled=True)
     by_loc = by_loc.reshape(quad_size, pair_rows, PAIR, piece).transpose(0, 2, 1, 3)
+    rows_out = pair_rows // PAIR
+    by_loc = by_loc.reshape(quad_size, PAIR, PAIR, rows_out, piece)
+    by_loc = jnp.stack([by_loc[:, 0], by_loc[:, 1, ::-1]], axis=1)
     by_loc = by_loc.reshape(quad_size * PAIR, pair_rows, piece)
     rows_here = lax.all_to_all(by_loc, ("tq", "th"), 0, 0, tiled=True)
     all_background = gather_chan(rows_here)
+    by_parity = all_background.reshape(chan_size, quad_size, PAIR, pair_rows, piece).transpose(0, 2, 1, 3, 4)
+    padded = jnp.pad(by_parity, ((0, 0), (0, 0), (1, 1), (0, 0), (0, 0)))
 
-    rows_out = pair_rows // PAIR
-    give_rows = lax.dynamic_slice_in_dim(all_background, (1 - pair_index) * rows_out, rows_out, axis=2)
-    keep_rows = lax.dynamic_slice_in_dim(all_background, pair_index * rows_out, rows_out, axis=2)
-    sent = swap_pair(lag_block(give_rows, all_analysis, cycle_total, max_lag, lag_total))
-    summed = lag_block(keep_rows, all_analysis, cycle_total, max_lag, lag_total) + sent
+    def own_rows(lag):
+        start = 1 + lag // 2
+        return padded[:, lag % 2, start:start + quad_size, :rows_out]
+
+    def partner_rows(lag):
+        start = 1 + lag // 2
+        return padded[:, lag % 2, start:start + quad_size, rows_out:]
+
+    sent = swap_pair(lag_block(partner_rows, even, odd, max_lag, lag_total))
+    summed = lag_block(own_rows, even, odd, max_lag, lag_total) + sent
 
     denominators = []
     for offset in range(max_lag + 1):

time: 284 us -> 291 us (1.025)
  waiting for transfers between devices: 155 us -> 161 us
    all_to_all x1, waiting for transfers between devices: 33.5 us -> 63.1 us  [body(): rows_here = lax.all_to_all(by_loc, ('tq', 'th'), 0, 0, tiled=True)]
    ppermute x2, waiting for transfers between devices: 66.9 us -> 40.4 us  [swap_pair(): return lax.ppermute(x, 'th', [(0, 1), (1, 0)])]
    all_gather x1, waiting for transfers between devices: 17.2 us -> 21.6 us  [body(): other_parity = lax.all_gather(by_piece(got), 'tq', axis=1, tiled=True)]
    dot_general x10 -> x20, matrix products: 25.1 us -> 24.5 us  [contract(): lax.dot_general(left, right, (((0, 1, 3), (0, 1, 3)), ((), ())), preferre...]
  transfers between devices with their start and end apart: 7 -> 7, of which waited for: 5 -> 4; matrix products, arithmetic and copies ran while one was open for 12% -> 9% of each run, Pallas kernels for 0% -> 0%
where the time goes in v7:
time: 291 us
  waiting for transfers between devices  161 us (55%)
  other arithmetic  32.3 us (11%)
  blocking collectives  25.5 us (9%)
  matrix products  24.5 us (8%)
  local copies, waits for them, and re-layouts  20.4 us (7%)
  between operations  15.5 us (5%)
  starting transfers between devices  10.8 us (4%)
    all_to_all x1, waiting for transfers between devices, body(): rows_here = lax.all_to_all(by_loc, ('tq', 'th'), 0, 0, tiled=True)  63.1 us
    ppermute x2, waiting for transfers between devices, swap_pair(): return lax.ppermute(x, 'th', [(0, 1), (1, 0)])  40.4 us
    ppermute x2, waiting for transfers between devices, gather_chan(): got = lax.ppermute(held, 'chan', [(c, c ^ 1 << bit) for c in range(size)])  36.3 us
    all_to_all x1, blocking collectives, body(): by_loc = lax.all_to_all(split_b, 'chan', 2, 0, tiled=True)  25.5 us
    dot_general x20, matrix products, contract(): lax.dot_general(left, right, (((0, 1, 3), (0, 1, 3)), ((), ())), preferre...  24.5 us
    all_gather x1, waiting for transfers between devices, body(): other_parity = lax.all_gather(by_piece(got), 'tq', axis=1, tiled=True)  21.6 us
    another operation x2, other arithmetic, gather_chan(): jnp.stack([first, second], axis=1).reshape((-1,) + x.shape)  8.18 us
    select_n x1, other arithmetic, body(): keep = jnp.where(pair_index == 0, halves[:, 0], halves[:, 1])  6.66 us
  transfers between devices with their start and end apart: 7, of which 4 were waited for; matrix products, arithmetic and copies ran while one was open for 9% of the time, Pallas kernels for 0%

profile of v7, /device:TPU:0, one launch (start us, length us, event | category | flops | bytes accessed | tf_op | source)
XLA Modules:
  0.0 290.6 jit_solution(918875343514113210)
XLA Ops:
  6.5 4.3 %squeeze.56 = bf16[416,2,1024]{2,1,0:T(2,128)(2,1)S(1)} reshape(bf16[1,416,2048]{2,1,0:T(8,128)(2,1)} %param.3) | data formatting | bytes 3407872 | tf_op jit(solution)/shard_map/squeeze | solution.py:57
  13.5 6.7 %fusion = (bf16[416,1024]{1,0:T(8,128)(2,1)S(1)}, bf16[416,1,1024]{2,1,0:T(2,128)(2,1)S(1)}) fusion(pred[]{:T(512)S(6)} %eq.22, bf16[416,2,1024]{2,1,0:T(2,128)(2,1)S(1)} %broadcast_select_fusion.2), kind=kLoop, calls=%fused_computation.19 | loop fusion | flops 851968 | bytes 3407873 | tf_op jit(solution)/shard_map/jit(_where)/select_n | solution.py:61
  20.2 1.5 select_n.80
  21.8 3.9 %squeeze.54 = bf16[416,2,4,256]{3,2,1,0:T(4,128)(2,1)S(1)} reshape(bf16[1,416,2048]{2,1,0:T(8,128)(2,1)} %param.4) | data formatting | bytes 3407872 | tf_op jit(solution)/shard_map/squeeze | solution.py:58
  27.0 25.5 %all_to_all.20 = bf16[416,2,4,256]{3,0,1,2:T(8,128)(2,1)S(1)} all-to-all(bf16[416,2,4,256]{3,0,1,2:T(8,128)(2,1)S(1)} %copy_select_fusion), channel_id=1, replica_groups=mesh['tq'=4,'th'=2,'chan'=4] {'chan'}, dimensions={2} | all-to-all | bytes 3407872 | tf_op jit(solution)/shard_map/all_to_all | solution.py:73
  53.7 2.5 pad_maximum_fusion.2
  56.2 5.8 %all-to-all-start.1 = ((bf16[8,416,256]{2,1,0:T(8,128)(2,1)}), bf16[8,416,256]{2,1,0:T(8,128)(2,1)S(1)}, u32[]{:S(2)}, u32[]{:S(2)}) async-start(bf16[8,416,256]{2,1,0:T(8,128)(2,1)} %bitcast.361), calls=%async_computation.1 | async-start | bytes 3407872 | tf_op jit(solution)/shard_map/all_to_all | solution.py:79
  63.3 2.0 collective-permute-start.2
  65.2 63.1 %all-to-all-done.1 = bf16[8,416,256]{2,1,0:T(8,128)(2,1)S(1)} async-done(((bf16[8,416,256]{2,1,0:T(8,128)(2,1)}), bf16[8,416,256]{2,1,0:T(8,128)(2,1)S(1)}, u32[]{:S(2)}, u32[]{:S(2)}) %all-to-all-start.1) | async-done | bytes 1703968 | tf_op jit(solution)/shard_map/all_to_all | solution.py:79
  128.4 1.5 collective-permute-start
  129.8 1.5 reshape.43
  131.4 36.3 %collective-permute-done = bf16[1,8,416,256]{3,2,1,0:T(8,128)(2,1)} collective-permute-done((bf16[1,8,416,256]{3,2,1,0:T(8,128)(2,1)S(1)}, bf16[1,8,416,256]{3,2,1,0:T(8,128)(2,1)}, u32[]{:S(2)}, u32[]{:S(2)}) %collective-permute-start) | collective-permute-done | bytes 1703968 | tf_op jit(solution)/shard_map/ppermute | solution.py:19
  167.7 2.2 broadcast_select_fusion.6
  169.8 2.1 pad_maximum_fusion.1
  175.3 21.6 %all-gather.7.cloned.1.call-done = bf16[4,1664,256]{2,0,1:T(4,128)(2,1)} async-done(((bf16[4,416,256]{2,0,1:T(4,128)(2,1)}), bf16[4,1664,256]{2,0,1:T(4,128)(2,1)}) %all-gather.7.cloned.1.call-update) | async-done | bytes 3407888 | tf_op jit(solution)/shard_map/all_gather | solution.py:68
  196.9 3.4 %broadcast_select_fusion.1 = (bf16[8,832,256]{2,0,1:T(8,128)(2,1)S(1)}, bf16[8,832,256]{2,0,1:T(8,128)(2,1)S(1)}) fusion(bf16[8,832,256]{2,0,1:T(8,128)(2,1)} %bitcast.365, bf16[8,832,256]{2,0,1:T(8,128)(2,1)} %bitcast.366, pred[]{:T(512)S(6)} %eq.22), kind=kLoop, calls=%fused_computation.14 | loop fusion | flops 3407872 | bytes 13631489 | tf_op jit(solution)/shard_map/jit(_where)/select_n | solution.py:69
  200.4 4.6 %select_bitcast_fusion.1 = (bf16[2,1,8,416,256]{4,3,2,0,1:T(8,128)(2,1)}, bf16[2,1,8,416,256]{4,3,2,0,1:T(8,128)(2,1)}) fusion(bf16[2,8,416,256]{3,2,1,0:T(8,128)(2,1)} %collective-permute-done.1, pred[]{:T(512)S(6)} %eq.18, bf16[1,8,416,256]{3,2,1,0:T(8,128)(2,1)S(1)} %get-tuple-element.12, bf16[1,8,416,256]{3,2,1,0:T(8,128)(2,1)S(1)} %get-tuple-element.11), kind=kLoop, calls=%fused_computation.12 | loop fusion | flops 5111808 | bytes 13631489 | tf_op jit(solution)/shard_map/stack | solution.py:23
  204.9 3.6 %pad_maximum_fusion = bf16[2,2,8,416,256]{4,3,2,0,1:T(8,128)(2,1)S(1)} fusion(bf16[2,1,8,416,256]{4,3,2,0,1:T(8,128)(2,1)} %get-tuple-element.10, bf16[2,1,8,416,256]{4,3,2,0,1:T(8,128)(2,1)} %get-tuple-element.9), kind=kLoop, calls=%fused_computation.8 | loop fusion | flops 3407872 | bytes 13631488 | tf_op jit(solution)/shard_map/stack | solution.py:23
  208.6 3.2 %copy.53 = bf16[2,2,8,416,256]{4,3,2,1,0:T(8,128)(2,1)} copy(bf16[2,2,8,416,256]{4,3,2,0,1:T(8,128)(2,1)S(1)} %pad_maximum_fusion) | data formatting | bytes 13631488 | tf_op jit(solution)/shard_map/stack | solution.py:23
  211.8 3.5 %copy.139 = bf16[4,4,2,416,256]{4,3,1,0,2:T(8,128)(2,1)S(1)} copy(bf16[4,4,2,416,256]{4,3,2,1,0:T(8,128)(2,1)} %bitcast.359) | data formatting | bytes 13631488 | tf_op jit(solution)/shard_map/reshape;reshape | solution.py:81
  226.2 1.5 fusion.51
  233.8 1.5 collective-permute-start.3
  241.4 40.4 %collective-permute-done.3 = f32[208,5,416]{2,0,1:T(8,128)S(1)} collective-permute-done((f32[208,5,416]{2,0,1:T(8,128)S(1)}, f32[208,5,416]{2,0,1:T(8,128)S(1)}, u32[]{:S(2)}, u32[]{:S(2)}) %collective-permute-start.3) | collective-permute-done | bytes 1730592 | tf_op jit(solution)/shard_map/ppermute | solution.py:10
  281.9 1.9 add_divide_fusion
  (42 shorter events, 30.9 us)
Async XLA Ops:
  6.5 4.4 %copy-start.1 = (s32[8]{0:T(128)S(1)}, s32[8]{0:T(128)}, u32[]{:S(2)}) copy-start(s32[8]{0:T(128)} %param.5) | copy-start | bytes 100
  6.5 168.8 %all-gather.5.cloned.1.call-start = ((), (), s32[]{:S(2)}) async-start(), calls=%async_computation.2 | async-start | bytes 4259840 | tf_op jit(solution)/shard_map/all_gather | solution.py:66
  56.2 72.2 %all-to-all-start.1 = ((bf16[8,416,256]{2,1,0:T(8,128)(2,1)}), bf16[8,416,256]{2,1,0:T(8,128)(2,1)S(1)}, u32[]{:S(2)}, u32[]{:S(2)}) async-start(bf16[8,416,256]{2,1,0:T(8,128)(2,1)} %bitcast.361), calls=%async_computation.1 | async-start | bytes 3407872 | tf_op jit(solution)/shard_map/all_to_all | solution.py:79
  62.0 135.0 %all-gather.7.cloned.1.call-start = ((), (), s32[]{:S(2)}) async-start(), calls=%async_computation.3 | async-start | bytes 4259840 | tf_op jit(solution)/shard_map/all_gather | solution.py:68
  63.3 66.6 %collective-permute-start.2 = (bf16[416,1024]{1,0:T(8,128)(2,1)}, bf16[416,1024]{1,0:T(8,128)(2,1)S(1)}, u32[]{:S(2)}, u32[]{:S(2)}) collective-permute-start(bf16[416,1024]{1,0:T(8,128)(2,1)} %bitcast.314), channel_id=1, source_target_pairs={{0,4},{4,0},{1,5},{5,1},{2,6},{6,2},{3,7},{7,3},{8,12},{12,8},{9,1... | collective-permute-start | bytes 2555912 | tf_op jit(solution)/shard_map/ppermute | solution.py:10
  128.4 3.0 %copy-start = (bf16[8,416,256]{2,1,0:T(8,128)(2,1)}, bf16[8,416,256]{2,1,0:T(8,128)(2,1)S(1)}, u32[]{:S(2)}) copy-start(bf16[8,416,256]{2,1,0:T(8,128)(2,1)S(1)} %all-to-all-done.1) | copy-start | bytes 5111812
  128.4 39.3 %collective-permute-start = (bf16[1,8,416,256]{3,2,1,0:T(8,128)(2,1)S(1)}, bf16[1,8,416,256]{3,2,1,0:T(8,128)(2,1)}, u32[]{:S(2)}, u32[]{:S(2)}) collective-permute-start(bf16[1,8,416,256]{3,2,1,0:T(8,128)(2,1)S(1)} %bitcast.360), channel_id=1, source_target_pairs={{0,2},{1,3},{2,0},{3,1},{4,6},{5,7},{6,4},{7,5},{8,10},{9,11},{10,... | collective-permute-start | bytes 5111816 | tf_op jit(solution)/shard_map/ppermute | solution.py:19
  172.0 28.4 %collective-permute-start.1 = (bf16[2,8,416,256]{3,2,1,0:T(8,128)(2,1)}, bf16[2,8,416,256]{3,2,1,0:T(8,128)(2,1)}, u32[]{:S(2)}, u32[]{:S(2)}) collective-permute-start(bf16[2,8,416,256]{3,2,1,0:T(8,128)(2,1)} %pad_maximum_fusion.1), channel_id=1, source_target_pairs={{0,1},{1,0},{2,3},{3,2},{4,5},{5,4},{6,7},{7,6},{8,9},{9,8},{10,11... | collective-permute-start | bytes 10223624 | tf_op jit(solution)/shard_map/ppermute | solution.py:19
  233.8 48.1 %collective-permute-start.3 = (f32[208,5,416]{2,0,1:T(8,128)S(1)}, f32[208,5,416]{2,0,1:T(8,128)S(1)}, u32[]{:S(2)}, u32[]{:S(2)}) collective-permute-start(f32[208,5,416]{2,0,1:T(8,128)S(1)} %fusion.78), channel_id=1, source_target_pairs={{0,4},{4,0},{1,5},{5,1},{2,6},{6,2},{3,7},{7,3},{8,12},{12,8},{9,1... | collective-permute-start | bytes 5191688 | tf_op jit(solution)/shard_map/ppermute | solution.py:10
Sparse Core Ops, SparseCore 0:
  21.9 101.9 all-gather.4
  131.5 65.3 all-gather.6

commit v8 on v5

--- a/solution.py
+++ b/solution.py
@@ -30,13 +30,16 @@
     )
 
 
-def lag_block(background, analysis, cycle_total, max_lag, lag_total):
-    pieces = [None] * lag_total
-    for offset in range(max_lag + 1):
-        span = cycle_total - offset
-        pieces[max_lag + offset] = contract(background[:, offset:], analysis[:, :span])
-        if offset > 0:
-            pieces[max_lag - offset] = contract(background[:, :span], analysis[:, offset:])
+def lag_block(background, analysis, cycle_total, max_lag, lags):
+    pieces = []
+    for k in lags:
+        offset = k - max_lag
+        if offset >= 0:
+            span = cycle_total - offset
+            pieces.append(contract(background[:, offset:], analysis[:, :span]))
+        else:
+            span = cycle_total + offset
+            pieces.append(contract(background[:, :span], analysis[:, -offset:]))
     return jnp.stack(pieces, axis=1)
 
 
@@ -70,15 +73,21 @@
     split_b = local_background.reshape(width_block, PAIR, chan_size, piece)
     by_loc = lax.all_to_all(split_b, "chan", 2, 0, tiled=True)
     by_loc = by_loc.reshape(quad_size, pair_rows, PAIR, piece).transpose(0, 2, 1, 3)
+    rows_out = pair_rows // PAIR
+    by_loc = by_loc.reshape(quad_size, PAIR, PAIR, rows_out, piece)
+    by_loc = jnp.stack([by_loc[:, 0], by_loc[:, 1, ::-1]], axis=1)
     by_loc = by_loc.reshape(quad_size * PAIR, pair_rows, piece)
     rows_here = lax.all_to_all(by_loc, ("tq", "th"), 0, 0, tiled=True)
     all_background = gather_chan(rows_here)
 
-    rows_out = pair_rows // PAIR
-    give_rows = lax.dynamic_slice_in_dim(all_background, (1 - pair_index) * rows_out, rows_out, axis=2)
-    keep_rows = lax.dynamic_slice_in_dim(all_background, pair_index * rows_out, rows_out, axis=2)
-    sent = swap_pair(lag_block(give_rows, all_analysis, cycle_total, max_lag, lag_total))
-    summed = lag_block(keep_rows, all_analysis, cycle_total, max_lag, lag_total) + sent
+    keep_rows = all_background[:, :, :rows_out]
+    give_rows = all_background[:, :, rows_out:]
+    early = (0, 1)
+    late = tuple(k for k in range(lag_total) if k not in early)
+    sent_early = swap_pair(lag_block(give_rows, all_analysis, cycle_total, max_lag, early))
+    sent_late = swap_pair(lag_block(give_rows, all_analysis, cycle_total, max_lag, late))
+    own = lag_block(keep_rows, all_analysis, cycle_total, max_lag, tuple(range(lag_total)))
+    summed = own + jnp.concatenate([sent_early, sent_late], axis=1)
 
     denominators = []
     for offset in range(max_lag + 1):

time: 283 us -> 289 us (1.021)
  waiting for transfers between devices: 100 us -> 92.9 us
  local copies, waits for them, and re-layouts: 18.6 us -> 24.8 us
  blocking collectives: 87.6 us -> 92.2 us
  other arithmetic: 26.4 us -> 30.2 us
    all_to_all x1, waiting for transfers between devices: 9.99 us -> 0.01 us  [body(): by_loc = lax.all_to_all(split_b, 'chan', 2, 0, tiled=True)]
    ppermute x2, waiting for transfers between devices: 40.8 us -> 34.9 us  [gather_chan(): got = lax.ppermute(held, 'chan', [(c, c ^ 1 << bit) for c in range(size)])]
    ppermute x2 -> x3, waiting for transfers between devices: 44.5 us -> 50 us  [swap_pair(): return lax.ppermute(x, 'th', [(0, 1), (1, 0)])]
    all_to_all x1, blocking collectives: 87.6 us -> 92.2 us  [body(): rows_here = lax.all_to_all(by_loc, ('tq', 'th'), 0, 0, tiled=True)]
    slice x0 -> x1, local copies, waits for them, and re-layouts: none -> 4.4 us  [body(): by_loc = jnp.stack([by_loc[:, 0], by_loc[:, 1, ::-1]], axis=1)]
    another operation x0 -> x3, other arithmetic: none -> 4.02 us  [the longest x1 3.86 us: body(): by_loc = jnp.stack([by_loc[:, 0], by_loc[:, 1, ::-1]], axis=1)]
    rev x0 -> x1, local copies, waits for them, and re-layouts: none -> 3.21 us  [body(): by_loc = jnp.stack([by_loc[:, 0], by_loc[:, 1, ::-1]], axis=1)]
    all_gather x1, waiting for transfers between devices: 4.73 us -> 7.93 us  [body(): all_analysis = lax.all_gather(pair_analysis, 'tq', axis=1, tiled=True)]
  transfers between devices with their start and end apart: 6 -> 7, of which waited for: 6 -> 6; matrix products, arithmetic and copies ran while one was open for 13% -> 20% of each run, Pallas kernels for 0% -> 0%
where the time goes in v8:
time: 289 us; the launch traced here: 288 us
  waiting for transfers between devices  92.9 us (32%)
  blocking collectives  92.2 us (32%)
  other arithmetic  30.2 us (10%)
  local copies, waits for them, and re-layouts  24.8 us (9%)
  matrix products  22.5 us (8%)
  between operations  15.5 us (5%)
  starting transfers between devices  10.3 us (4%)
    all_to_all x1, blocking collectives, body(): rows_here = lax.all_to_all(by_loc, ('tq', 'th'), 0, 0, tiled=True)  92.2 us
    ppermute x3, waiting for transfers between devices, swap_pair(): return lax.ppermute(x, 'th', [(0, 1), (1, 0)])  50 us
    ppermute x2, waiting for transfers between devices, gather_chan(): got = lax.ppermute(held, 'chan', [(c, c ^ 1 << bit) for c in range(size)])  34.9 us
    dot_general x10, matrix products, contract(): lax.dot_general(left, right, (((0, 1, 3), (0, 1, 3)), ((), ())), preferre...  22.5 us
    all_gather x1, waiting for transfers between devices, body(): all_analysis = lax.all_gather(pair_analysis, 'tq', axis=1, tiled=True)  7.93 us
    select_n x1, other arithmetic, body(): keep = jnp.where(pair_index == 0, halves[:, 0], halves[:, 1])  6.66 us
    another operation x2, other arithmetic, gather_chan(): jnp.stack([first, second], axis=1).reshape((-1,) + x.shape)  5.87 us
  transfers between devices with their start and end apart: 7, of which 6 were waited for; matrix products, arithmetic and copies ran while one was open for 20% of the time, Pallas kernels for 0%

profile of v8, /device:TPU:0, one launch (start us, length us, event | category | flops | bytes accessed | tf_op | source)
XLA Modules:
  0.0 288.3 jit_solution(1310101113609232615)
XLA Ops:
  8.5 3.9 %squeeze.4 = bf16[416,2,4,256]{3,2,1,0:T(4,128)(2,1)S(1)} reshape(bf16[1,416,2048]{2,1,0:T(8,128)(2,1)} %param.4) | data formatting | bytes 3407872 | tf_op jit(solution)/shard_map/squeeze | solution.py:63
  13.2 2.5 copy.27
  15.7 4.2 %all-to-all-start = ((bf16[416,2,4,256]{3,1,0,2:T(2,128)(2,1)}), bf16[416,2,4,256]{3,1,0,2:T(2,128)(2,1)S(1)}, u32[]{:S(2)}, u32[]{:S(2)}) async-start(bf16[416,2,4,256]{3,1,0,2:T(2,128)(2,1)} %copy.27), calls=%async_computation | async-start | bytes 3407872 | tf_op jit(solution)/shard_map/all_to_all | solution.py:74
  20.6 4.3 %squeeze.5 = bf16[416,2,1024]{2,1,0:T(2,128)(2,1)S(1)} reshape(bf16[1,416,2048]{2,1,0:T(8,128)(2,1)} %param.3) | data formatting | bytes 3407872 | tf_op jit(solution)/shard_map/squeeze | solution.py:62
  26.3 6.7 %fusion.29 = (bf16[416,1024]{1,0:T(8,128)(2,1)S(1)}, bf16[416,1,1024]{2,1,0:T(2,128)(2,1)S(1)}) fusion(pred[]{:T(512)S(6)} %eq.21, bf16[416,2,1024]{2,1,0:T(2,128)(2,1)S(1)} %broadcast_select_fusion), kind=kLoop, calls=%fused_computation.37 | loop fusion | flops 851968 | bytes 3407873 | tf_op jit(solution)/shard_map/jit(_where)/select_n | solution.py:66
  34.2 2.3 collective-permute-start.2
  37.3 19.1 %collective-permute-done.2 = bf16[416,1024]{1,0:T(8,128)(2,1)} collective-permute-done((bf16[416,1024]{1,0:T(8,128)(2,1)}, bf16[416,1024]{1,0:T(8,128)(2,1)}, u32[]{:S(2)}, u32[]{:S(2)}) %collective-permute-start.2) | collective-permute-done | bytes 852000 | tf_op jit(solution)/shard_map/ppermute | solution.py:10
  56.4 2.2 stack.81
  60.1 4.4 %fusion.102 = (bf16[4,1,2,208,256]{4,1,3,2,0:T(2,128)(2,1)S(1)}, bf16[4,1,2,208,256]{4,1,3,2,0:T(2,128)(2,1)}) fusion(bf16[4,2,2,208,256]{4,1,3,2,0:T(2,128)(2,1)S(1)} %bitcast.100), kind=kLoop, calls=%fused_computation.69 | loop fusion | bytes 3407872 | tf_op jit(solution)/shard_map/slice | solution.py:78
  64.5 3.2 %rev.3 = bf16[4,1,2,208,256]{4,1,3,2,0:T(2,128)(2,1)S(1)} reverse(bf16[4,1,2,208,256]{4,1,3,2,0:T(2,128)(2,1)} %get-tuple-element.12), dimensions={2} | reverse | bytes 1703936 | tf_op jit(solution)/shard_map/rev | solution.py:78
  67.7 3.9 %pad_maximum_fusion.2 = bf16[4,2,2,208,256]{4,1,3,2,0:T(2,128)(2,1)S(1)} fusion(bf16[4,1,2,208,256]{4,1,3,2,0:T(2,128)(2,1)S(1)} %rev.3, bf16[4,1,2,208,256]{4,1,3,2,0:T(2,128)(2,1)S(1)} %get-tuple-element.11), kind=kLoop, calls=%fused_computation.38 | loop fusion | flops 3407872 | bytes 3407872 | tf_op jit(solution)/shard_map/stack | solution.py:78
  71.9 92.2 %all_to_all.20 = bf16[8,416,256]{2,1,0:T(8,128)(2,1)S(1)} all-to-all(bf16[8,416,256]{2,1,0:T(8,128)(2,1)S(1)} %bitcast.112), channel_id=1, replica_groups=mesh['tq'=4,'th'=2,'chan'=4] {'tq','th'}, dimensions={0} | all-to-all | bytes 3407872 | tf_op jit(solution)/shard_map/all_to_all | solution.py:80
  165.6 31.9 %collective-permute-done = bf16[1,8,416,256]{3,2,1,0:T(8,128)(2,1)} collective-permute-done((bf16[1,8,416,256]{3,2,1,0:T(8,128)(2,1)S(1)}, bf16[1,8,416,256]{3,2,1,0:T(8,128)(2,1)}, u32[]{:S(2)}, u32[]{:S(2)}) %collective-permute-start) | collective-permute-done | bytes 1703968 | tf_op jit(solution)/shard_map/ppermute | solution.py:19
  197.5 2.2 broadcast_select_fusion.5
  199.7 2.1 pad_maximum_fusion.1
  205.2 3.0 %collective-permute-done.1 = bf16[2,8,416,256]{3,2,1,0:T(8,128)(2,1)} collective-permute-done((bf16[2,8,416,256]{3,2,1,0:T(8,128)(2,1)}, bf16[2,8,416,256]{3,2,1,0:T(8,128)(2,1)}, u32[]{:S(2)}, u32[]{:S(2)}) %collective-permute-start.1) | collective-permute-done | bytes 3407904 | tf_op jit(solution)/shard_map/ppermute | solution.py:19
  208.2 2.4 select_bitcast_fusion.1
  210.6 3.4 %pad_maximum_fusion = bf16[2,2,8,416,256]{4,3,2,1,0:T(8,128)(2,1)} fusion(bf16[2,1,8,416,256]{4,3,2,1,0:T(8,128)(2,1)S(1)} %get-tuple-element.8, bf16[2,1,8,416,256]{4,3,2,1,0:T(8,128)(2,1)S(1)} %get-tuple-element.7), kind=kLoop, calls=%fused_computation | loop fusion | flops 3407872 | bytes 13631488 | tf_op jit(solution)/shard_map/stack | solution.py:23
  214.0 7.9 %all-gather.2.cloned.1.call-done = bf16[4,8,416,256]{3,2,1,0:T(8,128)(2,1)} async-done(((bf16[4,2,416,256]{3,2,1,0:T(8,128)(2,1)}), bf16[4,8,416,256]{3,2,1,0:T(8,128)(2,1)}) %all-gather.2.cloned.1.call-update) | async-done | bytes 6815760 | tf_op jit(solution)/shard_map/all_gather | solution.py:71
  222.0 5.7 %fusion.50 = f32[208,1,416]{2,0,1:T(8,128)S(1)} fusion(bf16[4,8,416,256]{3,2,1,0:T(8,128)(2,1)} %all-gather.2.cloned.1.call-done, bf16[4,8,416,256]{3,2,1,0:T(8,128)(2,1)} %bitcast.101), kind=kOutput, calls=%fused_computation.50 | convolution fusion | flops 1240465408 | bytes 9291776 | tf_op jit(solution)/shard_map/dot_general | solution.py:28
  232.8 2.2 fusion.37
  242.9 2.2 fusion.34
  248.7 4.4 %collective-permute-done.3 = f32[208,2,416]{2,0,1:T(8,128)S(1)} collective-permute-done((f32[208,2,416]{2,0,1:T(8,128)S(1)}, f32[208,2,416]{2,0,1:T(8,128)S(1)}, u32[]{:S(2)}, u32[]{:S(2)}) %collective-permute-start.3) | collective-permute-done | bytes 692256 | tf_op jit(solution)/shard_map/ppermute | solution.py:10
  253.1 26.5 %collective-permute-done.4 = f32[208,3,416]{2,0,1:T(8,128)S(1)} collective-permute-done((f32[208,3,416]{2,0,1:T(8,128)S(1)}, f32[208,3,416]{2,0,1:T(8,128)S(1)}, u32[]{:S(2)}, u32[]{:S(2)}) %collective-permute-start.4) | collective-permute-done | bytes 1038368 | tf_op jit(solution)/shard_map/ppermute | solution.py:10
  (39 shorter events, 30.0 us)
Async XLA Ops:
  15.7 44.4 %all-to-all-start = ((bf16[416,2,4,256]{3,1,0,2:T(2,128)(2,1)}), bf16[416,2,4,256]{3,1,0,2:T(2,128)(2,1)S(1)}, u32[]{:S(2)}, u32[]{:S(2)}) async-start(bf16[416,2,4,256]{3,1,0,2:T(2,128)(2,1)} %copy.27), calls=%async_computation | async-start | bytes 3407872 | tf_op jit(solution)/shard_map/all_to_all | solution.py:74
  20.0 202.0 %all-gather.2.cloned.1.call-start = ((), (), s32[]{:S(2)}) async-start(), calls=%async_computation.2 | async-start | bytes 8519680 | tf_op jit(solution)/shard_map/all_gather | solution.py:71
  34.2 22.2 %collective-permute-start.2 = (bf16[416,1024]{1,0:T(8,128)(2,1)}, bf16[416,1024]{1,0:T(8,128)(2,1)}, u32[]{:S(2)}, u32[]{:S(2)}) collective-permute-start(bf16[416,1024]{1,0:T(8,128)(2,1)} %bitcast.99), channel_id=1, source_target_pairs={{0,4},{4,0},{1,5},{5,1},{2,6},{6,2},{3,7},{7,3},{8,12},{12,8},{9,1... | collective-permute-start | bytes 2555912 | tf_op jit(solution)/shard_map/ppermute | solution.py:10
  164.1 1.5 copy-start.1
  164.1 33.4 %collective-permute-start = (bf16[1,8,416,256]{3,2,1,0:T(8,128)(2,1)S(1)}, bf16[1,8,416,256]{3,2,1,0:T(8,128)(2,1)}, u32[]{:S(2)}, u32[]{:S(2)}) collective-permute-start(bf16[1,8,416,256]{3,2,1,0:T(8,128)(2,1)S(1)} %bitcast.111), channel_id=1, source_target_pairs={{0,2},{1,3},{2,0},{3,1},{4,6},{5,7},{6,4},{7,5},{8,10},{9,11},{10,... | collective-permute-start | bytes 5111816 | tf_op jit(solution)/shard_map/ppermute | solution.py:19
  199.7 2.8 copy-start.2
  201.8 6.4 %collective-permute-start.1 = (bf16[2,8,416,256]{3,2,1,0:T(8,128)(2,1)}, bf16[2,8,416,256]{3,2,1,0:T(8,128)(2,1)}, u32[]{:S(2)}, u32[]{:S(2)}) collective-permute-start(bf16[2,8,416,256]{3,2,1,0:T(8,128)(2,1)} %pad_maximum_fusion.1), channel_id=1, source_target_pairs={{0,1},{1,0},{2,3},{3,2},{4,5},{5,4},{6,7},{7,6},{8,9},{9,8},{10,11... | collective-permute-start | bytes 10223624 | tf_op jit(solution)/shard_map/ppermute | solution.py:19
  222.0 5.7 %copy-start = (bf16[2,2,8,416,256]{4,3,2,1,0:T(8,128)(2,1)S(1)}, bf16[2,2,8,416,256]{4,3,2,1,0:T(8,128)(2,1)}, u32[]{:S(2)}) copy-start(bf16[2,2,8,416,256]{4,3,2,1,0:T(8,128)(2,1)} %pad_maximum_fusion) | copy-start | bytes 20447236
  222.0 7.5 %copy-start.3 = (bf16[4,8,416,256]{3,2,1,0:T(8,128)(2,1)S(1)}, bf16[4,8,416,256]{3,2,1,0:T(8,128)(2,1)}, u32[]{:S(2)}) copy-start(bf16[4,8,416,256]{3,2,1,0:T(8,128)(2,1)} %all-gather.2.cloned.1.call-done) | copy-start | bytes 20447236
  231.2 21.9 %collective-permute-start.3 = (f32[208,2,416]{2,0,1:T(8,128)S(1)}, f32[208,2,416]{2,0,1:T(8,128)S(1)}, u32[]{:S(2)}, u32[]{:S(2)}) collective-permute-start(f32[208,2,416]{2,0,1:T(8,128)S(1)} %pad_maximum_fusion.4), channel_id=1, source_target_pairs={{0,4},{4,0},{1,5},{5,1},{2,6},{6,2},{3,7},{7,3},{8,12},{12,8},{9,1... | collective-permute-start | bytes 2076680 | tf_op jit(solution)/shard_map/ppermute | solution.py:10
  238.7 40.9 %collective-permute-start.4 = (f32[208,3,416]{2,0,1:T(8,128)S(1)}, f32[208,3,416]{2,0,1:T(8,128)S(1)}, u32[]{:S(2)}, u32[]{:S(2)}) collective-permute-start(f32[208,3,416]{2,0,1:T(8,128)S(1)} %pad_maximum_fusion.3), channel_id=1, source_target_pairs={{0,4},{4,0},{1,5},{5,1},{2,6},{6,2},{3,7},{7,3},{8,12},{12,8},{9,1... | collective-permute-start | bytes 3115016 | tf_op jit(solution)/shard_map/ppermute | solution.py:10
Sparse Core Ops, SparseCore 0:
  60.2 161.6 all-gather.1

commit v9 on v5

--- a/solution.py
+++ b/solution.py
@@ -22,6 +22,20 @@
         second = jnp.where(low, got, held)
         held = jnp.concatenate([first, second], axis=0) if bit == bits - 1 else jnp.stack([first, second], axis=1).reshape((-1,) + x.shape)
     return held
+
+
+def relay_gather(block, size):
+    me = lax.axis_index("tq")
+    from_left = from_right = block
+    lefts, rights = [], []
+    for _ in range(size - 1):
+        from_left = lax.ppermute(from_left, "tq", [(i, i + 1) for i in range(size - 1)])
+        from_right = lax.ppermute(from_right, "tq", [(i + 1, i) for i in range(size - 1)])
+        lefts.append(from_left)
+        rights.append(from_right)
+    stacked = jnp.concatenate(lefts[::-1] + [block] + rights, axis=1)
+    width = block.shape[1]
+    return lax.dynamic_slice_in_dim(stacked, (size - 1 - me) * width, size * width, axis=1)
 
 
 def contract(left, right):
@@ -65,7 +79,7 @@
     got = swap_pair(give)
     pair_analysis = jnp.where(pair_index == 0, jnp.stack([keep, got]), jnp.stack([got, keep]))
     pair_analysis = pair_analysis.reshape(PAIR, width_block, chan_size, piece).transpose(2, 0, 1, 3)
-    all_analysis = lax.all_gather(pair_analysis, "tq", axis=1, tiled=True)
+    all_analysis = relay_gather(pair_analysis, quad_size)
 
     split_b = local_background.reshape(width_block, PAIR, chan_size, piece)
     by_loc = lax.all_to_all(split_b, "chan", 2, 0, tiled=True)

time: 283 us -> 300 us (1.060)
  blocking collectives: 87.6 us -> 0 us
  waiting for transfers between devices: 100 us -> 159 us
  starting transfers between devices: 9.43 us -> 34.8 us
  matrix products: 25.1 us -> 41.2 us
  local copies, waits for them, and re-layouts: 18.6 us -> 33.6 us
  between operations: 15.5 us -> 2.2 us
    ppermute x0 -> x6, waiting for transfers between devices: none -> 91.8 us  [the longest x3 91.8 us: relay_gather(): lax.ppermute(from_left, 'tq', [(i, i + 1) for i in range(size - 1)])]
    all_to_all x1 -> x0, blocking collectives: 87.6 us -> none  [body(): rows_here = lax.all_to_all(by_loc, ('tq', 'th'), 0, 0, tiled=True)]
    ppermute x2, waiting for transfers between devices: 40.8 us -> 0.01 us  [gather_chan(): got = lax.ppermute(held, 'chan', [(c, c ^ 1 << bit) for c in range(size)])]
    ppermute x0 -> x6, starting transfers between devices: none -> 21.3 us  [the longest x3 17.4 us: relay_gather(): lax.ppermute(from_left, 'tq', [(i, i + 1) for i in range(size - 1)])]
    dot_general x10, matrix products: 25.1 us -> 41.2 us  [contract(): lax.dot_general(left, right, (((0, 1, 3), (0, 1, 3)), ((), ())), preferre...]
    unnamed x11 -> x38, local copies, waits for them, and re-layouts: 1.32 us -> 13.6 us
    all_to_all x0 -> x1, starting transfers between devices: none -> 6.56 us  [body(): rows_here = lax.all_to_all(by_loc, ('tq', 'th'), 0, 0, tiled=True)]
    all_to_all x1, waiting for transfers between devices: 9.99 us -> 16.4 us  [body(): by_loc = lax.all_to_all(split_b, 'chan', 2, 0, tiled=True)]
  transfers between devices with their start and end apart: 6 -> 12, of which waited for: 6 -> 6; matrix products, arithmetic and copies ran while one was open for 13% -> 18% of each run, Pallas kernels for 0% -> 0%
where the time goes in v9:
time: 300 us; the launch traced here: 298 us
  waiting for transfers between devices  159 us (53%)
  matrix products  41.2 us (14%)
  starting transfers between devices  34.8 us (12%)
  local copies, waits for them, and re-layouts  33.6 us (11%)
  other arithmetic  27.7 us (9%)
    ppermute x3, waiting for transfers between devices, relay_gather(): lax.ppermute(from_left, 'tq', [(i, i + 1) for i in range(size - 1)])  91.8 us
    ppermute x2, waiting for transfers between devices, swap_pair(): return lax.ppermute(x, 'th', [(0, 1), (1, 0)])  50.6 us
    dot_general x10, matrix products, contract(): lax.dot_general(left, right, (((0, 1, 3), (0, 1, 3)), ((), ())), preferre...  41.2 us
    ppermute x3, starting transfers between devices, relay_gather(): lax.ppermute(from_left, 'tq', [(i, i + 1) for i in range(size - 1)])  17.4 us
    all_to_all x1, waiting for transfers between devices, body(): by_loc = lax.all_to_all(split_b, 'chan', 2, 0, tiled=True)  16.4 us
    unnamed x38, local copies, waits for them, and re-layouts  13.6 us
    select_n x1, other arithmetic, body(): keep = jnp.where(pair_index == 0, halves[:, 0], halves[:, 1])  6.66 us
    all_to_all x1, starting transfers between devices, body(): rows_here = lax.all_to_all(by_loc, ('tq', 'th'), 0, 0, tiled=True)  6.56 us
  transfers between devices with their start and end apart: 12, of which 6 were waited for; matrix products, arithmetic and copies ran while one was open for 18% of the time, Pallas kernels for 0%

profile of v9, /device:TPU:0, one launch (start us, length us, event | category | flops | bytes accessed | tf_op | source)
XLA Modules:
  0.0 298.3 jit_solution(5053429505177075729)
XLA Ops:
  0.0 3.9 %squeeze.4 = bf16[416,2,4,256]{3,2,1,0:T(4,128)(2,1)S(1)} reshape(bf16[1,416,2048]{2,1,0:T(8,128)(2,1)} %param.4) | data formatting | bytes 3407872 | tf_op jit(solution)/shard_map/squeeze | solution.py:74
  8.6 4.2 %all-to-all-start = ((bf16[416,2,4,256]{3,1,0,2:T(2,128)(2,1)}), bf16[416,2,4,256]{3,1,0,2:T(2,128)(2,1)S(1)}, u32[]{:S(2)}, u32[]{:S(2)}) async-start(bf16[416,2,4,256]{3,1,0,2:T(2,128)(2,1)} %copy.23), calls=%async_computation | async-start | bytes 3407872 | tf_op jit(solution)/shard_map/all_to_all | solution.py:85
  12.8 4.3 %squeeze.5 = bf16[416,2,1024]{2,1,0:T(2,128)(2,1)S(1)} reshape(bf16[1,416,2048]{2,1,0:T(8,128)(2,1)} %param.3) | data formatting | bytes 3407872 | tf_op jit(solution)/shard_map/squeeze | solution.py:73
  17.8 16.4 %all-to-all-done = bf16[416,2,4,256]{3,1,0,2:T(2,128)(2,1)S(1)} async-done(((bf16[416,2,4,256]{3,1,0,2:T(2,128)(2,1)}), bf16[416,2,4,256]{3,1,0,2:T(2,128)(2,1)S(1)}, u32[]{:S(2)}, u32[]{:S(2)}) %all-to-all-start) | async-done | bytes 1703968 | tf_op jit(solution)/shard_map/all_to_all | solution.py:85
  35.7 6.6 %all-to-all-start.1 = ((bf16[8,416,256]{2,1,0:T(8,128)(2,1)}), bf16[8,416,256]{2,1,0:T(8,128)(2,1)S(1)}, u32[]{:S(2)}, u32[]{:S(2)}) async-start(bf16[8,416,256]{2,1,0:T(8,128)(2,1)} %bitcast.4), calls=%async_computation.1 | async-start | bytes 3407872 | tf_op jit(solution)/shard_map/all_to_all | solution.py:88
  43.6 6.7 %fusion.30 = (bf16[416,1024]{1,0:T(8,128)(2,1)S(1)}, bf16[416,1,1024]{2,1,0:T(2,128)(2,1)S(1)}) fusion(pred[]{:T(512)S(6)} %eq.21, bf16[416,2,1024]{2,1,0:T(2,128)(2,1)S(1)} %broadcast_select_fusion), kind=kLoop, calls=%fused_computation.38 | loop fusion | flops 851968 | bytes 3407873 | tf_op jit(solution)/shard_map/jit(_where)/select_n | solution.py:77
  54.2 27.7 %collective-permute-done.2 = bf16[416,1024]{1,0:T(8,128)(2,1)} collective-permute-done((bf16[416,1024]{1,0:T(8,128)(2,1)}, bf16[416,1024]{1,0:T(8,128)(2,1)}, u32[]{:S(2)}, u32[]{:S(2)}) %collective-permute-start.2) | collective-permute-done | bytes 852000 | tf_op jit(solution)/shard_map/ppermute | solution.py:10
  85.5 4.0 %collective-permute-start.3 = (bf16[4,2,416,256]{3,2,1,0:T(8,128)(2,1)}, bf16[4,2,416,256]{3,2,1,0:T(8,128)(2,1)}, u32[]{:S(2)}, u32[]{:S(2)}) collective-permute-start(bf16[4,2,416,256]{3,2,1,0:T(8,128)(2,1)} %fusion.31), channel_id=1, source_target_pairs={{0,8},{8,16},{16,24},{1,9},{9,17},{17,25},{2,10},{10,18},{18,26},{... | collective-permute-start | bytes 5111816 | tf_op jit(solution)/shard_map/ppermute | solution.py:32
  91.6 32.2 %collective-permute-done.3 = bf16[4,2,416,256]{3,2,1,0:T(8,128)(2,1)} collective-permute-done((bf16[4,2,416,256]{3,2,1,0:T(8,128)(2,1)}, bf16[4,2,416,256]{3,2,1,0:T(8,128)(2,1)}, u32[]{:S(2)}, u32[]{:S(2)}) %collective-permute-start.3) | collective-permute-done | bytes 1703968 | tf_op jit(solution)/shard_map/ppermute | solution.py:32
  123.8 5.6 %collective-permute-start.4 = (bf16[4,2,416,256]{3,2,1,0:T(8,128)(2,1)}, bf16[4,2,416,256]{3,2,1,0:T(8,128)(2,1)}, u32[]{:S(2)}, u32[]{:S(2)}) collective-permute-start(bf16[4,2,416,256]{3,2,1,0:T(8,128)(2,1)} %collective-permute-done.3), channel_id=1, source_target_pairs={{0,8},{8,16},{16,24},{1,9},{9,17},{17,25},{2,10},{10,18},{18,26},{... | collective-permute-start | bytes 5111816 | tf_op jit(solution)/shard_map/ppermute | solution.py:32
  135.0 27.7 %collective-permute-done.4 = bf16[4,2,416,256]{3,2,1,0:T(8,128)(2,1)} collective-permute-done((bf16[4,2,416,256]{3,2,1,0:T(8,128)(2,1)}, bf16[4,2,416,256]{3,2,1,0:T(8,128)(2,1)}, u32[]{:S(2)}, u32[]{:S(2)}) %collective-permute-start.4) | collective-permute-done | bytes 1703968 | tf_op jit(solution)/shard_map/ppermute | solution.py:32
  162.7 7.8 %collective-permute-start.5 = (bf16[4,2,416,256]{3,2,1,0:T(8,128)(2,1)}, bf16[4,2,416,256]{3,2,1,0:T(8,128)(2,1)}, u32[]{:S(2)}, u32[]{:S(2)}) collective-permute-start(bf16[4,2,416,256]{3,2,1,0:T(8,128)(2,1)} %collective-permute-done.4), channel_id=1, source_target_pairs={{0,8},{8,16},{16,24},{1,9},{9,17},{17,25},{2,10},{10,18},{18,26},{... | collective-permute-start | bytes 5111816 | tf_op jit(solution)/shard_map/ppermute | solution.py:32
  171.8 31.8 %collective-permute-done.5 = bf16[4,2,416,256]{3,2,1,0:T(8,128)(2,1)} collective-permute-done((bf16[4,2,416,256]{3,2,1,0:T(8,128)(2,1)}, bf16[4,2,416,256]{3,2,1,0:T(8,128)(2,1)}, u32[]{:S(2)}, u32[]{:S(2)}) %collective-permute-start.5) | collective-permute-done | bytes 1703968 | tf_op jit(solution)/shard_map/ppermute | solution.py:32
  213.6 4.4 %copy-done.6 = bf16[4,14,416,256]{3,2,1,0:T(8,128)(2,1)} copy-done((bf16[4,14,416,256]{3,2,1,0:T(8,128)(2,1)}, bf16[4,14,416,256]{3,2,1,0:T(8,128)(2,1)S(1)}, u32[]{:S(2)}) %copy-start.6) | copy-done | bytes 11927576
  218.0 3.4 %select_bitcast_fusion.1 = (bf16[2,1,8,416,256]{4,3,2,0,1:T(8,128)(2,1)S(1)}, bf16[2,1,8,416,256]{4,3,2,0,1:T(8,128)(2,1)}) fusion(bf16[2,8,416,256]{3,2,1,0:T(8,128)(2,1)} %collective-permute-done.1, pred[]{:T(512)S(6)} %eq.17, bf16[1,8,416,256]{3,2,1,0:T(8,128)(2,1)S(1)} %get-tuple-element.10, bf16[1,8,416,256]{3,2,1,0:T(8,128)(2,1)S(1)} %get-tuple-element.9), kind=kLoop, calls=%fused_computation.23 | loop fusion | flops 5111808 | bytes 13631489 | tf_op jit(solution)/shard_map/stack | solution.py:23
  224.0 3.2 %copy.25 = bf16[2,2,8,416,256]{4,3,2,1,0:T(8,128)(2,1)} copy(bf16[2,2,8,416,256]{4,3,2,0,1:T(8,128)(2,1)S(1)} %pad_maximum_fusion) | data formatting | bytes 13631488 | tf_op jit(solution)/shard_map/stack | solution.py:23
  227.2 5.8 %fusion.47 = f32[208,5,416]{2,0,1:T(8,128)} fusion(bf16[4,14,416,256]{3,2,1,0:T(8,128)(2,1)} %copy-done.6, s32[]{:T(128)S(6)} %add.24, bf16[4,8,416,256]{3,2,1,0:T(8,128)(2,1)} %bitcast.107, s32[]{:T(128)S(6)} %select_n.99), kind=kOutput, calls=%fused_computation.47 | convolution fusion | flops 1063256064 | bytes 8945672 | tf_op jit(solution)/shard_map/dot_general | solution.py:42
  233.0 5.5 %fusion.87 = f32[208,5,416]{2,0,1:T(8,128)} fusion(f32[208,5,416]{2,0,1:T(8,128)} %fusion.47, bf16[4,14,416,256]{3,2,1,0:T(8,128)(2,1)} %copy-done.6, s32[]{:T(128)S(6)} %add.25, bf16[4,8,416,256]{3,2,1,0:T(8,128)(2,1)S(1)} %bitcast.109, s32[]{:T(128)S(6)} %select_n.99), kind=kOutput, calls=%fused_computation.55 | convolution fusion | flops 1240465408 | bytes 9797640 | tf_op jit(solution)/shard_map/dot_general | solution.py:42
  238.6 6.0 %fusion.117 = f32[208,5,416]{2,0,1:T(8,128)} fusion(f32[208,5,416]{2,0,1:T(8,128)} %fusion.87, bf16[4,14,416,256]{3,2,1,0:T(8,128)(2,1)} %copy-done.6, s32[]{:T(128)S(6)} %select_n.98, bf16[4,8,416,256]{3,2,1,0:T(8,128)(2,1)S(1)} %bitcast.110, s32[]{:T(128)S(6)} %select_n.99), kind=kOutput, calls=%fused_computation.61 | convolution fusion | flops 1417674752 | bytes 10649608 | tf_op jit(solution)/shard_map/dot_general | solution.py:42
  253.1 5.1 %fusion.37 = f32[208,5,416]{2,0,1:T(8,128)S(1)} fusion(bf16[4,14,416,256]{3,2,1,0:T(8,128)(2,1)} %copy-done.6, s32[]{:T(128)S(6)} %add.24, bf16[4,8,416,256]{3,2,1,0:T(8,128)(2,1)} %bitcast.108, s32[]{:T(128)S(6)} %select_n.89), kind=kOutput, calls=%fused_computation.45 | convolution fusion | flops 1063256064 | bytes 8945672 | tf_op jit(solution)/shard_map/dot_general | solution.py:42
  258.2 4.8 %fusion.77 = f32[208,5,416]{2,0,1:T(8,128)S(1)} fusion(f32[208,5,416]{2,0,1:T(8,128)S(1)} %fusion.37, bf16[4,14,416,256]{3,2,1,0:T(8,128)(2,1)} %copy-done.6, s32[]{:T(128)S(6)} %add.25, bf16[4,8,416,256]{3,2,1,0:T(8,128)(2,1)S(1)} %bitcast.115, s32[]{:T(128)S(6)} %select_n.89), kind=kOutput, calls=%fused_computation.53 | convolution fusion | flops 1240465408 | bytes 9797640 | tf_op jit(solution)/shard_map/dot_general | solution.py:42
  263.0 5.3 %fusion.127 = f32[208,5,416]{2,0,1:T(8,128)S(1)} fusion(f32[208,5,416]{2,0,1:T(8,128)S(1)} %fusion.77, bf16[4,14,416,256]{3,2,1,0:T(8,128)(2,1)} %copy-done.6, s32[]{:T(128)S(6)} %select_n.98, bf16[4,8,416,256]{3,2,1,0:T(8,128)(2,1)S(1)} %bitcast.116, s32[]{:T(128)S(6)} %select_n.89), kind=kOutput, calls=%fused_computation.63 | convolution fusion | flops 1417674752 | bytes 10649608 | tf_op jit(solution)/shard_map/dot_general | solution.py:42
  271.9 22.9 %collective-permute-done.9 = f32[208,5,416]{2,0,1:T(8,128)} collective-permute-done((f32[208,5,416]{2,0,1:T(8,128)}, f32[208,5,416]{2,0,1:T(8,128)}, u32[]{:S(2)}, u32[]{:S(2)}) %collective-permute-start.9) | collective-permute-done | bytes 1730592 | tf_op jit(solution)/shard_map/ppermute | solution.py:10
  294.8 3.5 %add_divide_fusion = f32[208,5,416]{2,0,1:T(8,128)} fusion(f32[208,5,416]{2,0,1:T(8,128)S(1)} %fusion.57, f32[208,5,416]{2,0,1:T(8,128)} %collective-permute-done.9, f32[5]{0:T(128)S(1)} %stack.92), kind=kLoop, calls=%fused_computation.27 | loop fusion | flops 865280 | bytes 5191700 | tf_op jit(solution)/shard_map/div | solution.py:104
  (77 shorter events, 47.2 us)
Async XLA Ops:
  8.6 25.7 %all-to-all-start = ((bf16[416,2,4,256]{3,1,0,2:T(2,128)(2,1)}), bf16[416,2,4,256]{3,1,0,2:T(2,128)(2,1)S(1)}, u32[]{:S(2)}, u32[]{:S(2)}) async-start(bf16[416,2,4,256]{3,1,0,2:T(2,128)(2,1)} %copy.23), calls=%async_computation | async-start | bytes 3407872 | tf_op jit(solution)/shard_map/all_to_all | solution.py:85
  35.7 55.2 %all-to-all-start.1 = ((bf16[8,416,256]{2,1,0:T(8,128)(2,1)}), bf16[8,416,256]{2,1,0:T(8,128)(2,1)S(1)}, u32[]{:S(2)}, u32[]{:S(2)}) async-start(bf16[8,416,256]{2,1,0:T(8,128)(2,1)} %bitcast.4), calls=%async_computation.1 | async-start | bytes 3407872 | tf_op jit(solution)/shard_map/all_to_all | solution.py:88
  51.5 30.5 %collective-permute-start.2 = (bf16[416,1024]{1,0:T(8,128)(2,1)}, bf16[416,1024]{1,0:T(8,128)(2,1)}, u32[]{:S(2)}, u32[]{:S(2)}) collective-permute-start(bf16[416,1024]{1,0:T(8,128)(2,1)} %bitcast.106), channel_id=1, source_target_pairs={{0,4},{4,0},{1,5},{5,1},{2,6},{6,2},{3,7},{7,3},{8,12},{12,8},{9,1... | collective-permute-start | bytes 2555912 | tf_op jit(solution)/shard_map/ppermute | solution.py:10
  54.2 31.3 %copy-start = (bf16[1,416,4,256]{3,1,0,2:T(8,128)(2,1)}, bf16[1,416,4,256]{3,1,0,2:T(8,128)(2,1)S(1)}, u32[]{:S(2)}) copy-start(bf16[1,416,4,256]{3,1,0,2:T(8,128)(2,1)S(1)} %copy.26) | copy-start | bytes 2555908
  84.1 5.5 %copy-start.2 = (bf16[1,416,4,256]{3,1,0,2:T(8,128)(2,1)}, bf16[1,416,4,256]{3,1,0,2:T(8,128)(2,1)S(1)}, u32[]{:S(2)}) copy-start(bf16[1,416,4,256]{3,1,0,2:T(8,128)(2,1)S(1)} %copy.27) | copy-start | bytes 2555908
  85.5 38.3 %collective-permute-start.3 = (bf16[4,2,416,256]{3,2,1,0:T(8,128)(2,1)}, bf16[4,2,416,256]{3,2,1,0:T(8,128)(2,1)}, u32[]{:S(2)}, u32[]{:S(2)}) collective-permute-start(bf16[4,2,416,256]{3,2,1,0:T(8,128)(2,1)} %fusion.31), channel_id=1, source_target_pairs={{0,8},{8,16},{16,24},{1,9},{9,17},{17,25},{2,10},{10,18},{18,26},{... | collective-permute-start | bytes 5111816 | tf_op jit(solution)/shard_map/ppermute | solution.py:32
  89.6 39.8 %collective-permute-start.6 = (bf16[4,2,416,256]{3,2,1,0:T(8,128)(2,1)}, bf16[4,2,416,256]{3,2,1,0:T(8,128)(2,1)}, u32[]{:S(2)}, u32[]{:S(2)}) collective-permute-start(bf16[4,2,416,256]{3,2,1,0:T(8,128)(2,1)} %fusion.31), channel_id=1, source_target_pairs={{8,0},{16,8},{24,16},{9,1},{17,9},{25,17},{10,2},{18,10},{26,18},{... | collective-permute-start | bytes 5111816 | tf_op jit(solution)/shard_map/ppermute | solution.py:33
  90.9 39.8 %copy-start.5 = (bf16[8,416,256]{2,1,0:T(8,128)(2,1)}, bf16[8,416,256]{2,1,0:T(8,128)(2,1)S(1)}, u32[]{:S(2)}) copy-start(bf16[8,416,256]{2,1,0:T(8,128)(2,1)S(1)} %all-to-all-done.1) | copy-start | bytes 5111812
  90.9 39.8 %collective-permute-start = (bf16[1,8,416,256]{3,2,1,0:T(8,128)(2,1)S(1)}, bf16[1,8,416,256]{3,2,1,0:T(8,128)(2,1)}, u32[]{:S(2)}, u32[]{:S(2)}) collective-permute-start(bf16[1,8,416,256]{3,2,1,0:T(8,128)(2,1)S(1)} %bitcast.119), channel_id=1, source_target_pairs={{0,2},{1,3},{2,0},{3,1},{4,6},{5,7},{6,4},{7,5},{8,10},{9,11},{10,... | collective-permute-start | bytes 5111816 | tf_op jit(solution)/shard_map/ppermute | solution.py:19
  123.8 38.9 %collective-permute-start.4 = (bf16[4,2,416,256]{3,2,1,0:T(8,128)(2,1)}, bf16[4,2,416,256]{3,2,1,0:T(8,128)(2,1)}, u32[]{:S(2)}, u32[]{:S(2)}) collective-permute-start(bf16[4,2,416,256]{3,2,1,0:T(8,128)(2,1)} %collective-permute-done.3), channel_id=1, source_target_pairs={{0,8},{8,16},{16,24},{1,9},{9,17},{17,25},{2,10},{10,18},{18,26},{... | collective-permute-start | bytes 5111816 | tf_op jit(solution)/shard_map/ppermute | solution.py:32
  129.4 41.1 %collective-permute-start.7 = (bf16[4,2,416,256]{3,2,1,0:T(8,128)(2,1)}, bf16[4,2,416,256]{3,2,1,0:T(8,128)(2,1)}, u32[]{:S(2)}, u32[]{:S(2)}) collective-permute-start(bf16[4,2,416,256]{3,2,1,0:T(8,128)(2,1)} %collective-permute-done.6), channel_id=1, source_target_pairs={{8,0},{16,8},{24,16},{9,1},{17,9},{25,17},{10,2},{18,10},{26,18},{... | collective-permute-start | bytes 5111816 | tf_op jit(solution)/shard_map/ppermute | solution.py:33
  135.0 83.0 %collective-permute-start.1 = (bf16[2,8,416,256]{3,2,1,0:T(8,128)(2,1)}, bf16[2,8,416,256]{3,2,1,0:T(8,128)(2,1)}, u32[]{:S(2)}, u32[]{:S(2)}) collective-permute-start(bf16[2,8,416,256]{3,2,1,0:T(8,128)(2,1)} %pad_maximum_fusion.1), channel_id=1, source_target_pairs={{0,1},{1,0},{2,3},{3,2},{4,5},{5,4},{6,7},{7,6},{8,9},{9,8},{10,11... | collective-permute-start | bytes 10223624 | tf_op jit(solution)/shard_map/ppermute | solution.py:19
  162.7 40.9 %collective-permute-start.5 = (bf16[4,2,416,256]{3,2,1,0:T(8,128)(2,1)}, bf16[4,2,416,256]{3,2,1,0:T(8,128)(2,1)}, u32[]{:S(2)}, u32[]{:S(2)}) collective-permute-start(bf16[4,2,416,256]{3,2,1,0:T(8,128)(2,1)} %collective-permute-done.4), channel_id=1, source_target_pairs={{0,8},{8,16},{16,24},{1,9},{9,17},{17,25},{2,10},{10,18},{18,26},{... | collective-permute-start | bytes 5111816 | tf_op jit(solution)/shard_map/ppermute | solution.py:32
  170.5 41.5 %collective-permute-start.8 = (bf16[4,2,416,256]{3,2,1,0:T(8,128)(2,1)}, bf16[4,2,416,256]{3,2,1,0:T(8,128)(2,1)}, u32[]{:S(2)}, u32[]{:S(2)}) collective-permute-start(bf16[4,2,416,256]{3,2,1,0:T(8,128)(2,1)} %collective-permute-done.7), channel_id=1, source_target_pairs={{8,0},{16,8},{24,16},{9,1},{17,9},{25,17},{10,2},{18,10},{26,18},{... | collective-permute-start | bytes 5111816 | tf_op jit(solution)/shard_map/ppermute | solution.py:33
  227.2 5.8 %copy-start.4 = (bf16[2,2,8,416,256]{4,3,2,1,0:T(8,128)(2,1)S(1)}, bf16[2,2,8,416,256]{4,3,2,1,0:T(8,128)(2,1)}, u32[]{:S(2)}) copy-start(bf16[2,2,8,416,256]{4,3,2,1,0:T(8,128)(2,1)} %copy.25) | copy-start | bytes 20447236
  233.0 11.6 %slice-start.2 = ((s8[11927552]{0:T(1024)(128)(4,1)}), s8[4194304]{0:T(1024)(128)(4,1)S(1)}, s32[]{:S(2)}) async-start(s8[11927552]{0:T(1024)(128)(4,1)} %bitcast.120), calls=%async_computation.4 | async-start | bytes 8388608
  233.0 11.6 %slice-start.3 = ((s8[11927552]{0:T(1024)(128)(4,1)}), s8[4194304]{0:T(1024)(128)(4,1)S(1)}, s32[]{:S(2)}) async-start(s8[11927552]{0:T(1024)(128)(4,1)} %bitcast.120), calls=%async_computation.5 | async-start | bytes 8388608
  238.6 6.0 %slice-start.4 = ((s8[11927552]{0:T(1024)(128)(4,1)}), s8[3538944]{0:T(1024)(128)(4,1)S(1)}, s32[]{:S(2)}) async-start(s8[11927552]{0:T(1024)(128)(4,1)} %bitcast.120), calls=%async_computation.6 | async-start | bytes 7077888
  247.3 10.8 %slice-start = ((s8[6815744]{0:T(1024)(128)(4,1)}), s8[2621440]{0:T(1024)(128)(4,1)S(1)}, s32[]{:S(2)}) async-start(s8[6815744]{0:T(1024)(128)(4,1)} %bitcast.113), calls=%async_computation.2 | async-start | bytes 5242880
  249.8 45.0 %collective-permute-start.9 = (f32[208,5,416]{2,0,1:T(8,128)}, f32[208,5,416]{2,0,1:T(8,128)}, u32[]{:S(2)}, u32[]{:S(2)}) collective-permute-start(f32[208,5,416]{2,0,1:T(8,128)} %fusion.67), channel_id=1, source_target_pairs={{0,4},{4,0},{1,5},{5,1},{2,6},{6,2},{3,7},{7,3},{8,12},{12,8},{9,1... | collective-permute-start | bytes 5191688 | tf_op jit(solution)/shard_map/ppermute | solution.py:10
  253.1 5.1 %slice-start.1 = ((s8[6815744]{0:T(1024)(128)(4,1)}), s8[4194304]{0:T(1024)(128)(4,1)S(1)}, s32[]{:S(2)}) async-start(s8[6815744]{0:T(1024)(128)(4,1)} %bitcast.113), calls=%async_computation.3 | async-start | bytes 8388608
  258.2 10.1 %slice-start.5 = ((s8[11927552]{0:T(1024)(128)(4,1)}), s8[4194304]{0:T(1024)(128)(4,1)S(1)}, s32[]{:S(2)}) async-start(s8[11927552]{0:T(1024)(128)(4,1)} %bitcast.122), calls=%async_computation.7 | async-start | bytes 8388608
  258.2 10.1 %slice-start.6 = ((s8[11927552]{0:T(1024)(128)(4,1)}), s8[4194304]{0:T(1024)(128)(4,1)S(1)}, s32[]{:S(2)}) async-start(s8[11927552]{0:T(1024)(128)(4,1)} %bitcast.122), calls=%async_computation.8 | async-start | bytes 8388608
  263.0 5.3 %slice-start.7 = ((s8[11927552]{0:T(1024)(128)(4,1)}), s8[3538944]{0:T(1024)(128)(4,1)S(1)}, s32[]{:S(2)}) async-start(s8[11927552]{0:T(1024)(128)(4,1)} %bitcast.122), calls=%async_computation.9 | async-start | bytes 7077888
  (4 other events, 15.0 us)

commit v10 on v9

--- a/solution.py
+++ b/solution.py
@@ -77,6 +77,7 @@
     keep = jnp.where(pair_index == 0, halves[:, 0], halves[:, 1])
     give = jnp.where(pair_index == 0, halves[:, 1], halves[:, 0])
     got = swap_pair(give)
+    got, local_background = lax.optimization_barrier((got, local_background))
     pair_analysis = jnp.where(pair_index == 0, jnp.stack([keep, got]), jnp.stack([got, keep]))
     pair_analysis = pair_analysis.reshape(PAIR, width_block, chan_size, piece).transpose(2, 0, 1, 3)
     all_analysis = relay_gather(pair_analysis, quad_size)

time: 300 us -> 323 us (1.077)
  blocking collectives: 0 us -> 24.3 us
  local copies, waits for them, and re-layouts: 33.6 us -> 29.2 us
  starting transfers between devices: 34.8 us -> 38.8 us
    all_to_all x1, waiting for transfers between devices: 0.01 us -> 30.2 us  [body(): rows_here = lax.all_to_all(by_loc, ('tq', 'th'), 0, 0, tiled=True)]
    all_to_all x0 -> x1, blocking collectives: none -> 24.3 us  [body(): by_loc = lax.all_to_all(split_b, 'chan', 2, 0, tiled=True)]
    all_to_all x1 -> x0, waiting for transfers between devices: 16.4 us -> none  [body(): by_loc = lax.all_to_all(split_b, 'chan', 2, 0, tiled=True)]
    ppermute x2, waiting for transfers between devices: 50.6 us -> 41.7 us  [swap_pair(): return lax.ppermute(x, 'th', [(0, 1), (1, 0)])]
    ppermute x3, starting transfers between devices: 17.4 us -> 24.6 us  [relay_gather(): lax.ppermute(from_left, 'tq', [(i, i + 1) for i in range(size - 1)])]
    ppermute x3, waiting for transfers between devices: 91.8 us -> 86.3 us  [relay_gather(): lax.ppermute(from_left, 'tq', [(i, i + 1) for i in range(size - 1)])]
    all_to_all x1 -> x0, starting transfers between devices: 4.24 us -> none  [body(): by_loc = lax.all_to_all(split_b, 'chan', 2, 0, tiled=True)]
    squeeze x1 -> x0, local copies, waits for them, and re-layouts: 3.95 us -> none  [body(): background_dep[0]]
  transfers between devices with their start and end apart: 12 -> 11, of which waited for: 6 -> 6; matrix products, arithmetic and copies ran while one was open for 18% -> 12% of each run, Pallas kernels for 0% -> 0%
where the time goes in v10:
time: 323 us; the launch traced here: 322 us
  waiting for transfers between devices  158 us (49%)
  matrix products  41.2 us (13%)
  starting transfers between devices  38.8 us (12%)
  local copies, waits for them, and re-layouts  29.2 us (9%)
  other arithmetic  27.9 us (9%)
  blocking collectives  24.3 us (8%)
    ppermute x3, waiting for transfers between devices, relay_gather(): lax.ppermute(from_left, 'tq', [(i, i + 1) for i in range(size - 1)])  86.3 us
    ppermute x2, waiting for transfers between devices, swap_pair(): return lax.ppermute(x, 'th', [(0, 1), (1, 0)])  41.7 us
    dot_general x10, matrix products, contract(): lax.dot_general(left, right, (((0, 1, 3), (0, 1, 3)), ((), ())), preferre...  41.2 us
    all_to_all x1, waiting for transfers between devices, body(): rows_here = lax.all_to_all(by_loc, ('tq', 'th'), 0, 0, tiled=True)  30.2 us
    ppermute x3, starting transfers between devices, relay_gather(): lax.ppermute(from_left, 'tq', [(i, i + 1) for i in range(size - 1)])  24.6 us
    all_to_all x1, blocking collectives, body(): by_loc = lax.all_to_all(split_b, 'chan', 2, 0, tiled=True)  24.3 us
    unnamed x42, local copies, waits for them, and re-layouts  12.7 us
    select_n x1, other arithmetic, body(): keep = jnp.where(pair_index == 0, halves[:, 0], halves[:, 1])  7.56 us
  transfers between devices with their start and end apart: 11, of which 6 were waited for; matrix products, arithmetic and copies ran while one was open for 12% of the time, Pallas kernels for 0%

profile of v10, /device:TPU:0, one launch (start us, length us, event | category | flops | bytes accessed | tf_op | source)
XLA Modules:
  0.0 322.0 jit_solution(3586605601364806383)
XLA Ops:
  0.0 4.4 %squeeze.4 = bf16[416,2,1024]{2,1,0:T(2,128)(2,1)S(1)} reshape(bf16[1,416,2048]{2,1,0:T(8,128)(2,1)} %param.3) | data formatting | bytes 3407872 | tf_op jit(solution)/shard_map/squeeze | solution.py:73
  7.0 7.6 %fusion.30 = (bf16[416,1024]{1,0:T(8,128)(2,1)}, bf16[416,1,1024]{2,1,0:T(2,128)(2,1)S(1)}) fusion(pred[]{:T(512)S(6)} %eq.19, bf16[416,2,1024]{2,1,0:T(2,128)(2,1)S(1)} %broadcast_select_fusion), kind=kLoop, calls=%fused_computation.38 | loop fusion | flops 851968 | bytes 3407873 | tf_op jit(solution)/shard_map/jit(_where)/select_n | solution.py:77
  14.9 3.0 collective-permute-start
  18.7 18.3 %collective-permute-done = bf16[416,1024]{1,0:T(8,128)(2,1)} collective-permute-done((bf16[416,1024]{1,0:T(8,128)(2,1)S(1)}, bf16[416,1024]{1,0:T(8,128)(2,1)}, u32[]{:S(2)}, u32[]{:S(2)}) %collective-permute-start) | collective-permute-done | bytes 852000 | tf_op jit(solution)/shard_map/ppermute | solution.py:10
  39.6 24.3 %all_to_all.20 = bf16[416,2,4,256]{3,1,0,2:T(2,128)(2,1)S(1)} all-to-all(bf16[416,2,4,256]{3,1,0,2:T(2,128)(2,1)S(1)} %copy.23), channel_id=1, replica_groups=mesh['tq'=4,'th'=2,'chan'=4] {'chan'}, dimensions={2} | all-to-all | bytes 3407872 | tf_op jit(solution)/shard_map/all_to_all | solution.py:86
  65.4 5.8 %all-to-all-start.1 = ((bf16[8,416,256]{2,1,0:T(8,128)(2,1)}), bf16[8,416,256]{2,1,0:T(8,128)(2,1)S(1)}, u32[]{:S(2)}, u32[]{:S(2)}) async-start(bf16[8,416,256]{2,1,0:T(8,128)(2,1)} %bitcast.5), calls=%async_computation.1 | async-start | bytes 3407872 | tf_op jit(solution)/shard_map/all_to_all | solution.py:89
  75.9 5.1 %collective-permute-start.3 = (bf16[4,2,416,256]{3,2,1,0:T(8,128)(2,1)}, bf16[4,2,416,256]{3,2,1,0:T(8,128)(2,1)}, u32[]{:S(2)}, u32[]{:S(2)}) collective-permute-start(bf16[4,2,416,256]{3,2,1,0:T(8,128)(2,1)} %fusion.31), channel_id=1, source_target_pairs={{0,8},{8,16},{16,24},{1,9},{9,17},{17,25},{2,10},{10,18},{18,26},{... | collective-permute-start | bytes 5111816 | tf_op jit(solution)/shard_map/ppermute | solution.py:32
  82.3 30.2 %all-to-all-done.1 = bf16[8,416,256]{2,1,0:T(8,128)(2,1)S(1)} async-done(((bf16[8,416,256]{2,1,0:T(8,128)(2,1)}), bf16[8,416,256]{2,1,0:T(8,128)(2,1)S(1)}, u32[]{:S(2)}, u32[]{:S(2)}) %all-to-all-start.1) | async-done | bytes 1703968 | tf_op jit(solution)/shard_map/all_to_all | solution.py:89
  112.8 22.6 %collective-permute-done.3 = bf16[4,2,416,256]{3,2,1,0:T(8,128)(2,1)} collective-permute-done((bf16[4,2,416,256]{3,2,1,0:T(8,128)(2,1)}, bf16[4,2,416,256]{3,2,1,0:T(8,128)(2,1)}, u32[]{:S(2)}, u32[]{:S(2)}) %collective-permute-start.3) | collective-permute-done | bytes 1703968 | tf_op jit(solution)/shard_map/ppermute | solution.py:32
  135.4 13.9 %collective-permute-start.4 = (bf16[4,2,416,256]{3,2,1,0:T(8,128)(2,1)}, bf16[4,2,416,256]{3,2,1,0:T(8,128)(2,1)}, u32[]{:S(2)}, u32[]{:S(2)}) collective-permute-start(bf16[4,2,416,256]{3,2,1,0:T(8,128)(2,1)} %collective-permute-done.3), channel_id=1, source_target_pairs={{0,8},{8,16},{16,24},{1,9},{9,17},{17,25},{2,10},{10,18},{18,26},{... | collective-permute-start | bytes 5111816 | tf_op jit(solution)/shard_map/ppermute | solution.py:32
  154.8 30.2 %collective-permute-done.4 = bf16[4,2,416,256]{3,2,1,0:T(8,128)(2,1)} collective-permute-done((bf16[4,2,416,256]{3,2,1,0:T(8,128)(2,1)}, bf16[4,2,416,256]{3,2,1,0:T(8,128)(2,1)}, u32[]{:S(2)}, u32[]{:S(2)}) %collective-permute-start.4) | collective-permute-done | bytes 1703968 | tf_op jit(solution)/shard_map/ppermute | solution.py:32
  185.0 5.6 %collective-permute-start.5 = (bf16[4,2,416,256]{3,2,1,0:T(8,128)(2,1)}, bf16[4,2,416,256]{3,2,1,0:T(8,128)(2,1)}, u32[]{:S(2)}, u32[]{:S(2)}) collective-permute-start(bf16[4,2,416,256]{3,2,1,0:T(8,128)(2,1)} %collective-permute-done.4), channel_id=1, source_target_pairs={{0,8},{8,16},{16,24},{1,9},{9,17},{17,25},{2,10},{10,18},{18,26},{... | collective-permute-start | bytes 5111816 | tf_op jit(solution)/shard_map/ppermute | solution.py:32
  191.9 33.6 %collective-permute-done.5 = bf16[4,2,416,256]{3,2,1,0:T(8,128)(2,1)} collective-permute-done((bf16[4,2,416,256]{3,2,1,0:T(8,128)(2,1)}, bf16[4,2,416,256]{3,2,1,0:T(8,128)(2,1)}, u32[]{:S(2)}, u32[]{:S(2)}) %collective-permute-start.5) | collective-permute-done | bytes 1703968 | tf_op jit(solution)/shard_map/ppermute | solution.py:32
  235.5 4.4 %copy-done.8 = bf16[4,14,416,256]{3,2,1,0:T(8,128)(2,1)} copy-done((bf16[4,14,416,256]{3,2,1,0:T(8,128)(2,1)}, bf16[4,14,416,256]{3,2,1,0:T(8,128)(2,1)S(1)}, u32[]{:S(2)}) %copy-start.8) | copy-done | bytes 11927576
  239.9 3.4 %select_bitcast_fusion.1 = (bf16[2,1,8,416,256]{4,3,2,0,1:T(8,128)(2,1)S(1)}, bf16[2,1,8,416,256]{4,3,2,0,1:T(8,128)(2,1)}) fusion(bf16[2,8,416,256]{3,2,1,0:T(8,128)(2,1)} %collective-permute-done.2, pred[]{:T(512)S(6)} %eq.17, bf16[1,8,416,256]{3,2,1,0:T(8,128)(2,1)S(1)} %get-tuple-element.14, bf16[1,8,416,256]{3,2,1,0:T(8,128)(2,1)S(1)} %get-tuple-element.13), kind=kLoop, calls=%fused_computation.23 | loop fusion | flops 5111808 | bytes 13631489 | tf_op jit(solution)/shard_map/stack | solution.py:23
  245.9 3.2 %copy.25 = bf16[2,2,8,416,256]{4,3,2,1,0:T(8,128)(2,1)} copy(bf16[2,2,8,416,256]{4,3,2,0,1:T(8,128)(2,1)S(1)} %pad_maximum_fusion) | data formatting | bytes 13631488 | tf_op jit(solution)/shard_map/stack | solution.py:23
  249.1 5.8 %fusion.47 = f32[208,5,416]{2,0,1:T(8,128)} fusion(bf16[4,14,416,256]{3,2,1,0:T(8,128)(2,1)} %copy-done.8, s32[]{:T(128)S(6)} %add.22, bf16[4,8,416,256]{3,2,1,0:T(8,128)(2,1)} %bitcast.109, s32[]{:T(128)S(6)} %select_n.98), kind=kOutput, calls=%fused_computation.47 | convolution fusion | flops 1063256064 | bytes 8945672 | tf_op jit(solution)/shard_map/dot_general | solution.py:42
  254.9 5.5 %fusion.87 = f32[208,5,416]{2,0,1:T(8,128)} fusion(f32[208,5,416]{2,0,1:T(8,128)} %fusion.47, bf16[4,14,416,256]{3,2,1,0:T(8,128)(2,1)} %copy-done.8, s32[]{:T(128)S(6)} %add.23, bf16[4,8,416,256]{3,2,1,0:T(8,128)(2,1)S(1)} %bitcast.111, s32[]{:T(128)S(6)} %select_n.98), kind=kOutput, calls=%fused_computation.55 | convolution fusion | flops 1240465408 | bytes 9797640 | tf_op jit(solution)/shard_map/dot_general | solution.py:42
  260.5 6.0 %fusion.117 = f32[208,5,416]{2,0,1:T(8,128)} fusion(f32[208,5,416]{2,0,1:T(8,128)} %fusion.87, bf16[4,14,416,256]{3,2,1,0:T(8,128)(2,1)} %copy-done.8, s32[]{:T(128)S(6)} %select_n.97, bf16[4,8,416,256]{3,2,1,0:T(8,128)(2,1)S(1)} %bitcast.112, s32[]{:T(128)S(6)} %select_n.98), kind=kOutput, calls=%fused_computation.61 | convolution fusion | flops 1417674752 | bytes 10649608 | tf_op jit(solution)/shard_map/dot_general | solution.py:42
  276.2 5.0 %fusion.37 = f32[208,5,416]{2,0,1:T(8,128)S(1)} fusion(bf16[4,14,416,256]{3,2,1,0:T(8,128)(2,1)} %copy-done.8, s32[]{:T(128)S(6)} %add.22, bf16[4,8,416,256]{3,2,1,0:T(8,128)(2,1)} %bitcast.110, s32[]{:T(128)S(6)} %select_n.92), kind=kOutput, calls=%fused_computation.45 | convolution fusion | flops 1063256064 | bytes 8945672 | tf_op jit(solution)/shard_map/dot_general | solution.py:42
  281.3 4.8 %fusion.77 = f32[208,5,416]{2,0,1:T(8,128)S(1)} fusion(f32[208,5,416]{2,0,1:T(8,128)S(1)} %fusion.37, bf16[4,14,416,256]{3,2,1,0:T(8,128)(2,1)} %copy-done.8, s32[]{:T(128)S(6)} %add.23, bf16[4,8,416,256]{3,2,1,0:T(8,128)(2,1)S(1)} %bitcast.117, s32[]{:T(128)S(6)} %select_n.92), kind=kOutput, calls=%fused_computation.53 | convolution fusion | flops 1240465408 | bytes 9797640 | tf_op jit(solution)/shard_map/dot_general | solution.py:42
  286.1 5.3 %fusion.127 = f32[208,5,416]{2,0,1:T(8,128)S(1)} fusion(f32[208,5,416]{2,0,1:T(8,128)S(1)} %fusion.77, bf16[4,14,416,256]{3,2,1,0:T(8,128)(2,1)} %copy-done.8, s32[]{:T(128)S(6)} %select_n.97, bf16[4,8,416,256]{3,2,1,0:T(8,128)(2,1)S(1)} %bitcast.118, s32[]{:T(128)S(6)} %select_n.92), kind=kOutput, calls=%fused_computation.63 | convolution fusion | flops 1417674752 | bytes 10649608 | tf_op jit(solution)/shard_map/dot_general | solution.py:42
  295.0 23.5 %collective-permute-done.9 = f32[208,5,416]{2,0,1:T(8,128)} collective-permute-done((f32[208,5,416]{2,0,1:T(8,128)}, f32[208,5,416]{2,0,1:T(8,128)}, u32[]{:S(2)}, u32[]{:S(2)}) %collective-permute-start.9) | collective-permute-done | bytes 1730592 | tf_op jit(solution)/shard_map/ppermute | solution.py:10
  318.5 3.5 %add_divide_fusion = f32[208,5,416]{2,0,1:T(8,128)} fusion(f32[208,5,416]{2,0,1:T(8,128)S(1)} %fusion.57, f32[208,5,416]{2,0,1:T(8,128)} %collective-permute-done.9, f32[5]{0:T(128)S(1)} %stack.92), kind=kLoop, calls=%fused_computation.27 | loop fusion | flops 865280 | bytes 5191700 | tf_op jit(solution)/shard_map/div | solution.py:105
  (80 shorter events, 44.9 us)
Async XLA Ops:
  7.0 11.5 %copy-start.7 = (bf16[1,416,2048]{2,1,0:T(8,128)(2,1)S(1)}, bf16[1,416,2048]{2,1,0:T(8,128)(2,1)}, u32[]{:S(2)}) copy-start(bf16[1,416,2048]{2,1,0:T(8,128)(2,1)} %param.4) | copy-start | bytes 5111812
  14.9 22.1 %collective-permute-start = (bf16[416,1024]{1,0:T(8,128)(2,1)S(1)}, bf16[416,1024]{1,0:T(8,128)(2,1)}, u32[]{:S(2)}, u32[]{:S(2)}) collective-permute-start(bf16[416,1024]{1,0:T(8,128)(2,1)S(1)} %bitcast.122), channel_id=1, source_target_pairs={{0,4},{4,0},{1,5},{5,1},{2,6},{6,2},{3,7},{7,3},{8,12},{12,8},{9,1... | collective-permute-start | bytes 2555912 | tf_op jit(solution)/shard_map/ppermute | solution.py:10
  63.9 7.3 %copy-start.6 = (bf16[416,1024]{1,0:T(8,128)(2,1)S(1)}, bf16[416,1024]{1,0:T(8,128)(2,1)}, u32[]{:S(2)}) copy-start(bf16[416,1024]{1,0:T(8,128)(2,1)} %get-tuple-element.15) | copy-start | bytes 2555908
  65.4 47.1 %all-to-all-start.1 = ((bf16[8,416,256]{2,1,0:T(8,128)(2,1)}), bf16[8,416,256]{2,1,0:T(8,128)(2,1)S(1)}, u32[]{:S(2)}, u32[]{:S(2)}) async-start(bf16[8,416,256]{2,1,0:T(8,128)(2,1)} %bitcast.5), calls=%async_computation.1 | async-start | bytes 3407872 | tf_op jit(solution)/shard_map/all_to_all | solution.py:89
  74.4 6.6 %copy-start.2 = (bf16[1,416,4,256]{3,1,0,2:T(8,128)(2,1)}, bf16[1,416,4,256]{3,1,0,2:T(8,128)(2,1)S(1)}, u32[]{:S(2)}) copy-start(bf16[1,416,4,256]{3,1,0,2:T(8,128)(2,1)S(1)} %copy.27) | copy-start | bytes 2555908
  75.9 59.5 %collective-permute-start.3 = (bf16[4,2,416,256]{3,2,1,0:T(8,128)(2,1)}, bf16[4,2,416,256]{3,2,1,0:T(8,128)(2,1)}, u32[]{:S(2)}, u32[]{:S(2)}) collective-permute-start(bf16[4,2,416,256]{3,2,1,0:T(8,128)(2,1)} %fusion.31), channel_id=1, source_target_pairs={{0,8},{8,16},{16,24},{1,9},{9,17},{17,25},{2,10},{10,18},{18,26},{... | collective-permute-start | bytes 5111816 | tf_op jit(solution)/shard_map/ppermute | solution.py:32
  81.0 68.3 %collective-permute-start.6 = (bf16[4,2,416,256]{3,2,1,0:T(8,128)(2,1)}, bf16[4,2,416,256]{3,2,1,0:T(8,128)(2,1)}, u32[]{:S(2)}, u32[]{:S(2)}) collective-permute-start(bf16[4,2,416,256]{3,2,1,0:T(8,128)(2,1)} %fusion.31), channel_id=1, source_target_pairs={{8,0},{16,8},{24,16},{9,1},{17,9},{25,17},{10,2},{18,10},{26,18},{... | collective-permute-start | bytes 5111816 | tf_op jit(solution)/shard_map/ppermute | solution.py:33
  112.5 38.1 %copy-start.5 = (bf16[8,416,256]{2,1,0:T(8,128)(2,1)}, bf16[8,416,256]{2,1,0:T(8,128)(2,1)S(1)}, u32[]{:S(2)}) copy-start(bf16[8,416,256]{2,1,0:T(8,128)(2,1)S(1)} %all-to-all-done.1) | copy-start | bytes 5111812
  112.5 38.1 %collective-permute-start.1 = (bf16[1,8,416,256]{3,2,1,0:T(8,128)(2,1)S(1)}, bf16[1,8,416,256]{3,2,1,0:T(8,128)(2,1)}, u32[]{:S(2)}, u32[]{:S(2)}) collective-permute-start(bf16[1,8,416,256]{3,2,1,0:T(8,128)(2,1)S(1)} %bitcast.121), channel_id=1, source_target_pairs={{0,2},{1,3},{2,0},{3,1},{4,6},{5,7},{6,4},{7,5},{8,10},{9,11},{10,... | collective-permute-start | bytes 5111816 | tf_op jit(solution)/shard_map/ppermute | solution.py:19
  135.4 49.6 %collective-permute-start.4 = (bf16[4,2,416,256]{3,2,1,0:T(8,128)(2,1)}, bf16[4,2,416,256]{3,2,1,0:T(8,128)(2,1)}, u32[]{:S(2)}, u32[]{:S(2)}) collective-permute-start(bf16[4,2,416,256]{3,2,1,0:T(8,128)(2,1)} %collective-permute-done.3), channel_id=1, source_target_pairs={{0,8},{8,16},{16,24},{1,9},{9,17},{17,25},{2,10},{10,18},{18,26},{... | collective-permute-start | bytes 5111816 | tf_op jit(solution)/shard_map/ppermute | solution.py:32
  149.3 41.3 %collective-permute-start.7 = (bf16[4,2,416,256]{3,2,1,0:T(8,128)(2,1)}, bf16[4,2,416,256]{3,2,1,0:T(8,128)(2,1)}, u32[]{:S(2)}, u32[]{:S(2)}) collective-permute-start(bf16[4,2,416,256]{3,2,1,0:T(8,128)(2,1)} %collective-permute-done.6), channel_id=1, source_target_pairs={{8,0},{16,8},{24,16},{9,1},{17,9},{25,17},{10,2},{18,10},{26,18},{... | collective-permute-start | bytes 5111816 | tf_op jit(solution)/shard_map/ppermute | solution.py:33
  154.8 85.0 %collective-permute-start.2 = (bf16[2,8,416,256]{3,2,1,0:T(8,128)(2,1)}, bf16[2,8,416,256]{3,2,1,0:T(8,128)(2,1)}, u32[]{:S(2)}, u32[]{:S(2)}) collective-permute-start(bf16[2,8,416,256]{3,2,1,0:T(8,128)(2,1)} %pad_maximum_fusion.1), channel_id=1, source_target_pairs={{0,1},{1,0},{2,3},{3,2},{4,5},{5,4},{6,7},{7,6},{8,9},{9,8},{10,11... | collective-permute-start | bytes 10223624 | tf_op jit(solution)/shard_map/ppermute | solution.py:19
  185.0 40.5 %collective-permute-start.5 = (bf16[4,2,416,256]{3,2,1,0:T(8,128)(2,1)}, bf16[4,2,416,256]{3,2,1,0:T(8,128)(2,1)}, u32[]{:S(2)}, u32[]{:S(2)}) collective-permute-start(bf16[4,2,416,256]{3,2,1,0:T(8,128)(2,1)} %collective-permute-done.4), channel_id=1, source_target_pairs={{0,8},{8,16},{16,24},{1,9},{9,17},{17,25},{2,10},{10,18},{18,26},{... | collective-permute-start | bytes 5111816 | tf_op jit(solution)/shard_map/ppermute | solution.py:32
  190.6 43.3 %collective-permute-start.8 = (bf16[4,2,416,256]{3,2,1,0:T(8,128)(2,1)}, bf16[4,2,416,256]{3,2,1,0:T(8,128)(2,1)}, u32[]{:S(2)}, u32[]{:S(2)}) collective-permute-start(bf16[4,2,416,256]{3,2,1,0:T(8,128)(2,1)} %collective-permute-done.7), channel_id=1, source_target_pairs={{8,0},{16,8},{24,16},{9,1},{17,9},{25,17},{10,2},{18,10},{26,18},{... | collective-permute-start | bytes 5111816 | tf_op jit(solution)/shard_map/ppermute | solution.py:33
  249.1 5.8 %copy-start.4 = (bf16[2,2,8,416,256]{4,3,2,1,0:T(8,128)(2,1)S(1)}, bf16[2,2,8,416,256]{4,3,2,1,0:T(8,128)(2,1)}, u32[]{:S(2)}) copy-start(bf16[2,2,8,416,256]{4,3,2,1,0:T(8,128)(2,1)} %copy.25) | copy-start | bytes 20447236
  254.9 11.6 %slice-start.2 = ((s8[11927552]{0:T(1024)(128)(4,1)}), s8[4194304]{0:T(1024)(128)(4,1)S(1)}, s32[]{:S(2)}) async-start(s8[11927552]{0:T(1024)(128)(4,1)} %bitcast.123), calls=%async_computation.4 | async-start | bytes 8388608
  254.9 11.6 %slice-start.3 = ((s8[11927552]{0:T(1024)(128)(4,1)}), s8[4194304]{0:T(1024)(128)(4,1)S(1)}, s32[]{:S(2)}) async-start(s8[11927552]{0:T(1024)(128)(4,1)} %bitcast.123), calls=%async_computation.5 | async-start | bytes 8388608
  260.5 6.0 %slice-start.4 = ((s8[11927552]{0:T(1024)(128)(4,1)}), s8[3538944]{0:T(1024)(128)(4,1)S(1)}, s32[]{:S(2)}) async-start(s8[11927552]{0:T(1024)(128)(4,1)} %bitcast.123), calls=%async_computation.6 | async-start | bytes 7077888
  269.2 12.0 %slice-start = ((s8[6815744]{0:T(1024)(128)(4,1)}), s8[2621440]{0:T(1024)(128)(4,1)S(1)}, s32[]{:S(2)}) async-start(s8[6815744]{0:T(1024)(128)(4,1)} %bitcast.115), calls=%async_computation.2 | async-start | bytes 5242880
  271.7 46.8 %collective-permute-start.9 = (f32[208,5,416]{2,0,1:T(8,128)}, f32[208,5,416]{2,0,1:T(8,128)}, u32[]{:S(2)}, u32[]{:S(2)}) collective-permute-start(f32[208,5,416]{2,0,1:T(8,128)} %fusion.67), channel_id=1, source_target_pairs={{0,4},{4,0},{1,5},{5,1},{2,6},{6,2},{3,7},{7,3},{8,12},{12,8},{9,1... | collective-permute-start | bytes 5191688 | tf_op jit(solution)/shard_map/ppermute | solution.py:10
  276.2 5.1 %slice-start.1 = ((s8[6815744]{0:T(1024)(128)(4,1)}), s8[4194304]{0:T(1024)(128)(4,1)S(1)}, s32[]{:S(2)}) async-start(s8[6815744]{0:T(1024)(128)(4,1)} %bitcast.115), calls=%async_computation.3 | async-start | bytes 8388608
  281.2 10.1 %slice-start.5 = ((s8[11927552]{0:T(1024)(128)(4,1)}), s8[4194304]{0:T(1024)(128)(4,1)S(1)}, s32[]{:S(2)}) async-start(s8[11927552]{0:T(1024)(128)(4,1)} %bitcast.125), calls=%async_computation.7 | async-start | bytes 8388608
  281.3 10.1 %slice-start.6 = ((s8[11927552]{0:T(1024)(128)(4,1)}), s8[4194304]{0:T(1024)(128)(4,1)S(1)}, s32[]{:S(2)}) async-start(s8[11927552]{0:T(1024)(128)(4,1)} %bitcast.125), calls=%async_computation.8 | async-start | bytes 8388608
  286.0 5.3 %slice-start.7 = ((s8[11927552]{0:T(1024)(128)(4,1)}), s8[3538944]{0:T(1024)(128)(4,1)S(1)}, s32[]{:S(2)}) async-start(s8[11927552]{0:T(1024)(128)(4,1)} %bitcast.125), calls=%async_computation.9 | async-start | bytes 7077888
  (5 other events, 19.3 us)

commit v11 on v5

--- a/solution.py
+++ b/solution.py
@@ -72,11 +72,13 @@
     by_loc = by_loc.reshape(quad_size, pair_rows, PAIR, piece).transpose(0, 2, 1, 3)
     by_loc = by_loc.reshape(quad_size * PAIR, pair_rows, piece)
     rows_here = lax.all_to_all(by_loc, ("tq", "th"), 0, 0, tiled=True)
-    all_background = gather_chan(rows_here)
+    rows_out = pair_rows // PAIR
+    swapped = jnp.concatenate([rows_here[:, rows_out:], rows_here[:, :rows_out]], axis=1)
+    own_first = jnp.where(pair_index == 0, rows_here, swapped)
+    all_background = gather_chan(own_first)
 
-    rows_out = pair_rows // PAIR
-    give_rows = lax.dynamic_slice_in_dim(all_background, (1 - pair_index) * rows_out, rows_out, axis=2)
-    keep_rows = lax.dynamic_slice_in_dim(all_background, pair_index * rows_out, rows_out, axis=2)
+    keep_rows = all_background[:, :, :rows_out]
+    give_rows = all_background[:, :, rows_out:]
     sent = swap_pair(lag_block(give_rows, all_analysis, cycle_total, max_lag, lag_total))
     summed = lag_block(keep_rows, all_analysis, cycle_total, max_lag, lag_total) + sent
 

time: 283 us -> 290 us (1.025)
  blocking collectives: 87.6 us -> 0 us
  waiting for transfers between devices: 100 us -> 185 us
  starting transfers between devices: 9.43 us -> 16 us
  local copies, waits for them, and re-layouts: 18.6 us -> 23.7 us
  matrix products: 25.1 us -> 22.1 us
    all_to_all x1 -> x0, blocking collectives: 87.6 us -> none  [body(): rows_here = lax.all_to_all(by_loc, ('tq', 'th'), 0, 0, tiled=True)]
    all_to_all x0 -> x1, waiting for transfers between devices: none -> 71.7 us  [body(): rows_here = lax.all_to_all(by_loc, ('tq', 'th'), 0, 0, tiled=True)]
    all_gather x1, waiting for transfers between devices: 4.73 us -> 25.9 us  [body(): all_analysis = lax.all_gather(pair_analysis, 'tq', axis=1, tiled=True)]
    ppermute x2, waiting for transfers between devices: 44.5 us -> 56.6 us  [swap_pair(): return lax.ppermute(x, 'th', [(0, 1), (1, 0)])]
    all_to_all x1, waiting for transfers between devices: 9.99 us -> 0.01 us  [body(): by_loc = lax.all_to_all(split_b, 'chan', 2, 0, tiled=True)]
    ppermute x2, waiting for transfers between devices: 40.8 us -> 31.2 us  [gather_chan(): got = lax.ppermute(held, 'chan', [(c, c ^ 1 << bit) for c in range(size)])]
    all_to_all x0 -> x1, starting transfers between devices: none -> 6.06 us  [body(): rows_here = lax.all_to_all(by_loc, ('tq', 'th'), 0, 0, tiled=True)]
    dot_general x10, matrix products: 25.1 us -> 22.1 us  [contract(): lax.dot_general(left, right, (((0, 1, 3), (0, 1, 3)), ((), ())), preferre...]
  transfers between devices with their start and end apart: 6 -> 7, of which waited for: 6 -> 6; matrix products, arithmetic and copies ran while one was open for 13% -> 16% of each run, Pallas kernels for 0% -> 0%
where the time goes in v11:
time: 290 us; the launch traced here: 289 us
  waiting for transfers between devices  185 us (64%)
  other arithmetic  26.8 us (9%)
  local copies, waits for them, and re-layouts  23.7 us (8%)
  matrix products  22.1 us (8%)
  starting transfers between devices  16 us (6%)
  between operations  15.4 us (5%)
    all_to_all x1, waiting for transfers between devices, body(): rows_here = lax.all_to_all(by_loc, ('tq', 'th'), 0, 0, tiled=True)  71.7 us
    ppermute x2, waiting for transfers between devices, swap_pair(): return lax.ppermute(x, 'th', [(0, 1), (1, 0)])  56.6 us
    ppermute x2, waiting for transfers between devices, gather_chan(): got = lax.ppermute(held, 'chan', [(c, c ^ 1 << bit) for c in range(size)])  31.2 us
    all_gather x1, waiting for transfers between devices, body(): all_analysis = lax.all_gather(pair_analysis, 'tq', axis=1, tiled=True)  25.9 us
    dot_general x10, matrix products, contract(): lax.dot_general(left, right, (((0, 1, 3), (0, 1, 3)), ((), ())), preferre...  22.1 us
    select_n x1, other arithmetic, body(): keep = jnp.where(pair_index == 0, halves[:, 0], halves[:, 1])  6.66 us
    another operation x2, other arithmetic, gather_chan(): jnp.stack([first, second], axis=1).reshape((-1,) + x.shape)  6.12 us
    all_to_all x1, starting transfers between devices, body(): rows_here = lax.all_to_all(by_loc, ('tq', 'th'), 0, 0, tiled=True)  6.06 us
  transfers between devices with their start and end apart: 7, of which 6 were waited for; matrix products, arithmetic and copies ran while one was open for 16% of the time, Pallas kernels for 0%

profile of v11, /device:TPU:0, one launch (start us, length us, event | category | flops | bytes accessed | tf_op | source)
XLA Modules:
  0.0 289.5 jit_solution(5266648132232974180)
XLA Ops:
  8.5 3.9 %squeeze.4 = bf16[416,2,4,256]{3,2,1,0:T(4,128)(2,1)S(1)} reshape(bf16[1,416,2048]{2,1,0:T(8,128)(2,1)} %param.4) | data formatting | bytes 3407872 | tf_op jit(solution)/shard_map/squeeze | solution.py:60
  13.1 2.5 copy.23
  15.6 4.2 %all-to-all-start = ((bf16[416,2,4,256]{3,1,0,2:T(2,128)(2,1)}), bf16[416,2,4,256]{3,1,0,2:T(2,128)(2,1)S(1)}, u32[]{:S(2)}, u32[]{:S(2)}) async-start(bf16[416,2,4,256]{3,1,0,2:T(2,128)(2,1)} %copy.23), calls=%async_computation | async-start | bytes 3407872 | tf_op jit(solution)/shard_map/all_to_all | solution.py:71
  20.4 4.3 %squeeze.5 = bf16[416,2,1024]{2,1,0:T(2,128)(2,1)S(1)} reshape(bf16[1,416,2048]{2,1,0:T(8,128)(2,1)} %param.3) | data formatting | bytes 3407872 | tf_op jit(solution)/shard_map/squeeze | solution.py:59
  26.1 6.7 %fusion.28 = (bf16[416,1024]{1,0:T(8,128)(2,1)S(1)}, bf16[416,1,1024]{2,1,0:T(2,128)(2,1)S(1)}) fusion(pred[]{:T(512)S(6)} %eq.20, bf16[416,2,1024]{2,1,0:T(2,128)(2,1)S(1)} %broadcast_select_fusion), kind=kLoop, calls=%fused_computation.36 | loop fusion | flops 851968 | bytes 3407873 | tf_op jit(solution)/shard_map/jit(_where)/select_n | solution.py:63
  34.0 2.3 collective-permute-start.2
  37.0 19.1 %collective-permute-done.2 = bf16[416,1024]{1,0:T(8,128)(2,1)} collective-permute-done((bf16[416,1024]{1,0:T(8,128)(2,1)}, bf16[416,1024]{1,0:T(8,128)(2,1)}, u32[]{:S(2)}, u32[]{:S(2)}) %collective-permute-start.2) | collective-permute-done | bytes 852000 | tf_op jit(solution)/shard_map/ppermute | solution.py:10
  56.2 2.7 stack.74
  61.7 6.1 %all-to-all-start.1 = ((bf16[8,416,256]{2,1,0:T(8,128)(2,1)}), bf16[8,416,256]{2,1,0:T(8,128)(2,1)S(1)}, u32[]{:S(2)}, u32[]{:S(2)}) async-start(bf16[8,416,256]{2,1,0:T(8,128)(2,1)} %bitcast.4), calls=%async_computation.1 | async-start | bytes 3407872 | tf_op jit(solution)/shard_map/all_to_all | solution.py:74
  69.2 71.7 %all-to-all-done.1 = bf16[8,416,256]{2,1,0:T(8,128)(2,1)S(1)} async-done(((bf16[8,416,256]{2,1,0:T(8,128)(2,1)}), bf16[8,416,256]{2,1,0:T(8,128)(2,1)S(1)}, u32[]{:S(2)}, u32[]{:S(2)}) %all-to-all-start.1) | async-done | bytes 1703968 | tf_op jit(solution)/shard_map/all_to_all | solution.py:74
  143.3 28.2 %collective-permute-done = bf16[1,8,416,256]{3,2,1,0:T(8,128)(2,1)} collective-permute-done((bf16[1,8,416,256]{3,2,1,0:T(8,128)(2,1)S(1)}, bf16[1,8,416,256]{3,2,1,0:T(8,128)(2,1)}, u32[]{:S(2)}, u32[]{:S(2)}) %collective-permute-start) | collective-permute-done | bytes 1703968 | tf_op jit(solution)/shard_map/ppermute | solution.py:19
  171.5 2.2 broadcast_select_fusion.5
  173.7 2.1 pad_maximum_fusion.1
  179.2 3.0 %collective-permute-done.1 = bf16[2,8,416,256]{3,2,1,0:T(8,128)(2,1)} collective-permute-done((bf16[2,8,416,256]{3,2,1,0:T(8,128)(2,1)}, bf16[2,8,416,256]{3,2,1,0:T(8,128)(2,1)}, u32[]{:S(2)}, u32[]{:S(2)}) %collective-permute-start.1) | collective-permute-done | bytes 3407904 | tf_op jit(solution)/shard_map/ppermute | solution.py:19
  182.2 3.5 %select_bitcast_fusion.1 = (bf16[2,1,8,416,256]{4,3,2,0,1:T(8,128)(2,1)S(1)}, bf16[2,1,8,416,256]{4,3,2,0,1:T(8,128)(2,1)}) fusion(bf16[2,8,416,256]{3,2,1,0:T(8,128)(2,1)} %collective-permute-done.1, pred[]{:T(512)S(6)} %eq.18, bf16[1,8,416,256]{3,2,1,0:T(8,128)(2,1)S(1)} %get-tuple-element.10, bf16[1,8,416,256]{3,2,1,0:T(8,128)(2,1)S(1)} %get-tuple-element.9), kind=kLoop, calls=%fused_computation.23 | loop fusion | flops 5111808 | bytes 13631489 | tf_op jit(solution)/shard_map/stack | solution.py:23
  185.8 2.6 pad_maximum_fusion
  188.3 3.3 %copy.25 = bf16[2,2,8,416,256]{4,3,2,1,0:T(8,128)(2,1)} copy(bf16[2,2,8,416,256]{4,3,2,0,1:T(8,128)(2,1)S(1)} %pad_maximum_fusion) | data formatting | bytes 13631488 | tf_op jit(solution)/shard_map/stack | solution.py:23
  191.6 25.9 %all-gather.2.cloned.1.call-done = bf16[4,8,416,256]{3,2,1,0:T(8,128)(2,1)} async-done(((bf16[4,2,416,256]{3,2,1,0:T(8,128)(2,1)}), bf16[4,8,416,256]{3,2,1,0:T(8,128)(2,1)}) %all-gather.2.cloned.1.call-update) | async-done | bytes 6815760 | tf_op jit(solution)/shard_map/all_gather | solution.py:68
  217.6 5.0 %fusion.98 = f32[208,5,416]{2,0,1:T(8,128)S(1)} fusion(bf16[4,8,416,256]{3,2,1,0:T(8,128)(2,1)} %all-gather.2.cloned.1.call-done, bf16[4,8,416,256]{3,2,1,0:T(8,128)(2,1)} %bitcast.106), kind=kOutput, calls=%fused_computation.59 | convolution fusion | flops 1063256064 | bytes 8093696 | tf_op jit(solution)/shard_map/dot_general | solution.py:28
  222.7 1.9 copy-done.3
  226.6 2.2 fusion.40
  235.5 1.9 fusion.48
  237.5 2.2 fusion.34
  243.3 37.5 %collective-permute-done.3 = f32[208,5,416]{2,0,1:T(8,128)S(1)} collective-permute-done((f32[208,5,416]{2,0,1:T(8,128)S(1)}, f32[208,5,416]{2,0,1:T(8,128)S(1)}, u32[]{:S(2)}, u32[]{:S(2)}) %collective-permute-start.3) | collective-permute-done | bytes 1730592 | tf_op jit(solution)/shard_map/ppermute | solution.py:10
  (36 shorter events, 28.9 us)
Async XLA Ops:
  15.6 44.6 %all-to-all-start = ((bf16[416,2,4,256]{3,1,0,2:T(2,128)(2,1)}), bf16[416,2,4,256]{3,1,0,2:T(2,128)(2,1)S(1)}, u32[]{:S(2)}, u32[]{:S(2)}) async-start(bf16[416,2,4,256]{3,1,0,2:T(2,128)(2,1)} %copy.23), calls=%async_computation | async-start | bytes 3407872 | tf_op jit(solution)/shard_map/all_to_all | solution.py:71
  34.0 22.2 %collective-permute-start.2 = (bf16[416,1024]{1,0:T(8,128)(2,1)}, bf16[416,1024]{1,0:T(8,128)(2,1)}, u32[]{:S(2)}, u32[]{:S(2)}) collective-permute-start(bf16[416,1024]{1,0:T(8,128)(2,1)} %bitcast.105), channel_id=1, source_target_pairs={{0,4},{4,0},{1,5},{5,1},{2,6},{6,2},{3,7},{7,3},{8,12},{12,8},{9,1... | collective-permute-start | bytes 2555912 | tf_op jit(solution)/shard_map/ppermute | solution.py:10
  61.7 79.2 %all-to-all-start.1 = ((bf16[8,416,256]{2,1,0:T(8,128)(2,1)}), bf16[8,416,256]{2,1,0:T(8,128)(2,1)S(1)}, u32[]{:S(2)}, u32[]{:S(2)}) async-start(bf16[8,416,256]{2,1,0:T(8,128)(2,1)} %bitcast.4), calls=%async_computation.1 | async-start | bytes 3407872 | tf_op jit(solution)/shard_map/all_to_all | solution.py:74
  67.7 149.8 %all-gather.2.cloned.1.call-start = ((), (), s32[]{:S(2)}) async-start(), calls=%async_computation.2 | async-start | bytes 8519680 | tf_op jit(solution)/shard_map/all_gather | solution.py:68
  141.5 1.9 copy-start.1
  141.5 30.0 %collective-permute-start = (bf16[1,8,416,256]{3,2,1,0:T(8,128)(2,1)S(1)}, bf16[1,8,416,256]{3,2,1,0:T(8,128)(2,1)}, u32[]{:S(2)}, u32[]{:S(2)}) collective-permute-start(bf16[1,8,416,256]{3,2,1,0:T(8,128)(2,1)S(1)} %fusion.29), channel_id=1, source_target_pairs={{0,2},{1,3},{2,0},{3,1},{4,6},{5,7},{6,4},{7,5},{8,10},{9,11},{10,... | collective-permute-start | bytes 5111816 | tf_op jit(solution)/shard_map/ppermute | solution.py:19
  173.7 2.8 copy-start.2
  175.8 6.4 %collective-permute-start.1 = (bf16[2,8,416,256]{3,2,1,0:T(8,128)(2,1)}, bf16[2,8,416,256]{3,2,1,0:T(8,128)(2,1)}, u32[]{:S(2)}, u32[]{:S(2)}) collective-permute-start(bf16[2,8,416,256]{3,2,1,0:T(8,128)(2,1)} %pad_maximum_fusion.1), channel_id=1, source_target_pairs={{0,1},{1,0},{2,3},{3,2},{4,5},{5,4},{6,7},{7,6},{8,9},{9,8},{10,11... | collective-permute-start | bytes 10223624 | tf_op jit(solution)/shard_map/ppermute | solution.py:19
  217.6 5.2 %copy-start = (bf16[2,2,8,416,256]{4,3,2,1,0:T(8,128)(2,1)S(1)}, bf16[2,2,8,416,256]{4,3,2,1,0:T(8,128)(2,1)}, u32[]{:S(2)}) copy-start(bf16[2,2,8,416,256]{4,3,2,1,0:T(8,128)(2,1)} %copy.25) | copy-start | bytes 20447236
  217.6 7.1 %copy-start.3 = (bf16[4,8,416,256]{3,2,1,0:T(8,128)(2,1)S(1)}, bf16[4,8,416,256]{3,2,1,0:T(8,128)(2,1)}, u32[]{:S(2)}) copy-start(bf16[4,8,416,256]{3,2,1,0:T(8,128)(2,1)} %all-gather.2.cloned.1.call-done) | copy-start | bytes 20447236
  232.4 48.4 %collective-permute-start.3 = (f32[208,5,416]{2,0,1:T(8,128)S(1)}, f32[208,5,416]{2,0,1:T(8,128)S(1)}, u32[]{:S(2)}, u32[]{:S(2)}) collective-permute-start(f32[208,5,416]{2,0,1:T(8,128)S(1)} %fusion.118), channel_id=1, source_target_pairs={{0,4},{4,0},{1,5},{5,1},{2,6},{6,2},{3,7},{7,3},{8,12},{12,8},{9,1... | collective-permute-start | bytes 5191688 | tf_op jit(solution)/shard_map/ppermute | solution.py:10
Sparse Core Ops, SparseCore 0:
  70.1 147.3 all-gather.1

commit v12 on v5

--- a/solution.py
+++ b/solution.py
@@ -59,9 +59,10 @@
     local_analysis = jnp.where(valid_cols, analysis_dep[0], jnp.zeros((), jnp.bfloat16))
     local_background = jnp.where(valid_cols, background_dep[0], jnp.zeros((), jnp.bfloat16))
 
-    halves = local_analysis.reshape(width_block, PAIR, half)
-    keep = jnp.where(pair_index == 0, halves[:, 0], halves[:, 1])
-    give = jnp.where(pair_index == 0, halves[:, 1], halves[:, 0])
+    low_half = local_analysis[:, :half]
+    high_half = local_analysis[:, half:]
+    keep = jnp.where(pair_index == 0, low_half, high_half)
+    give = jnp.where(pair_index == 0, high_half, low_half)
     got = swap_pair(give)
     pair_analysis = jnp.where(pair_index == 0, jnp.stack([keep, got]), jnp.stack([got, keep]))
     pair_analysis = pair_analysis.reshape(PAIR, width_block, chan_size, piece).transpose(2, 0, 1, 3)

time: 283 us -> 272 us (0.961)
  local copies, waits for them, and re-layouts: 18.6 us -> 13.1 us
  other arithmetic: 26.4 us -> 20.9 us
    select_n x1, other arithmetic: 6.66 us -> 1.02 us  [body(): keep = jnp.where(pair_index == 0, low_half, high_half)]
    squeeze x1 -> x0, local copies, waits for them, and re-layouts: 4.35 us -> none  [body(): analysis_dep[0]]
  transfers between devices with their start and end apart: 6 -> 6, of which waited for: 6 -> 6; matrix products, arithmetic and copies ran while one was open for 13% -> 14% of each run, Pallas kernels for 0% -> 0%
where the time goes in v12:
time: 272 us
  waiting for transfers between devices  100 us (37%)
  blocking collectives  87.7 us (32%)
  matrix products  25.1 us (9%)
  other arithmetic  20.9 us (8%)
  between operations  15.4 us (6%)
  local copies, waits for them, and re-layouts  13.1 us (5%)
  starting transfers between devices  9.44 us (3%)
    all_to_all x1, blocking collectives, body(): rows_here = lax.all_to_all(by_loc, ('tq', 'th'), 0, 0, tiled=True)  87.7 us
    ppermute x2, waiting for transfers between devices, swap_pair(): return lax.ppermute(x, 'th', [(0, 1), (1, 0)])  44.6 us
    ppermute x2, waiting for transfers between devices, gather_chan(): got = lax.ppermute(held, 'chan', [(c, c ^ 1 << bit) for c in range(size)])  40.8 us
    dot_general x10, matrix products, contract(): lax.dot_general(left, right, (((0, 1, 3), (0, 1, 3)), ((), ())), preferre...  25.1 us
    all_to_all x1, waiting for transfers between devices, body(): by_loc = lax.all_to_all(split_b, 'chan', 2, 0, tiled=True)  9.95 us
    another operation x2, other arithmetic, gather_chan(): jnp.stack([first, second], axis=1).reshape((-1,) + x.shape)  6.09 us
  transfers between devices with their start and end apart: 6, of which 6 were waited for; matrix products, arithmetic and copies ran while one was open for 14% of the time, Pallas kernels for 0%

profile of v12, /device:TPU:0, one launch (start us, length us, event | category | flops | bytes accessed | tf_op | source)
XLA Modules:
  0.0 271.5 jit_solution(517943039089006851)
XLA Ops:
  11.0 2.9 %collective-permute-start.2 = (bf16[416,1024]{1,0:T(8,128)(2,1)}, bf16[416,1024]{1,0:T(8,128)(2,1)}, u32[]{:S(2)}, u32[]{:S(2)}) collective-permute-start(bf16[416,1024]{1,0:T(8,128)(2,1)} %get-tuple-element.12), channel_id=1, source_target_pairs={{0,4},{4,0},{1,5},{5,1},{2,6},{6,2},{3,7},{7,3},{8,12},{12,8},{9,1... | collective-permute-start | bytes 2555912 | tf_op jit(solution)/shard_map/ppermute | solution.py:10
  14.5 3.9 %squeeze.6 = bf16[416,2,4,256]{3,2,1,0:T(4,128)(2,1)S(1)} reshape(bf16[1,416,2048]{2,1,0:T(8,128)(2,1)} %param.4) | data formatting | bytes 3407872 | tf_op jit(solution)/shard_map/squeeze | solution.py:60
  19.1 2.6 copy.17
  21.7 3.6 %all-to-all-start = ((bf16[416,2,4,256]{3,1,0,2:T(2,128)(2,1)}), bf16[416,2,4,256]{3,1,0,2:T(2,128)(2,1)S(1)}, u32[]{:S(2)}, u32[]{:S(2)}) async-start(bf16[416,2,4,256]{3,1,0,2:T(2,128)(2,1)} %copy.17), calls=%async_computation | async-start | bytes 3407872 | tf_op jit(solution)/shard_map/all_to_all | solution.py:72
  26.1 7.1 %collective-permute-done.2 = bf16[416,1024]{1,0:T(8,128)(2,1)} collective-permute-done((bf16[416,1024]{1,0:T(8,128)(2,1)}, bf16[416,1024]{1,0:T(8,128)(2,1)}, u32[]{:S(2)}, u32[]{:S(2)}) %collective-permute-start.2) | collective-permute-done | bytes 852000 | tf_op jit(solution)/shard_map/ppermute | solution.py:10
  33.2 2.0 stack.77
  36.8 9.9 %all-to-all-done = bf16[416,2,4,256]{3,1,0,2:T(2,128)(2,1)S(1)} async-done(((bf16[416,2,4,256]{3,1,0,2:T(2,128)(2,1)}), bf16[416,2,4,256]{3,1,0,2:T(2,128)(2,1)S(1)}, u32[]{:S(2)}, u32[]{:S(2)}) %all-to-all-start) | async-done | bytes 1703968 | tf_op jit(solution)/shard_map/all_to_all | solution.py:72
  47.0 87.7 %all_to_all.20 = bf16[8,416,256]{2,1,0:T(8,128)(2,1)S(1)} all-to-all(bf16[8,416,256]{2,1,0:T(8,128)(2,1)S(1)} %bitcast.117), channel_id=1, replica_groups=mesh['tq'=4,'th'=2,'chan'=4] {'tq','th'}, dimensions={0} | all-to-all | bytes 3407872 | tf_op jit(solution)/shard_map/all_to_all | solution.py:75
  136.0 37.8 %collective-permute-done = bf16[1,8,416,256]{3,2,1,0:T(8,128)(2,1)} collective-permute-done((bf16[1,8,416,256]{3,2,1,0:T(8,128)(2,1)S(1)}, bf16[1,8,416,256]{3,2,1,0:T(8,128)(2,1)}, u32[]{:S(2)}, u32[]{:S(2)}) %collective-permute-start) | collective-permute-done | bytes 1703968 | tf_op jit(solution)/shard_map/ppermute | solution.py:19
  173.8 2.2 broadcast_select_fusion.2
  176.0 2.1 pad_maximum_fusion.1
  181.4 3.1 %collective-permute-done.1 = bf16[2,8,416,256]{3,2,1,0:T(8,128)(2,1)} collective-permute-done((bf16[2,8,416,256]{3,2,1,0:T(8,128)(2,1)}, bf16[2,8,416,256]{3,2,1,0:T(8,128)(2,1)}, u32[]{:S(2)}, u32[]{:S(2)}) %collective-permute-start.1) | collective-permute-done | bytes 3407904 | tf_op jit(solution)/shard_map/ppermute | solution.py:19
  184.5 3.5 %select_bitcast_fusion.1 = (bf16[2,1,8,416,256]{4,3,2,0,1:T(8,128)(2,1)S(1)}, bf16[2,1,8,416,256]{4,3,2,0,1:T(8,128)(2,1)}) fusion(bf16[2,8,416,256]{3,2,1,0:T(8,128)(2,1)} %collective-permute-done.1, pred[]{:T(512)S(6)} %eq.17, bf16[1,8,416,256]{3,2,1,0:T(8,128)(2,1)S(1)} %get-tuple-element.10, bf16[1,8,416,256]{3,2,1,0:T(8,128)(2,1)S(1)} %get-tuple-element.9), kind=kLoop, calls=%fused_computation.19 | loop fusion | flops 5111808 | bytes 13631489 | tf_op jit(solution)/shard_map/stack | solution.py:23
  188.0 2.6 pad_maximum_fusion
  190.6 3.3 %copy.19 = bf16[2,2,8,416,256]{4,3,2,1,0:T(8,128)(2,1)} copy(bf16[2,2,8,416,256]{4,3,2,0,1:T(8,128)(2,1)S(1)} %pad_maximum_fusion) | data formatting | bytes 13631488 | tf_op jit(solution)/shard_map/stack | solution.py:23
  193.8 4.7 %all-gather.2.cloned.1.call-done = bf16[4,8,416,256]{3,2,1,0:T(8,128)(2,1)} async-done(((bf16[4,2,416,256]{3,2,1,0:T(8,128)(2,1)}), bf16[4,8,416,256]{3,2,1,0:T(8,128)(2,1)}) %all-gather.2.cloned.1.call-update) | async-done | bytes 6815760 | tf_op jit(solution)/shard_map/all_gather | solution.py:69
  198.6 5.0 %fusion.96 = f32[208,5,416]{2,0,1:T(8,128)S(1)} fusion(bf16[4,8,416,256]{3,2,1,0:T(8,128)(2,1)} %all-gather.2.cloned.1.call-done, bf16[4,8,416,256]{3,2,1,0:T(8,128)(2,1)} %bitcast.106, s32[]{:T(128)S(6)} %select_n.78), kind=kOutput, calls=%fused_computation.54 | convolution fusion | flops 1063256064 | bytes 8945668 | tf_op jit(solution)/shard_map/dot_general | solution.py:28
  203.7 4.8 %fusion.44 = f32[208,5,416]{2,0,1:T(8,128)S(1)} fusion(f32[208,5,416]{2,0,1:T(8,128)S(1)} %fusion.96, bf16[4,8,416,256]{3,2,1,0:T(8,128)(2,1)} %all-gather.2.cloned.1.call-done, bf16[4,8,416,256]{3,2,1,0:T(8,128)(2,1)S(1)} %bitcast.107, s32[]{:T(128)S(6)} %select_n.78), kind=kOutput, calls=%fused_computation.42 | convolution fusion | flops 1240465408 | bytes 9797636 | tf_op jit(solution)/shard_map/dot_general | solution.py:28
  208.6 2.2 fusion.78
  210.8 1.9 fusion.64
  217.6 1.9 fusion.34
  219.5 2.2 fusion.72
  221.7 1.9 fusion.54
  225.3 37.4 %collective-permute-done.3 = f32[208,5,416]{2,0,1:T(8,128)S(1)} collective-permute-done((f32[208,5,416]{2,0,1:T(8,128)S(1)}, f32[208,5,416]{2,0,1:T(8,128)S(1)}, u32[]{:S(2)}, u32[]{:S(2)}) %collective-permute-start.3) | collective-permute-done | bytes 1730592 | tf_op jit(solution)/shard_map/ppermute | solution.py:10
  (34 shorter events, 19.7 us)
Async XLA Ops:
  11.0 22.2 %collective-permute-start.2 = (bf16[416,1024]{1,0:T(8,128)(2,1)}, bf16[416,1024]{1,0:T(8,128)(2,1)}, u32[]{:S(2)}, u32[]{:S(2)}) collective-permute-start(bf16[416,1024]{1,0:T(8,128)(2,1)} %get-tuple-element.12), channel_id=1, source_target_pairs={{0,4},{4,0},{1,5},{5,1},{2,6},{6,2},{3,7},{7,3},{8,12},{12,8},{9,1... | collective-permute-start | bytes 2555912 | tf_op jit(solution)/shard_map/ppermute | solution.py:10
  21.7 25.0 %all-to-all-start = ((bf16[416,2,4,256]{3,1,0,2:T(2,128)(2,1)}), bf16[416,2,4,256]{3,1,0,2:T(2,128)(2,1)S(1)}, u32[]{:S(2)}, u32[]{:S(2)}) async-start(bf16[416,2,4,256]{3,1,0,2:T(2,128)(2,1)} %copy.17), calls=%async_computation | async-start | bytes 3407872 | tf_op jit(solution)/shard_map/all_to_all | solution.py:72
  25.3 173.3 %all-gather.2.cloned.1.call-start = ((), (), s32[]{:S(2)}) async-start(), calls=%async_computation.2 | async-start | bytes 8519680 | tf_op jit(solution)/shard_map/all_gather | solution.py:69
  134.6 1.4 copy-start.1
  134.6 39.1 %collective-permute-start = (bf16[1,8,416,256]{3,2,1,0:T(8,128)(2,1)S(1)}, bf16[1,8,416,256]{3,2,1,0:T(8,128)(2,1)}, u32[]{:S(2)}, u32[]{:S(2)}) collective-permute-start(bf16[1,8,416,256]{3,2,1,0:T(8,128)(2,1)S(1)} %bitcast.116), channel_id=1, source_target_pairs={{0,2},{1,3},{2,0},{3,1},{4,6},{5,7},{6,4},{7,5},{8,10},{9,11},{10,... | collective-permute-start | bytes 5111816 | tf_op jit(solution)/shard_map/ppermute | solution.py:19
  176.0 2.7 %copy-start.2 = (s32[8]{0:T(128)S(1)}, s32[8]{0:T(128)}, u32[]{:S(2)}) copy-start(s32[8]{0:T(128)} %param.5) | copy-start | bytes 100
  178.1 6.4 %collective-permute-start.1 = (bf16[2,8,416,256]{3,2,1,0:T(8,128)(2,1)}, bf16[2,8,416,256]{3,2,1,0:T(8,128)(2,1)}, u32[]{:S(2)}, u32[]{:S(2)}) collective-permute-start(bf16[2,8,416,256]{3,2,1,0:T(8,128)(2,1)} %pad_maximum_fusion.1), channel_id=1, source_target_pairs={{0,1},{1,0},{2,3},{3,2},{4,5},{5,4},{6,7},{7,6},{8,9},{9,8},{10,11... | collective-permute-start | bytes 10223624 | tf_op jit(solution)/shard_map/ppermute | solution.py:19
  198.6 5.2 %copy-start = (bf16[2,2,8,416,256]{4,3,2,1,0:T(8,128)(2,1)S(1)}, bf16[2,2,8,416,256]{4,3,2,1,0:T(8,128)(2,1)}, u32[]{:S(2)}) copy-start(bf16[2,2,8,416,256]{4,3,2,1,0:T(8,128)(2,1)} %copy.19) | copy-start | bytes 20447236
  198.6 10.0 %slice-start = ((s8[6815744]{0:T(1024)(128)(4,1)}), s8[4194304]{0:T(1024)(128)(4,1)S(1)}, s32[]{:S(2)}) async-start(s8[6815744]{0:T(1024)(128)(4,1)} %bitcast.118), calls=%async_computation.3 | async-start | bytes 8388608
  203.7 4.8 %slice-start.1 = ((s8[6815744]{0:T(1024)(128)(4,1)}), s8[2621440]{0:T(1024)(128)(4,1)S(1)}, s32[]{:S(2)}) async-start(s8[6815744]{0:T(1024)(128)(4,1)} %bitcast.118), calls=%async_computation.4 | async-start | bytes 5242880
  214.4 48.4 %collective-permute-start.3 = (f32[208,5,416]{2,0,1:T(8,128)S(1)}, f32[208,5,416]{2,0,1:T(8,128)S(1)}, u32[]{:S(2)}, u32[]{:S(2)}) collective-permute-start(f32[208,5,416]{2,0,1:T(8,128)S(1)} %fusion.116), channel_id=1, source_target_pairs={{0,4},{4,0},{1,5},{5,1},{2,6},{6,2},{3,7},{7,3},{8,12},{12,8},{9,1... | collective-permute-start | bytes 5191688 | tf_op jit(solution)/shard_map/ppermute | solution.py:10
Sparse Core Ops, SparseCore 0:
  36.9 161.6 all-gather.1

commit v13 on v12

--- a/solution.py
+++ b/solution.py
@@ -30,13 +30,16 @@
     )
 
 
-def lag_block(background, analysis, cycle_total, max_lag, lag_total):
-    pieces = [None] * lag_total
-    for offset in range(max_lag + 1):
-        span = cycle_total - offset
-        pieces[max_lag + offset] = contract(background[:, offset:], analysis[:, :span])
-        if offset > 0:
-            pieces[max_lag - offset] = contract(background[:, :span], analysis[:, offset:])
+def lag_block(background, analysis, cycle_total, max_lag, lags):
+    pieces = []
+    for k in lags:
+        offset = k - max_lag
+        if offset >= 0:
+            span = cycle_total - offset
+            pieces.append(contract(background[:, offset:], analysis[:, :span]))
+        else:
+            span = cycle_total + offset
+            pieces.append(contract(background[:, :span], analysis[:, -offset:]))
     return jnp.stack(pieces, axis=1)
 
 
@@ -78,8 +81,13 @@
     rows_out = pair_rows // PAIR
     give_rows = lax.dynamic_slice_in_dim(all_background, (1 - pair_index) * rows_out, rows_out, axis=2)
     keep_rows = lax.dynamic_slice_in_dim(all_background, pair_index * rows_out, rows_out, axis=2)
-    sent = swap_pair(lag_block(give_rows, all_analysis, cycle_total, max_lag, lag_total))
-    summed = lag_block(keep_rows, all_analysis, cycle_total, max_lag, lag_total) + sent
+    outer = (0, lag_total - 1)
+    inner = tuple(range(1, lag_total - 1))
+    sent_outer = swap_pair(lag_block(give_rows, all_analysis, cycle_total, max_lag, outer))
+    sent_inner = swap_pair(lag_block(give_rows, all_analysis, cycle_total, max_lag, inner))
+    own = lag_block(keep_rows, all_analysis, cycle_total, max_lag, range(lag_total))
+    sent = jnp.concatenate([sent_outer[:, :1], sent_inner, sent_outer[:, 1:]], axis=1)
+    summed = own + sent
 
     denominators = []
     for offset in range(max_lag + 1):

time: 272 us -> 268 us (0.985)
  waiting for transfers between devices: 100 us -> 95.7 us
    ppermute x2 -> x3, waiting for transfers between devices: 44.6 us -> 40.4 us  [swap_pair(): return lax.ppermute(x, 'th', [(0, 1), (1, 0)])]
  transfers between devices with their start and end apart: 6 -> 7, of which waited for: 6 -> 6; matrix products, arithmetic and copies ran while one was open for 14% -> 15% of each run, Pallas kernels for 0% -> 0%
where the time goes in v13:
time: 268 us
  waiting for transfers between devices  95.7 us (36%)
  blocking collectives  87.6 us (33%)
  matrix products  22.5 us (8%)
  other arithmetic  21.4 us (8%)
  between operations  15.6 us (6%)
  local copies, waits for them, and re-layouts  14.8 us (6%)
  starting transfers between devices  10.1 us (4%)
    all_to_all x1, blocking collectives, body(): rows_here = lax.all_to_all(by_loc, ('tq', 'th'), 0, 0, tiled=True)  87.6 us
    ppermute x2, waiting for transfers between devices, gather_chan(): got = lax.ppermute(held, 'chan', [(c, c ^ 1 << bit) for c in range(size)])  40.6 us
    ppermute x3, waiting for transfers between devices, swap_pair(): return lax.ppermute(x, 'th', [(0, 1), (1, 0)])  40.4 us
    dot_general x10, matrix products, contract(): lax.dot_general(left, right, (((0, 1, 3), (0, 1, 3)), ((), ())), preferre...  22.5 us
    all_to_all x1, waiting for transfers between devices, body(): by_loc = lax.all_to_all(split_b, 'chan', 2, 0, tiled=True)  10.1 us
    another operation x2, other arithmetic, gather_chan(): jnp.stack([first, second], axis=1).reshape((-1,) + x.shape)  6.08 us
  transfers between devices with their start and end apart: 7, of which 6 were waited for; matrix products, arithmetic and copies ran while one was open for 15% of the time, Pallas kernels for 0%

profile of v13, /device:TPU:0, one launch (start us, length us, event | category | flops | bytes accessed | tf_op | source)
XLA Modules:
  0.0 267.7 jit_solution(9591879111939129706)
XLA Ops:
  11.2 2.9 %collective-permute-start.2 = (bf16[416,1024]{1,0:T(8,128)(2,1)}, bf16[416,1024]{1,0:T(8,128)(2,1)}, u32[]{:S(2)}, u32[]{:S(2)}) collective-permute-start(bf16[416,1024]{1,0:T(8,128)(2,1)} %get-tuple-element.12), channel_id=1, source_target_pairs={{0,4},{4,0},{1,5},{5,1},{2,6},{6,2},{3,7},{7,3},{8,12},{12,8},{9,1... | collective-permute-start | bytes 2555912 | tf_op jit(solution)/shard_map/ppermute | solution.py:10
  14.8 3.9 %squeeze.6 = bf16[416,2,4,256]{3,2,1,0:T(4,128)(2,1)S(1)} reshape(bf16[1,416,2048]{2,1,0:T(8,128)(2,1)} %param.4) | data formatting | bytes 3407872 | tf_op jit(solution)/shard_map/squeeze | solution.py:63
  19.4 2.5 copy.17
  22.0 3.6 %all-to-all-start = ((bf16[416,2,4,256]{3,1,0,2:T(2,128)(2,1)}), bf16[416,2,4,256]{3,1,0,2:T(2,128)(2,1)S(1)}, u32[]{:S(2)}, u32[]{:S(2)}) async-start(bf16[416,2,4,256]{3,1,0,2:T(2,128)(2,1)} %copy.17), calls=%async_computation | async-start | bytes 3407872 | tf_op jit(solution)/shard_map/all_to_all | solution.py:75
  26.4 7.0 %collective-permute-done.2 = bf16[416,1024]{1,0:T(8,128)(2,1)} collective-permute-done((bf16[416,1024]{1,0:T(8,128)(2,1)}, bf16[416,1024]{1,0:T(8,128)(2,1)}, u32[]{:S(2)}, u32[]{:S(2)}) %collective-permute-start.2) | collective-permute-done | bytes 852000 | tf_op jit(solution)/shard_map/ppermute | solution.py:10
  33.4 2.0 stack.80
  37.0 10.1 %all-to-all-done = bf16[416,2,4,256]{3,1,0,2:T(2,128)(2,1)S(1)} async-done(((bf16[416,2,4,256]{3,1,0,2:T(2,128)(2,1)}), bf16[416,2,4,256]{3,1,0,2:T(2,128)(2,1)S(1)}, u32[]{:S(2)}, u32[]{:S(2)}) %all-to-all-start) | async-done | bytes 1703968 | tf_op jit(solution)/shard_map/all_to_all | solution.py:75
  47.2 87.6 %all_to_all.20 = bf16[8,416,256]{2,1,0:T(8,128)(2,1)S(1)} all-to-all(bf16[8,416,256]{2,1,0:T(8,128)(2,1)S(1)} %bitcast.107), channel_id=1, replica_groups=mesh['tq'=4,'th'=2,'chan'=4] {'tq','th'}, dimensions={0} | all-to-all | bytes 3407872 | tf_op jit(solution)/shard_map/all_to_all | solution.py:78
  136.2 37.8 %collective-permute-done = bf16[1,8,416,256]{3,2,1,0:T(8,128)(2,1)} collective-permute-done((bf16[1,8,416,256]{3,2,1,0:T(8,128)(2,1)S(1)}, bf16[1,8,416,256]{3,2,1,0:T(8,128)(2,1)}, u32[]{:S(2)}, u32[]{:S(2)}) %collective-permute-start) | collective-permute-done | bytes 1703968 | tf_op jit(solution)/shard_map/ppermute | solution.py:19
  173.9 2.2 broadcast_select_fusion.2
  176.2 2.1 pad_maximum_fusion.1
  181.8 2.8 %collective-permute-done.1 = bf16[2,8,416,256]{3,2,1,0:T(8,128)(2,1)} collective-permute-done((bf16[2,8,416,256]{3,2,1,0:T(8,128)(2,1)}, bf16[2,8,416,256]{3,2,1,0:T(8,128)(2,1)}, u32[]{:S(2)}, u32[]{:S(2)}) %collective-permute-start.1) | collective-permute-done | bytes 3407904 | tf_op jit(solution)/shard_map/ppermute | solution.py:19
  184.7 3.5 %select_bitcast_fusion.1 = (bf16[2,1,8,416,256]{4,3,2,0,1:T(8,128)(2,1)S(1)}, bf16[2,1,8,416,256]{4,3,2,0,1:T(8,128)(2,1)}) fusion(bf16[2,8,416,256]{3,2,1,0:T(8,128)(2,1)} %collective-permute-done.1, pred[]{:T(512)S(6)} %eq.17, bf16[1,8,416,256]{3,2,1,0:T(8,128)(2,1)S(1)} %get-tuple-element.10, bf16[1,8,416,256]{3,2,1,0:T(8,128)(2,1)S(1)} %get-tuple-element.9), kind=kLoop, calls=%fused_computation.19 | loop fusion | flops 5111808 | bytes 13631489 | tf_op jit(solution)/shard_map/stack | solution.py:23
  188.2 2.6 pad_maximum_fusion
  190.7 3.3 %copy.19 = bf16[2,2,8,416,256]{4,3,2,1,0:T(8,128)(2,1)} copy(bf16[2,2,8,416,256]{4,3,2,0,1:T(8,128)(2,1)S(1)} %pad_maximum_fusion) | data formatting | bytes 13631488 | tf_op jit(solution)/shard_map/stack | solution.py:23
  194.0 4.7 %all-gather.2.cloned.1.call-done = bf16[4,8,416,256]{3,2,1,0:T(8,128)(2,1)} async-done(((bf16[4,2,416,256]{3,2,1,0:T(8,128)(2,1)}), bf16[4,8,416,256]{3,2,1,0:T(8,128)(2,1)}) %all-gather.2.cloned.1.call-update) | async-done | bytes 6815760 | tf_op jit(solution)/shard_map/all_gather | solution.py:72
  198.8 5.7 %fusion.40 = f32[208,1,416]{2,0,1:T(8,128)S(1)} fusion(bf16[4,8,416,256]{3,2,1,0:T(8,128)(2,1)} %all-gather.2.cloned.1.call-done, bf16[4,8,416,256]{3,2,1,0:T(8,128)(2,1)} %bitcast.96, s32[]{:T(128)S(6)} %select_n.78), kind=kOutput, calls=%fused_computation.43 | convolution fusion | flops 1240465408 | bytes 9717764 | tf_op jit(solution)/shard_map/dot_general | solution.py:28
  206.2 1.9 fusion.55
  208.2 2.2 fusion.66
  217.7 1.9 fusion.35
  219.7 2.2 fusion.63
  221.8 1.9 fusion.50
  225.5 33.4 %collective-permute-done.3 = f32[208,2,416]{2,0,1:T(8,128)S(1)} collective-permute-done((f32[208,2,416]{2,0,1:T(8,128)S(1)}, f32[208,2,416]{2,0,1:T(8,128)S(1)}, u32[]{:S(2)}, u32[]{:S(2)}) %collective-permute-start.3) | collective-permute-done | bytes 692256 | tf_op jit(solution)/shard_map/ppermute | solution.py:10
  258.9 1.9 fusion.16
  (36 shorter events, 22.4 us)
Async XLA Ops:
  11.2 22.2 %collective-permute-start.2 = (bf16[416,1024]{1,0:T(8,128)(2,1)}, bf16[416,1024]{1,0:T(8,128)(2,1)}, u32[]{:S(2)}, u32[]{:S(2)}) collective-permute-start(bf16[416,1024]{1,0:T(8,128)(2,1)} %get-tuple-element.12), channel_id=1, source_target_pairs={{0,4},{4,0},{1,5},{5,1},{2,6},{6,2},{3,7},{7,3},{8,12},{12,8},{9,1... | collective-permute-start | bytes 2555912 | tf_op jit(solution)/shard_map/ppermute | solution.py:10
  22.0 25.0 %all-to-all-start = ((bf16[416,2,4,256]{3,1,0,2:T(2,128)(2,1)}), bf16[416,2,4,256]{3,1,0,2:T(2,128)(2,1)S(1)}, u32[]{:S(2)}, u32[]{:S(2)}) async-start(bf16[416,2,4,256]{3,1,0,2:T(2,128)(2,1)} %copy.17), calls=%async_computation | async-start | bytes 3407872 | tf_op jit(solution)/shard_map/all_to_all | solution.py:75
  25.6 173.2 %all-gather.2.cloned.1.call-start = ((), (), s32[]{:S(2)}) async-start(), calls=%async_computation.2 | async-start | bytes 8519680 | tf_op jit(solution)/shard_map/all_gather | solution.py:72
  134.8 1.4 copy-start.1
  134.8 39.1 %collective-permute-start = (bf16[1,8,416,256]{3,2,1,0:T(8,128)(2,1)S(1)}, bf16[1,8,416,256]{3,2,1,0:T(8,128)(2,1)}, u32[]{:S(2)}, u32[]{:S(2)}) collective-permute-start(bf16[1,8,416,256]{3,2,1,0:T(8,128)(2,1)S(1)} %bitcast.106), channel_id=1, source_target_pairs={{0,2},{1,3},{2,0},{3,1},{4,6},{5,7},{6,4},{7,5},{8,10},{9,11},{10,... | collective-permute-start | bytes 5111816 | tf_op jit(solution)/shard_map/ppermute | solution.py:19
  176.1 2.8 %copy-start.2 = (s32[8]{0:T(128)S(1)}, s32[8]{0:T(128)}, u32[]{:S(2)}) copy-start(s32[8]{0:T(128)} %param.5) | copy-start | bytes 100
  178.3 6.4 %collective-permute-start.1 = (bf16[2,8,416,256]{3,2,1,0:T(8,128)(2,1)}, bf16[2,8,416,256]{3,2,1,0:T(8,128)(2,1)}, u32[]{:S(2)}, u32[]{:S(2)}) collective-permute-start(bf16[2,8,416,256]{3,2,1,0:T(8,128)(2,1)} %pad_maximum_fusion.1), channel_id=1, source_target_pairs={{0,1},{1,0},{2,3},{3,2},{4,5},{5,4},{6,7},{7,6},{8,9},{9,8},{10,11... | collective-permute-start | bytes 10223624 | tf_op jit(solution)/shard_map/ppermute | solution.py:19
  198.8 5.7 %copy-start = (bf16[2,2,8,416,256]{4,3,2,1,0:T(8,128)(2,1)S(1)}, bf16[2,2,8,416,256]{4,3,2,1,0:T(8,128)(2,1)}, u32[]{:S(2)}) copy-start(bf16[2,2,8,416,256]{4,3,2,1,0:T(8,128)(2,1)} %copy.19) | copy-start | bytes 20447236
  198.8 7.5 %copy-start.3 = (bf16[4,8,416,256]{3,2,1,0:T(8,128)(2,1)S(1)}, bf16[4,8,416,256]{3,2,1,0:T(8,128)(2,1)}, u32[]{:S(2)}) copy-start(bf16[4,8,416,256]{3,2,1,0:T(8,128)(2,1)} %all-gather.2.cloned.1.call-done) | copy-start | bytes 20447236
  210.4 48.4 %collective-permute-start.4 = (f32[208,3,416]{2,0,1:T(8,128)S(1)}, f32[208,3,416]{2,0,1:T(8,128)S(1)}, u32[]{:S(2)}, u32[]{:S(2)}) collective-permute-start(f32[208,3,416]{2,0,1:T(8,128)S(1)} %pad_maximum_fusion.2), channel_id=1, source_target_pairs={{0,4},{4,0},{1,5},{5,1},{2,6},{6,2},{3,7},{7,3},{8,12},{12,8},{9,1... | collective-permute-start | bytes 3115016 | tf_op jit(solution)/shard_map/ppermute | solution.py:10
  215.4 43.4 %collective-permute-start.3 = (f32[208,2,416]{2,0,1:T(8,128)S(1)}, f32[208,2,416]{2,0,1:T(8,128)S(1)}, u32[]{:S(2)}, u32[]{:S(2)}) collective-permute-start(f32[208,2,416]{2,0,1:T(8,128)S(1)} %pad_maximum_fusion.3), channel_id=1, source_target_pairs={{0,4},{4,0},{1,5},{5,1},{2,6},{6,2},{3,7},{7,3},{8,12},{12,8},{9,1... | collective-permute-start | bytes 2076680 | tf_op jit(solution)/shard_map/ppermute | solution.py:10
Sparse Core Ops, SparseCore 0:
  37.1 161.6 all-gather.1

commit v14 on v13

--- a/solution.py
+++ b/solution.py
@@ -18,10 +18,15 @@
     for bit in reversed(range(bits)):
         got = lax.ppermute(held, "chan", [(c, c ^ (1 << bit)) for c in range(size)])
         low = ((me >> bit) & 1) == 0
-        first = jnp.where(low, held, got)
-        second = jnp.where(low, got, held)
-        held = jnp.concatenate([first, second], axis=0) if bit == bits - 1 else jnp.stack([first, second], axis=1).reshape((-1,) + x.shape)
+        held = jnp.concatenate([jnp.where(low, held, got), jnp.where(low, got, held)], axis=0)
     return held
+
+
+def bit_reversed(x, axis, size):
+    bits = size.bit_length() - 1
+    shape = x.shape[:axis] + (2,) * bits + x.shape[axis + 1:]
+    order = list(range(axis)) + [axis + bits - 1 - k for k in range(bits)] + list(range(axis + bits, len(shape)))
+    return x.reshape(shape).transpose(order).reshape(x.shape)
 
 
 def contract(left, right):
@@ -69,6 +74,7 @@
     got = swap_pair(give)
     pair_analysis = jnp.where(pair_index == 0, jnp.stack([keep, got]), jnp.stack([got, keep]))
     pair_analysis = pair_analysis.reshape(PAIR, width_block, chan_size, piece).transpose(2, 0, 1, 3)
+    pair_analysis = bit_reversed(pair_analysis, 0, chan_size)
     all_analysis = lax.all_gather(pair_analysis, "tq", axis=1, tiled=True)
 
     split_b = local_background.reshape(width_block, PAIR, chan_size, piece)

time: 268 us -> 268 us (level)
  local copies, waits for them, and re-layouts: 14.8 us -> 9.42 us
  waiting for transfers between devices: 95.7 us -> 100 us
    another operation x2 -> x0, other arithmetic: 6.08 us -> none  [gather_chan(): jnp.stack([first, second], axis=1).reshape((-1,) + x.shape)]
    all_gather x1, waiting for transfers between devices: 4.72 us -> 10.7 us  [body(): all_analysis = lax.all_gather(pair_analysis, 'tq', axis=1, tiled=True)]
    another operation x1 -> x0, local copies, waits for them, and re-layouts: 3.29 us -> none  [gather_chan(): jnp.stack([first, second], axis=1).reshape((-1,) + x.shape)]
    all_to_all x1, waiting for transfers between devices: 10.1 us -> 7.36 us  [body(): by_loc = lax.all_to_all(split_b, 'chan', 2, 0, tiled=True)]
  transfers between devices with their start and end apart: 7 -> 7, of which waited for: 6 -> 6; matrix products, arithmetic and copies ran while one was open for 15% -> 13% of each run, Pallas kernels for 0% -> 0%
where the time goes in v14:
time: 268 us
  waiting for transfers between devices  100 us (37%)
  blocking collectives  89.9 us (34%)
  matrix products  22.9 us (9%)
  other arithmetic  20.3 us (8%)
  between operations  15.5 us (6%)
  local copies, waits for them, and re-layouts  9.42 us (4%)
  starting transfers between devices  9.38 us (4%)
    all_to_all x1, blocking collectives, body(): rows_here = lax.all_to_all(by_loc, ('tq', 'th'), 0, 0, tiled=True)  89.9 us
    ppermute x3, waiting for transfers between devices, swap_pair(): return lax.ppermute(x, 'th', [(0, 1), (1, 0)])  41.9 us
    ppermute x2, waiting for transfers between devices, gather_chan(): got = lax.ppermute(held, 'chan', [(c, c ^ 1 << bit) for c in range(size)])  40.5 us
    dot_general x10, matrix products, contract(): lax.dot_general(left, right, (((0, 1, 3), (0, 1, 3)), ((), ())), preferre...  22.9 us
    all_gather x1, waiting for transfers between devices, body(): all_analysis = lax.all_gather(pair_analysis, 'tq', axis=1, tiled=True)  10.7 us
    all_to_all x1, waiting for transfers between devices, body(): by_loc = lax.all_to_all(split_b, 'chan', 2, 0, tiled=True)  7.36 us
  transfers between devices with their start and end apart: 7, of which 6 were waited for; matrix products, arithmetic and copies ran while one was open for 13% of the time, Pallas kernels for 0%

profile of v14, /device:TPU:0, one launch (start us, length us, event | category | flops | bytes accessed | tf_op | source)
XLA Modules:
  0.0 267.9 jit_solution(13486219042650855444)
XLA Ops:
  11.1 2.9 %collective-permute-start.2 = (bf16[416,1024]{1,0:T(8,128)(2,1)}, bf16[416,1024]{1,0:T(8,128)(2,1)}, u32[]{:S(2)}, u32[]{:S(2)}) collective-permute-start(bf16[416,1024]{1,0:T(8,128)(2,1)} %get-tuple-element.14), channel_id=1, source_target_pairs={{0,4},{4,0},{1,5},{5,1},{2,6},{6,2},{3,7},{7,3},{8,12},{12,8},{9,1... | collective-permute-start | bytes 2555912 | tf_op jit(solution)/shard_map/ppermute | solution.py:10
  14.0 3.9 %squeeze.6 = bf16[416,2,4,256]{3,2,1,0:T(4,128)(2,1)S(1)} reshape(bf16[1,416,2048]{2,1,0:T(8,128)(2,1)} %param.4) | data formatting | bytes 3407872 | tf_op jit(solution)/shard_map/squeeze | solution.py:68
  18.6 1.8 copy_select_fusion
  20.5 3.6 %all-to-all-start = ((bf16[416,2,4,256]{3,0,1,2:T(8,128)(2,1)}), bf16[416,2,4,256]{3,0,1,2:T(8,128)(2,1)S(1)}, u32[]{:S(2)}, u32[]{:S(2)}) async-start(bf16[416,2,4,256]{3,0,1,2:T(8,128)(2,1)} %copy_select_fusion), calls=%async_computation | async-start | bytes 3407872 | tf_op jit(solution)/shard_map/all_to_all | solution.py:81
  24.7 8.5 %collective-permute-done.2 = bf16[416,1024]{1,0:T(8,128)(2,1)} collective-permute-done((bf16[416,1024]{1,0:T(8,128)(2,1)}, bf16[416,1024]{1,0:T(8,128)(2,1)}, u32[]{:S(2)}, u32[]{:S(2)}) %collective-permute-start.2) | collective-permute-done | bytes 852000 | tf_op jit(solution)/shard_map/ppermute | solution.py:10
  33.3 2.0 stack.68
  38.2 7.4 %all-to-all-done = bf16[416,2,4,256]{3,0,1,2:T(8,128)(2,1)S(1)} async-done(((bf16[416,2,4,256]{3,0,1,2:T(8,128)(2,1)}), bf16[416,2,4,256]{3,0,1,2:T(8,128)(2,1)S(1)}, u32[]{:S(2)}, u32[]{:S(2)}) %all-to-all-start) | async-done | bytes 1703968 | tf_op jit(solution)/shard_map/all_to_all | solution.py:81
  45.5 89.9 %all_to_all.20 = bf16[8,416,256]{2,1,0:T(8,128)(2,1)S(1)} all-to-all(bf16[8,416,256]{2,1,0:T(8,128)(2,1)S(1)} %bitcast.106), channel_id=1, replica_groups=mesh['tq'=4,'th'=2,'chan'=4] {'tq','th'}, dimensions={0} | all-to-all | bytes 3407872 | tf_op jit(solution)/shard_map/all_to_all | solution.py:84
  136.6 37.5 %collective-permute-done = bf16[1,8,416,256]{3,2,1,0:T(8,128)(2,1)} collective-permute-done((bf16[1,8,416,256]{3,2,1,0:T(8,128)(2,1)S(1)}, bf16[1,8,416,256]{3,2,1,0:T(8,128)(2,1)}, u32[]{:S(2)}, u32[]{:S(2)}) %collective-permute-start) | collective-permute-done | bytes 1703968 | tf_op jit(solution)/shard_map/ppermute | solution.py:19
  174.2 2.2 broadcast_select_fusion.3
  176.4 2.1 pad_maximum_fusion
  181.9 2.9 %collective-permute-done.1 = bf16[2,8,416,256]{3,2,1,0:T(8,128)(2,1)} collective-permute-done((bf16[2,8,416,256]{3,2,1,0:T(8,128)(2,1)}, bf16[2,8,416,256]{3,2,1,0:T(8,128)(2,1)}, u32[]{:S(2)}, u32[]{:S(2)}) %collective-permute-start.1) | collective-permute-done | bytes 3407904 | tf_op jit(solution)/shard_map/ppermute | solution.py:19
  184.9 2.2 broadcast_select_fusion
  187.1 2.0 fusion.16
  189.1 10.7 %all-gather.2.cloned.1.call-done = bf16[4,8,416,256]{3,2,1,0:T(8,128)(2,1)} async-done(((bf16[4,2,416,256]{3,2,1,0:T(8,128)(2,1)}), bf16[4,8,416,256]{3,2,1,0:T(8,128)(2,1)}) %all-gather.2.cloned.1.call-update) | async-done | bytes 6815760 | tf_op jit(solution)/shard_map/all_gather | solution.py:78
  199.8 6.3 %convolution_bitcast_fusion = f32[208,1,416]{2,0,1:T(8,128)S(1)} fusion(bf16[4,8,208,256]{3,2,1,0:T(8,128)(2,1)} %get-tuple-element.7, bf16[4,8,416,256]{3,2,1,0:T(8,128)(2,1)} %all-gather.2.cloned.1.call-done), kind=kOutput, calls=%fused_computation.40 | convolution fusion | flops 1417674752 | bytes 10569728 | tf_op jit(solution)/shard_map/dot_general | solution.py:33
  206.7 1.9 fusion.26
  208.6 1.9 fusion.35
  218.0 1.9 fusion.23
  219.9 2.2 fusion.38
  222.1 1.9 fusion.32
  224.0 1.7 fusion.51
  225.7 33.3 %collective-permute-done.3 = f32[208,2,416]{2,0,1:T(8,128)S(1)} collective-permute-done((f32[208,2,416]{2,0,1:T(8,128)S(1)}, f32[208,2,416]{2,0,1:T(8,128)S(1)}, u32[]{:S(2)}, u32[]{:S(2)}) %collective-permute-start.3) | collective-permute-done | bytes 692256 | tf_op jit(solution)/shard_map/ppermute | solution.py:10
  259.1 1.9 fusion.18
  (33 shorter events, 19.4 us)
Async XLA Ops:
  11.1 22.2 %collective-permute-start.2 = (bf16[416,1024]{1,0:T(8,128)(2,1)}, bf16[416,1024]{1,0:T(8,128)(2,1)}, u32[]{:S(2)}, u32[]{:S(2)}) collective-permute-start(bf16[416,1024]{1,0:T(8,128)(2,1)} %get-tuple-element.14), channel_id=1, source_target_pairs={{0,4},{4,0},{1,5},{5,1},{2,6},{6,2},{3,7},{7,3},{8,12},{12,8},{9,1... | collective-permute-start | bytes 2555912 | tf_op jit(solution)/shard_map/ppermute | solution.py:10
  20.5 25.0 %all-to-all-start = ((bf16[416,2,4,256]{3,0,1,2:T(8,128)(2,1)}), bf16[416,2,4,256]{3,0,1,2:T(8,128)(2,1)S(1)}, u32[]{:S(2)}, u32[]{:S(2)}) async-start(bf16[416,2,4,256]{3,0,1,2:T(8,128)(2,1)} %copy_select_fusion), calls=%async_computation | async-start | bytes 3407872 | tf_op jit(solution)/shard_map/all_to_all | solution.py:81
  24.1 175.7 %all-gather.2.cloned.1.call-start = ((), (), s32[]{:S(2)}) async-start(), calls=%async_computation.2 | async-start | bytes 8519680 | tf_op jit(solution)/shard_map/all_gather | solution.py:78
  135.5 1.2 copy-start
  135.5 38.7 %collective-permute-start = (bf16[1,8,416,256]{3,2,1,0:T(8,128)(2,1)S(1)}, bf16[1,8,416,256]{3,2,1,0:T(8,128)(2,1)}, u32[]{:S(2)}, u32[]{:S(2)}) collective-permute-start(bf16[1,8,416,256]{3,2,1,0:T(8,128)(2,1)S(1)} %bitcast.107), channel_id=1, source_target_pairs={{0,2},{1,3},{2,0},{3,1},{4,6},{5,7},{6,4},{7,5},{8,10},{9,11},{10,... | collective-permute-start | bytes 5111816 | tf_op jit(solution)/shard_map/ppermute | solution.py:19
  176.4 2.7 %copy-start.2 = (s32[8]{0:T(128)S(1)}, s32[8]{0:T(128)}, u32[]{:S(2)}) copy-start(s32[8]{0:T(128)} %param.5) | copy-start | bytes 100
  178.5 6.4 %collective-permute-start.1 = (bf16[2,8,416,256]{3,2,1,0:T(8,128)(2,1)}, bf16[2,8,416,256]{3,2,1,0:T(8,128)(2,1)}, u32[]{:S(2)}, u32[]{:S(2)}) collective-permute-start(bf16[2,8,416,256]{3,2,1,0:T(8,128)(2,1)} %pad_maximum_fusion), channel_id=1, source_target_pairs={{0,1},{1,0},{2,3},{3,2},{4,5},{5,4},{6,7},{7,6},{8,9},{9,8},{10,11... | collective-permute-start | bytes 10223624 | tf_op jit(solution)/shard_map/ppermute | solution.py:19
  199.8 6.3 %copy-start.1 = (bf16[4,8,208,256]{3,2,1,0:T(8,128)(2,1)S(1)}, bf16[4,8,208,256]{3,2,1,0:T(8,128)(2,1)}, u32[]{:S(2)}) copy-start(bf16[4,8,208,256]{3,2,1,0:T(8,128)(2,1)} %get-tuple-element.7) | copy-start | bytes 10223620
  199.8 6.9 %copy-start.3 = (bf16[4,8,416,256]{3,2,1,0:T(8,128)(2,1)S(1)}, bf16[4,8,416,256]{3,2,1,0:T(8,128)(2,1)}, u32[]{:S(2)}) copy-start(bf16[4,8,416,256]{3,2,1,0:T(8,128)(2,1)} %all-gather.2.cloned.1.call-done) | copy-start | bytes 20447236
  210.7 48.4 %collective-permute-start.4 = (f32[208,3,416]{2,0,1:T(8,128)S(1)}, f32[208,3,416]{2,0,1:T(8,128)S(1)}, u32[]{:S(2)}, u32[]{:S(2)}) collective-permute-start(f32[208,3,416]{2,0,1:T(8,128)S(1)} %pad_maximum_fusion.1), channel_id=1, source_target_pairs={{0,4},{4,0},{1,5},{5,1},{2,6},{6,2},{3,7},{7,3},{8,12},{12,8},{9,1... | collective-permute-start | bytes 3115016 | tf_op jit(solution)/shard_map/ppermute | solution.py:10
  215.7 43.3 %collective-permute-start.3 = (f32[208,2,416]{2,0,1:T(8,128)S(1)}, f32[208,2,416]{2,0,1:T(8,128)S(1)}, u32[]{:S(2)}, u32[]{:S(2)}) collective-permute-start(f32[208,2,416]{2,0,1:T(8,128)S(1)} %pad_maximum_fusion.2), channel_id=1, source_target_pairs={{0,4},{4,0},{1,5},{5,1},{2,6},{6,2},{3,7},{7,3},{8,12},{12,8},{9,1... | collective-permute-start | bytes 2076680 | tf_op jit(solution)/shard_map/ppermute | solution.py:10
Sparse Core Ops, SparseCore 0:
  38.3 161.4 all-gather.1

commit v15 on v14

--- a/solution.py
+++ b/solution.py
@@ -71,11 +71,17 @@
     high_half = local_analysis[:, half:]
     keep = jnp.where(pair_index == 0, low_half, high_half)
     give = jnp.where(pair_index == 0, high_half, low_half)
+    def by_piece(x):
+        pieces_first = x.reshape(width_block, chan_size, piece).transpose(1, 0, 2)
+        return bit_reversed(pieces_first, 0, chan_size)[:, None]
+
+    same_parity = lax.all_gather(by_piece(keep), "tq", axis=1, tiled=True)
     got = swap_pair(give)
-    pair_analysis = jnp.where(pair_index == 0, jnp.stack([keep, got]), jnp.stack([got, keep]))
-    pair_analysis = pair_analysis.reshape(PAIR, width_block, chan_size, piece).transpose(2, 0, 1, 3)
-    pair_analysis = bit_reversed(pair_analysis, 0, chan_size)
-    all_analysis = lax.all_gather(pair_analysis, "tq", axis=1, tiled=True)
+    other_parity = lax.all_gather(by_piece(got), "tq", axis=1, tiled=True)
+    in_order = jnp.stack([same_parity, other_parity], axis=2)
+    swapped = jnp.stack([other_parity, same_parity], axis=2)
+    all_analysis = jnp.where(pair_index == 0, in_order, swapped)
+    all_analysis = all_analysis.reshape(chan_size, cycle_total, width_block, piece)
 
     split_b = local_background.reshape(width_block, PAIR, chan_size, piece)
     by_loc = lax.all_to_all(split_b, "chan", 2, 0, tiled=True)

time: 268 us -> 263 us (0.981)
  blocking collectives: 89.9 us -> 25.8 us
  waiting for transfers between devices: 100 us -> 162 us
  matrix products: 22.9 us -> 18.7 us
  local copies, waits for them, and re-layouts: 9.42 us -> 5.6 us
  other arithmetic: 20.3 us -> 23.4 us
    all_to_all x1, blocking collectives: 89.9 us -> 25.8 us  [body(): by_loc = lax.all_to_all(split_b, 'chan', 2, 0, tiled=True)]
    all_to_all x1, waiting for transfers between devices: 7.36 us -> 37.7 us  [body(): rows_here = lax.all_to_all(by_loc, ('tq', 'th'), 0, 0, tiled=True)]
    ppermute x3, waiting for transfers between devices: 41.9 us -> 66.5 us  [swap_pair(): return lax.ppermute(x, 'th', [(0, 1), (1, 0)])]
    all_gather x1 -> x2, waiting for transfers between devices: 10.7 us -> 19.7 us  [the longest x1 19.7 us: body(): other_parity = lax.all_gather(by_piece(got), 'tq', axis=1, tiled=True)]
    select_n x0 -> x1, other arithmetic: none -> 6.83 us  [body(): all_analysis = jnp.where(pair_index == 0, in_order, swapped)]
    dot_general x10, matrix products: 22.9 us -> 18.7 us  [contract(): lax.dot_general(left, right, (((0, 1, 3), (0, 1, 3)), ((), ())), preferre...]
    reshape x0 -> x6, local copies, waits for them, and re-layouts: none -> 4.11 us  [the longest x4 2.87 us: bit_reversed(): return x.reshape(shape).transpose(order).reshape(x.shape)]
    ppermute x2, waiting for transfers between devices: 40.5 us -> 37.6 us  [gather_chan(): got = lax.ppermute(held, 'chan', [(c, c ^ 1 << bit) for c in range(size)])]
  transfers between devices with their start and end apart: 7 -> 8, of which waited for: 6 -> 5; matrix products, arithmetic and copies ran while one was open for 13% -> 10% of each run, Pallas kernels for 0% -> 0%
where the time goes in v15:
time: 263 us
  waiting for transfers between devices  162 us (62%)
  blocking collectives  25.8 us (10%)
  other arithmetic  23.4 us (9%)
  matrix products  18.7 us (7%)
  between operations  15.6 us (6%)
  starting transfers between devices  12 us (5%)
  local copies, waits for them, and re-layouts  5.6 us (2%)
    ppermute x3, waiting for transfers between devices, swap_pair(): return lax.ppermute(x, 'th', [(0, 1), (1, 0)])  66.5 us
    all_to_all x1, waiting for transfers between devices, body(): rows_here = lax.all_to_all(by_loc, ('tq', 'th'), 0, 0, tiled=True)  37.7 us
    ppermute x2, waiting for transfers between devices, gather_chan(): got = lax.ppermute(held, 'chan', [(c, c ^ 1 << bit) for c in range(size)])  37.6 us
    all_to_all x1, blocking collectives, body(): by_loc = lax.all_to_all(split_b, 'chan', 2, 0, tiled=True)  25.8 us
    all_gather x1, waiting for transfers between devices, body(): other_parity = lax.all_gather(by_piece(got), 'tq', axis=1, tiled=True)  19.7 us
    dot_general x10, matrix products, contract(): lax.dot_general(left, right, (((0, 1, 3), (0, 1, 3)), ((), ())), preferre...  18.7 us
    select_n x1, other arithmetic, body(): all_analysis = jnp.where(pair_index == 0, in_order, swapped)  6.83 us
    all_to_all x1, starting transfers between devices, body(): rows_here = lax.all_to_all(by_loc, ('tq', 'th'), 0, 0, tiled=True)  6.32 us
  transfers between devices with their start and end apart: 8, of which 5 were waited for; matrix products, arithmetic and copies ran while one was open for 10% of the time, Pallas kernels for 0%

profile of v15, /device:TPU:0, one launch (start us, length us, event | category | flops | bytes accessed | tf_op | source)
XLA Modules:
  0.0 262.6 jit_solution(7242584351720105484)
XLA Ops:
  8.5 1.6 bitcast_select_fusion
  15.9 25.8 %all_to_all.20 = bf16[416,2,4,256]{3,0,1,2:T(8,128)(2,1)} all-to-all(bf16[416,2,4,256]{3,0,1,2:T(8,128)(2,1)S(1)} %copy_select_fusion), channel_id=1, replica_groups=mesh['tq'=4,'th'=2,'chan'=4] {'chan'}, dimensions={2} | all-to-all | bytes 3407872 | tf_op jit(solution)/shard_map/all_to_all | solution.py:87
  41.7 6.3 %all-to-all-start.1 = ((bf16[8,416,256]{2,1,0:T(8,128)(2,1)}), bf16[8,416,256]{2,1,0:T(8,128)(2,1)S(1)}, u32[]{:S(2)}, u32[]{:S(2)}) async-start(bf16[8,416,256]{2,1,0:T(8,128)(2,1)} %bitcast.4), calls=%async_computation.1 | async-start | bytes 3407872 | tf_op jit(solution)/shard_map/all_to_all | solution.py:90
  48.0 2.0 collective-permute-start.2
  50.1 29.9 %collective-permute-done.2 = bf16[416,1024]{1,0:T(8,128)(2,1)S(1)} collective-permute-done((bf16[416,1024]{1,0:T(8,128)(2,1)S(1)}, bf16[416,1024]{1,0:T(8,128)(2,1)S(1)}, u32[]{:S(2)}, u32[]{:S(2)}) %collective-permute-start.2) | collective-permute-done | bytes 852000 | tf_op jit(solution)/shard_map/ppermute | solution.py:10
  82.1 37.7 %all-to-all-done.1 = bf16[8,416,256]{2,1,0:T(8,128)(2,1)S(1)} async-done(((bf16[8,416,256]{2,1,0:T(8,128)(2,1)}), bf16[8,416,256]{2,1,0:T(8,128)(2,1)S(1)}, u32[]{:S(2)}, u32[]{:S(2)}) %all-to-all-start.1) | async-done | bytes 1703968 | tf_op jit(solution)/shard_map/all_to_all | solution.py:90
  121.2 37.6 %collective-permute-done = bf16[1,8,416,256]{3,2,1,0:T(8,128)(2,1)} collective-permute-done((bf16[1,8,416,256]{3,2,1,0:T(8,128)(2,1)S(1)}, bf16[1,8,416,256]{3,2,1,0:T(8,128)(2,1)}, u32[]{:S(2)}, u32[]{:S(2)}) %collective-permute-start) | collective-permute-done | bytes 1703968 | tf_op jit(solution)/shard_map/ppermute | solution.py:19
  158.9 2.2 broadcast_select_fusion.3
  161.1 2.1 pad_maximum_fusion
  166.6 19.7 %all-gather.5.cloned.1.call-done = bf16[4,4,416,256]{3,2,1,0:T(8,128)(2,1)} async-done(((bf16[4,1,416,256]{3,2,1,0:T(8,128)(2,1)}), bf16[4,4,416,256]{3,2,1,0:T(8,128)(2,1)}) %all-gather.5.cloned.1.call-update) | async-done | bytes 3407888 | tf_op jit(solution)/shard_map/all_gather | solution.py:80
  186.4 6.8 %maximum_select_fusion = bf16[4,4,2,416,256]{4,3,2,1,0:T(8,128)(2,1)S(1)} fusion(bf16[4,4,1,416,256]{4,3,2,1,0:T(8,128)(2,1)} %bitcast.130, bf16[4,4,1,416,256]{4,3,2,1,0:T(8,128)(2,1)} %bitcast.129, pred[]{:T(512)S(6)} %eq.21), kind=kLoop, calls=%fused_computation.4 | loop fusion | flops 10223616 | bytes 13631489 | tf_op jit(solution)/shard_map/jit(_where)/select_n | solution.py:83
  193.2 2.2 broadcast_select_fusion
  196.1 2.2 convolution_bitcast_fusion
  198.3 1.9 fusion.25
  200.2 1.9 fusion.34
  202.2 1.7 fusion.44
  203.8 1.7 fusion.53
  207.9 1.7 fusion.41
  209.6 1.9 fusion.22
  211.5 2.2 fusion.37
  213.7 1.9 fusion.31
  215.6 1.7 fusion.50
  217.3 36.5 %collective-permute-done.3 = f32[208,2,416]{2,0,1:T(8,128)S(1)} collective-permute-done((f32[208,2,416]{2,0,1:T(8,128)S(1)}, f32[208,2,416]{2,0,1:T(8,128)S(1)}, u32[]{:S(2)}, u32[]{:S(2)}) %collective-permute-start.3) | collective-permute-done | bytes 692256 | tf_op jit(solution)/shard_map/ppermute | solution.py:10
  253.9 1.9 fusion.18
  (38 shorter events, 15.9 us)
Async XLA Ops:
  6.5 160.1 %all-gather.3.cloned.1.call-start = ((), (), s32[]{:S(2)}) async-start(), calls=%async_computation.2 | async-start | bytes 4259840 | tf_op jit(solution)/shard_map/all_gather | solution.py:78
  11.1 2.1 copy-start.1
  15.9 32.1 %copy-start.2 = (bf16[416,1024]{1,0:T(8,128)(2,1)S(1)}, bf16[416,1024]{1,0:T(8,128)(2,1)}, u32[]{:S(2)}) copy-start(bf16[416,1024]{1,0:T(8,128)(2,1)} %get-tuple-element.14) | copy-start | bytes 2555908
  41.7 78.1 %all-to-all-start.1 = ((bf16[8,416,256]{2,1,0:T(8,128)(2,1)}), bf16[8,416,256]{2,1,0:T(8,128)(2,1)S(1)}, u32[]{:S(2)}, u32[]{:S(2)}) async-start(bf16[8,416,256]{2,1,0:T(8,128)(2,1)} %bitcast.4), calls=%async_computation.1 | async-start | bytes 3407872 | tf_op jit(solution)/shard_map/all_to_all | solution.py:90
  48.0 138.4 %all-gather.5.cloned.1.call-start = ((), (), s32[]{:S(2)}) async-start(), calls=%async_computation.3 | async-start | bytes 4259840 | tf_op jit(solution)/shard_map/all_gather | solution.py:80
  48.0 32.0 %collective-permute-start.2 = (bf16[416,1024]{1,0:T(8,128)(2,1)S(1)}, bf16[416,1024]{1,0:T(8,128)(2,1)S(1)}, u32[]{:S(2)}, u32[]{:S(2)}) collective-permute-start(bf16[416,1024]{1,0:T(8,128)(2,1)S(1)} %copy-done.2), channel_id=1, source_target_pairs={{0,4},{4,0},{1,5},{5,1},{2,6},{6,2},{3,7},{7,3},{8,12},{12,8},{9,1... | collective-permute-start | bytes 2555912 | tf_op jit(solution)/shard_map/ppermute | solution.py:10
  119.8 1.4 copy-start
  119.8 39.1 %collective-permute-start = (bf16[1,8,416,256]{3,2,1,0:T(8,128)(2,1)S(1)}, bf16[1,8,416,256]{3,2,1,0:T(8,128)(2,1)}, u32[]{:S(2)}, u32[]{:S(2)}) collective-permute-start(bf16[1,8,416,256]{3,2,1,0:T(8,128)(2,1)S(1)} %bitcast.124), channel_id=1, source_target_pairs={{0,2},{1,3},{2,0},{3,1},{4,6},{5,7},{6,4},{7,5},{8,10},{9,11},{10,... | collective-permute-start | bytes 5111816 | tf_op jit(solution)/shard_map/ppermute | solution.py:19
  161.1 2.7 %copy-start.3 = (s32[8]{0:T(128)S(1)}, s32[8]{0:T(128)}, u32[]{:S(2)}) copy-start(s32[8]{0:T(128)} %param.5) | copy-start | bytes 100
  163.2 30.0 %collective-permute-start.1 = (bf16[2,8,416,256]{3,2,1,0:T(8,128)(2,1)}, bf16[2,8,416,256]{3,2,1,0:T(8,128)(2,1)}, u32[]{:S(2)}, u32[]{:S(2)}) collective-permute-start(bf16[2,8,416,256]{3,2,1,0:T(8,128)(2,1)} %pad_maximum_fusion), channel_id=1, source_target_pairs={{0,1},{1,0},{2,3},{3,2},{4,5},{5,4},{6,7},{7,6},{8,9},{9,8},{10,11... | collective-permute-start | bytes 10223624 | tf_op jit(solution)/shard_map/ppermute | solution.py:19
  205.7 48.2 %collective-permute-start.4 = (f32[208,3,416]{2,0,1:T(8,128)S(1)}, f32[208,3,416]{2,0,1:T(8,128)S(1)}, u32[]{:S(2)}, u32[]{:S(2)}) collective-permute-start(f32[208,3,416]{2,0,1:T(8,128)S(1)} %pad_maximum_fusion.1), channel_id=1, source_target_pairs={{0,4},{4,0},{1,5},{5,1},{2,6},{6,2},{3,7},{7,3},{8,12},{12,8},{9,1... | collective-permute-start | bytes 3115016 | tf_op jit(solution)/shard_map/ppermute | solution.py:10
  207.3 46.5 %collective-permute-start.3 = (f32[208,2,416]{2,0,1:T(8,128)S(1)}, f32[208,2,416]{2,0,1:T(8,128)S(1)}, u32[]{:S(2)}, u32[]{:S(2)}) collective-permute-start(f32[208,2,416]{2,0,1:T(8,128)S(1)} %pad_maximum_fusion.2), channel_id=1, source_target_pairs={{0,4},{4,0},{1,5},{5,1},{2,6},{6,2},{3,7},{7,3},{8,12},{12,8},{9,1... | collective-permute-start | bytes 2076680 | tf_op jit(solution)/shard_map/ppermute | solution.py:10
Sparse Core Ops, SparseCore 0:
  13.4 104.5 all-gather.2
  119.6 66.7 all-gather.4

commit v16 on v15

--- a/solution.py
+++ b/solution.py
@@ -78,10 +78,10 @@
     same_parity = lax.all_gather(by_piece(keep), "tq", axis=1, tiled=True)
     got = swap_pair(give)
     other_parity = lax.all_gather(by_piece(got), "tq", axis=1, tiled=True)
-    in_order = jnp.stack([same_parity, other_parity], axis=2)
-    swapped = jnp.stack([other_parity, same_parity], axis=2)
-    all_analysis = jnp.where(pair_index == 0, in_order, swapped)
-    all_analysis = all_analysis.reshape(chan_size, cycle_total, width_block, piece)
+    slots = jnp.zeros(same_parity.shape[:2] + (PAIR,) + same_parity.shape[2:], jnp.bfloat16)
+    slots = lax.dynamic_update_slice_in_dim(slots, same_parity[:, :, None], pair_index, axis=2)
+    slots = lax.dynamic_update_slice_in_dim(slots, other_parity[:, :, None], 1 - pair_index, axis=2)
+    all_analysis = slots.reshape(chan_size, cycle_total, width_block, piece)
 
     split_b = local_background.reshape(width_block, PAIR, chan_size, piece)
     by_loc = lax.all_to_all(split_b, "chan", 2, 0, tiled=True)

time: 263 us -> 276 us (1.049)
  matrix products: 18.7 us -> 45.3 us
  waiting for transfers between devices: 162 us -> 145 us
  local copies, waits for them, and re-layouts: 5.6 us -> 15.1 us
  other arithmetic: 23.4 us -> 16.5 us
    ppermute x3, waiting for transfers between devices: 66.5 us -> 23.2 us  [swap_pair(): return lax.ppermute(x, 'th', [(0, 1), (1, 0)])]
    all_to_all x1, waiting for transfers between devices: 37.7 us -> 69.7 us  [body(): rows_here = lax.all_to_all(by_loc, ('tq', 'th'), 0, 0, tiled=True)]
    dot_general x10, matrix products: 18.7 us -> 45.3 us  [contract(): lax.dot_general(left, right, (((0, 1, 3), (0, 1, 3)), ((), ())), preferre...]
    select_n x2 -> x1, other arithmetic: 7.84 us -> 1.02 us  [body(): give = jnp.where(pair_index == 0, high_half, low_half)]
    dynamic_update_slice x0 -> x2, local copies, waits for them, and re-layouts: none -> 5.85 us  [the longest x1 3.94 us: body(): lax.dynamic_update_slice_in_dim(slots, other_parity[:, :, None], 1 - pair...]
    broadcast_in_dim x0 -> x1, local copies, waits for them, and re-layouts: none -> 3.6 us  [body(): jnp.zeros(same_parity.shape[:2] + (PAIR,) + same_parity.shape[2:], jnp.bf...]
    all_gather x1, waiting for transfers between devices: 19.7 us -> 16.9 us  [body(): other_parity = lax.all_gather(by_piece(got), 'tq', axis=1, tiled=True)]
  transfers between devices with their start and end apart: 8 -> 8, of which waited for: 5 -> 4; matrix products, arithmetic and copies ran while one was open for 10% -> 15% of each run, Pallas kernels for 0% -> 0%
where the time goes in v16:
time: 276 us
  waiting for transfers between devices  145 us (53%)
  matrix products  45.3 us (16%)
  blocking collectives  25.8 us (9%)
  other arithmetic  16.5 us (6%)
  between operations  15.5 us (6%)
  local copies, waits for them, and re-layouts  15.1 us (5%)
  starting transfers between devices  12 us (4%)
    all_to_all x1, waiting for transfers between devices, body(): rows_here = lax.all_to_all(by_loc, ('tq', 'th'), 0, 0, tiled=True)  69.7 us
    dot_general x10, matrix products, contract(): lax.dot_general(left, right, (((0, 1, 3), (0, 1, 3)), ((), ())), preferre...  45.3 us
    ppermute x2, waiting for transfers between devices, gather_chan(): got = lax.ppermute(held, 'chan', [(c, c ^ 1 << bit) for c in range(size)])  35.5 us
    all_to_all x1, blocking collectives, body(): by_loc = lax.all_to_all(split_b, 'chan', 2, 0, tiled=True)  25.8 us
    ppermute x3, waiting for transfers between devices, swap_pair(): return lax.ppermute(x, 'th', [(0, 1), (1, 0)])  23.2 us
    all_gather x1, waiting for transfers between devices, body(): other_parity = lax.all_gather(by_piece(got), 'tq', axis=1, tiled=True)  16.9 us
    all_to_all x1, starting transfers between devices, body(): rows_here = lax.all_to_all(by_loc, ('tq', 'th'), 0, 0, tiled=True)  6.31 us
  transfers between devices with their start and end apart: 8, of which 4 were waited for; matrix products, arithmetic and copies ran while one was open for 15% of the time, Pallas kernels for 0%

profile of v16, /device:TPU:0, one launch (start us, length us, event | category | flops | bytes accessed | tf_op | source)
XLA Modules:
  0.0 275.5 jit_solution(3464176032333336405)
XLA Ops:
  15.9 25.8 %all_to_all.20 = bf16[416,2,4,256]{3,0,1,2:T(8,128)(2,1)} all-to-all(bf16[416,2,4,256]{3,0,1,2:T(8,128)(2,1)S(1)} %copy_select_fusion), channel_id=1, replica_groups=mesh['tq'=4,'th'=2,'chan'=4] {'chan'}, dimensions={2} | all-to-all | bytes 3407872 | tf_op jit(solution)/shard_map/all_to_all | solution.py:87
  41.6 6.3 %all-to-all-start.1 = ((bf16[8,416,256]{2,1,0:T(8,128)(2,1)}), bf16[8,416,256]{2,1,0:T(8,128)(2,1)S(1)}, u32[]{:S(2)}, u32[]{:S(2)}) async-start(bf16[8,416,256]{2,1,0:T(8,128)(2,1)} %bitcast.4), calls=%async_computation.1 | async-start | bytes 3407872 | tf_op jit(solution)/shard_map/all_to_all | solution.py:90
  48.0 2.0 collective-permute-start.2
  50.0 69.7 %all-to-all-done.1 = bf16[8,416,256]{2,1,0:T(8,128)(2,1)S(1)} async-done(((bf16[8,416,256]{2,1,0:T(8,128)(2,1)}), bf16[8,416,256]{2,1,0:T(8,128)(2,1)S(1)}, u32[]{:S(2)}, u32[]{:S(2)}) %all-to-all-start.1) | async-done | bytes 1703968 | tf_op jit(solution)/shard_map/all_to_all | solution.py:90
  123.3 35.5 %collective-permute-done = bf16[1,8,416,256]{3,2,1,0:T(8,128)(2,1)} collective-permute-done((bf16[1,8,416,256]{3,2,1,0:T(8,128)(2,1)S(1)}, bf16[1,8,416,256]{3,2,1,0:T(8,128)(2,1)}, u32[]{:S(2)}, u32[]{:S(2)}) %collective-permute-start) | collective-permute-done | bytes 1703968 | tf_op jit(solution)/shard_map/ppermute | solution.py:19
  158.8 2.2 broadcast_select_fusion.3
  161.0 2.0 pad_maximum_fusion
  166.4 3.6 %broadcast_in_dim.42 = bf16[4,4,2,416,256]{4,3,2,1,0:T(8,128)(2,1)} broadcast(bf16[]{:T(256)} %constant.27.clone.1), dimensions={} | broadcast | bytes 6815746 | tf_op jit(solution)/shard_map/broadcast_in_dim | solution.py:81
  170.0 1.9 bitcast_dynamic-update-slice_fusion.1
  172.0 16.9 %all-gather.5.cloned.1.call-done = bf16[4,4,416,256]{3,2,1,0:T(8,128)(2,1)} async-done(((bf16[4,1,416,256]{3,2,1,0:T(8,128)(2,1)}), bf16[4,4,416,256]{3,2,1,0:T(8,128)(2,1)}) %all-gather.5.cloned.1.call-update) | async-done | bytes 3407888 | tf_op jit(solution)/shard_map/all_gather | solution.py:80
  188.9 3.9 %bitcast_dynamic-update-slice_fusion = bf16[4,4,2,416,256]{4,3,2,1,0:T(8,128)(2,1)} fusion(bf16[4,4,2,416,256]{4,3,2,1,0:T(8,128)(2,1)} %bitcast_dynamic-update-slice_fusion.1, s32[]{:T(128)S(6)} %select_n.74, bf16[4,4,416,256]{3,2,1,0:T(8,128)(2,1)} %all-gather.5.cloned.1.call-done), kind=kLoop, calls=%fused_computation.23 | loop fusion | bytes 6815748 | tf_op jit(solution)/shard_map/dynamic_update_slice | solution.py:83
  192.8 2.2 broadcast_select_fusion
  195.7 5.1 %convolution_bitcast_fusion = f32[208,1,416]{2,0,1:T(8,128)S(1)} fusion(bf16[4,8,208,256]{3,2,1,0:T(8,128)(2,1)S(1)} %get-tuple-element.7, bf16[4,8,416,256]{3,2,1,0:T(8,128)(2,1)} %bitcast.15), kind=kOutput, calls=%fused_computation.40 | convolution fusion | flops 1417674752 | bytes 10569728 | tf_op jit(solution)/shard_map/dot_general | solution.py:33
  200.8 4.6 %fusion.25 = f32[208,1,416]{2,0,1:T(8,128)S(1)} fusion(bf16[4,8,208,256]{3,2,1,0:T(8,128)(2,1)S(1)} %get-tuple-element.7, bf16[4,8,416,256]{3,2,1,0:T(8,128)(2,1)} %bitcast.15), kind=kOutput, calls=%fused_computation.36 | convolution fusion | flops 1240465408 | bytes 9717760 | tf_op jit(solution)/shard_map/dot_general | solution.py:33
  205.5 4.6 %fusion.34 = f32[208,1,416]{2,0,1:T(8,128)S(1)} fusion(bf16[4,8,208,256]{3,2,1,0:T(8,128)(2,1)S(1)} %get-tuple-element.7, bf16[4,8,416,256]{3,2,1,0:T(8,128)(2,1)} %bitcast.15), kind=kOutput, calls=%fused_computation.39 | convolution fusion | flops 1240465408 | bytes 9717760 | tf_op jit(solution)/shard_map/dot_general | solution.py:33
  210.1 4.1 %fusion.44 = f32[208,1,416]{2,0,1:T(8,128)S(1)} fusion(bf16[4,8,208,256]{3,2,1,0:T(8,128)(2,1)S(1)} %get-tuple-element.7, bf16[4,8,416,256]{3,2,1,0:T(8,128)(2,1)} %bitcast.15), kind=kOutput, calls=%fused_computation.45 | convolution fusion | flops 1063256064 | bytes 8865792 | tf_op jit(solution)/shard_map/dot_general | solution.py:33
  214.3 4.1 %fusion.53 = f32[208,1,416]{2,0,1:T(8,128)S(1)} fusion(bf16[4,8,208,256]{3,2,1,0:T(8,128)(2,1)S(1)} %get-tuple-element.7, bf16[4,8,416,256]{3,2,1,0:T(8,128)(2,1)} %bitcast.15), kind=kOutput, calls=%fused_computation.48 | convolution fusion | flops 1063256064 | bytes 8865792 | tf_op jit(solution)/shard_map/dot_general | solution.py:33
  220.7 4.1 %fusion.41 = f32[208,5,416]{2,0,1:T(8,128)S(1)} fusion(bf16[4,8,208,256]{3,2,1,0:T(8,128)(2,1)S(1)} %get-tuple-element.8, bf16[4,8,416,256]{3,2,1,0:T(8,128)(2,1)} %bitcast.15), kind=kOutput, calls=%fused_computation.44 | convolution fusion | flops 1063256064 | bytes 8945664 | tf_op jit(solution)/shard_map/dot_general | solution.py:33
  224.9 4.6 %fusion.22 = f32[208,5,416]{2,0,1:T(8,128)S(1)} fusion(f32[208,5,416]{2,0,1:T(8,128)S(1)} %fusion.41, bf16[4,8,208,256]{3,2,1,0:T(8,128)(2,1)S(1)} %get-tuple-element.8, bf16[4,8,416,256]{3,2,1,0:T(8,128)(2,1)} %bitcast.15), kind=kOutput, calls=%fused_computation.35 | convolution fusion | flops 1240465408 | bytes 9797632 | tf_op jit(solution)/shard_map/dot_general | solution.py:33
  229.5 5.1 %fusion.37 = f32[208,5,416]{2,0,1:T(8,128)S(1)} fusion(f32[208,5,416]{2,0,1:T(8,128)S(1)} %fusion.22, bf16[4,8,208,256]{3,2,1,0:T(8,128)(2,1)S(1)} %get-tuple-element.8, bf16[4,8,416,256]{3,2,1,0:T(8,128)(2,1)} %bitcast.15), kind=kOutput, calls=%fused_computation.42 | convolution fusion | flops 1417674752 | bytes 10649600 | tf_op jit(solution)/shard_map/dot_general | solution.py:33
  234.6 4.6 %fusion.31 = f32[208,5,416]{2,0,1:T(8,128)S(1)} fusion(f32[208,5,416]{2,0,1:T(8,128)S(1)} %fusion.37, bf16[4,8,208,256]{3,2,1,0:T(8,128)(2,1)S(1)} %get-tuple-element.8, bf16[4,8,416,256]{3,2,1,0:T(8,128)(2,1)} %bitcast.15), kind=kOutput, calls=%fused_computation.38 | convolution fusion | flops 1240465408 | bytes 9797632 | tf_op jit(solution)/shard_map/dot_general | solution.py:33
  239.3 4.1 %fusion.50 = f32[208,5,416]{2,0,1:T(8,128)S(1)} fusion(f32[208,5,416]{2,0,1:T(8,128)S(1)} %fusion.31, bf16[4,8,208,256]{3,2,1,0:T(8,128)(2,1)S(1)} %get-tuple-element.8, bf16[4,8,416,256]{3,2,1,0:T(8,128)(2,1)} %bitcast.15), kind=kOutput, calls=%fused_computation.47 | convolution fusion | flops 1063256064 | bytes 8945664 | tf_op jit(solution)/shard_map/dot_general | solution.py:33
  243.4 23.2 %collective-permute-done.3 = f32[208,2,416]{2,0,1:T(8,128)S(1)} collective-permute-done((f32[208,2,416]{2,0,1:T(8,128)S(1)}, f32[208,2,416]{2,0,1:T(8,128)S(1)}, u32[]{:S(2)}, u32[]{:S(2)}) %collective-permute-start.3) | collective-permute-done | bytes 692256 | tf_op jit(solution)/shard_map/ppermute | solution.py:10
  266.7 1.9 fusion.18
  (42 shorter events, 17.4 us)
Async XLA Ops:
  6.5 159.9 %all-gather.3.cloned.1.call-start = ((), (), s32[]{:S(2)}) async-start(), calls=%async_computation.2 | async-start | bytes 4259840 | tf_op jit(solution)/shard_map/all_gather | solution.py:78
  11.1 2.1 copy-start.2
  15.9 32.1 %copy-start.3 = (bf16[416,1024]{1,0:T(8,128)(2,1)S(1)}, bf16[416,1024]{1,0:T(8,128)(2,1)}, u32[]{:S(2)}) copy-start(bf16[416,1024]{1,0:T(8,128)(2,1)} %get-tuple-element.13) | copy-start | bytes 2555908
  41.6 78.1 %all-to-all-start.1 = ((bf16[8,416,256]{2,1,0:T(8,128)(2,1)}), bf16[8,416,256]{2,1,0:T(8,128)(2,1)S(1)}, u32[]{:S(2)}, u32[]{:S(2)}) async-start(bf16[8,416,256]{2,1,0:T(8,128)(2,1)} %bitcast.4), calls=%async_computation.1 | async-start | bytes 3407872 | tf_op jit(solution)/shard_map/all_to_all | solution.py:90
  47.9 140.9 %all-gather.5.cloned.1.call-start = ((), (), s32[]{:S(2)}) async-start(), calls=%async_computation.3 | async-start | bytes 4259840 | tf_op jit(solution)/shard_map/all_gather | solution.py:80
  48.0 73.2 %collective-permute-start.2 = (bf16[416,1024]{1,0:T(8,128)(2,1)S(1)}, bf16[416,1024]{1,0:T(8,128)(2,1)S(1)}, u32[]{:S(2)}, u32[]{:S(2)}) collective-permute-start(bf16[416,1024]{1,0:T(8,128)(2,1)S(1)} %copy-done.3), channel_id=1, source_target_pairs={{0,4},{4,0},{1,5},{5,1},{2,6},{6,2},{3,7},{7,3},{8,12},{12,8},{9,1... | collective-permute-start | bytes 2555912 | tf_op jit(solution)/shard_map/ppermute | solution.py:10
  119.8 3.5 %copy-start = (bf16[8,416,256]{2,1,0:T(8,128)(2,1)}, bf16[8,416,256]{2,1,0:T(8,128)(2,1)S(1)}, u32[]{:S(2)}) copy-start(bf16[8,416,256]{2,1,0:T(8,128)(2,1)S(1)} %all-to-all-done.1) | copy-start | bytes 5111812
  119.8 39.1 %collective-permute-start = (bf16[1,8,416,256]{3,2,1,0:T(8,128)(2,1)S(1)}, bf16[1,8,416,256]{3,2,1,0:T(8,128)(2,1)}, u32[]{:S(2)}, u32[]{:S(2)}) collective-permute-start(bf16[1,8,416,256]{3,2,1,0:T(8,128)(2,1)S(1)} %bitcast.116), channel_id=1, source_target_pairs={{0,2},{1,3},{2,0},{3,1},{4,6},{5,7},{6,4},{7,5},{8,10},{9,11},{10,... | collective-permute-start | bytes 5111816 | tf_op jit(solution)/shard_map/ppermute | solution.py:19
  161.0 2.6 copy-start.4
  163.0 29.8 %collective-permute-start.1 = (bf16[2,8,416,256]{3,2,1,0:T(8,128)(2,1)}, bf16[2,8,416,256]{3,2,1,0:T(8,128)(2,1)}, u32[]{:S(2)}, u32[]{:S(2)}) collective-permute-start(bf16[2,8,416,256]{3,2,1,0:T(8,128)(2,1)} %pad_maximum_fusion), channel_id=1, source_target_pairs={{0,1},{1,0},{2,3},{3,2},{4,5},{5,4},{6,7},{7,6},{8,9},{9,8},{10,11... | collective-permute-start | bytes 10223624 | tf_op jit(solution)/shard_map/ppermute | solution.py:19
  166.4 3.6 %copy-start.1 = (bf16[4,4,416,256]{3,2,1,0:T(8,128)(2,1)S(1)}, bf16[4,4,416,256]{3,2,1,0:T(8,128)(2,1)}, u32[]{:S(2)}) copy-start(bf16[4,4,416,256]{3,2,1,0:T(8,128)(2,1)} %all-gather.3.cloned.1.call-done) | copy-start | bytes 10223620
  218.5 48.2 %collective-permute-start.4 = (f32[208,3,416]{2,0,1:T(8,128)S(1)}, f32[208,3,416]{2,0,1:T(8,128)S(1)}, u32[]{:S(2)}, u32[]{:S(2)}) collective-permute-start(f32[208,3,416]{2,0,1:T(8,128)S(1)} %pad_maximum_fusion.1), channel_id=1, source_target_pairs={{0,4},{4,0},{1,5},{5,1},{2,6},{6,2},{3,7},{7,3},{8,12},{12,8},{9,1... | collective-permute-start | bytes 3115016 | tf_op jit(solution)/shard_map/ppermute | solution.py:10
  220.0 46.6 %collective-permute-start.3 = (f32[208,2,416]{2,0,1:T(8,128)S(1)}, f32[208,2,416]{2,0,1:T(8,128)S(1)}, u32[]{:S(2)}, u32[]{:S(2)}) collective-permute-start(f32[208,2,416]{2,0,1:T(8,128)S(1)} %pad_maximum_fusion.2), channel_id=1, source_target_pairs={{0,4},{4,0},{1,5},{5,1},{2,6},{6,2},{3,7},{7,3},{8,12},{12,8},{9,1... | collective-permute-start | bytes 2076680 | tf_op jit(solution)/shard_map/ppermute | solution.py:10
Sparse Core Ops, SparseCore 0:
  13.3 104.5 all-gather.2
  123.4 65.4 all-gather.4

commit v17 on v15

--- a/solution.py
+++ b/solution.py
@@ -95,7 +95,23 @@
     keep_rows = lax.dynamic_slice_in_dim(all_background, pair_index * rows_out, rows_out, axis=2)
     outer = (0, lag_total - 1)
     inner = tuple(range(1, lag_total - 1))
-    sent_outer = swap_pair(lag_block(give_rows, all_analysis, cycle_total, max_lag, outer))
+    def parity_cycles(x, parity):
+        return jnp.where(parity == 0, x[:, 0::PAIR], x[:, 1::PAIR])
+
+    give_same = parity_cycles(give_rows, pair_index)
+    give_other = parity_cycles(give_rows, 1 - pair_index)
+    shift = max_lag // PAIR
+    outer_parts = []
+    for k in outer:
+        if k < max_lag:
+            left, right = slice(None, quad_size - shift), slice(shift, None)
+        else:
+            left, right = slice(shift, None), slice(None, quad_size - shift)
+        outer_parts.append(
+            contract(give_same[:, left], same_parity[:, right])
+            + contract(give_other[:, left], other_parity[:, right])
+        )
+    sent_outer = swap_pair(jnp.stack(outer_parts, axis=1))
     sent_inner = swap_pair(lag_block(give_rows, all_analysis, cycle_total, max_lag, inner))
     own = lag_block(keep_rows, all_analysis, cycle_total, max_lag, range(lag_total))
     sent = jnp.concatenate([sent_outer[:, :1], sent_inner, sent_outer[:, 1:]], axis=1)

time: 263 us -> 269 us (1.023)
  local copies, waits for them, and re-layouts: 5.6 us -> 10.6 us
    select_n x0 -> x1, local copies, waits for them, and re-layouts: none -> 3.45 us  [body(): all_analysis = jnp.where(pair_index == 0, in_order, swapped)]
    reshape x4 -> x0, local copies, waits for them, and re-layouts: 2.87 us -> none  [bit_reversed(): return x.reshape(shape).transpose(order).reshape(x.shape)]
    dot_general x10 -> x12, matrix products: 18.7 us -> 19.1 us  [contract(): lax.dot_general(left, right, (((0, 1, 3), (0, 1, 3)), ((), ())), preferre...]
  transfers between devices with their start and end apart: 8 -> 8, of which waited for: 5 -> 6; matrix products, arithmetic and copies ran while one was open for 10% -> 11% of each run, Pallas kernels for 0% -> 0%
where the time goes in v17:
time: 269 us; the launch traced here: 268 us
  waiting for transfers between devices  162 us (60%)
  blocking collectives  25.8 us (10%)
  other arithmetic  23.3 us (9%)
  matrix products  19.1 us (7%)
  between operations  15.6 us (6%)
  starting transfers between devices  12 us (4%)
  local copies, waits for them, and re-layouts  10.6 us (4%)
    ppermute x3, waiting for transfers between devices, swap_pair(): return lax.ppermute(x, 'th', [(0, 1), (1, 0)])  66.4 us
    all_to_all x1, waiting for transfers between devices, body(): rows_here = lax.all_to_all(by_loc, ('tq', 'th'), 0, 0, tiled=True)  38.1 us
    ppermute x2, waiting for transfers between devices, gather_chan(): got = lax.ppermute(held, 'chan', [(c, c ^ 1 << bit) for c in range(size)])  37.6 us
    all_to_all x1, blocking collectives, body(): by_loc = lax.all_to_all(split_b, 'chan', 2, 0, tiled=True)  25.8 us
    all_gather x1, waiting for transfers between devices, body(): other_parity = lax.all_gather(by_piece(got), 'tq', axis=1, tiled=True)  19.9 us
    dot_general x12, matrix products, contract(): lax.dot_general(left, right, (((0, 1, 3), (0, 1, 3)), ((), ())), preferre...  19.1 us
    select_n x1, other arithmetic, body(): all_analysis = jnp.where(pair_index == 0, in_order, swapped)  6.8 us
    all_to_all x1, starting transfers between devices, body(): rows_here = lax.all_to_all(by_loc, ('tq', 'th'), 0, 0, tiled=True)  6.3 us
  transfers between devices with their start and end apart: 8, of which 6 were waited for; matrix products, arithmetic and copies ran while one was open for 11% of the time, Pallas kernels for 0%

profile of v17, /device:TPU:0, one launch (start us, length us, event | category | flops | bytes accessed | tf_op | source)
XLA Modules:
  0.0 268.4 jit_solution(17603343529021341803)
XLA Ops:
  8.5 1.6 bitcast_select_fusion
  15.4 25.8 %all_to_all.20 = bf16[416,2,4,256]{3,0,1,2:T(8,128)(2,1)} all-to-all(bf16[416,2,4,256]{3,0,1,2:T(8,128)(2,1)S(1)} %copy_select_fusion), channel_id=1, replica_groups=mesh['tq'=4,'th'=2,'chan'=4] {'chan'}, dimensions={2} | all-to-all | bytes 3407872 | tf_op jit(solution)/shard_map/all_to_all | solution.py:87
  41.1 6.3 %all-to-all-start.1 = ((bf16[8,416,256]{2,1,0:T(8,128)(2,1)}), bf16[8,416,256]{2,1,0:T(8,128)(2,1)S(1)}, u32[]{:S(2)}, u32[]{:S(2)}) async-start(bf16[8,416,256]{2,1,0:T(8,128)(2,1)} %bitcast.4), calls=%async_computation.1 | async-start | bytes 3407872 | tf_op jit(solution)/shard_map/all_to_all | solution.py:90
  47.5 2.0 collective-permute-start.2
  49.5 29.9 %collective-permute-done.2 = bf16[416,1024]{1,0:T(8,128)(2,1)S(1)} collective-permute-done((bf16[416,1024]{1,0:T(8,128)(2,1)S(1)}, bf16[416,1024]{1,0:T(8,128)(2,1)S(1)}, u32[]{:S(2)}, u32[]{:S(2)}) %collective-permute-start.2) | collective-permute-done | bytes 852000 | tf_op jit(solution)/shard_map/ppermute | solution.py:10
  81.2 38.1 %all-to-all-done.1 = bf16[8,416,256]{2,1,0:T(8,128)(2,1)S(1)} async-done(((bf16[8,416,256]{2,1,0:T(8,128)(2,1)}), bf16[8,416,256]{2,1,0:T(8,128)(2,1)S(1)}, u32[]{:S(2)}, u32[]{:S(2)}) %all-to-all-start.1) | async-done | bytes 1703968 | tf_op jit(solution)/shard_map/all_to_all | solution.py:90
  120.8 37.6 %collective-permute-done = bf16[1,8,416,256]{3,2,1,0:T(8,128)(2,1)} collective-permute-done((bf16[1,8,416,256]{3,2,1,0:T(8,128)(2,1)S(1)}, bf16[1,8,416,256]{3,2,1,0:T(8,128)(2,1)}, u32[]{:S(2)}, u32[]{:S(2)}) %collective-permute-start) | collective-permute-done | bytes 1703968 | tf_op jit(solution)/shard_map/ppermute | solution.py:19
  158.4 2.2 broadcast_select_fusion.5
  160.6 2.0 pad_maximum_fusion
  166.1 19.9 %all-gather.5.cloned.1.call-done = bf16[4,4,416,256]{3,2,1,0:T(8,128)(2,1)} async-done(((bf16[4,1,416,256]{3,2,1,0:T(8,128)(2,1)}), bf16[4,4,416,256]{3,2,1,0:T(8,128)(2,1)}) %all-gather.5.cloned.1.call-update) | async-done | bytes 3407888 | tf_op jit(solution)/shard_map/all_gather | solution.py:80
  186.0 6.8 %maximum_select_fusion = bf16[4,4,2,416,256]{4,3,1,0,2:T(8,128)(2,1)S(1)} fusion(bf16[4,4,1,416,256]{4,3,1,0,2:T(8,128)(2,1)} %bitcast.144, bf16[4,4,1,416,256]{4,3,1,0,2:T(8,128)(2,1)} %bitcast.143, pred[]{:T(512)S(6)} %eq.25), kind=kLoop, calls=%fused_computation.4 | loop fusion | flops 10223616 | bytes 13631489 | tf_op jit(solution)/shard_map/jit(_where)/select_n | solution.py:83
  192.8 3.4 %copy.15 = bf16[4,4,2,416,256]{4,3,2,1,0:T(8,128)(2,1)} copy(bf16[4,4,2,416,256]{4,3,1,0,2:T(8,128)(2,1)S(1)} %maximum_select_fusion) | data formatting | bytes 13631488 | tf_op jit(solution)/shard_map/jit(_where)/select_n | solution.py:83
  196.3 2.4 broadcast_select_fusion
  200.6 1.9 fusion.29
  202.5 1.9 fusion.38
  204.5 2.2 convolution_bitcast_fusion
  213.8 1.7 fusion.57
  215.4 1.9 fusion.26
  217.4 2.2 fusion.41
  219.5 1.9 fusion.35
  221.5 1.7 fusion.63
  223.2 10.2 %collective-permute-done.3 = f32[208,2,416]{2,0,1:T(8,128)S(1)} collective-permute-done((f32[208,2,416]{2,0,1:T(8,128)S(1)}, f32[208,2,416]{2,0,1:T(8,128)S(1)}, u32[]{:S(2)}, u32[]{:S(2)}) %collective-permute-start.3) | collective-permute-done | bytes 692256 | tf_op jit(solution)/shard_map/ppermute | solution.py:10
  233.5 26.2 %collective-permute-done.4 = f32[208,3,416]{2,0,1:T(8,128)S(1)} collective-permute-done((f32[208,3,416]{2,0,1:T(8,128)S(1)}, f32[208,3,416]{2,0,1:T(8,128)S(1)}, u32[]{:S(2)}, u32[]{:S(2)}) %collective-permute-start.4) | collective-permute-done | bytes 1038368 | tf_op jit(solution)/shard_map/ppermute | solution.py:10
  259.6 1.9 fusion.22
  (50 shorter events, 21.0 us)
Async XLA Ops:
  6.5 159.5 %all-gather.3.cloned.1.call-start = ((), (), s32[]{:S(2)}) async-start(), calls=%async_computation.2 | async-start | bytes 4259840 | tf_op jit(solution)/shard_map/all_gather | solution.py:78
  11.0 1.8 copy-start.3
  15.4 32.1 %copy-start.4 = (bf16[416,1024]{1,0:T(8,128)(2,1)S(1)}, bf16[416,1024]{1,0:T(8,128)(2,1)}, u32[]{:S(2)}) copy-start(bf16[416,1024]{1,0:T(8,128)(2,1)} %get-tuple-element.14) | copy-start | bytes 2555908
  41.1 78.2 %all-to-all-start.1 = ((bf16[8,416,256]{2,1,0:T(8,128)(2,1)}), bf16[8,416,256]{2,1,0:T(8,128)(2,1)S(1)}, u32[]{:S(2)}, u32[]{:S(2)}) async-start(bf16[8,416,256]{2,1,0:T(8,128)(2,1)} %bitcast.4), calls=%async_computation.1 | async-start | bytes 3407872 | tf_op jit(solution)/shard_map/all_to_all | solution.py:90
  47.4 138.6 %all-gather.5.cloned.1.call-start = ((), (), s32[]{:S(2)}) async-start(), calls=%async_computation.3 | async-start | bytes 4259840 | tf_op jit(solution)/shard_map/all_gather | solution.py:80
  47.5 32.0 %collective-permute-start.2 = (bf16[416,1024]{1,0:T(8,128)(2,1)S(1)}, bf16[416,1024]{1,0:T(8,128)(2,1)S(1)}, u32[]{:S(2)}, u32[]{:S(2)}) collective-permute-start(bf16[416,1024]{1,0:T(8,128)(2,1)S(1)} %copy-done.4), channel_id=1, source_target_pairs={{0,4},{4,0},{1,5},{5,1},{2,6},{6,2},{3,7},{7,3},{8,12},{12,8},{9,1... | collective-permute-start | bytes 2555912 | tf_op jit(solution)/shard_map/ppermute | solution.py:10
  119.3 1.4 copy-start
  119.3 39.0 %collective-permute-start = (bf16[1,8,416,256]{3,2,1,0:T(8,128)(2,1)S(1)}, bf16[1,8,416,256]{3,2,1,0:T(8,128)(2,1)}, u32[]{:S(2)}, u32[]{:S(2)}) collective-permute-start(bf16[1,8,416,256]{3,2,1,0:T(8,128)(2,1)S(1)} %bitcast.136), channel_id=1, source_target_pairs={{0,2},{1,3},{2,0},{3,1},{4,6},{5,7},{6,4},{7,5},{8,10},{9,11},{10,... | collective-permute-start | bytes 5111816 | tf_op jit(solution)/shard_map/ppermute | solution.py:19
  160.6 2.0 copy-start.5
  162.6 33.6 %collective-permute-start.1 = (bf16[2,8,416,256]{3,2,1,0:T(8,128)(2,1)}, bf16[2,8,416,256]{3,2,1,0:T(8,128)(2,1)}, u32[]{:S(2)}, u32[]{:S(2)}) collective-permute-start(bf16[2,8,416,256]{3,2,1,0:T(8,128)(2,1)} %pad_maximum_fusion), channel_id=1, source_target_pairs={{0,1},{1,0},{2,3},{3,2},{4,5},{5,4},{6,7},{7,6},{8,9},{9,8},{10,11... | collective-permute-start | bytes 10223624 | tf_op jit(solution)/shard_map/ppermute | solution.py:19
  196.3 3.2 %slice-start = ((s8[6815744]{0:T(1024)(128)(4,1)}), s8[4194304]{0:T(1024)(128)(4,1)S(1)}, s32[]{:S(2)}) async-start(s8[6815744]{0:T(1024)(128)(4,1)} %bitcast.126), calls=%async_computation.4 | async-start | bytes 8388608
  198.6 2.0 slice-start.1
  204.4 2.2 copy-start.2
  207.6 2.0 copy-start.1
  211.5 21.9 %collective-permute-start.3 = (f32[208,2,416]{2,0,1:T(8,128)S(1)}, f32[208,2,416]{2,0,1:T(8,128)S(1)}, u32[]{:S(2)}, u32[]{:S(2)}) collective-permute-start(f32[208,2,416]{2,0,1:T(8,128)S(1)} %pad_maximum_fusion.2), channel_id=1, source_target_pairs={{0,4},{4,0},{1,5},{5,1},{2,6},{6,2},{3,7},{7,3},{8,12},{12,8},{9,1... | collective-permute-start | bytes 2076680 | tf_op jit(solution)/shard_map/ppermute | solution.py:10
  213.1 46.5 %collective-permute-start.4 = (f32[208,3,416]{2,0,1:T(8,128)S(1)}, f32[208,3,416]{2,0,1:T(8,128)S(1)}, u32[]{:S(2)}, u32[]{:S(2)}) collective-permute-start(f32[208,3,416]{2,0,1:T(8,128)S(1)} %pad_maximum_fusion.1), channel_id=1, source_target_pairs={{0,4},{4,0},{1,5},{5,1},{2,6},{6,2},{3,7},{7,3},{8,12},{12,8},{9,1... | collective-permute-start | bytes 3115016 | tf_op jit(solution)/shard_map/ppermute | solution.py:10
Sparse Core Ops, SparseCore 0:
  12.9 104.6 all-gather.2
  119.2 66.7 all-gather.4

commit v18 on v17

--- a/solution.py
+++ b/solution.py
@@ -78,11 +78,6 @@
     same_parity = lax.all_gather(by_piece(keep), "tq", axis=1, tiled=True)
     got = swap_pair(give)
     other_parity = lax.all_gather(by_piece(got), "tq", axis=1, tiled=True)
-    in_order = jnp.stack([same_parity, other_parity], axis=2)
-    swapped = jnp.stack([other_parity, same_parity], axis=2)
-    all_analysis = jnp.where(pair_index == 0, in_order, swapped)
-    all_analysis = all_analysis.reshape(chan_size, cycle_total, width_block, piece)
-
     split_b = local_background.reshape(width_block, PAIR, chan_size, piece)
     by_loc = lax.all_to_all(split_b, "chan", 2, 0, tiled=True)
     by_loc = by_loc.reshape(quad_size, pair_rows, PAIR, piece).transpose(0, 2, 1, 3)
@@ -111,7 +106,14 @@
             contract(give_same[:, left], same_parity[:, right])
             + contract(give_other[:, left], other_parity[:, right])
         )
-    sent_outer = swap_pair(jnp.stack(outer_parts, axis=1))
+    outer_partial, same_late, other_late = lax.optimization_barrier(
+        (jnp.stack(outer_parts, axis=1), same_parity, other_parity)
+    )
+    sent_outer = swap_pair(outer_partial)
+    in_order = jnp.stack([same_late, other_late], axis=2)
+    swapped = jnp.stack([other_late, same_late], axis=2)
+    all_analysis = jnp.where(pair_index == 0, in_order, swapped)
+    all_analysis = all_analysis.reshape(chan_size, cycle_total, width_block, piece)
     sent_inner = swap_pair(lag_block(give_rows, all_analysis, cycle_total, max_lag, inner))
     own = lag_block(keep_rows, all_analysis, cycle_total, max_lag, range(lag_total))
     sent = jnp.concatenate([sent_outer[:, :1], sent_inner, sent_outer[:, 1:]], axis=1)

time: 269 us -> 312 us (1.16)
  waiting for transfers between devices: 162 us -> 220 us
  blocking collectives: 25.8 us -> 0 us
  matrix products: 19.1 us -> 27.7 us
  starting transfers between devices: 12 us -> 16.2 us
  other arithmetic: 23.3 us -> 19.2 us
    all_gather x1, waiting for transfers between devices: 0.01 us -> 66.7 us  [body(): same_parity = lax.all_gather(by_piece(keep), 'tq', axis=1, tiled=True)]
    all_to_all x1, waiting for transfers between devices: 38.1 us -> 70.7 us  [body(): rows_here = lax.all_to_all(by_loc, ('tq', 'th'), 0, 0, tiled=True)]
    ppermute x3, waiting for transfers between devices: 66.4 us -> 36.3 us  [swap_pair(): return lax.ppermute(x, 'th', [(0, 1), (1, 0)])]
    all_to_all x1 -> x0, blocking collectives: 25.8 us -> none  [body(): by_loc = lax.all_to_all(split_b, 'chan', 2, 0, tiled=True)]
    all_gather x1, waiting for transfers between devices: 19.9 us -> 0.01 us  [body(): other_parity = lax.all_gather(by_piece(got), 'tq', axis=1, tiled=True)]
    all_to_all x0 -> x1, waiting for transfers between devices: none -> 17.3 us  [body(): by_loc = lax.all_to_all(split_b, 'chan', 2, 0, tiled=True)]
    ppermute x2, waiting for transfers between devices: 37.6 us -> 28.7 us  [gather_chan(): got = lax.ppermute(held, 'chan', [(c, c ^ 1 << bit) for c in range(size)])]
    dot_general x12, matrix products: 19.1 us -> 27.7 us  [contract(): lax.dot_general(left, right, (((0, 1, 3), (0, 1, 3)), ((), ())), preferre...]
  transfers between devices with their start and end apart: 8 -> 9, of which waited for: 6 -> 6; matrix products, arithmetic and copies ran while one was open for 11% -> 11% of each run, Pallas kernels for 0% -> 0%
where the time goes in v18:
time: 312 us
  waiting for transfers between devices  220 us (71%)
  matrix products  27.7 us (9%)
  other arithmetic  19.2 us (6%)
  starting transfers between devices  16.2 us (5%)
  between operations  15.6 us (5%)
  local copies, waits for them, and re-layouts  13.6 us (4%)
    all_to_all x1, waiting for transfers between devices, body(): rows_here = lax.all_to_all(by_loc, ('tq', 'th'), 0, 0, tiled=True)  70.7 us
    all_gather x1, waiting for transfers between devices, body(): same_parity = lax.all_gather(by_piece(keep), 'tq', axis=1, tiled=True)  66.7 us
    ppermute x3, waiting for transfers between devices, swap_pair(): return lax.ppermute(x, 'th', [(0, 1), (1, 0)])  36.3 us
    ppermute x2, waiting for transfers between devices, gather_chan(): got = lax.ppermute(held, 'chan', [(c, c ^ 1 << bit) for c in range(size)])  28.7 us
    dot_general x12, matrix products, contract(): lax.dot_general(left, right, (((0, 1, 3), (0, 1, 3)), ((), ())), preferre...  27.7 us
    all_to_all x1, waiting for transfers between devices, body(): by_loc = lax.all_to_all(split_b, 'chan', 2, 0, tiled=True)  17.3 us
    all_to_all x1, starting transfers between devices, body(): rows_here = lax.all_to_all(by_loc, ('tq', 'th'), 0, 0, tiled=True)  6.63 us
  transfers between devices with their start and end apart: 9, of which 6 were waited for; matrix products, arithmetic and copies ran while one was open for 11% of the time, Pallas kernels for 0%

profile of v18, /device:TPU:0, one launch (start us, length us, event | category | flops | bytes accessed | tf_op | source)
XLA Modules:
  0.0 311.9 jit_solution(14852415322694223840)
XLA Ops:
  8.6 3.9 %squeeze.6 = bf16[416,2,4,256]{3,2,1,0:T(4,128)(2,1)S(1)} reshape(bf16[1,416,2048]{2,1,0:T(8,128)(2,1)} %param.4) | data formatting | bytes 3407872 | tf_op jit(solution)/shard_map/squeeze | solution.py:68
  14.4 4.4 %all-to-all-start = ((bf16[416,2,4,256]{3,0,1,2:T(8,128)(2,1)}), bf16[416,2,4,256]{3,0,1,2:T(8,128)(2,1)}, u32[]{:S(2)}, u32[]{:S(2)}) async-start(bf16[416,2,4,256]{3,0,1,2:T(8,128)(2,1)} %copy_select_fusion), calls=%async_computation | async-start | bytes 3407872 | tf_op jit(solution)/shard_map/all_to_all | solution.py:82
  20.7 2.9 collective-permute-start.2
  23.7 17.3 %all-to-all-done = bf16[416,2,4,256]{3,0,1,2:T(8,128)(2,1)} async-done(((bf16[416,2,4,256]{3,0,1,2:T(8,128)(2,1)}), bf16[416,2,4,256]{3,0,1,2:T(8,128)(2,1)}, u32[]{:S(2)}, u32[]{:S(2)}) %all-to-all-start) | async-done | bytes 1703968 | tf_op jit(solution)/shard_map/all_to_all | solution.py:82
  41.0 6.6 %all-to-all-start.1 = ((bf16[8,416,256]{2,1,0:T(8,128)(2,1)}), bf16[8,416,256]{2,1,0:T(8,128)(2,1)S(1)}, u32[]{:S(2)}, u32[]{:S(2)}) async-start(bf16[8,416,256]{2,1,0:T(8,128)(2,1)} %bitcast.4), calls=%async_computation.1 | async-start | bytes 3407872 | tf_op jit(solution)/shard_map/all_to_all | solution.py:85
  49.5 70.7 %all-to-all-done.1 = bf16[8,416,256]{2,1,0:T(8,128)(2,1)S(1)} async-done(((bf16[8,416,256]{2,1,0:T(8,128)(2,1)}), bf16[8,416,256]{2,1,0:T(8,128)(2,1)S(1)}, u32[]{:S(2)}, u32[]{:S(2)}) %all-to-all-start.1) | async-done | bytes 1703968 | tf_op jit(solution)/shard_map/all_to_all | solution.py:85
  121.3 28.7 %collective-permute-done = bf16[1,8,416,256]{3,2,1,0:T(8,128)(2,1)} collective-permute-done((bf16[1,8,416,256]{3,2,1,0:T(8,128)(2,1)S(1)}, bf16[1,8,416,256]{3,2,1,0:T(8,128)(2,1)}, u32[]{:S(2)}, u32[]{:S(2)}) %collective-permute-start) | collective-permute-done | bytes 1703968 | tf_op jit(solution)/shard_map/ppermute | solution.py:19
  150.1 2.2 broadcast_select_fusion.5
  152.3 2.1 pad_maximum_fusion
  154.3 2.7 reshape.39
  162.8 2.2 broadcast_select_fusion
  165.0 2.0 fusion.12
  167.0 4.7 %fusion.51 = f32[208,416]{1,0:T(8,128)} fusion(bf16[4,4,416,256]{3,2,1,0:T(8,128)(2,1)} %all-gather.5.cloned.1.call-done, pred[]{:T(512)S(6)} %eq.26, bf16[4,8,208,256]{3,2,1,0:T(8,128)(2,1)S(1)} %get-tuple-element.13), kind=kOutput, calls=%fused_computation.51 | convolution fusion | flops 532480000 | bytes 6309889 | tf_op jit(solution)/shard_map/dot_general | solution.py:33
  173.5 66.7 %all-gather.3.cloned.1.call-done = bf16[4,4,416,256]{3,2,1,0:T(8,128)(2,1)} async-done(((bf16[4,1,416,256]{3,2,1,0:T(8,128)(2,1)}), bf16[4,4,416,256]{3,2,1,0:T(8,128)(2,1)}) %all-gather.3.cloned.1.call-update) | async-done | bytes 3407888 | tf_op jit(solution)/shard_map/all_gather | solution.py:78
  240.2 2.9 fusion.69
  246.9 3.9 %fusion.29 = f32[208,1,416]{2,0,1:T(8,128)S(1)} fusion(bf16[4,8,208,256]{3,2,1,0:T(8,128)(2,1)} %copy-done.2, bf16[4,8,416,256]{3,2,1,0:T(8,128)(2,1)S(1)} %bitcast.126), kind=kOutput, calls=%fused_computation.41 | convolution fusion | flops 1240465408 | bytes 9717760 | tf_op jit(solution)/shard_map/dot_general | solution.py:33
  250.9 1.9 fusion.38
  252.9 2.2 convolution_bitcast_fusion
  259.0 1.9 fusion.26
  260.9 2.2 fusion.41
  263.1 1.9 fusion.35
  266.8 10.2 %collective-permute-done.3 = f32[208,2,416]{2,0,1:T(8,128)S(1)} collective-permute-done((f32[208,2,416]{2,0,1:T(8,128)S(1)}, f32[208,2,416]{2,0,1:T(8,128)S(1)}, u32[]{:S(2)}, u32[]{:S(2)}) %collective-permute-start.3) | collective-permute-done | bytes 692256 | tf_op jit(solution)/shard_map/ppermute | solution.py:10
  277.0 26.2 %collective-permute-done.4 = f32[208,3,416]{2,0,1:T(8,128)S(1)} collective-permute-done((f32[208,3,416]{2,0,1:T(8,128)S(1)}, f32[208,3,416]{2,0,1:T(8,128)S(1)}, u32[]{:S(2)}, u32[]{:S(2)}) %collective-permute-start.4) | collective-permute-done | bytes 1038368 | tf_op jit(solution)/shard_map/ppermute | solution.py:10
  303.2 1.9 fusion.22
  (54 shorter events, 23.9 us)
Async XLA Ops:
  12.6 7.0 %copy-start.7 = (bf16[1,416,2048]{2,1,0:T(8,128)(2,1)S(1)}, bf16[1,416,2048]{2,1,0:T(8,128)(2,1)}, u32[]{:S(2)}) copy-start(bf16[1,416,2048]{2,1,0:T(8,128)(2,1)} %param.3) | copy-start | bytes 5111812
  14.4 26.6 %all-to-all-start = ((bf16[416,2,4,256]{3,0,1,2:T(8,128)(2,1)}), bf16[416,2,4,256]{3,0,1,2:T(8,128)(2,1)}, u32[]{:S(2)}, u32[]{:S(2)}) async-start(bf16[416,2,4,256]{3,0,1,2:T(8,128)(2,1)} %copy_select_fusion), calls=%async_computation | async-start | bytes 3407872 | tf_op jit(solution)/shard_map/all_to_all | solution.py:82
  20.7 26.9 %collective-permute-start.2 = (bf16[416,1024]{1,0:T(8,128)(2,1)S(1)}, bf16[416,1024]{1,0:T(8,128)(2,1)S(1)}, u32[]{:S(2)}, u32[]{:S(2)}) collective-permute-start(bf16[416,1024]{1,0:T(8,128)(2,1)S(1)} %get-tuple-element.20), channel_id=1, source_target_pairs={{0,4},{4,0},{1,5},{5,1},{2,6},{6,2},{3,7},{7,3},{8,12},{12,8},{9,1... | collective-permute-start | bytes 2555912 | tf_op jit(solution)/shard_map/ppermute | solution.py:10
  41.0 79.1 %all-to-all-start.1 = ((bf16[8,416,256]{2,1,0:T(8,128)(2,1)}), bf16[8,416,256]{2,1,0:T(8,128)(2,1)S(1)}, u32[]{:S(2)}, u32[]{:S(2)}) async-start(bf16[8,416,256]{2,1,0:T(8,128)(2,1)} %bitcast.4), calls=%async_computation.1 | async-start | bytes 3407872 | tf_op jit(solution)/shard_map/all_to_all | solution.py:85
  47.6 119.4 %all-gather.5.cloned.1.call-start = ((), (), s32[]{:S(2)}) async-start(), calls=%async_computation.3 | async-start | bytes 4259840 | tf_op jit(solution)/shard_map/all_gather | solution.py:80
  49.4 190.7 %all-gather.3.cloned.1.call-start = ((), (), s32[]{:S(2)}) async-start(), calls=%async_computation.2 | async-start | bytes 4259840 | tf_op jit(solution)/shard_map/all_gather | solution.py:78
  120.1 1.2 copy-start
  120.1 29.9 %collective-permute-start = (bf16[1,8,416,256]{3,2,1,0:T(8,128)(2,1)S(1)}, bf16[1,8,416,256]{3,2,1,0:T(8,128)(2,1)}, u32[]{:S(2)}, u32[]{:S(2)}) collective-permute-start(bf16[1,8,416,256]{3,2,1,0:T(8,128)(2,1)S(1)} %bitcast.134), channel_id=1, source_target_pairs={{0,2},{1,3},{2,0},{3,1},{4,6},{5,7},{6,4},{7,5},{8,10},{9,11},{10,... | collective-permute-start | bytes 5111816 | tf_op jit(solution)/shard_map/ppermute | solution.py:19
  154.3 5.0 %copy-start.8 = (s32[8]{0:T(128)S(1)}, s32[8]{0:T(128)}, u32[]{:S(2)}) copy-start(s32[8]{0:T(128)} %param.5) | copy-start | bytes 100
  154.3 8.5 %collective-permute-start.1 = (bf16[2,8,416,256]{3,2,1,0:T(8,128)(2,1)}, bf16[2,8,416,256]{3,2,1,0:T(8,128)(2,1)}, u32[]{:S(2)}, u32[]{:S(2)}) collective-permute-start(bf16[2,8,416,256]{3,2,1,0:T(8,128)(2,1)} %pad_maximum_fusion), channel_id=1, source_target_pairs={{0,1},{1,0},{2,3},{3,2},{4,5},{5,4},{6,7},{7,6},{8,9},{9,8},{10,11... | collective-permute-start | bytes 10223624 | tf_op jit(solution)/shard_map/ppermute | solution.py:19
  167.0 76.0 %copy-start.2 = (bf16[4,8,208,256]{3,2,1,0:T(8,128)(2,1)}, bf16[4,8,208,256]{3,2,1,0:T(8,128)(2,1)S(1)}, u32[]{:S(2)}) copy-start(bf16[4,8,208,256]{3,2,1,0:T(8,128)(2,1)S(1)} %get-tuple-element.13) | copy-start | bytes 10223620
  167.0 4.7 %copy-start.4 = (bf16[4,4,416,256]{3,2,1,0:T(8,128)(2,1)S(1)}, bf16[4,4,416,256]{3,2,1,0:T(8,128)(2,1)}, u32[]{:S(2)}) copy-start(bf16[4,4,416,256]{3,2,1,0:T(8,128)(2,1)} %all-gather.5.cloned.1.call-done) | copy-start | bytes 10223620
  240.2 2.9 copy-start.6
  240.2 2.9 copy-start.9
  243.1 2.0 copy-start.5
  246.9 4.0 %copy-start.3 = (bf16[4,8,208,256]{3,2,1,0:T(8,128)(2,1)S(1)}, bf16[4,8,208,256]{3,2,1,0:T(8,128)(2,1)}, u32[]{:S(2)}) copy-start(bf16[4,8,208,256]{3,2,1,0:T(8,128)(2,1)} %copy-done.2) | copy-start | bytes 10223620
  252.9 4.5 %copy-start.1 = (bf16[4,8,208,256]{3,2,1,0:T(8,128)(2,1)S(1)}, bf16[4,8,208,256]{3,2,1,0:T(8,128)(2,1)}, u32[]{:S(2)}) copy-start(bf16[4,8,208,256]{3,2,1,0:T(8,128)(2,1)} %get-tuple-element.14) | copy-start | bytes 10223620
  255.0 21.9 %collective-permute-start.3 = (f32[208,2,416]{2,0,1:T(8,128)S(1)}, f32[208,2,416]{2,0,1:T(8,128)S(1)}, u32[]{:S(2)}, u32[]{:S(2)}) collective-permute-start(f32[208,2,416]{2,0,1:T(8,128)S(1)} %pad_maximum_fusion.2), channel_id=1, source_target_pairs={{0,4},{4,0},{1,5},{5,1},{2,6},{6,2},{3,7},{7,3},{8,12},{12,8},{9,1... | collective-permute-start | bytes 2076680 | tf_op jit(solution)/shard_map/ppermute | solution.py:10
  256.7 46.5 %collective-permute-start.4 = (f32[208,3,416]{2,0,1:T(8,128)S(1)}, f32[208,3,416]{2,0,1:T(8,128)S(1)}, u32[]{:S(2)}, u32[]{:S(2)}) collective-permute-start(f32[208,3,416]{2,0,1:T(8,128)S(1)} %pad_maximum_fusion.1), channel_id=1, source_target_pairs={{0,4},{4,0},{1,5},{5,1},{2,6},{6,2},{3,7},{7,3},{8,12},{12,8},{9,1... | collective-permute-start | bytes 3115016 | tf_op jit(solution)/shard_map/ppermute | solution.py:10
Sparse Core Ops, SparseCore 0:
  50.0 92.2 all-gather.4
  159.4 80.6 all-gather.2

commit v19 on v15

--- a/solution.py
+++ b/solution.py
@@ -93,12 +93,14 @@
     rows_out = pair_rows // PAIR
     give_rows = lax.dynamic_slice_in_dim(all_background, (1 - pair_index) * rows_out, rows_out, axis=2)
     keep_rows = lax.dynamic_slice_in_dim(all_background, pair_index * rows_out, rows_out, axis=2)
-    outer = (0, lag_total - 1)
+    first = (0,)
+    second = (lag_total - 1,)
     inner = tuple(range(1, lag_total - 1))
-    sent_outer = swap_pair(lag_block(give_rows, all_analysis, cycle_total, max_lag, outer))
+    sent_first = swap_pair(lag_block(give_rows, all_analysis, cycle_total, max_lag, first))
+    sent_second = swap_pair(lag_block(give_rows, all_analysis, cycle_total, max_lag, second))
     sent_inner = swap_pair(lag_block(give_rows, all_analysis, cycle_total, max_lag, inner))
     own = lag_block(keep_rows, all_analysis, cycle_total, max_lag, range(lag_total))
-    sent = jnp.concatenate([sent_outer[:, :1], sent_inner, sent_outer[:, 1:]], axis=1)
+    sent = jnp.concatenate([sent_first, sent_inner, sent_second], axis=1)
     summed = own + sent
 
     denominators = []

time: 263 us -> 263 us (level)
    ppermute x3 -> x4, starting transfers between devices: 4.2 us -> 5.66 us  [swap_pair(): return lax.ppermute(x, 'th', [(0, 1), (1, 0)])]
    ppermute x3 -> x4, waiting for transfers between devices: 66.5 us -> 65.1 us  [swap_pair(): return lax.ppermute(x, 'th', [(0, 1), (1, 0)])]
  transfers between devices with their start and end apart: 8 -> 9, of which waited for: 5 -> 6; matrix products, arithmetic and copies ran while one was open for 10% -> 10% of each run, Pallas kernels for 0% -> 0%
where the time goes in v19:
time: 263 us
  waiting for transfers between devices  160 us (61%)
  blocking collectives  25.8 us (10%)
  other arithmetic  23.4 us (9%)
  matrix products  18.7 us (7%)
  between operations  15.6 us (6%)
  starting transfers between devices  13.5 us (5%)
  local copies, waits for them, and re-layouts  5.55 us (2%)
    ppermute x4, waiting for transfers between devices, swap_pair(): return lax.ppermute(x, 'th', [(0, 1), (1, 0)])  65.1 us
    all_to_all x1, waiting for transfers between devices, body(): rows_here = lax.all_to_all(by_loc, ('tq', 'th'), 0, 0, tiled=True)  37.7 us
    ppermute x2, waiting for transfers between devices, gather_chan(): got = lax.ppermute(held, 'chan', [(c, c ^ 1 << bit) for c in range(size)])  37.6 us
    all_to_all x1, blocking collectives, body(): by_loc = lax.all_to_all(split_b, 'chan', 2, 0, tiled=True)  25.8 us
    all_gather x1, waiting for transfers between devices, body(): other_parity = lax.all_gather(by_piece(got), 'tq', axis=1, tiled=True)  19.7 us
    dot_general x10, matrix products, contract(): lax.dot_general(left, right, (((0, 1, 3), (0, 1, 3)), ((), ())), preferre...  18.7 us
    select_n x1, other arithmetic, body(): all_analysis = jnp.where(pair_index == 0, in_order, swapped)  6.83 us
    all_to_all x1, starting transfers between devices, body(): rows_here = lax.all_to_all(by_loc, ('tq', 'th'), 0, 0, tiled=True)  6.32 us
  transfers between devices with their start and end apart: 9, of which 6 were waited for; matrix products, arithmetic and copies ran while one was open for 10% of the time, Pallas kernels for 0%

profile of v19, /device:TPU:0, one launch (start us, length us, event | category | flops | bytes accessed | tf_op | source)
XLA Modules:
  0.0 262.6 jit_solution(17162626855421094375)
XLA Ops:
  15.9 25.8 %all_to_all.20 = bf16[416,2,4,256]{3,0,1,2:T(8,128)(2,1)} all-to-all(bf16[416,2,4,256]{3,0,1,2:T(8,128)(2,1)S(1)} %copy_select_fusion), channel_id=1, replica_groups=mesh['tq'=4,'th'=2,'chan'=4] {'chan'}, dimensions={2} | all-to-all | bytes 3407872 | tf_op jit(solution)/shard_map/all_to_all | solution.py:87
  41.7 6.3 %all-to-all-start.1 = ((bf16[8,416,256]{2,1,0:T(8,128)(2,1)}), bf16[8,416,256]{2,1,0:T(8,128)(2,1)S(1)}, u32[]{:S(2)}, u32[]{:S(2)}) async-start(bf16[8,416,256]{2,1,0:T(8,128)(2,1)} %bitcast.4), calls=%async_computation.1 | async-start | bytes 3407872 | tf_op jit(solution)/shard_map/all_to_all | solution.py:90
  48.0 2.0 collective-permute-start.2
  50.1 29.9 %collective-permute-done.2 = bf16[416,1024]{1,0:T(8,128)(2,1)S(1)} collective-permute-done((bf16[416,1024]{1,0:T(8,128)(2,1)S(1)}, bf16[416,1024]{1,0:T(8,128)(2,1)S(1)}, u32[]{:S(2)}, u32[]{:S(2)}) %collective-permute-start.2) | collective-permute-done | bytes 852000 | tf_op jit(solution)/shard_map/ppermute | solution.py:10
  82.1 37.7 %all-to-all-done.1 = bf16[8,416,256]{2,1,0:T(8,128)(2,1)S(1)} async-done(((bf16[8,416,256]{2,1,0:T(8,128)(2,1)}), bf16[8,416,256]{2,1,0:T(8,128)(2,1)S(1)}, u32[]{:S(2)}, u32[]{:S(2)}) %all-to-all-start.1) | async-done | bytes 1703968 | tf_op jit(solution)/shard_map/all_to_all | solution.py:90
  121.2 37.6 %collective-permute-done = bf16[1,8,416,256]{3,2,1,0:T(8,128)(2,1)} collective-permute-done((bf16[1,8,416,256]{3,2,1,0:T(8,128)(2,1)S(1)}, bf16[1,8,416,256]{3,2,1,0:T(8,128)(2,1)}, u32[]{:S(2)}, u32[]{:S(2)}) %collective-permute-start) | collective-permute-done | bytes 1703968 | tf_op jit(solution)/shard_map/ppermute | solution.py:19
  158.9 2.2 broadcast_select_fusion.3
  161.1 2.1 pad_maximum_fusion
  166.6 19.7 %all-gather.5.cloned.1.call-done = bf16[4,4,416,256]{3,2,1,0:T(8,128)(2,1)} async-done(((bf16[4,1,416,256]{3,2,1,0:T(8,128)(2,1)}), bf16[4,4,416,256]{3,2,1,0:T(8,128)(2,1)}) %all-gather.5.cloned.1.call-update) | async-done | bytes 3407888 | tf_op jit(solution)/shard_map/all_gather | solution.py:80
  186.4 6.8 %maximum_select_fusion = bf16[4,4,2,416,256]{4,3,2,1,0:T(8,128)(2,1)S(1)} fusion(bf16[4,4,1,416,256]{4,3,2,1,0:T(8,128)(2,1)} %bitcast.130, bf16[4,4,1,416,256]{4,3,2,1,0:T(8,128)(2,1)} %bitcast.129, pred[]{:T(512)S(6)} %eq.21), kind=kLoop, calls=%fused_computation.4 | loop fusion | flops 10223616 | bytes 13631489 | tf_op jit(solution)/shard_map/jit(_where)/select_n | solution.py:83
  193.2 2.2 broadcast_select_fusion
  196.1 2.2 convolution_bitcast_fusion
  198.3 1.9 fusion.25
  200.2 1.9 fusion.34
  202.2 1.7 fusion.44
  203.8 1.7 fusion.53
  207.2 1.7 fusion.41
  208.9 1.9 fusion.22
  210.8 2.2 fusion.37
  215.1 1.9 fusion.31
  217.0 1.7 fusion.50
  218.7 27.1 %collective-permute-done.3 = f32[208,1,416]{2,0,1:T(8,128)S(1)} collective-permute-done((f32[208,1,416]{2,0,1:T(8,128)S(1)}, f32[208,1,416]{2,0,1:T(8,128)S(1)}, u32[]{:S(2)}, u32[]{:S(2)}) %collective-permute-start.3) | collective-permute-done | bytes 346144 | tf_op jit(solution)/shard_map/ppermute | solution.py:10
  245.8 8.0 %collective-permute-done.5 = f32[208,1,416]{2,0,1:T(8,128)S(1)} collective-permute-done((f32[208,1,416]{2,0,1:T(8,128)S(1)}, f32[208,1,416]{2,0,1:T(8,128)S(1)}, u32[]{:S(2)}, u32[]{:S(2)}) %collective-permute-start.5) | collective-permute-done | bytes 346144 | tf_op jit(solution)/shard_map/ppermute | solution.py:10
  253.8 1.9 fusion.18
  (38 shorter events, 18.8 us)
Async XLA Ops:
  6.5 160.1 %all-gather.3.cloned.1.call-start = ((), (), s32[]{:S(2)}) async-start(), calls=%async_computation.2 | async-start | bytes 4259840 | tf_op jit(solution)/shard_map/all_gather | solution.py:78
  11.1 2.1 copy-start.1
  15.9 32.1 %copy-start.2 = (bf16[416,1024]{1,0:T(8,128)(2,1)S(1)}, bf16[416,1024]{1,0:T(8,128)(2,1)}, u32[]{:S(2)}) copy-start(bf16[416,1024]{1,0:T(8,128)(2,1)} %get-tuple-element.14) | copy-start | bytes 2555908
  41.7 78.1 %all-to-all-start.1 = ((bf16[8,416,256]{2,1,0:T(8,128)(2,1)}), bf16[8,416,256]{2,1,0:T(8,128)(2,1)S(1)}, u32[]{:S(2)}, u32[]{:S(2)}) async-start(bf16[8,416,256]{2,1,0:T(8,128)(2,1)} %bitcast.4), calls=%async_computation.1 | async-start | bytes 3407872 | tf_op jit(solution)/shard_map/all_to_all | solution.py:90
  48.0 138.4 %all-gather.5.cloned.1.call-start = ((), (), s32[]{:S(2)}) async-start(), calls=%async_computation.3 | async-start | bytes 4259840 | tf_op jit(solution)/shard_map/all_gather | solution.py:80
  48.0 32.0 %collective-permute-start.2 = (bf16[416,1024]{1,0:T(8,128)(2,1)S(1)}, bf16[416,1024]{1,0:T(8,128)(2,1)S(1)}, u32[]{:S(2)}, u32[]{:S(2)}) collective-permute-start(bf16[416,1024]{1,0:T(8,128)(2,1)S(1)} %copy-done.2), channel_id=1, source_target_pairs={{0,4},{4,0},{1,5},{5,1},{2,6},{6,2},{3,7},{7,3},{8,12},{12,8},{9,1... | collective-permute-start | bytes 2555912 | tf_op jit(solution)/shard_map/ppermute | solution.py:10
  119.8 1.4 copy-start
  119.8 39.1 %collective-permute-start = (bf16[1,8,416,256]{3,2,1,0:T(8,128)(2,1)S(1)}, bf16[1,8,416,256]{3,2,1,0:T(8,128)(2,1)}, u32[]{:S(2)}, u32[]{:S(2)}) collective-permute-start(bf16[1,8,416,256]{3,2,1,0:T(8,128)(2,1)S(1)} %bitcast.124), channel_id=1, source_target_pairs={{0,2},{1,3},{2,0},{3,1},{4,6},{5,7},{6,4},{7,5},{8,10},{9,11},{10,... | collective-permute-start | bytes 5111816 | tf_op jit(solution)/shard_map/ppermute | solution.py:19
  161.1 2.7 %copy-start.3 = (s32[8]{0:T(128)S(1)}, s32[8]{0:T(128)}, u32[]{:S(2)}) copy-start(s32[8]{0:T(128)} %param.5) | copy-start | bytes 100
  163.2 30.0 %collective-permute-start.1 = (bf16[2,8,416,256]{3,2,1,0:T(8,128)(2,1)}, bf16[2,8,416,256]{3,2,1,0:T(8,128)(2,1)}, u32[]{:S(2)}, u32[]{:S(2)}) collective-permute-start(bf16[2,8,416,256]{3,2,1,0:T(8,128)(2,1)} %pad_maximum_fusion), channel_id=1, source_target_pairs={{0,1},{1,0},{2,3},{3,2},{4,5},{5,4},{6,7},{7,6},{8,9},{9,8},{10,11... | collective-permute-start | bytes 10223624 | tf_op jit(solution)/shard_map/ppermute | solution.py:19
  205.7 48.1 %collective-permute-start.4 = (f32[208,3,416]{2,0,1:T(8,128)S(1)}, f32[208,3,416]{2,0,1:T(8,128)S(1)}, u32[]{:S(2)}, u32[]{:S(2)}) collective-permute-start(f32[208,3,416]{2,0,1:T(8,128)S(1)} %pad_maximum_fusion.1), channel_id=1, source_target_pairs={{0,4},{4,0},{1,5},{5,1},{2,6},{6,2},{3,7},{7,3},{8,12},{12,8},{9,1... | collective-permute-start | bytes 3115016 | tf_op jit(solution)/shard_map/ppermute | solution.py:10
  213.0 32.9 %collective-permute-start.3 = (f32[208,1,416]{2,0,1:T(8,128)S(1)}, f32[208,1,416]{2,0,1:T(8,128)S(1)}, u32[]{:S(2)}, u32[]{:S(2)}) collective-permute-start(f32[208,1,416]{2,0,1:T(8,128)S(1)} %fusion.44), channel_id=1, source_target_pairs={{0,4},{4,0},{1,5},{5,1},{2,6},{6,2},{3,7},{7,3},{8,12},{12,8},{9,1... | collective-permute-start | bytes 1038344 | tf_op jit(solution)/shard_map/ppermute | solution.py:10
  213.6 40.2 %collective-permute-start.5 = (f32[208,1,416]{2,0,1:T(8,128)S(1)}, f32[208,1,416]{2,0,1:T(8,128)S(1)}, u32[]{:S(2)}, u32[]{:S(2)}) collective-permute-start(f32[208,1,416]{2,0,1:T(8,128)S(1)} %fusion.53), channel_id=1, source_target_pairs={{0,4},{4,0},{1,5},{5,1},{2,6},{6,2},{3,7},{7,3},{8,12},{12,8},{9,1... | collective-permute-start | bytes 1038344 | tf_op jit(solution)/shard_map/ppermute | solution.py:10
Sparse Core Ops, SparseCore 0:
  13.4 104.5 all-gather.2
  119.6 66.7 all-gather.4

commit v20 on v19

--- a/solution.py
+++ b/solution.py
@@ -96,7 +96,11 @@
     first = (0,)
     second = (lag_total - 1,)
     inner = tuple(range(1, lag_total - 1))
-    sent_first = swap_pair(lag_block(give_rows, all_analysis, cycle_total, max_lag, first))
+    first_partial = lag_block(give_rows, all_analysis, cycle_total, max_lag, first)
+    first_partial, all_analysis, give_rows, keep_rows = lax.optimization_barrier(
+        (first_partial, all_analysis, give_rows, keep_rows)
+    )
+    sent_first = swap_pair(first_partial)
     sent_second = swap_pair(lag_block(give_rows, all_analysis, cycle_total, max_lag, second))
     sent_inner = swap_pair(lag_block(give_rows, all_analysis, cycle_total, max_lag, inner))
     own = lag_block(keep_rows, all_analysis, cycle_total, max_lag, range(lag_total))

time: 263 us -> 263 us (level)
  no operation moved by 1% of the time
where the time goes in v20:
time: 263 us
  waiting for transfers between devices  160 us (61%)
  blocking collectives  25.8 us (10%)
  other arithmetic  23.4 us (9%)
  matrix products  18.7 us (7%)
  between operations  15.6 us (6%)
  starting transfers between devices  13.5 us (5%)
  local copies, waits for them, and re-layouts  5.55 us (2%)
    ppermute x4, waiting for transfers between devices, swap_pair(): return lax.ppermute(x, 'th', [(0, 1), (1, 0)])  65.1 us
    all_to_all x1, waiting for transfers between devices, body(): rows_here = lax.all_to_all(by_loc, ('tq', 'th'), 0, 0, tiled=True)  37.7 us
    ppermute x2, waiting for transfers between devices, gather_chan(): got = lax.ppermute(held, 'chan', [(c, c ^ 1 << bit) for c in range(size)])  37.6 us
    all_to_all x1, blocking collectives, body(): by_loc = lax.all_to_all(split_b, 'chan', 2, 0, tiled=True)  25.8 us
    all_gather x1, waiting for transfers between devices, body(): other_parity = lax.all_gather(by_piece(got), 'tq', axis=1, tiled=True)  19.7 us
    dot_general x10, matrix products, contract(): lax.dot_general(left, right, (((0, 1, 3), (0, 1, 3)), ((), ())), preferre...  18.7 us
    select_n x1, other arithmetic, body(): all_analysis = jnp.where(pair_index == 0, in_order, swapped)  6.83 us
    all_to_all x1, starting transfers between devices, body(): rows_here = lax.all_to_all(by_loc, ('tq', 'th'), 0, 0, tiled=True)  6.32 us
  transfers between devices with their start and end apart: 9, of which 6 were waited for; matrix products, arithmetic and copies ran while one was open for 10% of the time, Pallas kernels for 0%

profile of v20, /device:TPU:0, one launch (start us, length us, event | category | flops | bytes accessed | tf_op | source)
XLA Modules:
  0.0 262.6 jit_solution(1113094250337948347)
XLA Ops:
  15.9 25.8 %all_to_all.20 = bf16[416,2,4,256]{3,0,1,2:T(8,128)(2,1)} all-to-all(bf16[416,2,4,256]{3,0,1,2:T(8,128)(2,1)S(1)} %copy_select_fusion), channel_id=1, replica_groups=mesh['tq'=4,'th'=2,'chan'=4] {'chan'}, dimensions={2} | all-to-all | bytes 3407872 | tf_op jit(solution)/shard_map/all_to_all | solution.py:87
  41.7 6.3 %all-to-all-start.1 = ((bf16[8,416,256]{2,1,0:T(8,128)(2,1)}), bf16[8,416,256]{2,1,0:T(8,128)(2,1)S(1)}, u32[]{:S(2)}, u32[]{:S(2)}) async-start(bf16[8,416,256]{2,1,0:T(8,128)(2,1)} %bitcast.4), calls=%async_computation.1 | async-start | bytes 3407872 | tf_op jit(solution)/shard_map/all_to_all | solution.py:90
  48.0 2.0 collective-permute-start.2
  50.1 29.9 %collective-permute-done.2 = bf16[416,1024]{1,0:T(8,128)(2,1)S(1)} collective-permute-done((bf16[416,1024]{1,0:T(8,128)(2,1)S(1)}, bf16[416,1024]{1,0:T(8,128)(2,1)S(1)}, u32[]{:S(2)}, u32[]{:S(2)}) %collective-permute-start.2) | collective-permute-done | bytes 852000 | tf_op jit(solution)/shard_map/ppermute | solution.py:10
  82.1 37.7 %all-to-all-done.1 = bf16[8,416,256]{2,1,0:T(8,128)(2,1)S(1)} async-done(((bf16[8,416,256]{2,1,0:T(8,128)(2,1)}), bf16[8,416,256]{2,1,0:T(8,128)(2,1)S(1)}, u32[]{:S(2)}, u32[]{:S(2)}) %all-to-all-start.1) | async-done | bytes 1703968 | tf_op jit(solution)/shard_map/all_to_all | solution.py:90
  121.2 37.6 %collective-permute-done = bf16[1,8,416,256]{3,2,1,0:T(8,128)(2,1)} collective-permute-done((bf16[1,8,416,256]{3,2,1,0:T(8,128)(2,1)S(1)}, bf16[1,8,416,256]{3,2,1,0:T(8,128)(2,1)}, u32[]{:S(2)}, u32[]{:S(2)}) %collective-permute-start) | collective-permute-done | bytes 1703968 | tf_op jit(solution)/shard_map/ppermute | solution.py:19
  158.9 2.2 broadcast_select_fusion.3
  161.1 2.1 pad_maximum_fusion
  166.6 19.7 %all-gather.5.cloned.1.call-done = bf16[4,4,416,256]{3,2,1,0:T(8,128)(2,1)} async-done(((bf16[4,1,416,256]{3,2,1,0:T(8,128)(2,1)}), bf16[4,4,416,256]{3,2,1,0:T(8,128)(2,1)}) %all-gather.5.cloned.1.call-update) | async-done | bytes 3407888 | tf_op jit(solution)/shard_map/all_gather | solution.py:80
  186.4 6.8 %maximum_select_fusion = bf16[4,4,2,416,256]{4,3,2,1,0:T(8,128)(2,1)S(1)} fusion(bf16[4,4,1,416,256]{4,3,2,1,0:T(8,128)(2,1)} %bitcast.130, bf16[4,4,1,416,256]{4,3,2,1,0:T(8,128)(2,1)} %bitcast.129, pred[]{:T(512)S(6)} %eq.21), kind=kLoop, calls=%fused_computation.4 | loop fusion | flops 10223616 | bytes 13631489 | tf_op jit(solution)/shard_map/jit(_where)/select_n | solution.py:83
  193.2 2.2 broadcast_select_fusion
  196.1 1.7 fusion.53
  197.8 1.9 fusion.25
  199.8 2.2 convolution_bitcast_fusion
  201.9 1.9 fusion.34
  203.9 1.7 fusion.44
  207.7 1.7 fusion.50
  209.4 1.9 fusion.22
  211.4 2.2 fusion.37
  215.1 1.9 fusion.31
  217.0 1.7 fusion.41
  218.7 27.1 %collective-permute-done.5 = f32[208,1,416]{2,0,1:T(8,128)S(1)} collective-permute-done((f32[208,1,416]{2,0,1:T(8,128)S(1)}, f32[208,1,416]{2,0,1:T(8,128)S(1)}, u32[]{:S(2)}, u32[]{:S(2)}) %collective-permute-start.5) | collective-permute-done | bytes 346144 | tf_op jit(solution)/shard_map/ppermute | solution.py:10
  245.8 8.0 %collective-permute-done.3 = f32[208,1,416]{2,0,1:T(8,128)S(1)} collective-permute-done((f32[208,1,416]{2,0,1:T(8,128)S(1)}, f32[208,1,416]{2,0,1:T(8,128)S(1)}, u32[]{:S(2)}, u32[]{:S(2)}) %collective-permute-start.3) | collective-permute-done | bytes 346144 | tf_op jit(solution)/shard_map/ppermute | solution.py:10
  253.8 1.9 fusion.18
  (38 shorter events, 18.8 us)
Async XLA Ops:
  6.5 160.1 %all-gather.3.cloned.1.call-start = ((), (), s32[]{:S(2)}) async-start(), calls=%async_computation.2 | async-start | bytes 4259840 | tf_op jit(solution)/shard_map/all_gather | solution.py:78
  11.1 2.1 copy-start.1
  15.9 32.1 %copy-start.2 = (bf16[416,1024]{1,0:T(8,128)(2,1)S(1)}, bf16[416,1024]{1,0:T(8,128)(2,1)}, u32[]{:S(2)}) copy-start(bf16[416,1024]{1,0:T(8,128)(2,1)} %get-tuple-element.22) | copy-start | bytes 2555908
  41.7 78.1 %all-to-all-start.1 = ((bf16[8,416,256]{2,1,0:T(8,128)(2,1)}), bf16[8,416,256]{2,1,0:T(8,128)(2,1)S(1)}, u32[]{:S(2)}, u32[]{:S(2)}) async-start(bf16[8,416,256]{2,1,0:T(8,128)(2,1)} %bitcast.4), calls=%async_computation.1 | async-start | bytes 3407872 | tf_op jit(solution)/shard_map/all_to_all | solution.py:90
  48.0 138.4 %all-gather.5.cloned.1.call-start = ((), (), s32[]{:S(2)}) async-start(), calls=%async_computation.3 | async-start | bytes 4259840 | tf_op jit(solution)/shard_map/all_gather | solution.py:80
  48.0 32.0 %collective-permute-start.2 = (bf16[416,1024]{1,0:T(8,128)(2,1)S(1)}, bf16[416,1024]{1,0:T(8,128)(2,1)S(1)}, u32[]{:S(2)}, u32[]{:S(2)}) collective-permute-start(bf16[416,1024]{1,0:T(8,128)(2,1)S(1)} %copy-done.2), channel_id=1, source_target_pairs={{0,4},{4,0},{1,5},{5,1},{2,6},{6,2},{3,7},{7,3},{8,12},{12,8},{9,1... | collective-permute-start | bytes 2555912 | tf_op jit(solution)/shard_map/ppermute | solution.py:10
  119.8 1.4 copy-start
  119.8 39.1 %collective-permute-start = (bf16[1,8,416,256]{3,2,1,0:T(8,128)(2,1)S(1)}, bf16[1,8,416,256]{3,2,1,0:T(8,128)(2,1)}, u32[]{:S(2)}, u32[]{:S(2)}) collective-permute-start(bf16[1,8,416,256]{3,2,1,0:T(8,128)(2,1)S(1)} %bitcast.124), channel_id=1, source_target_pairs={{0,2},{1,3},{2,0},{3,1},{4,6},{5,7},{6,4},{7,5},{8,10},{9,11},{10,... | collective-permute-start | bytes 5111816 | tf_op jit(solution)/shard_map/ppermute | solution.py:19
  161.1 2.7 %copy-start.3 = (s32[8]{0:T(128)S(1)}, s32[8]{0:T(128)}, u32[]{:S(2)}) copy-start(s32[8]{0:T(128)} %param.5) | copy-start | bytes 100
  163.2 30.0 %collective-permute-start.1 = (bf16[2,8,416,256]{3,2,1,0:T(8,128)(2,1)}, bf16[2,8,416,256]{3,2,1,0:T(8,128)(2,1)}, u32[]{:S(2)}, u32[]{:S(2)}) collective-permute-start(bf16[2,8,416,256]{3,2,1,0:T(8,128)(2,1)} %pad_maximum_fusion), channel_id=1, source_target_pairs={{0,1},{1,0},{2,3},{3,2},{4,5},{5,4},{6,7},{7,6},{8,9},{9,8},{10,11... | collective-permute-start | bytes 10223624 | tf_op jit(solution)/shard_map/ppermute | solution.py:19
  205.6 48.2 %collective-permute-start.4 = (f32[208,3,416]{2,0,1:T(8,128)S(1)}, f32[208,3,416]{2,0,1:T(8,128)S(1)}, u32[]{:S(2)}, u32[]{:S(2)}) collective-permute-start(f32[208,3,416]{2,0,1:T(8,128)S(1)} %pad_maximum_fusion.1), channel_id=1, source_target_pairs={{0,4},{4,0},{1,5},{5,1},{2,6},{6,2},{3,7},{7,3},{8,12},{12,8},{9,1... | collective-permute-start | bytes 3115016 | tf_op jit(solution)/shard_map/ppermute | solution.py:10
  207.2 38.6 %collective-permute-start.5 = (f32[208,1,416]{2,0,1:T(8,128)S(1)}, f32[208,1,416]{2,0,1:T(8,128)S(1)}, u32[]{:S(2)}, u32[]{:S(2)}) collective-permute-start(f32[208,1,416]{2,0,1:T(8,128)S(1)} %fusion.44), channel_id=1, source_target_pairs={{0,4},{4,0},{1,5},{5,1},{2,6},{6,2},{3,7},{7,3},{8,12},{12,8},{9,1... | collective-permute-start | bytes 1038344 | tf_op jit(solution)/shard_map/ppermute | solution.py:10
  213.5 40.3 %collective-permute-start.3 = (f32[208,1,416]{2,0,1:T(8,128)S(1)}, f32[208,1,416]{2,0,1:T(8,128)S(1)}, u32[]{:S(2)}, u32[]{:S(2)}) collective-permute-start(f32[208,1,416]{2,0,1:T(8,128)S(1)} %fusion.53), channel_id=1, source_target_pairs={{0,4},{4,0},{1,5},{5,1},{2,6},{6,2},{3,7},{7,3},{8,12},{12,8},{9,1... | collective-permute-start | bytes 1038344 | tf_op jit(solution)/shard_map/ppermute | solution.py:10
Sparse Core Ops, SparseCore 0:
  13.4 104.5 all-gather.2
  119.6 66.7 all-gather.4

commit v21 on v20

--- a/solution.py
+++ b/solution.py
@@ -27,6 +27,20 @@
     shape = x.shape[:axis] + (2,) * bits + x.shape[axis + 1:]
     order = list(range(axis)) + [axis + bits - 1 - k for k in range(bits)] + list(range(axis + bits, len(shape)))
     return x.reshape(shape).transpose(order).reshape(x.shape)
+
+
+def relay_gather(block, size):
+    me = lax.axis_index("tq")
+    from_left = from_right = block
+    lefts, rights = [], []
+    for _ in range(size - 1):
+        from_left = lax.ppermute(from_left, "tq", [(i, i + 1) for i in range(size - 1)])
+        from_right = lax.ppermute(from_right, "tq", [(i + 1, i) for i in range(size - 1)])
+        lefts.append(from_left)
+        rights.append(from_right)
+    stacked = jnp.concatenate(lefts[::-1] + [block] + rights, axis=1)
+    width = block.shape[1]
+    return lax.dynamic_slice_in_dim(stacked, (size - 1 - me) * width, size * width, axis=1)
 
 
 def contract(left, right):
@@ -77,7 +91,7 @@
 
     same_parity = lax.all_gather(by_piece(keep), "tq", axis=1, tiled=True)
     got = swap_pair(give)
-    other_parity = lax.all_gather(by_piece(got), "tq", axis=1, tiled=True)
+    other_parity = relay_gather(by_piece(got), quad_size)
     in_order = jnp.stack([same_parity, other_parity], axis=2)
     swapped = jnp.stack([other_parity, same_parity], axis=2)
     all_analysis = jnp.where(pair_index == 0, in_order, swapped)

time: 263 us -> 290 us (1.10)
  starting transfers between devices: 13.5 us -> 32.8 us
  local copies, waits for them, and re-layouts: 5.55 us -> 19.9 us
  waiting for transfers between devices: 160 us -> 153 us
    ppermute x0 -> x6, waiting for transfers between devices: none -> 60.5 us  [the longest x3 50.4 us: relay_gather(): lax.ppermute(from_left, 'tq', [(i, i + 1) for i in range(size - 1)])]
    ppermute x2, waiting for transfers between devices: 37.6 us -> 0.01 us  [gather_chan(): got = lax.ppermute(held, 'chan', [(c, c ^ 1 << bit) for c in range(size)])]
    ppermute x4, waiting for transfers between devices: 65.1 us -> 34.3 us  [swap_pair(): return lax.ppermute(x, 'th', [(0, 1), (1, 0)])]
    ppermute x0 -> x6, starting transfers between devices: none -> 20.7 us  [the longest x3 16.8 us: relay_gather(): lax.ppermute(from_left, 'tq', [(i, i + 1) for i in range(size - 1)])]
    all_to_all x1, waiting for transfers between devices: 37.7 us -> 58.3 us  [body(): rows_here = lax.all_to_all(by_loc, ('tq', 'th'), 0, 0, tiled=True)]
    all_gather x1 -> x0, waiting for transfers between devices: 19.7 us -> none  [body(): other_parity = lax.all_gather(by_piece(got), 'tq', axis=1, tiled=True)]
    unnamed x8 -> x14, local copies, waits for them, and re-layouts: 0.02 us -> 7.03 us
  transfers between devices with their start and end apart: 9 -> 14, of which waited for: 6 -> 8; matrix products, arithmetic and copies ran while one was open for 10% -> 14% of each run, Pallas kernels for 0% -> 0%
where the time goes in v21:
time: 290 us; the launch traced here: 289 us
  waiting for transfers between devices  153 us (53%)
  starting transfers between devices  32.8 us (11%)
  blocking collectives  25.6 us (9%)
  other arithmetic  23.6 us (8%)
  local copies, waits for them, and re-layouts  19.9 us (7%)
  matrix products  18.8 us (6%)
  between operations  15.5 us (5%)
    all_to_all x1, waiting for transfers between devices, body(): rows_here = lax.all_to_all(by_loc, ('tq', 'th'), 0, 0, tiled=True)  58.3 us
    ppermute x3, waiting for transfers between devices, relay_gather(): lax.ppermute(from_left, 'tq', [(i, i + 1) for i in range(size - 1)])  50.4 us
    ppermute x4, waiting for transfers between devices, swap_pair(): return lax.ppermute(x, 'th', [(0, 1), (1, 0)])  34.3 us
    all_to_all x1, blocking collectives, body(): by_loc = lax.all_to_all(split_b, 'chan', 2, 0, tiled=True)  25.6 us
    dot_general x10, matrix products, contract(): lax.dot_general(left, right, (((0, 1, 3), (0, 1, 3)), ((), ())), preferre...  18.8 us
    ppermute x3, starting transfers between devices, relay_gather(): lax.ppermute(from_left, 'tq', [(i, i + 1) for i in range(size - 1)])  16.8 us
    ppermute x3, waiting for transfers between devices, relay_gather(): lax.ppermute(from_right, 'tq', [(i + 1, i) for i in range(size - 1)])  10.1 us
    unnamed x14, local copies, waits for them, and re-layouts  7.03 us
  transfers between devices with their start and end apart: 14, of which 8 were waited for; matrix products, arithmetic and copies ran while one was open for 14% of the time, Pallas kernels for 0%

profile of v21, /device:TPU:0, one launch (start us, length us, event | category | flops | bytes accessed | tf_op | source)
XLA Modules:
  0.0 289.3 jit_solution(17918508686537502871)
XLA Ops:
  8.5 3.9 %squeeze.6 = bf16[416,2,4,256]{3,2,1,0:T(4,128)(2,1)S(1)} reshape(bf16[1,416,2048]{2,1,0:T(8,128)(2,1)} %param.4) | data formatting | bytes 3407872 | tf_op jit(solution)/shard_map/squeeze | solution.py:82
  13.1 25.6 %all_to_all.20 = bf16[416,2,4,256]{3,0,1,2:T(8,128)(2,1)} all-to-all(bf16[416,2,4,256]{3,0,1,2:T(8,128)(2,1)S(1)} %copy_select_fusion), channel_id=1, replica_groups=mesh['tq'=4,'th'=2,'chan'=4] {'chan'}, dimensions={2} | all-to-all | bytes 3407872 | tf_op jit(solution)/shard_map/all_to_all | solution.py:101
  38.8 6.3 %all-to-all-start.1 = ((bf16[8,416,256]{2,1,0:T(8,128)(2,1)}), bf16[8,416,256]{2,1,0:T(8,128)(2,1)S(1)}, u32[]{:S(2)}, u32[]{:S(2)}) async-start(bf16[8,416,256]{2,1,0:T(8,128)(2,1)} %bitcast.4), calls=%async_computation.1 | async-start | bytes 3407872 | tf_op jit(solution)/shard_map/all_to_all | solution.py:104
  48.7 2.0 reshape.39
  52.2 2.0 collective-permute-start.2
  54.2 58.3 %all-to-all-done.1 = bf16[8,416,256]{2,1,0:T(8,128)(2,1)S(1)} async-done(((bf16[8,416,256]{2,1,0:T(8,128)(2,1)}), bf16[8,416,256]{2,1,0:T(8,128)(2,1)S(1)}, u32[]{:S(2)}, u32[]{:S(2)}) %all-to-all-start.1) | async-done | bytes 1703968 | tf_op jit(solution)/shard_map/all_to_all | solution.py:104
  115.0 3.7 %collective-permute-start.3 = (bf16[4,1,416,256]{3,2,1,0:T(8,128)(2,1)}, bf16[4,1,416,256]{3,2,1,0:T(8,128)(2,1)}, u32[]{:S(2)}, u32[]{:S(2)}) collective-permute-start(bf16[4,1,416,256]{3,2,1,0:T(8,128)(2,1)} %bitcast.13), channel_id=1, source_target_pairs={{0,8},{8,16},{16,24},{1,9},{9,17},{17,25},{2,10},{10,18},{18,26},{... | collective-permute-start | bytes 2555912 | tf_op jit(solution)/shard_map/ppermute | solution.py:37
  120.0 31.7 %collective-permute-done.3 = bf16[4,1,416,256]{3,2,1,0:T(8,128)(2,1)} collective-permute-done((bf16[4,1,416,256]{3,2,1,0:T(8,128)(2,1)}, bf16[4,1,416,256]{3,2,1,0:T(8,128)(2,1)}, u32[]{:S(2)}, u32[]{:S(2)}) %collective-permute-start.3) | collective-permute-done | bytes 852000 | tf_op jit(solution)/shard_map/ppermute | solution.py:37
  151.6 7.8 %collective-permute-start.4 = (bf16[4,1,416,256]{3,2,1,0:T(8,128)(2,1)}, bf16[4,1,416,256]{3,2,1,0:T(8,128)(2,1)}, u32[]{:S(2)}, u32[]{:S(2)}) collective-permute-start(bf16[4,1,416,256]{3,2,1,0:T(8,128)(2,1)} %collective-permute-done.3), channel_id=1, source_target_pairs={{0,8},{8,16},{16,24},{1,9},{9,17},{17,25},{2,10},{10,18},{18,26},{... | collective-permute-start | bytes 2555912 | tf_op jit(solution)/shard_map/ppermute | solution.py:37
  159.5 2.2 broadcast_select_fusion.3
  161.7 2.1 pad_maximum_fusion
  165.9 11.2 %collective-permute-done.4 = bf16[4,1,416,256]{3,2,1,0:T(8,128)(2,1)} collective-permute-done((bf16[4,1,416,256]{3,2,1,0:T(8,128)(2,1)}, bf16[4,1,416,256]{3,2,1,0:T(8,128)(2,1)}, u32[]{:S(2)}, u32[]{:S(2)}) %collective-permute-start.4) | collective-permute-done | bytes 852000 | tf_op jit(solution)/shard_map/ppermute | solution.py:37
  177.2 5.3 %collective-permute-start.5 = (bf16[4,1,416,256]{3,2,1,0:T(8,128)(2,1)}, bf16[4,1,416,256]{3,2,1,0:T(8,128)(2,1)}, u32[]{:S(2)}, u32[]{:S(2)}) collective-permute-start(bf16[4,1,416,256]{3,2,1,0:T(8,128)(2,1)} %collective-permute-done.4), channel_id=1, source_target_pairs={{0,8},{8,16},{16,24},{1,9},{9,17},{17,25},{2,10},{10,18},{18,26},{... | collective-permute-start | bytes 2555912 | tf_op jit(solution)/shard_map/ppermute | solution.py:37
  183.2 4.8 %collective-permute-done.7 = bf16[4,1,416,256]{3,2,1,0:T(8,128)(2,1)} collective-permute-done((bf16[4,1,416,256]{3,2,1,0:T(8,128)(2,1)S(1)}, bf16[4,1,416,256]{3,2,1,0:T(8,128)(2,1)}, u32[]{:S(2)}, u32[]{:S(2)}) %collective-permute-start.7) | collective-permute-done | bytes 852000 | tf_op jit(solution)/shard_map/ppermute | solution.py:38
  191.8 7.5 %collective-permute-done.5 = bf16[4,1,416,256]{3,2,1,0:T(8,128)(2,1)} collective-permute-done((bf16[4,1,416,256]{3,2,1,0:T(8,128)(2,1)}, bf16[4,1,416,256]{3,2,1,0:T(8,128)(2,1)}, u32[]{:S(2)}, u32[]{:S(2)}) %collective-permute-start.5) | collective-permute-done | bytes 852000 | tf_op jit(solution)/shard_map/ppermute | solution.py:37
  205.5 5.3 %collective-permute-done.8 = bf16[4,1,416,256]{3,2,1,0:T(8,128)(2,1)} collective-permute-done((bf16[4,1,416,256]{3,2,1,0:T(8,128)(2,1)}, bf16[4,1,416,256]{3,2,1,0:T(8,128)(2,1)}, u32[]{:S(2)}, u32[]{:S(2)}) %collective-permute-start.8) | collective-permute-done | bytes 852000 | tf_op jit(solution)/shard_map/ppermute | solution.py:38
  212.0 2.1 dynamic-slice_bitcast_fusion
  214.1 6.9 %maximum_select_fusion = bf16[4,4,2,416,256]{4,3,2,1,0:T(8,128)(2,1)S(1)} fusion(bf16[4,4,1,416,256]{4,3,2,1,0:T(8,128)(2,1)} %dynamic-slice_bitcast_fusion, bf16[4,4,1,416,256]{4,3,2,1,0:T(8,128)(2,1)} %bitcast.129, pred[]{:T(512)S(6)} %eq.21), kind=kLoop, calls=%fused_computation.4 | loop fusion | flops 10223616 | bytes 13631489 | tf_op jit(solution)/shard_map/jit(_where)/select_n | solution.py:97
  221.0 2.2 broadcast_select_fusion
  227.5 2.2 convolution_bitcast_fusion
  239.1 2.2 fusion.37
  242.6 1.9 fusion.31
  246.2 27.4 %collective-permute-done.11 = f32[208,1,416]{2,0,1:T(8,128)S(1)} collective-permute-done((f32[208,1,416]{2,0,1:T(8,128)S(1)}, f32[208,1,416]{2,0,1:T(8,128)S(1)}, u32[]{:S(2)}, u32[]{:S(2)}) %collective-permute-start.11) | collective-permute-done | bytes 346144 | tf_op jit(solution)/shard_map/ppermute | solution.py:10
  273.6 6.9 %collective-permute-done.9 = f32[208,1,416]{2,0,1:T(8,128)S(1)} collective-permute-done((f32[208,1,416]{2,0,1:T(8,128)S(1)}, f32[208,1,416]{2,0,1:T(8,128)S(1)}, u32[]{:S(2)}, u32[]{:S(2)}) %collective-permute-start.9) | collective-permute-done | bytes 346144 | tf_op jit(solution)/shard_map/ppermute | solution.py:10
  (55 shorter events, 42.3 us)
Async XLA Ops:
  38.8 73.8 %all-to-all-start.1 = ((bf16[8,416,256]{2,1,0:T(8,128)(2,1)}), bf16[8,416,256]{2,1,0:T(8,128)(2,1)S(1)}, u32[]{:S(2)}, u32[]{:S(2)}) async-start(bf16[8,416,256]{2,1,0:T(8,128)(2,1)} %bitcast.4), calls=%async_computation.1 | async-start | bytes 3407872 | tf_op jit(solution)/shard_map/all_to_all | solution.py:104
  45.1 169.0 %all-gather.2.cloned.1.call-start = ((), (), s32[]{:S(2)}) async-start(), calls=%async_computation.2 | async-start | bytes 4259840 | tf_op jit(solution)/shard_map/all_gather | solution.py:92
  52.2 60.7 %collective-permute-start.2 = (bf16[416,1024]{1,0:T(8,128)(2,1)}, bf16[416,1024]{1,0:T(8,128)(2,1)S(1)}, u32[]{:S(2)}, u32[]{:S(2)}) collective-permute-start(bf16[416,1024]{1,0:T(8,128)(2,1)} %get-tuple-element.22), channel_id=1, source_target_pairs={{0,4},{4,0},{1,5},{5,1},{2,6},{6,2},{3,7},{7,3},{8,12},{12,8},{9,1... | collective-permute-start | bytes 2555912 | tf_op jit(solution)/shard_map/ppermute | solution.py:10
  112.5 46.9 %copy-start = (bf16[8,416,256]{2,1,0:T(8,128)(2,1)}, bf16[8,416,256]{2,1,0:T(8,128)(2,1)S(1)}, u32[]{:S(2)}) copy-start(bf16[8,416,256]{2,1,0:T(8,128)(2,1)S(1)} %all-to-all-done.1) | copy-start | bytes 5111812
  112.5 46.9 %collective-permute-start = (bf16[1,8,416,256]{3,2,1,0:T(8,128)(2,1)S(1)}, bf16[1,8,416,256]{3,2,1,0:T(8,128)(2,1)}, u32[]{:S(2)}, u32[]{:S(2)}) collective-permute-start(bf16[1,8,416,256]{3,2,1,0:T(8,128)(2,1)S(1)} %bitcast.124), channel_id=1, source_target_pairs={{0,2},{1,3},{2,0},{3,1},{4,6},{5,7},{6,4},{7,5},{8,10},{9,11},{10,... | collective-permute-start | bytes 5111816 | tf_op jit(solution)/shard_map/ppermute | solution.py:19
  115.0 36.7 %collective-permute-start.3 = (bf16[4,1,416,256]{3,2,1,0:T(8,128)(2,1)}, bf16[4,1,416,256]{3,2,1,0:T(8,128)(2,1)}, u32[]{:S(2)}, u32[]{:S(2)}) collective-permute-start(bf16[4,1,416,256]{3,2,1,0:T(8,128)(2,1)} %bitcast.13), channel_id=1, source_target_pairs={{0,8},{8,16},{16,24},{1,9},{9,17},{17,25},{2,10},{10,18},{18,26},{... | collective-permute-start | bytes 2555912 | tf_op jit(solution)/shard_map/ppermute | solution.py:37
  118.7 45.1 %collective-permute-start.6 = (bf16[4,1,416,256]{3,2,1,0:T(8,128)(2,1)}, bf16[4,1,416,256]{3,2,1,0:T(8,128)(2,1)S(1)}, u32[]{:S(2)}, u32[]{:S(2)}) collective-permute-start(bf16[4,1,416,256]{3,2,1,0:T(8,128)(2,1)} %bitcast.13), channel_id=1, source_target_pairs={{8,0},{16,8},{24,16},{9,1},{17,9},{25,17},{10,2},{18,10},{26,18},{... | collective-permute-start | bytes 2555912 | tf_op jit(solution)/shard_map/ppermute | solution.py:38
  151.6 25.5 %collective-permute-start.4 = (bf16[4,1,416,256]{3,2,1,0:T(8,128)(2,1)}, bf16[4,1,416,256]{3,2,1,0:T(8,128)(2,1)}, u32[]{:S(2)}, u32[]{:S(2)}) collective-permute-start(bf16[4,1,416,256]{3,2,1,0:T(8,128)(2,1)} %collective-permute-done.3), channel_id=1, source_target_pairs={{0,8},{8,16},{16,24},{1,9},{9,17},{17,25},{2,10},{10,18},{18,26},{... | collective-permute-start | bytes 2555912 | tf_op jit(solution)/shard_map/ppermute | solution.py:37
  161.7 20.8 %copy-start.3 = (s32[8]{0:T(128)S(1)}, s32[8]{0:T(128)}, u32[]{:S(2)}) copy-start(s32[8]{0:T(128)} %param.5) | copy-start | bytes 100
  163.7 57.2 %collective-permute-start.1 = (bf16[2,8,416,256]{3,2,1,0:T(8,128)(2,1)}, bf16[2,8,416,256]{3,2,1,0:T(8,128)(2,1)}, u32[]{:S(2)}, u32[]{:S(2)}) collective-permute-start(bf16[2,8,416,256]{3,2,1,0:T(8,128)(2,1)} %pad_maximum_fusion), channel_id=1, source_target_pairs={{0,1},{1,0},{2,3},{3,2},{4,5},{5,4},{6,7},{7,6},{8,9},{9,8},{10,11... | collective-permute-start | bytes 10223624 | tf_op jit(solution)/shard_map/ppermute | solution.py:19
  163.7 0.9 copy-start.1
  164.6 23.3 %collective-permute-start.7 = (bf16[4,1,416,256]{3,2,1,0:T(8,128)(2,1)S(1)}, bf16[4,1,416,256]{3,2,1,0:T(8,128)(2,1)}, u32[]{:S(2)}, u32[]{:S(2)}) collective-permute-start(bf16[4,1,416,256]{3,2,1,0:T(8,128)(2,1)S(1)} %collective-permute-done.6), channel_id=1, source_target_pairs={{8,0},{16,8},{24,16},{9,1},{17,9},{25,17},{10,2},{18,10},{26,18},{... | collective-permute-start | bytes 2555912 | tf_op jit(solution)/shard_map/ppermute | solution.py:38
  177.2 22.2 %collective-permute-start.5 = (bf16[4,1,416,256]{3,2,1,0:T(8,128)(2,1)}, bf16[4,1,416,256]{3,2,1,0:T(8,128)(2,1)}, u32[]{:S(2)}, u32[]{:S(2)}) collective-permute-start(bf16[4,1,416,256]{3,2,1,0:T(8,128)(2,1)} %collective-permute-done.4), channel_id=1, source_target_pairs={{0,8},{8,16},{16,24},{1,9},{9,17},{17,25},{2,10},{10,18},{18,26},{... | collective-permute-start | bytes 2555912 | tf_op jit(solution)/shard_map/ppermute | solution.py:37
  188.0 22.8 %collective-permute-start.8 = (bf16[4,1,416,256]{3,2,1,0:T(8,128)(2,1)}, bf16[4,1,416,256]{3,2,1,0:T(8,128)(2,1)}, u32[]{:S(2)}, u32[]{:S(2)}) collective-permute-start(bf16[4,1,416,256]{3,2,1,0:T(8,128)(2,1)} %collective-permute-done.7), channel_id=1, source_target_pairs={{8,0},{16,8},{24,16},{9,1},{17,9},{25,17},{10,2},{18,10},{26,18},{... | collective-permute-start | bytes 2555912 | tf_op jit(solution)/shard_map/ppermute | solution.py:38
  191.8 12.4 %copy-start.2 = (bf16[4,1,416,256]{3,2,1,0:T(8,128)(2,1)S(1)}, bf16[4,1,416,256]{3,2,1,0:T(8,128)(2,1)}, u32[]{:S(2)}) copy-start(bf16[4,1,416,256]{3,2,1,0:T(8,128)(2,1)} %copy-done.1) | copy-start | bytes 2555908
  233.4 47.1 %collective-permute-start.10 = (f32[208,3,416]{2,0,1:T(8,128)S(1)}, f32[208,3,416]{2,0,1:T(8,128)S(1)}, u32[]{:S(2)}, u32[]{:S(2)}) collective-permute-start(f32[208,3,416]{2,0,1:T(8,128)S(1)} %pad_maximum_fusion.1), channel_id=1, source_target_pairs={{0,4},{4,0},{1,5},{5,1},{2,6},{6,2},{3,7},{7,3},{8,12},{12,8},{9,1... | collective-permute-start | bytes 3115016 | tf_op jit(solution)/shard_map/ppermute | solution.py:10
  234.7 38.9 %collective-permute-start.11 = (f32[208,1,416]{2,0,1:T(8,128)S(1)}, f32[208,1,416]{2,0,1:T(8,128)S(1)}, u32[]{:S(2)}, u32[]{:S(2)}) collective-permute-start(f32[208,1,416]{2,0,1:T(8,128)S(1)} %fusion.44), channel_id=1, source_target_pairs={{0,4},{4,0},{1,5},{5,1},{2,6},{6,2},{3,7},{7,3},{8,12},{12,8},{9,1... | collective-permute-start | bytes 1038344 | tf_op jit(solution)/shard_map/ppermute | solution.py:10
  241.3 39.2 %collective-permute-start.9 = (f32[208,1,416]{2,0,1:T(8,128)S(1)}, f32[208,1,416]{2,0,1:T(8,128)S(1)}, u32[]{:S(2)}, u32[]{:S(2)}) collective-permute-start(f32[208,1,416]{2,0,1:T(8,128)S(1)} %fusion.53), channel_id=1, source_target_pairs={{0,4},{4,0},{1,5},{5,1},{2,6},{6,2},{3,7},{7,3},{8,12},{12,8},{9,1... | collective-permute-start | bytes 1038344 | tf_op jit(solution)/shard_map/ppermute | solution.py:10
Sparse Core Ops, SparseCore 0:
  52.3 98.3 all-gather.1

commit v22 on v20

--- a/solution.py
+++ b/solution.py
@@ -83,9 +83,10 @@
     all_analysis = jnp.where(pair_index == 0, in_order, swapped)
     all_analysis = all_analysis.reshape(chan_size, cycle_total, width_block, piece)
 
-    split_b = local_background.reshape(width_block, PAIR, chan_size, piece)
-    by_loc = lax.all_to_all(split_b, "chan", 2, 0, tiled=True)
-    by_loc = by_loc.reshape(quad_size, pair_rows, PAIR, piece).transpose(0, 2, 1, 3)
+    chunks = [local_background[:, k * piece:(k + 1) * piece] for k in range(PAIR * chan_size)]
+    split_b = jnp.stack(chunks, axis=0).reshape(PAIR, chan_size, width_block, piece)
+    by_loc = lax.all_to_all(split_b, "chan", 1, 1, tiled=True)
+    by_loc = by_loc.reshape(PAIR, quad_size, pair_rows, piece).transpose(1, 0, 2, 3)
     by_loc = by_loc.reshape(quad_size * PAIR, pair_rows, piece)
     rows_here = lax.all_to_all(by_loc, ("tq", "th"), 0, 0, tiled=True)
     all_background = gather_chan(rows_here)

time: 263 us -> 265 us (level)
  waiting for transfers between devices: 160 us -> 164 us
  transfers between devices with their start and end apart: 9 -> 9, of which waited for: 6 -> 6; matrix products, arithmetic and copies ran while one was open for 10% -> 9% of each run, Pallas kernels for 0% -> 0%
where the time goes in v22:
time: 265 us
  waiting for transfers between devices  164 us (62%)
  blocking collectives  25.8 us (10%)
  other arithmetic  22.6 us (9%)
  matrix products  18.7 us (7%)
  between operations  15.6 us (6%)
  starting transfers between devices  13.5 us (5%)
  local copies, waits for them, and re-layouts  4.57 us (2%)
    ppermute x4, waiting for transfers between devices, swap_pair(): return lax.ppermute(x, 'th', [(0, 1), (1, 0)])  65.1 us
    all_to_all x1, waiting for transfers between devices, body(): rows_here = lax.all_to_all(by_loc, ('tq', 'th'), 0, 0, tiled=True)  39.9 us
    ppermute x2, waiting for transfers between devices, gather_chan(): got = lax.ppermute(held, 'chan', [(c, c ^ 1 << bit) for c in range(size)])  37.6 us
    all_to_all x1, blocking collectives, body(): by_loc = lax.all_to_all(split_b, 'chan', 1, 1, tiled=True)  25.8 us
    all_gather x1, waiting for transfers between devices, body(): other_parity = lax.all_gather(by_piece(got), 'tq', axis=1, tiled=True)  21.4 us
    dot_general x10, matrix products, contract(): lax.dot_general(left, right, (((0, 1, 3), (0, 1, 3)), ((), ())), preferre...  18.7 us
    select_n x1, other arithmetic, body(): all_analysis = jnp.where(pair_index == 0, in_order, swapped)  6.83 us
    all_to_all x1, starting transfers between devices, body(): rows_here = lax.all_to_all(by_loc, ('tq', 'th'), 0, 0, tiled=True)  6.32 us
  transfers between devices with their start and end apart: 9, of which 6 were waited for; matrix products, arithmetic and copies ran while one was open for 9% of the time, Pallas kernels for 0%

profile of v22, /device:TPU:0, one launch (start us, length us, event | category | flops | bytes accessed | tf_op | source)
XLA Modules:
  0.0 264.7 jit_solution(5334743539468007731)
XLA Ops:
  8.5 2.2 bitcast_select_fusion
  14.3 25.8 %all_to_all.10 = bf16[2,4,416,256]{3,2,0,1:T(8,128)(2,1)} all-to-all(bf16[2,4,416,256]{3,2,0,1:T(8,128)(2,1)S(1)} %copy.4), channel_id=1, replica_groups=mesh['tq'=4,'th'=2,'chan'=4] {'chan'}, dimensions={1} | all-to-all | bytes 3407872 | tf_op jit(solution)/shard_map/all_to_all | solution.py:88
  40.0 6.3 %all-to-all-start.1 = ((bf16[8,416,256]{2,1,0:T(8,128)(2,1)}), bf16[8,416,256]{2,1,0:T(8,128)(2,1)S(1)}, u32[]{:S(2)}, u32[]{:S(2)}) async-start(bf16[8,416,256]{2,1,0:T(8,128)(2,1)} %bitcast.11), calls=%async_computation.1 | async-start | bytes 3407872 | tf_op jit(solution)/shard_map/all_to_all | solution.py:91
  46.4 2.0 collective-permute-start.2
  48.4 29.9 %collective-permute-done.2 = bf16[416,1024]{1,0:T(8,128)(2,1)S(1)} collective-permute-done((bf16[416,1024]{1,0:T(8,128)(2,1)S(1)}, bf16[416,1024]{1,0:T(8,128)(2,1)S(1)}, u32[]{:S(2)}, u32[]{:S(2)}) %collective-permute-start.2) | collective-permute-done | bytes 852000 | tf_op jit(solution)/shard_map/ppermute | solution.py:10
  80.5 39.9 %all-to-all-done.1 = bf16[8,416,256]{2,1,0:T(8,128)(2,1)S(1)} async-done(((bf16[8,416,256]{2,1,0:T(8,128)(2,1)}), bf16[8,416,256]{2,1,0:T(8,128)(2,1)S(1)}, u32[]{:S(2)}, u32[]{:S(2)}) %all-to-all-start.1) | async-done | bytes 1703968 | tf_op jit(solution)/shard_map/all_to_all | solution.py:91
  121.8 37.6 %collective-permute-done = bf16[1,8,416,256]{3,2,1,0:T(8,128)(2,1)} collective-permute-done((bf16[1,8,416,256]{3,2,1,0:T(8,128)(2,1)S(1)}, bf16[1,8,416,256]{3,2,1,0:T(8,128)(2,1)}, u32[]{:S(2)}, u32[]{:S(2)}) %collective-permute-start) | collective-permute-done | bytes 1703968 | tf_op jit(solution)/shard_map/ppermute | solution.py:19
  159.4 2.2 broadcast_select_fusion.3
  161.6 2.1 pad_maximum_fusion
  167.1 21.4 %all-gather.5.cloned.1.call-done = bf16[4,4,416,256]{3,2,1,0:T(8,128)(2,1)} async-done(((bf16[4,1,416,256]{3,2,1,0:T(8,128)(2,1)}), bf16[4,4,416,256]{3,2,1,0:T(8,128)(2,1)}) %all-gather.5.cloned.1.call-update) | async-done | bytes 3407888 | tf_op jit(solution)/shard_map/all_gather | solution.py:80
  188.5 6.8 %maximum_select_fusion = bf16[4,4,2,416,256]{4,3,2,1,0:T(8,128)(2,1)S(1)} fusion(bf16[4,4,1,416,256]{4,3,2,1,0:T(8,128)(2,1)} %bitcast.159, bf16[4,4,1,416,256]{4,3,2,1,0:T(8,128)(2,1)} %bitcast.158, pred[]{:T(512)S(6)} %eq.21), kind=kLoop, calls=%fused_computation.4 | loop fusion | flops 10223616 | bytes 13631489 | tf_op jit(solution)/shard_map/jit(_where)/select_n | solution.py:83
  195.3 2.2 broadcast_select_fusion
  199.9 1.9 fusion.25
  201.9 2.2 convolution_bitcast_fusion
  204.0 1.9 fusion.34
  206.0 1.7 fusion.44
  209.8 1.7 fusion.50
  211.5 1.9 fusion.22
  213.5 2.2 fusion.37
  217.2 1.9 fusion.31
  219.1 1.7 fusion.41
  220.8 27.2 %collective-permute-done.5 = f32[208,1,416]{2,0,1:T(8,128)S(1)} collective-permute-done((f32[208,1,416]{2,0,1:T(8,128)S(1)}, f32[208,1,416]{2,0,1:T(8,128)S(1)}, u32[]{:S(2)}, u32[]{:S(2)}) %collective-permute-start.5) | collective-permute-done | bytes 346144 | tf_op jit(solution)/shard_map/ppermute | solution.py:10
  247.9 8.0 %collective-permute-done.3 = f32[208,1,416]{2,0,1:T(8,128)S(1)} collective-permute-done((f32[208,1,416]{2,0,1:T(8,128)S(1)}, f32[208,1,416]{2,0,1:T(8,128)S(1)}, u32[]{:S(2)}, u32[]{:S(2)}) %collective-permute-start.3) | collective-permute-done | bytes 346144 | tf_op jit(solution)/shard_map/ppermute | solution.py:10
  255.9 1.9 fusion.18
  (42 shorter events, 16.6 us)
Async XLA Ops:
  6.5 160.6 %all-gather.3.cloned.1.call-start = ((), (), s32[]{:S(2)}) async-start(), calls=%async_computation.2 | async-start | bytes 4259840 | tf_op jit(solution)/shard_map/all_gather | solution.py:78
  14.2 32.1 %copy-start.1 = (bf16[416,1024]{1,0:T(8,128)(2,1)S(1)}, bf16[416,1024]{1,0:T(8,128)(2,1)}, u32[]{:S(2)}) copy-start(bf16[416,1024]{1,0:T(8,128)(2,1)} %get-tuple-element.22) | copy-start | bytes 2555908
  40.0 80.3 %all-to-all-start.1 = ((bf16[8,416,256]{2,1,0:T(8,128)(2,1)}), bf16[8,416,256]{2,1,0:T(8,128)(2,1)S(1)}, u32[]{:S(2)}, u32[]{:S(2)}) async-start(bf16[8,416,256]{2,1,0:T(8,128)(2,1)} %bitcast.11), calls=%async_computation.1 | async-start | bytes 3407872 | tf_op jit(solution)/shard_map/all_to_all | solution.py:91
  46.3 142.1 %all-gather.5.cloned.1.call-start = ((), (), s32[]{:S(2)}) async-start(), calls=%async_computation.3 | async-start | bytes 4259840 | tf_op jit(solution)/shard_map/all_gather | solution.py:80
  46.4 32.0 %collective-permute-start.2 = (bf16[416,1024]{1,0:T(8,128)(2,1)S(1)}, bf16[416,1024]{1,0:T(8,128)(2,1)S(1)}, u32[]{:S(2)}, u32[]{:S(2)}) collective-permute-start(bf16[416,1024]{1,0:T(8,128)(2,1)S(1)} %copy-done.1), channel_id=1, source_target_pairs={{0,4},{4,0},{1,5},{5,1},{2,6},{6,2},{3,7},{7,3},{8,12},{12,8},{9,1... | collective-permute-start | bytes 2555912 | tf_op jit(solution)/shard_map/ppermute | solution.py:10
  120.3 1.5 copy-start
  120.3 39.0 %collective-permute-start = (bf16[1,8,416,256]{3,2,1,0:T(8,128)(2,1)S(1)}, bf16[1,8,416,256]{3,2,1,0:T(8,128)(2,1)}, u32[]{:S(2)}, u32[]{:S(2)}) collective-permute-start(bf16[1,8,416,256]{3,2,1,0:T(8,128)(2,1)S(1)} %bitcast.153), channel_id=1, source_target_pairs={{0,2},{1,3},{2,0},{3,1},{4,6},{5,7},{6,4},{7,5},{8,10},{9,11},{10,... | collective-permute-start | bytes 5111816 | tf_op jit(solution)/shard_map/ppermute | solution.py:19
  161.6 2.7 %copy-start.2 = (s32[8]{0:T(128)S(1)}, s32[8]{0:T(128)}, u32[]{:S(2)}) copy-start(s32[8]{0:T(128)} %param.5) | copy-start | bytes 100
  163.6 31.6 %collective-permute-start.1 = (bf16[2,8,416,256]{3,2,1,0:T(8,128)(2,1)}, bf16[2,8,416,256]{3,2,1,0:T(8,128)(2,1)}, u32[]{:S(2)}, u32[]{:S(2)}) collective-permute-start(bf16[2,8,416,256]{3,2,1,0:T(8,128)(2,1)} %pad_maximum_fusion), channel_id=1, source_target_pairs={{0,1},{1,0},{2,3},{3,2},{4,5},{5,4},{6,7},{7,6},{8,9},{9,8},{10,11... | collective-permute-start | bytes 10223624 | tf_op jit(solution)/shard_map/ppermute | solution.py:19
  207.8 48.1 %collective-permute-start.4 = (f32[208,3,416]{2,0,1:T(8,128)S(1)}, f32[208,3,416]{2,0,1:T(8,128)S(1)}, u32[]{:S(2)}, u32[]{:S(2)}) collective-permute-start(f32[208,3,416]{2,0,1:T(8,128)S(1)} %pad_maximum_fusion.1), channel_id=1, source_target_pairs={{0,4},{4,0},{1,5},{5,1},{2,6},{6,2},{3,7},{7,3},{8,12},{12,8},{9,1... | collective-permute-start | bytes 3115016 | tf_op jit(solution)/shard_map/ppermute | solution.py:10
  209.3 38.6 %collective-permute-start.5 = (f32[208,1,416]{2,0,1:T(8,128)S(1)}, f32[208,1,416]{2,0,1:T(8,128)S(1)}, u32[]{:S(2)}, u32[]{:S(2)}) collective-permute-start(f32[208,1,416]{2,0,1:T(8,128)S(1)} %fusion.44), channel_id=1, source_target_pairs={{0,4},{4,0},{1,5},{5,1},{2,6},{6,2},{3,7},{7,3},{8,12},{12,8},{9,1... | collective-permute-start | bytes 1038344 | tf_op jit(solution)/shard_map/ppermute | solution.py:10
  215.6 40.3 %collective-permute-start.3 = (f32[208,1,416]{2,0,1:T(8,128)S(1)}, f32[208,1,416]{2,0,1:T(8,128)S(1)}, u32[]{:S(2)}, u32[]{:S(2)}) collective-permute-start(f32[208,1,416]{2,0,1:T(8,128)S(1)} %fusion.53), channel_id=1, source_target_pairs={{0,4},{4,0},{1,5},{5,1},{2,6},{6,2},{3,7},{7,3},{8,12},{12,8},{9,1... | collective-permute-start | bytes 1038344 | tf_op jit(solution)/shard_map/ppermute | solution.py:10
Sparse Core Ops, SparseCore 0:
  13.9 106.1 all-gather.2
  121.7 66.7 all-gather.4

commit v23 on v20

--- a/solution.py
+++ b/solution.py
@@ -67,10 +67,8 @@
     local_analysis = jnp.where(valid_cols, analysis_dep[0], jnp.zeros((), jnp.bfloat16))
     local_background = jnp.where(valid_cols, background_dep[0], jnp.zeros((), jnp.bfloat16))
 
-    low_half = local_analysis[:, :half]
-    high_half = local_analysis[:, half:]
-    keep = jnp.where(pair_index == 0, low_half, high_half)
-    give = jnp.where(pair_index == 0, high_half, low_half)
+    keep = lax.dynamic_slice_in_dim(local_analysis, pair_index * half, half, axis=1)
+    give = lax.dynamic_slice_in_dim(local_analysis, (1 - pair_index) * half, half, axis=1)
     def by_piece(x):
         pieces_first = x.reshape(width_block, chan_size, piece).transpose(1, 0, 2)
         return bit_reversed(pieces_first, 0, chan_size)[:, None]

time: 263 us -> 267 us (1.015)
  local copies, waits for them, and re-layouts: 5.55 us -> 10.5 us
    select_n x0 -> x1, local copies, waits for them, and re-layouts: none -> 3.39 us  [body(): all_analysis = jnp.where(pair_index == 0, in_order, swapped)]
    reshape x4 -> x0, local copies, waits for them, and re-layouts: 2.87 us -> none  [bit_reversed(): return x.reshape(shape).transpose(order).reshape(x.shape)]
  transfers between devices with their start and end apart: 9 -> 9, of which waited for: 6 -> 6; matrix products, arithmetic and copies ran while one was open for 10% -> 11% of each run, Pallas kernels for 0% -> 0%
where the time goes in v23:
time: 267 us
  waiting for transfers between devices  160 us (60%)
  blocking collectives  25.8 us (10%)
  other arithmetic  22.6 us (8%)
  matrix products  18.7 us (7%)
  between operations  15.5 us (6%)
  starting transfers between devices  13.5 us (5%)
  local copies, waits for them, and re-layouts  10.5 us (4%)
    ppermute x4, waiting for transfers between devices, swap_pair(): return lax.ppermute(x, 'th', [(0, 1), (1, 0)])  65 us
    all_to_all x1, waiting for transfers between devices, body(): rows_here = lax.all_to_all(by_loc, ('tq', 'th'), 0, 0, tiled=True)  38 us
    ppermute x2, waiting for transfers between devices, gather_chan(): got = lax.ppermute(held, 'chan', [(c, c ^ 1 << bit) for c in range(size)])  37.7 us
    all_to_all x1, blocking collectives, body(): by_loc = lax.all_to_all(split_b, 'chan', 2, 0, tiled=True)  25.8 us
    all_gather x1, waiting for transfers between devices, body(): other_parity = lax.all_gather(by_piece(got), 'tq', axis=1, tiled=True)  19.7 us
    dot_general x10, matrix products, contract(): lax.dot_general(left, right, (((0, 1, 3), (0, 1, 3)), ((), ())), preferre...  18.7 us
    select_n x1, other arithmetic, body(): all_analysis = jnp.where(pair_index == 0, in_order, swapped)  6.81 us
    all_to_all x1, starting transfers between devices, body(): rows_here = lax.all_to_all(by_loc, ('tq', 'th'), 0, 0, tiled=True)  6.32 us
  transfers between devices with their start and end apart: 9, of which 6 were waited for; matrix products, arithmetic and copies ran while one was open for 11% of the time, Pallas kernels for 0%

profile of v23, /device:TPU:0, one launch (start us, length us, event | category | flops | bytes accessed | tf_op | source)
XLA Modules:
  0.0 267.0 jit_solution(7161143407412691257)
XLA Ops:
  15.7 25.8 %all_to_all.20 = bf16[416,2,4,256]{3,0,1,2:T(8,128)(2,1)} all-to-all(bf16[416,2,4,256]{3,0,1,2:T(8,128)(2,1)S(1)} %copy_select_fusion), channel_id=1, replica_groups=mesh['tq'=4,'th'=2,'chan'=4] {'chan'}, dimensions={2} | all-to-all | bytes 3407872 | tf_op jit(solution)/shard_map/all_to_all | solution.py:85
  41.5 6.3 %all-to-all-start.1 = ((bf16[8,416,256]{2,1,0:T(8,128)(2,1)}), bf16[8,416,256]{2,1,0:T(8,128)(2,1)S(1)}, u32[]{:S(2)}, u32[]{:S(2)}) async-start(bf16[8,416,256]{2,1,0:T(8,128)(2,1)} %bitcast.4), calls=%async_computation.1 | async-start | bytes 3407872 | tf_op jit(solution)/shard_map/all_to_all | solution.py:88
  47.8 2.0 collective-permute-start.2
  49.9 29.9 %collective-permute-done.2 = bf16[416,1024]{1,0:T(8,128)(2,1)S(1)} collective-permute-done((bf16[416,1024]{1,0:T(8,128)(2,1)S(1)}, bf16[416,1024]{1,0:T(8,128)(2,1)S(1)}, u32[]{:S(2)}, u32[]{:S(2)}) %collective-permute-start.2) | collective-permute-done | bytes 852000 | tf_op jit(solution)/shard_map/ppermute | solution.py:10
  81.5 38.0 %all-to-all-done.1 = bf16[8,416,256]{2,1,0:T(8,128)(2,1)S(1)} async-done(((bf16[8,416,256]{2,1,0:T(8,128)(2,1)}), bf16[8,416,256]{2,1,0:T(8,128)(2,1)S(1)}, u32[]{:S(2)}, u32[]{:S(2)}) %all-to-all-start.1) | async-done | bytes 1703968 | tf_op jit(solution)/shard_map/all_to_all | solution.py:88
  121.0 37.6 %collective-permute-done = bf16[1,8,416,256]{3,2,1,0:T(8,128)(2,1)} collective-permute-done((bf16[1,8,416,256]{3,2,1,0:T(8,128)(2,1)S(1)}, bf16[1,8,416,256]{3,2,1,0:T(8,128)(2,1)}, u32[]{:S(2)}, u32[]{:S(2)}) %collective-permute-start) | collective-permute-done | bytes 1703968 | tf_op jit(solution)/shard_map/ppermute | solution.py:19
  158.6 2.2 broadcast_select_fusion.3
  160.9 2.1 pad_maximum_fusion
  166.4 19.7 %all-gather.5.cloned.1.call-done = bf16[4,4,416,256]{3,2,0,1:T(8,128)(2,1)} async-done(((bf16[4,1,416,256]{3,2,0,1:T(8,128)(2,1)}), bf16[4,4,416,256]{3,2,0,1:T(8,128)(2,1)}) %all-gather.5.cloned.1.call-update) | async-done | bytes 3407888 | tf_op jit(solution)/shard_map/all_gather | solution.py:78
  186.1 6.8 %maximum_select_fusion = bf16[4,4,2,416,256]{4,3,0,1,2:T(8,128)(2,1)S(1)} fusion(bf16[4,4,1,416,256]{4,3,0,1,2:T(8,128)(2,1)} %bitcast.132, bf16[4,4,1,416,256]{4,3,0,1,2:T(8,128)(2,1)} %bitcast.131, pred[]{:T(512)S(6)} %eq.19), kind=kLoop, calls=%fused_computation.4 | loop fusion | flops 10223616 | bytes 13631489 | tf_op jit(solution)/shard_map/jit(_where)/select_n | solution.py:81
  192.9 3.4 %copy.33 = bf16[4,4,2,416,256]{4,3,2,1,0:T(8,128)(2,1)} copy(bf16[4,4,2,416,256]{4,3,0,1,2:T(8,128)(2,1)S(1)} %maximum_select_fusion) | data formatting | bytes 13631488 | tf_op jit(solution)/shard_map/jit(_where)/select_n | solution.py:81
  196.3 2.4 broadcast_select_fusion
  200.6 1.7 fusion.53
  202.3 1.9 fusion.25
  204.2 2.2 convolution_bitcast_fusion
  206.4 1.9 fusion.34
  208.3 1.7 fusion.44
  212.2 1.7 fusion.50
  213.9 1.9 fusion.22
  215.8 2.2 fusion.37
  219.5 1.9 fusion.31
  223.2 27.1 %collective-permute-done.5 = f32[208,1,416]{2,0,1:T(8,128)S(1)} collective-permute-done((f32[208,1,416]{2,0,1:T(8,128)S(1)}, f32[208,1,416]{2,0,1:T(8,128)S(1)}, u32[]{:S(2)}, u32[]{:S(2)}) %collective-permute-start.5) | collective-permute-done | bytes 346144 | tf_op jit(solution)/shard_map/ppermute | solution.py:10
  250.3 7.9 %collective-permute-done.3 = f32[208,1,416]{2,0,1:T(8,128)S(1)} collective-permute-done((f32[208,1,416]{2,0,1:T(8,128)S(1)}, f32[208,1,416]{2,0,1:T(8,128)S(1)}, u32[]{:S(2)}, u32[]{:S(2)}) %collective-permute-start.3) | collective-permute-done | bytes 346144 | tf_op jit(solution)/shard_map/ppermute | solution.py:10
  258.2 1.9 fusion.18
  (44 shorter events, 21.2 us)
Async XLA Ops:
  6.5 159.8 %all-gather.3.cloned.1.call-start = ((), (), s32[]{:S(2)}) async-start(), calls=%async_computation.2 | async-start | bytes 4259840 | tf_op jit(solution)/shard_map/all_gather | solution.py:76
  11.2 1.7 copy-start.1
  15.7 32.1 %copy-start.2 = (bf16[416,1024]{1,0:T(8,128)(2,1)S(1)}, bf16[416,1024]{1,0:T(8,128)(2,1)}, u32[]{:S(2)}) copy-start(bf16[416,1024]{1,0:T(8,128)(2,1)} %get-tuple-element.22) | copy-start | bytes 2555908
  41.5 78.1 %all-to-all-start.1 = ((bf16[8,416,256]{2,1,0:T(8,128)(2,1)}), bf16[8,416,256]{2,1,0:T(8,128)(2,1)S(1)}, u32[]{:S(2)}, u32[]{:S(2)}) async-start(bf16[8,416,256]{2,1,0:T(8,128)(2,1)} %bitcast.4), calls=%async_computation.1 | async-start | bytes 3407872 | tf_op jit(solution)/shard_map/all_to_all | solution.py:88
  47.8 138.3 %all-gather.5.cloned.1.call-start = ((), (), s32[]{:S(2)}) async-start(), calls=%async_computation.3 | async-start | bytes 4259840 | tf_op jit(solution)/shard_map/all_gather | solution.py:78
  47.8 32.0 %collective-permute-start.2 = (bf16[416,1024]{1,0:T(8,128)(2,1)S(1)}, bf16[416,1024]{1,0:T(8,128)(2,1)S(1)}, u32[]{:S(2)}, u32[]{:S(2)}) collective-permute-start(bf16[416,1024]{1,0:T(8,128)(2,1)S(1)} %copy-done.2), channel_id=1, source_target_pairs={{0,4},{4,0},{1,5},{5,1},{2,6},{6,2},{3,7},{7,3},{8,12},{12,8},{9,1... | collective-permute-start | bytes 2555912 | tf_op jit(solution)/shard_map/ppermute | solution.py:10
  119.5 1.4 copy-start
  119.5 39.1 %collective-permute-start = (bf16[1,8,416,256]{3,2,1,0:T(8,128)(2,1)S(1)}, bf16[1,8,416,256]{3,2,1,0:T(8,128)(2,1)}, u32[]{:S(2)}, u32[]{:S(2)}) collective-permute-start(bf16[1,8,416,256]{3,2,1,0:T(8,128)(2,1)S(1)} %bitcast.124), channel_id=1, source_target_pairs={{0,2},{1,3},{2,0},{3,1},{4,6},{5,7},{6,4},{7,5},{8,10},{9,11},{10,... | collective-permute-start | bytes 5111816 | tf_op jit(solution)/shard_map/ppermute | solution.py:19
  160.8 2.7 %copy-start.3 = (s32[8]{0:T(128)S(1)}, s32[8]{0:T(128)}, u32[]{:S(2)}) copy-start(s32[8]{0:T(128)} %param.5) | copy-start | bytes 100
  162.9 33.3 %collective-permute-start.1 = (bf16[2,8,416,256]{3,2,1,0:T(8,128)(2,1)}, bf16[2,8,416,256]{3,2,1,0:T(8,128)(2,1)}, u32[]{:S(2)}, u32[]{:S(2)}) collective-permute-start(bf16[2,8,416,256]{3,2,1,0:T(8,128)(2,1)} %pad_maximum_fusion), channel_id=1, source_target_pairs={{0,1},{1,0},{2,3},{3,2},{4,5},{5,4},{6,7},{7,6},{8,9},{9,8},{10,11... | collective-permute-start | bytes 10223624 | tf_op jit(solution)/shard_map/ppermute | solution.py:19
  196.3 3.2 %slice-start = ((s8[6815744]{0:T(1024)(128)(4,1)}), s8[4194304]{0:T(1024)(128)(4,1)S(1)}, s32[]{:S(2)}) async-start(s8[6815744]{0:T(1024)(128)(4,1)} %bitcast.112), calls=%async_computation.4 | async-start | bytes 8388608
  198.7 2.0 slice-start.1
  210.1 48.1 %collective-permute-start.4 = (f32[208,3,416]{2,0,1:T(8,128)S(1)}, f32[208,3,416]{2,0,1:T(8,128)S(1)}, u32[]{:S(2)}, u32[]{:S(2)}) collective-permute-start(f32[208,3,416]{2,0,1:T(8,128)S(1)} %pad_maximum_fusion.1), channel_id=1, source_target_pairs={{0,4},{4,0},{1,5},{5,1},{2,6},{6,2},{3,7},{7,3},{8,12},{12,8},{9,1... | collective-permute-start | bytes 3115016 | tf_op jit(solution)/shard_map/ppermute | solution.py:10
  211.7 38.6 %collective-permute-start.5 = (f32[208,1,416]{2,0,1:T(8,128)S(1)}, f32[208,1,416]{2,0,1:T(8,128)S(1)}, u32[]{:S(2)}, u32[]{:S(2)}) collective-permute-start(f32[208,1,416]{2,0,1:T(8,128)S(1)} %fusion.44), channel_id=1, source_target_pairs={{0,4},{4,0},{1,5},{5,1},{2,6},{6,2},{3,7},{7,3},{8,12},{12,8},{9,1... | collective-permute-start | bytes 1038344 | tf_op jit(solution)/shard_map/ppermute | solution.py:10
  218.0 40.2 %collective-permute-start.3 = (f32[208,1,416]{2,0,1:T(8,128)S(1)}, f32[208,1,416]{2,0,1:T(8,128)S(1)}, u32[]{:S(2)}, u32[]{:S(2)}) collective-permute-start(f32[208,1,416]{2,0,1:T(8,128)S(1)} %fusion.53), channel_id=1, source_target_pairs={{0,4},{4,0},{1,5},{5,1},{2,6},{6,2},{3,7},{7,3},{8,12},{12,8},{9,1... | collective-permute-start | bytes 1038344 | tf_op jit(solution)/shard_map/ppermute | solution.py:10
Sparse Core Ops, SparseCore 0:
  13.1 104.5 all-gather.2
  119.3 66.7 all-gather.4

commit v24 on v20

--- a/solution.py
+++ b/solution.py
@@ -78,9 +78,13 @@
     same_parity = lax.all_gather(by_piece(keep), "tq", axis=1, tiled=True)
     got = swap_pair(give)
     other_parity = lax.all_gather(by_piece(got), "tq", axis=1, tiled=True)
-    in_order = jnp.stack([same_parity, other_parity], axis=2)
-    swapped = jnp.stack([other_parity, same_parity], axis=2)
-    all_analysis = jnp.where(pair_index == 0, in_order, swapped)
+    all_analysis = lax.cond(
+        pair_index == 0,
+        lambda a, b: jnp.stack([a, b], axis=2),
+        lambda a, b: jnp.stack([b, a], axis=2),
+        same_parity,
+        other_parity,
+    )
     all_analysis = all_analysis.reshape(chan_size, cycle_total, width_block, piece)
 
     split_b = local_background.reshape(width_block, PAIR, chan_size, piece)

time: 263 us -> 270 us (1.027)
  local copies, waits for them, and re-layouts: 5.55 us -> 14.8 us
  other arithmetic: 23.4 us -> 19.1 us
  waiting for transfers between devices: 160 us -> 163 us
    all_to_all x1, waiting for transfers between devices: 37.7 us -> 69.8 us  [body(): rows_here = lax.all_to_all(by_loc, ('tq', 'th'), 0, 0, tiled=True)]
    ppermute x4, waiting for transfers between devices: 65.1 us -> 35 us  [swap_pair(): return lax.ppermute(x, 'th', [(0, 1), (1, 0)])]
    another operation x0 -> x2, local copies, waits for them, and re-layouts: none -> 8.67 us  [body(): jnp.stack([a, b], axis=2)]
    select_n x1 -> x0, other arithmetic: 6.83 us -> none  [body(): all_analysis = jnp.where(pair_index == 0, in_order, swapped)]
    reshape x4 -> x0, local copies, waits for them, and re-layouts: 2.87 us -> none  [bit_reversed(): return x.reshape(shape).transpose(order).reshape(x.shape)]
  transfers between devices with their start and end apart: 9 -> 9, of which waited for: 6 -> 5; matrix products, arithmetic and copies ran while one was open for 10% -> 11% of each run, Pallas kernels for 0% -> 0%
where the time goes in v24:
time: 270 us
  waiting for transfers between devices  163 us (60%)
  blocking collectives  25.8 us (10%)
  other arithmetic  19.1 us (7%)
  matrix products  18.7 us (7%)
  between operations  15.6 us (6%)
  local copies, waits for them, and re-layouts  14.8 us (5%)
  starting transfers between devices  13.4 us (5%)
    all_to_all x1, waiting for transfers between devices, body(): rows_here = lax.all_to_all(by_loc, ('tq', 'th'), 0, 0, tiled=True)  69.8 us
    ppermute x2, waiting for transfers between devices, gather_chan(): got = lax.ppermute(held, 'chan', [(c, c ^ 1 << bit) for c in range(size)])  35.9 us
    ppermute x4, waiting for transfers between devices, swap_pair(): return lax.ppermute(x, 'th', [(0, 1), (1, 0)])  35 us
    all_to_all x1, blocking collectives, body(): by_loc = lax.all_to_all(split_b, 'chan', 2, 0, tiled=True)  25.8 us
    all_gather x1, waiting for transfers between devices, body(): other_parity = lax.all_gather(by_piece(got), 'tq', axis=1, tiled=True)  22 us
    dot_general x10, matrix products, contract(): lax.dot_general(left, right, (((0, 1, 3), (0, 1, 3)), ((), ())), preferre...  18.7 us
    another operation x2, local copies, waits for them, and re-layouts, body(): jnp.stack([a, b], axis=2)  8.67 us
    all_to_all x1, starting transfers between devices, body(): rows_here = lax.all_to_all(by_loc, ('tq', 'th'), 0, 0, tiled=True)  6.31 us
  transfers between devices with their start and end apart: 9, of which 5 were waited for; matrix products, arithmetic and copies ran while one was open for 11% of the time, Pallas kernels for 0%

profile of v24, /device:TPU:0, one launch (start us, length us, event | category | flops | bytes accessed | tf_op | source)
XLA Modules:
  0.0 270.0 jit_solution(17773872677705625147)
XLA Ops:
  15.4 25.8 %all_to_all.20 = bf16[416,2,4,256]{3,0,1,2:T(8,128)(2,1)} all-to-all(bf16[416,2,4,256]{3,0,1,2:T(8,128)(2,1)S(1)} %copy_select_fusion), channel_id=1, replica_groups=mesh['tq'=4,'th'=2,'chan'=4] {'chan'}, dimensions={2} | all-to-all | bytes 3407872 | tf_op jit(solution)/shard_map/all_to_all | solution.py:91
  41.2 6.3 %all-to-all-start.1 = ((bf16[8,416,256]{2,1,0:T(8,128)(2,1)}), bf16[8,416,256]{2,1,0:T(8,128)(2,1)S(1)}, u32[]{:S(2)}, u32[]{:S(2)}) async-start(bf16[8,416,256]{2,1,0:T(8,128)(2,1)} %bitcast.10), calls=%async_computation.1 | async-start | bytes 3407872 | tf_op jit(solution)/shard_map/all_to_all | solution.py:94
  47.6 2.0 collective-permute-start.2
  49.6 69.8 %all-to-all-done.1 = bf16[8,416,256]{2,1,0:T(8,128)(2,1)S(1)} async-done(((bf16[8,416,256]{2,1,0:T(8,128)(2,1)}), bf16[8,416,256]{2,1,0:T(8,128)(2,1)S(1)}, u32[]{:S(2)}, u32[]{:S(2)}) %all-to-all-start.1) | async-done | bytes 1703968 | tf_op jit(solution)/shard_map/all_to_all | solution.py:94
  122.6 35.9 %collective-permute-done = bf16[1,8,416,256]{3,2,1,0:T(8,128)(2,1)} collective-permute-done((bf16[1,8,416,256]{3,2,1,0:T(8,128)(2,1)S(1)}, bf16[1,8,416,256]{3,2,1,0:T(8,128)(2,1)}, u32[]{:S(2)}, u32[]{:S(2)}) %collective-permute-start) | collective-permute-done | bytes 1703968 | tf_op jit(solution)/shard_map/ppermute | solution.py:19
  158.4 2.2 broadcast_select_fusion.3
  160.6 2.0 pad_maximum_fusion.2
  166.1 22.0 %all-gather.3.cloned.1.call-done = bf16[4,4,416,256]{3,2,0,1:T(8,128)(2,1)} async-done(((bf16[4,1,416,256]{3,2,0,1:T(8,128)(2,1)}), bf16[4,4,416,256]{3,2,0,1:T(8,128)(2,1)}) %all-gather.3.cloned.1.call-update) | async-done | bytes 3407888 | tf_op jit(solution)/shard_map/all_gather | solution.py:80
  188.2 11.3 %conditional.1 = (bf16[4,8,416,256]{3,2,1,0:T(8,128)(2,1)}) conditional(s32[]{:T(128)} %convert_element_type.12, (bf16[4,4,416,256]{3,2,0,1:T(8,128)(2,1)}, bf16[4,4,416,256]{3,2,0,1:T(8,128)(2,1)}) %tuple.30, (bf16[4,4,416,256]{3,2,0,1:T(8,128)(2,1)}, bf16[4,4,416,256]{3,2,0,1:T(8,128)(2,1)}) %tuple.31), branch_computations={%region_1.2_spmd, %region_2.3_spmd} | conditional | flops 3407872 | bytes 40894472 | solution.py:81
  188.2 5.2 %copy_bitcast_fusion.2 = (bf16[4,4,1,416,256]{4,3,1,0,2:T(8,128)(2,1)S(1)}, bf16[4,4,1,416,256]{4,3,1,0,2:T(8,128)(2,1)}) fusion(bf16[4,4,416,256]{3,2,0,1:T(8,128)(2,1)} %get-tuple-element.54, bf16[4,4,416,256]{3,2,0,1:T(8,128)(2,1)} %get-tuple-element.53), kind=kLoop, calls=%fused_computation.4 | loop fusion | bytes 13631488 | tf_op jit(solution)/shard_map/cond/branch_1_fun/stack | solution.py:83
  193.4 2.6 pad_maximum_fusion.1
  196.0 3.4 %copy.22 = bf16[4,4,2,416,256]{4,3,2,1,0:T(8,128)(2,1)} copy(bf16[4,4,2,416,256]{4,3,1,0,2:T(8,128)(2,1)S(1)} %pad_maximum_fusion.1) | data formatting | bytes 13631488 | tf_op jit(solution)/shard_map/cond/branch_1_fun/stack | solution.py:83
  199.4 2.4 broadcast_select_fusion
  203.8 1.7 fusion.53
  207.1 1.9 fusion.34
  209.1 2.2 convolution_bitcast_fusion
  211.2 1.9 fusion.25
  218.6 1.9 fusion.22
  220.5 2.2 fusion.37
  222.7 1.9 fusion.31
  224.6 1.7 fusion.41
  226.3 8.8 %collective-permute-done.3 = f32[208,1,416]{2,0,1:T(8,128)S(1)} collective-permute-done((f32[208,1,416]{2,0,1:T(8,128)S(1)}, f32[208,1,416]{2,0,1:T(8,128)S(1)}, u32[]{:S(2)}, u32[]{:S(2)}) %collective-permute-start.3) | collective-permute-done | bytes 346144 | tf_op jit(solution)/shard_map/ppermute | solution.py:10
  235.1 26.2 %collective-permute-done.4 = f32[208,3,416]{2,0,1:T(8,128)S(1)} collective-permute-done((f32[208,3,416]{2,0,1:T(8,128)S(1)}, f32[208,3,416]{2,0,1:T(8,128)S(1)}, u32[]{:S(2)}, u32[]{:S(2)}) %collective-permute-start.4) | collective-permute-done | bytes 1038368 | tf_op jit(solution)/shard_map/ppermute | solution.py:10
  261.3 1.9 fusion.18
  (46 shorter events, 22.6 us)
Async XLA Ops:
  6.5 159.6 %all-gather.5.cloned.1.call-start = ((), (), s32[]{:S(2)}) async-start(), calls=%async_computation.3 | async-start | bytes 4259840 | tf_op jit(solution)/shard_map/all_gather | solution.py:78
  11.1 2.3 copy-start.1
  15.4 32.1 %copy-start.2 = (bf16[416,1024]{1,0:T(8,128)(2,1)S(1)}, bf16[416,1024]{1,0:T(8,128)(2,1)}, u32[]{:S(2)}) copy-start(bf16[416,1024]{1,0:T(8,128)(2,1)} %get-tuple-element.68) | copy-start | bytes 2555908
  41.2 78.2 %all-to-all-start.1 = ((bf16[8,416,256]{2,1,0:T(8,128)(2,1)}), bf16[8,416,256]{2,1,0:T(8,128)(2,1)S(1)}, u32[]{:S(2)}, u32[]{:S(2)}) async-start(bf16[8,416,256]{2,1,0:T(8,128)(2,1)} %bitcast.10), calls=%async_computation.1 | async-start | bytes 3407872 | tf_op jit(solution)/shard_map/all_to_all | solution.py:94
  47.5 140.6 %all-gather.3.cloned.1.call-start = ((), (), s32[]{:S(2)}) async-start(), calls=%async_computation.2 | async-start | bytes 4259840 | tf_op jit(solution)/shard_map/all_gather | solution.py:80
  47.6 73.3 %collective-permute-start.2 = (bf16[416,1024]{1,0:T(8,128)(2,1)S(1)}, bf16[416,1024]{1,0:T(8,128)(2,1)S(1)}, u32[]{:S(2)}, u32[]{:S(2)}) collective-permute-start(bf16[416,1024]{1,0:T(8,128)(2,1)S(1)} %copy-done.2), channel_id=1, source_target_pairs={{0,4},{4,0},{1,5},{5,1},{2,6},{6,2},{3,7},{7,3},{8,12},{12,8},{9,1... | collective-permute-start | bytes 2555912 | tf_op jit(solution)/shard_map/ppermute | solution.py:10
  119.4 3.2 %copy-start = (bf16[8,416,256]{2,1,0:T(8,128)(2,1)}, bf16[8,416,256]{2,1,0:T(8,128)(2,1)S(1)}, u32[]{:S(2)}) copy-start(bf16[8,416,256]{2,1,0:T(8,128)(2,1)S(1)} %all-to-all-done.1) | copy-start | bytes 5111812
  119.4 39.0 %collective-permute-start = (bf16[1,8,416,256]{3,2,1,0:T(8,128)(2,1)S(1)}, bf16[1,8,416,256]{3,2,1,0:T(8,128)(2,1)}, u32[]{:S(2)}, u32[]{:S(2)}) collective-permute-start(bf16[1,8,416,256]{3,2,1,0:T(8,128)(2,1)S(1)} %bitcast.123), channel_id=1, source_target_pairs={{0,2},{1,3},{2,0},{3,1},{4,6},{5,7},{6,4},{7,5},{8,10},{9,11},{10,... | collective-permute-start | bytes 5111816 | tf_op jit(solution)/shard_map/ppermute | solution.py:19
  160.6 2.0 copy-start.3
  162.6 36.8 %collective-permute-start.1 = (bf16[2,8,416,256]{3,2,1,0:T(8,128)(2,1)}, bf16[2,8,416,256]{3,2,1,0:T(8,128)(2,1)}, u32[]{:S(2)}, u32[]{:S(2)}) collective-permute-start(bf16[2,8,416,256]{3,2,1,0:T(8,128)(2,1)} %pad_maximum_fusion.2), channel_id=1, source_target_pairs={{0,1},{1,0},{2,3},{3,2},{4,5},{5,4},{6,7},{7,6},{8,9},{9,8},{10,11... | collective-permute-start | bytes 10223624 | tf_op jit(solution)/shard_map/ppermute | solution.py:19
  199.4 3.2 %slice-start = ((s8[6815744]{0:T(1024)(128)(4,1)}), s8[4194304]{0:T(1024)(128)(4,1)S(1)}, s32[]{:S(2)}) async-start(s8[6815744]{0:T(1024)(128)(4,1)} %bitcast.121), calls=%async_computation.4 | async-start | bytes 8388608
  201.8 1.9 slice-start.1
  213.2 13.1 %collective-permute-start.5 = (f32[208,1,416]{2,0,1:T(8,128)S(1)}, f32[208,1,416]{2,0,1:T(8,128)S(1)}, u32[]{:S(2)}, u32[]{:S(2)}) collective-permute-start(f32[208,1,416]{2,0,1:T(8,128)S(1)} %fusion.44), channel_id=1, source_target_pairs={{0,4},{4,0},{1,5},{5,1},{2,6},{6,2},{3,7},{7,3},{8,12},{12,8},{9,1... | collective-permute-start | bytes 1038344 | tf_op jit(solution)/shard_map/ppermute | solution.py:10
  214.7 20.4 %collective-permute-start.3 = (f32[208,1,416]{2,0,1:T(8,128)S(1)}, f32[208,1,416]{2,0,1:T(8,128)S(1)}, u32[]{:S(2)}, u32[]{:S(2)}) collective-permute-start(f32[208,1,416]{2,0,1:T(8,128)S(1)} %fusion.53), channel_id=1, source_target_pairs={{0,4},{4,0},{1,5},{5,1},{2,6},{6,2},{3,7},{7,3},{8,12},{12,8},{9,1... | collective-permute-start | bytes 1038344 | tf_op jit(solution)/shard_map/ppermute | solution.py:10
  215.4 45.9 %collective-permute-start.4 = (f32[208,3,416]{2,0,1:T(8,128)S(1)}, f32[208,3,416]{2,0,1:T(8,128)S(1)}, u32[]{:S(2)}, u32[]{:S(2)}) collective-permute-start(f32[208,3,416]{2,0,1:T(8,128)S(1)} %pad_maximum_fusion.3), channel_id=1, source_target_pairs={{0,4},{4,0},{1,5},{5,1},{2,6},{6,2},{3,7},{7,3},{8,12},{12,8},{9,1... | collective-permute-start | bytes 3115016 | tf_op jit(solution)/shard_map/ppermute | solution.py:10
Sparse Core Ops, SparseCore 0:
  13.0 104.6 all-gather.4
  122.7 65.4 all-gather.2
